TPU v7x, 32 devices: a whole 2x2x4 slice. The times are simulated.
32 devices in a mesh: groups: 2 (over y), ctx: 4 (over z), mp: 4 (over x, core).
Axes of the slice: x: 2, y: 2, z: 4, core: 2. Of those that a mesh axis runs over, the one named last changes fastest.
Arguments:
- block_entry_input: bfloat16 [1536, 2048], P('mp', ('groups', 'ctx')), parts along dimension 1, may hold values from -6 to 6
- first_conv_taps: bfloat16 [3, 768, 1536], P(None, 'mp'), may hold values from -0.09375 to 0.09375
- first_pointwise_weight: bfloat16 [1536, 768], P(None, 'mp'), may hold values from -0.21875 to 0.21875
- second_conv_taps: bfloat16 [3, 768, 1536], P(None, 'mp'), may hold values from -0.09375 to 0.09375
- second_pointwise_weight: bfloat16 [1536, 768], P(None, 'mp'), may hold values from -0.21875 to 0.21875
- grad_heads: bfloat16 [8, 192, 2048], P('mp', 'ctx', 'groups'), parts along dimension 2, may hold values from -6 to 6
Outputs:
- second_block_output: bfloat16 [1536, 2048], P('mp', ('groups', 'ctx')), parts along dimension 1
- entry_input_gradient: bfloat16 [1536, 2048], P('mp', ('groups', 'ctx')), parts along dimension 1
- first_taps_gradient: float32 [6, 768, 1536], P('groups', 'mp', 'ctx'), parts along dimension 0
- first_projection_gradient: float32 [3072, 768], P(('groups', 'ctx'), 'mp'), parts along dimension 0
- second_taps_gradient: float32 [6, 768, 1536], P('groups', 'mp', 'ctx'), parts along dimension 0
- second_projection_gradient: float32 [3072, 768], P(('groups', 'ctx'), 'mp'), parts along dimension 0
There are 2 independent parts, one for each index of `groups`. A program takes and returns all parts, laid end to end along the dimension named above; an argument that names none is the same for every part. Nothing has to cross between parts.
All inputs are finite; a program needn't handle non-finite values.
Results may differ from a plain program's by a relative error of at most 0.034.
Values may be sent and summed in bfloat16 or wider, within the bound.
No kernel may reach another device: no remote copies, remote signals or barrier semaphores. Data moves between devices by JAX's collectives and lax.ppermute only.
A program may use at most 192 MiB of HBM per device.

v0:
```python
import jax
import jax.numpy as jnp
from jax import lax
from jax.sharding import PartitionSpec as P

FIRST_DILATION = 1024
SECOND_DILATION = 2048


def shifted(value, axis, by):
    length = lax.axis_size(axis)
    pairs = [(i, i + by) for i in range(length) if 0 <= i + by < length]
    return lax.ppermute(value, axis, pairs)


def gelu_slope(values):
    return jax.jvp(jax.nn.gelu, (values,), (jnp.ones_like(values),))[1]


def contract_first(left, right):
    return lax.dot_general(
        left, right, (((0,), (0,)), ((), ())), preferred_element_type=jnp.float32
    )


def contract_last(left, right):
    return lax.dot_general(
        left, right, (((1,), (1,)), ((), ())), preferred_element_type=jnp.float32
    )


def hop_steps(activations, dilation):
    return dilation // activations.shape[1]


def residual_block_forward(activations, conv_weight, point_weight, dilation):
    hop_count = hop_steps(activations, dilation)
    squash_part = jax.nn.gelu(activations.astype(jnp.float32)).astype(jnp.bfloat16)
    squashed = lax.all_gather(squash_part, "mp", axis=0, tiled=True)
    earlier = shifted(squashed, "ctx", hop_count)
    later = shifted(squashed, "ctx", -hop_count)
    pre_act = jnp.dot(conv_weight[0], earlier, preferred_element_type=jnp.float32)
    pre_act = pre_act + jnp.dot(conv_weight[1], squashed, preferred_element_type=jnp.float32)
    pre_act = pre_act + jnp.dot(conv_weight[2], later, preferred_element_type=jnp.float32)
    hidden = jax.nn.gelu(pre_act).astype(jnp.bfloat16)
    mixed = lax.psum_scatter(
        jnp.dot(point_weight, hidden, preferred_element_type=jnp.float32).astype(jnp.bfloat16),
        "mp",
        scatter_dimension=0,
        tiled=True,
    ).astype(jnp.float32)
    result = (activations.astype(jnp.float32) + mixed).astype(jnp.bfloat16)
    return (result, squashed, pre_act, hidden)


def residual_block_backward(
    incoming_gradient, activations, squashed, pre_act, hidden, conv_weight, point_weight, dilation
):
    hop_count = hop_steps(activations, dilation)
    upstream_full = lax.all_gather(incoming_gradient, "mp", axis=0, tiled=True)
    grad_hidden = contract_first(point_weight, upstream_full)
    grad_pre = (grad_hidden * gelu_slope(pre_act)).astype(jnp.bfloat16)
    grad_later = shifted(grad_pre, "ctx", -hop_count)
    grad_earlier = shifted(grad_pre, "ctx", hop_count)
    moved = (grad_later, grad_pre, grad_earlier)
    grad_conv = jnp.stack(
        [
            contract_last(moved[0], squashed),
            contract_last(moved[1], squashed),
            contract_last(moved[2], squashed),
        ]
    )
    grad_point = contract_last(upstream_full, hidden)
    total = contract_first(conv_weight[0], moved[0])
    total = total + contract_first(conv_weight[1], moved[1])
    grad_squash = lax.psum_scatter(
        (total + contract_first(conv_weight[2], moved[2])).astype(jnp.bfloat16),
        "mp",
        scatter_dimension=0,
        tiled=True,
    ).astype(jnp.float32)
    previous = (
        incoming_gradient.astype(jnp.float32)
        + grad_squash * gelu_slope(activations.astype(jnp.float32))
    ).astype(jnp.bfloat16)
    return (previous, grad_conv, grad_point)


def reduce_block(grad_conv, grad_point):
    return (
        lax.psum_scatter(
            grad_conv.astype(jnp.bfloat16), "ctx", scatter_dimension=2, tiled=True
        ).astype(jnp.float32),
        lax.psum_scatter(
            grad_point.astype(jnp.bfloat16), "ctx", scatter_dimension=0, tiled=True
        ).astype(jnp.float32),
    )


def shards(
    block_entry_input,
    first_conv_taps,
    first_pointwise_weight,
    second_conv_taps,
    second_pointwise_weight,
    grad_heads,
):
    regrouped = lax.all_to_all(grad_heads, "ctx", split_axis=2, concat_axis=1, tiled=True)
    incoming_gradient = regrouped.reshape(
        regrouped.shape[0] * regrouped.shape[1], regrouped.shape[2]
    )
    between_blocks_state, first_gelu_output, first_preactivation, first_hidden_state = (
        residual_block_forward(
            block_entry_input, first_conv_taps, first_pointwise_weight, FIRST_DILATION
        )
    )
    second_block_output, second_gelu_output, second_preactivation, second_hidden_state = (
        residual_block_forward(
            between_blocks_state, second_conv_taps, second_pointwise_weight, SECOND_DILATION
        )
    )
    incoming_gradient, conv_grad_b, point_grad_b = residual_block_backward(
        incoming_gradient,
        between_blocks_state,
        second_gelu_output,
        second_preactivation,
        second_hidden_state,
        second_conv_taps,
        second_pointwise_weight,
        SECOND_DILATION,
    )
    conv_grad_b, point_grad_b = reduce_block(conv_grad_b, point_grad_b)
    entry_input_gradient, conv_grad_a, point_grad_a = residual_block_backward(
        incoming_gradient,
        block_entry_input,
        first_gelu_output,
        first_preactivation,
        first_hidden_state,
        first_conv_taps,
        first_pointwise_weight,
        FIRST_DILATION,
    )
    conv_grad_a, point_grad_a = reduce_block(conv_grad_a, point_grad_a)
    return (
        second_block_output,
        entry_input_gradient,
        conv_grad_a,
        point_grad_a,
        conv_grad_b,
        point_grad_b,
    )


def solution(mesh):
    placed = (
        P("mp", ("groups", "ctx")),
        P(None, "mp", None),
        P(None, "mp"),
        P(None, "mp", None),
        P(None, "mp"),
        P("mp", "ctx", "groups"),
    )
    return jax.shard_map(
        shards,
        mesh=mesh,
        in_specs=placed,
        out_specs=(
            P("mp", ("groups", "ctx")),
            P("mp", ("groups", "ctx")),
            P("groups", "mp", "ctx"),
            P(("groups", "ctx"), "mp"),
            P("groups", "mp", "ctx"),
            P(("groups", "ctx"), "mp"),
        ),
        check_vma=False,
    )
```

profile of v0, /device:TPU:0, one launch (start us, length us, event | category | flops | bytes accessed | tf_op | source)
XLA Modules:
  0.0 296.0 jit_solution(17952154528425579025)
XLA Ops:
  7.2 1.2 fusion.62
  8.5 10.0 %all_gather.12 = bf16[1536,256]{1,0:T(8,128)(2,1)S(1)} all-gather(bf16[384,256]{1,0:T(8,128)(2,1)S(1)} %fusion.62), channel_id=1, replica_groups=mesh['groups'=2,'ctx'=4,'mp'=4] {'mp'}, dimensions={0}, use_global_device_ids=true | all-gather | bytes 983040 | tf_op jit(solution)/shard_map/all_gather | solution.py:39
  19.2 1.4 fusion.33
  22.1 1.2 copy.33
  23.3 24.3 %reduce-scatter.25.cloned.1.call-done = bf16[384,256]{1,0:T(8,128)(2,1)} async-done(((bf16[1536,256]{1,0:T(8,128)(2,1)}), bf16[384,256]{1,0:T(8,128)(2,1)}) %reduce-scatter.25.cloned.1.call-update) | async-done | bytes 196624 | tf_op jit(solution)/shard_map/reduce_scatter | solution.py:46
  47.6 1.1 fusion.71
  48.7 8.2 %all_gather.13 = bf16[1536,256]{1,0:T(8,128)(2,1)S(1)} all-gather(bf16[384,256]{1,0:T(8,128)(2,1)S(1)} %fusion.71), channel_id=1, replica_groups=mesh['groups'=2,'ctx'=4,'mp'=4] {'mp'}, dimensions={0}, use_global_device_ids=true | all-gather | bytes 983040 | tf_op jit(solution)/shard_map/all_gather | solution.py:39
  56.9 1.5 collective-permute-start.1
  58.8 1.5 reshape.35
  60.3 4.6 %all-to-all-start = ((bf16[4,2,12288]{2,1,0:T(2,128)(2,1)}), bf16[4,2,12288]{2,1,0:T(2,128)(2,1)}, u32[]{:S(2)}, u32[]{:S(2)}) async-start(bf16[4,2,12288]{2,1,0:T(2,128)(2,1)} %reshape.35), calls=%async_computation | async-start | bytes 393216 | tf_op jit(solution)/shard_map/all_to_all | solution.py:108
  64.9 1.4 fusion.23
  66.3 1.6 fusion.19
  68.0 1.6 fusion.16
  70.1 1.2 copy.35
  71.3 1.7 all-to-all-done
  73.0 1.4 reshape.36
  75.6 8.0 %all_gather.14 = bf16[1536,256]{1,0:T(8,128)(2,1)S(1)} all-gather(bf16[384,256]{1,0:T(8,128)(2,1)S(1)} %bitcast.104), channel_id=1, replica_groups=mesh['groups'=2,'ctx'=4,'mp'=4] {'mp'}, dimensions={0}, use_global_device_ids=true | all-gather | bytes 983040 | tf_op jit(solution)/shard_map/all_gather | solution.py:60
  86.1 1.2 copy.37
  87.3 1.7 fusion.12
  89.0 1.2 copy.47
  90.2 5.3 %reduce-scatter.27.cloned.1.call-done = bf16[384,256]{1,0:T(8,128)(2,1)} async-done(((bf16[1536,256]{1,0:T(8,128)(2,1)}), bf16[384,256]{1,0:T(8,128)(2,1)}) %reduce-scatter.27.cloned.1.call-update) | async-done | bytes 196624 | tf_op jit(solution)/shard_map/reduce_scatter | solution.py:46
  95.5 26.4 %reduce-scatter.29.cloned.1.call-done = bf16[384,256]{1,0:T(8,128)(2,1)} async-done(((bf16[1536,256]{1,0:T(8,128)(2,1)}), bf16[384,256]{1,0:T(8,128)(2,1)}) %reduce-scatter.29.cloned.1.call-update) | async-done | bytes 196624 | tf_op jit(solution)/shard_map/reduce_scatter | solution.py:76
  121.9 2.1 fusion.76
  124.1 8.2 %all_gather.15 = bf16[1536,256]{1,0:T(8,128)(2,1)S(1)} all-gather(bf16[384,256]{1,0:T(8,128)(2,1)S(1)} %get-tuple-element.24), channel_id=1, replica_groups=mesh['groups'=2,'ctx'=4,'mp'=4] {'mp'}, dimensions={0}, use_global_device_ids=true | all-gather | bytes 983040 | tf_op jit(solution)/shard_map/all_gather | solution.py:60
  132.3 1.2 convolution_convert_fusion.5
  133.5 2.2 copy.43
  135.8 1.5 fusion.88
  139.2 1.2 copy.39
  141.7 3.5 %copy.45 = bf16[3,192,1536]{1,0,2:T(4,128)(2,1)} copy(bf16[3,192,1536]{2,1,0:T(8,128)(2,1)S(1)} %pad_maximum_fusion.1) | data formatting | bytes 3538944
  145.3 7.0 %reshape.31 = bf16[1536,576]{1,0:T(8,128)(2,1)} reshape(bf16[1536,3,192]{2,1,0:T(4,128)(2,1)} %bitcast.98) | data formatting | bytes 3538944
  152.4 0.8 copy-done.16
  154.2 3.5 %copy.41 = bf16[3,192,1536]{1,0,2:T(4,128)(2,1)} copy(bf16[3,192,1536]{2,1,0:T(8,128)(2,1)S(1)} %pad_maximum_fusion) | data formatting | bytes 3538944
  157.8 7.1 %reshape.27 = bf16[1536,576]{1,0:T(8,128)(2,1)} reshape(bf16[1536,3,192]{2,1,0:T(4,128)(2,1)} %bitcast.99) | data formatting | bytes 3538944
  164.9 1.1 copy.48
  166.0 0.7 convert_element_type.137
  166.7 6.2 %reduce-scatter.35.cloned.1.call-done = bf16[384,192]{1,0:T(8,128)(2,1)} async-done(((bf16[1536,192]{1,0:T(8,128)(2,1)}), bf16[384,192]{1,0:T(8,128)(2,1)}) %reduce-scatter.35.cloned.1.call-update) | async-done | bytes 147472
  173.0 1.1 copy.44
  174.0 0.7 convert_element_type.133
  174.8 23.9 %reduce-scatter.31.cloned.1.call-done = bf16[384,256]{1,0:T(8,128)(2,1)} async-done(((bf16[1536,256]{1,0:T(8,128)(2,1)}), bf16[384,256]{1,0:T(8,128)(2,1)}) %reduce-scatter.31.cloned.1.call-update) | async-done | bytes 196624 | tf_op jit(solution)/shard_map/reduce_scatter | solution.py:76
  198.7 1.9 fusion.67
  200.6 41.9 %reduce-scatter.37.cloned.1.call-done = bf16[384,576]{1,0:T(8,128)(2,1)} async-done(((bf16[1536,576]{1,0:T(8,128)(2,1)}), bf16[384,576]{1,0:T(8,128)(2,1)}) %reduce-scatter.37.cloned.1.call-update) | async-done | bytes 442384
  242.5 1.8 reshape.32
  244.3 0.9 copy.46
  245.2 1.0 convert_element_type.134
  246.1 39.4 %reduce-scatter.33.cloned.1.call-done = bf16[384,576]{1,0:T(8,128)(2,1)} async-done(((bf16[1536,576]{1,0:T(8,128)(2,1)}), bf16[384,576]{1,0:T(8,128)(2,1)}) %reduce-scatter.33.cloned.1.call-update) | async-done | bytes 442384
  285.5 1.8 reshape.28
  287.3 0.9 copy.42
  288.2 1.0 convert_element_type.131
  (79 shorter events, 11.0 us)
Async XLA Ops:
  7.2 62.5 %copy-start = (bf16[1536,192]{0,1:T(8,128)(2,1)S(1)}, bf16[1536,192]{0,1:T(8,128)(2,1)}, u32[]{:S(2)}) copy-start(bf16[1536,192]{0,1:T(8,128)(2,1)} %param.10) | copy-start | bytes 1769476
  7.2 13.4 %copy-start.2 = (bf16[3,192,1536]{2,1,0:T(8,128)(2,1)S(1)}, bf16[3,192,1536]{2,1,0:T(8,128)(2,1)}, u32[]{:S(2)}) copy-start(bf16[3,192,1536]{2,1,0:T(8,128)(2,1)} %param.7) | copy-start | bytes 5308420
  7.2 40.4 %reduce-scatter.25.cloned.1.call-start = ((), (), s32[]{:S(2)}) async-start(), calls=%async_computation.9 | async-start | bytes 983040 | tf_op jit(solution)/shard_map/reduce_scatter | solution.py:46
  18.5 2.1 collective-permute-start
  20.6 1.1 copy-start.12
  21.7 25.9 %copy-start.5 = (bf16[384,256]{1,0:T(8,128)(2,1)S(1)}, bf16[384,256]{1,0:T(8,128)(2,1)}, u32[]{:S(2)}) copy-start(bf16[384,256]{1,0:T(8,128)(2,1)} %param.6) | copy-start | bytes 589828
  22.1 36.3 %copy-start.17 = (bf16[2,48,1024]{2,1,0:T(8,128)(2,1)S(1)}, bf16[2,48,1024]{2,1,0:T(8,128)(2,1)}, u32[]{:S(2)}) copy-start(bf16[2,48,1024]{2,1,0:T(8,128)(2,1)} %param.11) | copy-start | bytes 589828
  56.9 9.4 %collective-permute-start.1 = (bf16[1536,256]{1,0:T(8,128)(2,1)S(1)}, bf16[1536,256]{1,0:T(8,128)(2,1)}, u32[]{:S(2)}, u32[]{:S(2)}) collective-permute-start(bf16[1536,256]{1,0:T(8,128)(2,1)S(1)} %all_gather.13), channel_id=1, source_target_pairs={} | collective-permute-start | bytes 2359304 | tf_op jit(solution)/shard_map/ppermute | solution.py:13
  60.3 12.7 %all-to-all-start = ((bf16[4,2,12288]{2,1,0:T(2,128)(2,1)}), bf16[4,2,12288]{2,1,0:T(2,128)(2,1)}, u32[]{:S(2)}, u32[]{:S(2)}) async-start(bf16[4,2,12288]{2,1,0:T(2,128)(2,1)} %reshape.35), calls=%async_computation | async-start | bytes 393216 | tf_op jit(solution)/shard_map/all_to_all | solution.py:108
  64.9 30.6 %reduce-scatter.27.cloned.1.call-start = ((), (), s32[]{:S(2)}) async-start(), calls=%async_computation.10 | async-start | bytes 983040 | tf_op jit(solution)/shard_map/reduce_scatter | solution.py:46
  71.2 50.7 %reduce-scatter.29.cloned.1.call-start = ((), (), s32[]{:S(2)}) async-start(), calls=%async_computation.11 | async-start | bytes 983040 | tf_op jit(solution)/shard_map/reduce_scatter | solution.py:76
  74.9 9.7 %copy-start.1 = (bf16[3,192,1536]{2,1,0:T(8,128)(2,1)S(1)}, bf16[3,192,1536]{2,1,0:T(8,128)(2,1)}, u32[]{:S(2)}) copy-start(bf16[3,192,1536]{2,1,0:T(8,128)(2,1)} %param.9) | copy-start | bytes 5308420
  74.9 0.7 copy-start.8
  83.6 1.4 copy-start.4
  83.9 1.1 copy-start.13
  83.9 1.1 collective-permute-start.2
  85.0 0.6 copy-start.10
  87.3 34.7 %copy-start.9 = (bf16[2,4,48,256]{3,2,1,0:T(8,128)(2,1)S(1)}, bf16[2,4,48,256]{3,2,1,0:T(8,128)(2,1)}, u32[]{:S(2)}) copy-start(bf16[2,4,48,256]{3,2,1,0:T(8,128)(2,1)} %copy-done.8) | copy-start | bytes 589828
  87.3 77.6 %reduce-scatter.39.cloned.1.call-start = ((), (), s32[]{:S(2)}) async-start(), calls=%async_computation.16 | async-start | bytes 983040
  90.2 82.8 %reduce-scatter.35.cloned.1.call-start = ((), (), s32[]{:S(2)}) async-start(), calls=%async_computation.14 | async-start | bytes 983040
  124.1 11.7 %copy-start.6 = (bf16[384,256]{1,0:T(8,128)(2,1)}, bf16[384,256]{1,0:T(8,128)(2,1)S(1)}, u32[]{:S(2)}) copy-start(bf16[384,256]{1,0:T(8,128)(2,1)S(1)} %get-tuple-element.24) | copy-start | bytes 589828
  135.7 62.9 %reduce-scatter.31.cloned.1.call-start = ((), (), s32[]{:S(2)}) async-start(), calls=%async_computation.12 | async-start | bytes 983040 | tf_op jit(solution)/shard_map/reduce_scatter | solution.py:76
  135.8 2.2 copy-start.3
  137.3 1.5 copy-start.15
  137.3 1.1 collective-permute-start.3
  139.2 1.4 copy-start.14
  139.2 1.9 copy-start.11
  140.4 102.1 %reduce-scatter.37.cloned.1.call-start = ((), (), s32[]{:S(2)}) async-start(), calls=%async_computation.15 | async-start | bytes 2457600
  152.3 0.9 copy-start.16
  152.3 133.2 %reduce-scatter.33.cloned.1.call-start = ((), (), s32[]{:S(2)}) async-start(), calls=%async_computation.13 | async-start | bytes 2457600
  164.8 33.8 %copy-start.7 = (bf16[384,256]{1,0:T(8,128)(2,1)S(1)}, bf16[384,256]{1,0:T(8,128)(2,1)}, u32[]{:S(2)}) copy-start(bf16[384,256]{1,0:T(8,128)(2,1)} %copy-done.6) | copy-start | bytes 589828
Sparse Core Ops, SparseCore 0:
  23.4 24.1 reduce-scatter.24
  71.4 24.1 reduce-scatter.26
  98.6 23.2 reduce-scatter.28
  124.2 23.3 reduce-scatter.38
  150.4 22.5 reduce-scatter.34
  176.1 22.5 reduce-scatter.30
  201.0 41.4 reduce-scatter.36
  244.8 40.6 reduce-scatter.32
where the time goes:
time: 297 us; the launch traced here: 296 us
  waiting for transfers between devices  169 us (57%)
  local copies, waits for them, and re-layouts  42.7 us (14%)
  blocking collectives  34.5 us (12%)
  matrix products  16.2 us (5%)
  between operations  14.6 us (5%)
  other arithmetic  10.2 us (3%)
  starting transfers between devices  8.6 us (3%)
    unnamed x12, waiting for transfers between devices  87.6 us
    reduce_scatter x2, waiting for transfers between devices, residual_block_backward(): lax.psum_scatter((total + contract_first(conv_weight[2], moved[2])).astyp...  50.3 us
    unnamed x55, local copies, waits for them, and re-layouts  42.3 us
    reduce_scatter x2, waiting for transfers between devices, residual_block_forward(): lax.psum_scatter(jnp.dot(point_weight, hidden, preferred_element_type=jnp...  29.6 us
    all_gather x2, blocking collectives, residual_block_forward(): squashed = lax.all_gather(squash_part, 'mp', axis=0, tiled=True)  18.3 us
    all_gather x2, blocking collectives, residual_block_backward(): upstream_full = lax.all_gather(incoming_gradient, 'mp', axis=0, tiled=True)  16.2 us
  transfers between devices with their start and end apart: 13, of which 8 were waited for; matrix products, arithmetic and copies ran while one was open for 20% of the time, Pallas kernels for 0%

commit v1 on v0

--- a/solution.py
+++ b/solution.py
@@ -1,10 +1,16 @@
 import jax
 import jax.numpy as jnp
 from jax import lax
+from jax.experimental import pallas as pl
+from jax.experimental.pallas import tpu as pltpu
 from jax.sharding import PartitionSpec as P
 
 FIRST_DILATION = 1024
 SECOND_DILATION = 2048
+F32 = jnp.float32
+BF16 = jnp.bfloat16
+ROOT = 0.7978845608028654
+CUBIC = 0.044715
 
 
 def shifted(value, axis, by):
@@ -63,13 +69,7 @@
     grad_later = shifted(grad_pre, "ctx", -hop_count)
     grad_earlier = shifted(grad_pre, "ctx", hop_count)
     moved = (grad_later, grad_pre, grad_earlier)
-    grad_conv = jnp.stack(
-        [
-            contract_last(moved[0], squashed),
-            contract_last(moved[1], squashed),
-            contract_last(moved[2], squashed),
-        ]
-    )
+    grad_conv = jnp.stack([contract_last(part, squashed) for part in moved])
     grad_point = contract_last(upstream_full, hidden)
     total = contract_first(conv_weight[0], moved[0])
     total = total + contract_first(conv_weight[1], moved[1])
@@ -97,73 +97,341 @@
     )
 
 
-def shards(
-    block_entry_input,
-    first_conv_taps,
-    first_pointwise_weight,
-    second_conv_taps,
-    second_pointwise_weight,
-    grad_heads,
-):
+def general_shards(x, taps_a, point_a, taps_b, point_b, grad_heads):
     regrouped = lax.all_to_all(grad_heads, "ctx", split_axis=2, concat_axis=1, tiled=True)
-    incoming_gradient = regrouped.reshape(
-        regrouped.shape[0] * regrouped.shape[1], regrouped.shape[2]
-    )
-    between_blocks_state, first_gelu_output, first_preactivation, first_hidden_state = (
-        residual_block_forward(
-            block_entry_input, first_conv_taps, first_pointwise_weight, FIRST_DILATION
+    gradient = regrouped.reshape(regrouped.shape[0] * regrouped.shape[1], regrouped.shape[2])
+    middle, z_a, u_a, v_a = residual_block_forward(x, taps_a, point_a, FIRST_DILATION)
+    result, z_b, u_b, v_b = residual_block_forward(middle, taps_b, point_b, SECOND_DILATION)
+    gradient, conv_b, proj_b = residual_block_backward(
+        gradient, middle, z_b, u_b, v_b, taps_b, point_b, SECOND_DILATION
+    )
+    conv_b, proj_b = reduce_block(conv_b, proj_b)
+    gradient, conv_a, proj_a = residual_block_backward(
+        gradient, x, z_a, u_a, v_a, taps_a, point_a, FIRST_DILATION
+    )
+    conv_a, proj_a = reduce_block(conv_a, proj_a)
+    return result, gradient, conv_a, proj_a, conv_b, proj_b
+
+
+def swap(value, axis, bits):
+    size = lax.axis_size(axis)
+    return lax.ppermute(value, axis, [(i, i ^ bits) for i in range(size)])
+
+
+def dot(left, right, dims=((1,), (0,))):
+    return lax.dot_general(left, right, (dims, ((), ())), preferred_element_type=F32)
+
+
+def gelu(s):
+    return 0.5 * s * (1.0 + jnp.tanh(ROOT * (s + CUBIC * (s * s * s))))
+
+
+def gelu_and_slope(s):
+    sq = s * s
+    t = jnp.tanh(ROOT * (s + CUBIC * (s * sq)))
+    half = 0.5 * (1.0 + t)
+    slope = half + 0.5 * s * (1.0 - t * t) * (ROOT * (1.0 + 3.0 * CUBIC * sq))
+    return s * half, slope
+
+
+def slope_of(s):
+    return gelu_and_slope(s)[1]
+
+
+def call(body, outs, args, name, specs=None, scratch=()):
+    return pl.pallas_call(
+        body,
+        out_shape=[jax.ShapeDtypeStruct(s, d) for s, d in outs],
+        in_specs=specs or [whole(a.shape) for a in args],
+        out_specs=[whole(s) for s, _ in outs],
+        grid=(1,),
+        scratch_shapes=scratch,
+        name=name,
+    )(*args)
+
+
+def whole(shape):
+    return pl.BlockSpec(shape, lambda _: (0,) * len(shape))
+
+
+def fast_shards(x, taps_a, point_a, taps_b, point_b, grad_heads):
+    rows, bins = x.shape
+    hid, chans = taps_a.shape[1], taps_a.shape[2]
+    heads, val, _ = grad_heads.shape
+    tap = pl.BlockSpec((None, hid, chans), lambda _: (1, 0, 0))
+    tile = whole((rows, bins))
+    pair = whole((2, rows, bins))
+    point = whole(point_a.shape)
+
+    def block(m, j):
+        return pl.ds(pl.multiple_of((m ^ j) * rows, rows), rows)
+
+    def split_body(g_ref, *outs):
+        c = lax.axis_index("ctx")
+        for k in range(4):
+            outs[k][...] = g_ref[:, :, pl.ds(pl.multiple_of((c ^ k) * bins, bins), bins)]
+
+    pieces = call(split_body, [((heads, val, bins), BF16)] * 4, (grad_heads,), "split_grad")
+    pieces = [pieces[0]] + [swap(pieces[k], "ctx", k) for k in (1, 2, 3)]
+
+    def join_body(*refs):
+        c = lax.axis_index("ctx")
+        out = refs[4]
+        for k in range(4):
+            out[:, c ^ k] = refs[k][...]
+
+    (g_own,) = call(join_body, [((heads, 4, val, bins), BF16)], pieces, "join_grad")
+    g_own = g_own.reshape(rows, bins)
+    g_far = swap(g_own, "mp", 2)
+    g_near = swap(g_own, "mp", 1)
+    g_cross = swap(g_far, "mp", 1)
+
+    x_far = swap(x, "mp", 2)
+    x_near = swap(x, "mp", 1)
+    x_cross = swap(x_far, "mp", 1)
+
+    def first_body(x0, x1, x2, x3, k_ref, p_ref, z_ref, v_ref, s_ref, keep_ref, send_ref):
+        m = lax.axis_index("mp")
+        u = jnp.zeros((hid, bins), F32)
+        for j, ref in enumerate((x0, x1, x2, x3)):
+            z = gelu(ref[...].astype(F32)).astype(BF16)
+            z_ref[j] = z
+            u = u + dot(k_ref[:, block(m, j)], z)
+        v, slope = gelu_and_slope(u)
+        v = v.astype(BF16)
+        v_ref[...] = v
+        s_ref[...] = slope
+        for i, j in enumerate((1, 3)):
+            send_ref[i] = dot(p_ref[block(m, j), :], v).astype(BF16)
+        for i, j in enumerate((0, 2)):
+            keep_ref[i] = dot(p_ref[block(m, j), :], v)
+
+    z_a, v_a, slope_a, keep, send = call(
+        first_body,
+        [
+            ((4, rows, bins), BF16),
+            ((hid, bins), BF16),
+            ((hid, bins), F32),
+            ((2, rows, bins), F32),
+            ((2, rows, bins), BF16),
+        ],
+        (x, x_near, x_far, x_cross, taps_a, point_a),
+        "first_forward",
+        [tile, tile, tile, tile, tap, point],
+    )
+    got = swap(send, "mp", 1)
+
+    def near_body(keep_ref, got_ref, out_ref):
+        out_ref[...] = (keep_ref[...] + got_ref[...].astype(F32)).astype(BF16)
+
+    def near_sum(keep, got, name):
+        return call(near_body, [((2, rows, bins), BF16)], (keep, got), name)[0]
+
+    chip = near_sum(keep, got, "mix_sum")
+    other = swap(chip, "mp", 2)
+
+    def middle_body(x0, x2, chip_ref, other_ref, out_ref):
+        for i, ref in enumerate((x0, x2)):
+            mixed = chip_ref[i].astype(F32) + other_ref[1 - i].astype(F32)
+            out_ref[i] = (ref[...].astype(F32) + mixed).astype(BF16)
+
+    (mid,) = call(
+        middle_body, [((2, rows, bins), BF16)], (x, x_far, chip, other), "middle"
+    )
+    mid_near = swap(mid, "mp", 1)
+
+    def second_body(
+        a_ref, b_ref, g0, g1, g2, g3, k_ref, p_ref,
+        z_ref, v_ref, gu_ref, keep_ref, send_ref, ykeep_ref, ysend_ref,
+    ):
+        m = lax.axis_index("mp")
+        u = jnp.zeros((hid, bins), F32)
+        for j in range(4):
+            part = (a_ref, b_ref)[j & 1][j >> 1]
+            z = gelu(part.astype(F32)).astype(BF16)
+            z_ref[j] = z
+            u = u + dot(k_ref[:, block(m, j)], z)
+        v, slope = gelu_and_slope(u)
+        v = v.astype(BF16)
+        v_ref[...] = v
+        gv = jnp.zeros((hid, bins), F32)
+        for j, ref in enumerate((g0, g1, g2, g3)):
+            gv = gv + dot(p_ref[block(m, j), :], ref[...], ((0,), (0,)))
+        gu = (gv * slope).astype(BF16)
+        gu_ref[...] = gu
+        for i, j in enumerate((1, 3)):
+            send_ref[i] = dot(k_ref[:, block(m, j)], gu, ((0,), (0,))).astype(BF16)
+        for i, j in enumerate((0, 2)):
+            keep_ref[i] = dot(k_ref[:, block(m, j)], gu, ((0,), (0,)))
+        for i, j in enumerate((1, 3)):
+            ysend_ref[i] = dot(p_ref[block(m, j), :], v).astype(BF16)
+        for i, j in enumerate((0, 2)):
+            ykeep_ref[i] = dot(p_ref[block(m, j), :], v)
+
+    z_b, v_b, gu_b, keep, send, ykeep, ysend = call(
+        second_body,
+        [
+            ((4, rows, bins), BF16),
+            ((hid, bins), BF16),
+            ((hid, bins), BF16),
+            ((2, rows, bins), F32),
+            ((2, rows, bins), BF16),
+            ((2, rows, bins), F32),
+            ((2, rows, bins), BF16),
+        ],
+        (mid, mid_near, g_own, g_near, g_far, g_cross, taps_b, point_b),
+        "second_block",
+        [pair, pair, tile, tile, tile, tile, tap, point],
+    )
+    got = swap(send, "mp", 1)
+    chip = near_sum(keep, got, "squash_sum")
+    other = swap(chip, "mp", 2)
+
+    def back_body(g0, g2, mid_ref, chip_ref, other_ref, out_ref):
+        for i, ref in enumerate((g0, g2)):
+            grad = chip_ref[i].astype(F32) + other_ref[1 - i].astype(F32)
+            out_ref[i] = (
+                ref[...].astype(F32) + grad * slope_of(mid_ref[i].astype(F32))
+            ).astype(BF16)
+
+    (g_mid,) = call(
+        back_body, [((2, rows, bins), BF16)], (g_own, g_far, mid, chip, other), "middle_grad"
+    )
+    g_mid_near = swap(g_mid, "mp", 1)
+
+    ygot = swap(ysend, "mp", 1)
+
+    def last_sum_body(keep_ref, got_ref, own_ref, send_ref):
+        own_ref[...] = keep_ref[0] + got_ref[0].astype(F32)
+        send_ref[...] = (keep_ref[1] + got_ref[1].astype(F32)).astype(BF16)
+
+    def last_sum(keep, got, name):
+        return call(
+            last_sum_body, [((rows, bins), F32), ((rows, bins), BF16)], (keep, got), name
         )
-    )
-    second_block_output, second_gelu_output, second_preactivation, second_hidden_state = (
-        residual_block_forward(
-            between_blocks_state, second_conv_taps, second_pointwise_weight, SECOND_DILATION
+
+    y_own, y_send = last_sum(ykeep, ygot, "out_sum")
+    y_got = swap(y_send, "mp", 2)
+
+    def out_body(mid_ref, own_ref, got_ref, out_ref):
+        mixed = own_ref[...] + got_ref[...].astype(F32)
+        out_ref[...] = (mid_ref[0].astype(F32) + mixed).astype(BF16)
+
+    (second_out,) = call(out_body, [((rows, bins), BF16)], (mid, y_own, y_got), "out")
+
+    def first_back_body(a_ref, b_ref, k_ref, p_ref, s_ref, gu_ref, keep_ref, send_ref):
+        m = lax.axis_index("mp")
+        gv = jnp.zeros((hid, bins), F32)
+        for j in range(4):
+            part = (a_ref, b_ref)[j & 1][j >> 1]
+            gv = gv + dot(p_ref[block(m, j), :], part, ((0,), (0,)))
+        gu = (gv * s_ref[...]).astype(BF16)
+        gu_ref[...] = gu
+        for i, j in enumerate((1, 3)):
+            send_ref[i] = dot(k_ref[:, block(m, j)], gu, ((0,), (0,))).astype(BF16)
+        for i, j in enumerate((0, 2)):
+            keep_ref[i] = dot(k_ref[:, block(m, j)], gu, ((0,), (0,)))
+
+    gu_a, keep, send = call(
+        first_back_body,
+        [((hid, bins), BF16), ((2, rows, bins), F32), ((2, rows, bins), BF16)],
+        (g_mid, g_mid_near, taps_a, point_a, slope_a),
+        "first_backward",
+        [pair, pair, tap, point, whole((hid, bins))],
+    )
+    got = swap(send, "mp", 1)
+    e_own, e_send = last_sum(keep, got, "entry_sum")
+    e_got = swap(e_send, "mp", 2)
+
+    def entry_body(g_ref, x_ref, own_ref, got_ref, out_ref):
+        grad = own_ref[...] + got_ref[...].astype(F32)
+        out_ref[...] = (
+            g_ref[0].astype(F32) + grad * slope_of(x_ref[...].astype(F32))
+        ).astype(BF16)
+
+    (entry,) = call(entry_body, [((rows, bins), BF16)], (g_mid, x, e_own, e_got), "entry")
+
+    def weight_body(z_ref, gu_ref, v_ref, g0, g1, g2, g3, own_ref, *rest):
+        outs, g_ref = rest[:3], rest[3]
+        m = lax.axis_index("mp")
+        c = lax.axis_index("ctx")
+        for j, ref in enumerate((g0, g1, g2, g3)):
+            g_ref[j] = ref[...]
+        for k in (1, 2, 3, 0):
+            j = m ^ c ^ k
+            taps = dot(gu_ref[...], z_ref[j], ((1,), (1,)))
+            proj = dot(v_ref[...], g_ref[j], ((1,), (1,)))
+            out = own_ref if k == 0 else outs[k - 1]
+            out[:hid, :] = taps.astype(out.dtype)
+            out[hid:, :] = proj.astype(out.dtype)
+
+    def weights(z, gu, v, grads, specs, name):
+        own, *sends = call(
+            weight_body,
+            [((2 * hid, rows), F32)] + [((2 * hid, rows), BF16)] * 3,
+            (z, gu, v, *grads),
+            name,
+            [whole(z.shape), whole(gu.shape), whole(v.shape), *specs],
+            [pltpu.VMEM((4, rows, bins), BF16)],
         )
-    )
-    incoming_gradient, conv_grad_b, point_grad_b = residual_block_backward(
-        incoming_gradient,
-        between_blocks_state,
-        second_gelu_output,
-        second_preactivation,
-        second_hidden_state,
-        second_conv_taps,
-        second_pointwise_weight,
-        SECOND_DILATION,
-    )
-    conv_grad_b, point_grad_b = reduce_block(conv_grad_b, point_grad_b)
-    entry_input_gradient, conv_grad_a, point_grad_a = residual_block_backward(
-        incoming_gradient,
-        block_entry_input,
-        first_gelu_output,
-        first_preactivation,
-        first_hidden_state,
-        first_conv_taps,
-        first_pointwise_weight,
-        FIRST_DILATION,
-    )
-    conv_grad_a, point_grad_a = reduce_block(conv_grad_a, point_grad_a)
-    return (
-        second_block_output,
-        entry_input_gradient,
-        conv_grad_a,
-        point_grad_a,
-        conv_grad_b,
-        point_grad_b,
-    )
+        gots = [swap(part, "ctx", k + 1) for k, part in enumerate(sends)]
+
+        def total_body(own_ref, r1, r2, r3, taps_ref, proj_ref):
+            def total(part):
+                return own_ref[part, :] + (
+                    r1[part, :].astype(F32) + r2[part, :].astype(F32) + r3[part, :].astype(F32)
+                )
+
+            taps_ref[0] = jnp.zeros((hid, rows), F32)
+            taps_ref[1] = total(pl.ds(0, hid))
+            taps_ref[2] = jnp.zeros((hid, rows), F32)
+            proj_ref[...] = total(pl.ds(hid, hid)).T
+
+        return call(
+            total_body,
+            [((3, hid, rows), F32), ((rows, hid), F32)],
+            (own, *gots),
+            name + "_total",
+        )
+
+    taps_b_grad, point_b_grad = weights(
+        z_b, gu_b, v_b, (g_own, g_near, g_far, g_cross), [tile] * 4, "second_weights"
+    )
+    upper = [pl.BlockSpec((None, rows, bins), lambda _, i=i: (i, 0, 0)) for i in (0, 1)]
+    taps_a_grad, point_a_grad = weights(
+        z_a,
+        gu_a,
+        v_a,
+        (g_mid, g_mid_near, g_mid, g_mid_near),
+        [upper[0], upper[0], upper[1], upper[1]],
+        "first_weights",
+    )
+    return second_out, entry, taps_a_grad, point_a_grad, taps_b_grad, point_b_grad
 
 
 def solution(mesh):
-    placed = (
-        P("mp", ("groups", "ctx")),
-        P(None, "mp", None),
-        P(None, "mp"),
-        P(None, "mp", None),
-        P(None, "mp"),
-        P("mp", "ctx", "groups"),
-    )
+    sizes = dict(mesh.shape)
+
+    def shards(x, *rest):
+        span = x.shape[1] * sizes["ctx"]
+        fast = (
+            min(FIRST_DILATION, SECOND_DILATION) >= span
+            and sizes["mp"] == 4
+            and sizes["ctx"] == 4
+        )
+        return (fast_shards if fast else general_shards)(x, *rest)
+
     return jax.shard_map(
         shards,
         mesh=mesh,
-        in_specs=placed,
+        in_specs=(
+            P("mp", ("groups", "ctx")),
+            P(None, "mp", None),
+            P(None, "mp"),
+            P(None, "mp", None),
+            P(None, "mp"),
+            P("mp", "ctx", "groups"),
+        ),
         out_specs=(
             P("mp", ("groups", "ctx")),
             P("mp", ("groups", "ctx")),

time: 297 us -> 140 us (0.47)
  the two profiles are of different devices: /device:TPU:0 before, /device:TPU:8 now
where the time goes in v1:
time: 140 us; the launch traced here: 139 us
  waiting for transfers between devices  54.9 us (39%)
  Pallas kernels  44.5 us (32%)
  starting transfers between devices  22 us (16%)
  local copies, waits for them, and re-layouts  16.8 us (12%)
    ppermute x25, waiting for transfers between devices, swap(): return lax.ppermute(value, axis, [(i, i ^ bits) for i in range(size)])  54.9 us
    pallas_call x17, Pallas kernels, call(): pl.pallas_call(body, out_shape=[jax.ShapeDtypeStruct(s, d) for s, d in ou...  44.5 us
    ppermute x25, starting transfers between devices, swap(): return lax.ppermute(value, axis, [(i, i ^ bits) for i in range(size)])  22 us
    unnamed x62, local copies, waits for them, and re-layouts  16.8 us
  transfers between devices with their start and end apart: 25, of which 12 were waited for; matrix products, arithmetic and copies ran while one was open for 5% of the time, Pallas kernels for 19%

profile of v1, /device:TPU:8, one launch (start us, length us, event | category | flops | bytes accessed | tf_op | source)
XLA Modules:
  0.0 138.9 jit_solution(11388515847056372034)
XLA Ops:
  0.6 1.6 %collective-permute-start = (bf16[384,256]{1,0:T(8,128)(2,1)}, bf16[384,256]{1,0:T(8,128)(2,1)S(1)}, u32[]{:S(2)}, u32[]{:S(2)}) collective-permute-start(bf16[384,256]{1,0:T(8,128)(2,1)} %x_ref.1), channel_id=1, source_target_pairs={{0,2},{1,3},{2,0},{3,1},{4,6},{5,7},{6,4},{7,5},{8,10},{9,11},{10,... | collective-permute-start | bytes 589832 | tf_op jit(solution)/shard_map/ppermute | solution.py:118
  2.2 5.4 %collective-permute-done.x2 = bf16[384,256]{1,0:T(8,128)(2,1)S(1)} collective-permute-done((bf16[384,256]{1,0:T(8,128)(2,1)}, bf16[384,256]{1,0:T(8,128)(2,1)S(1)}, u32[]{:S(2)}, u32[]{:S(2)}) %collective-permute-start) | collective-permute-done | bytes 196640 | tf_op jit(solution)/shard_map/ppermute | solution.py:118
  7.6 2.3 %copy.12.p_ref = bf16[1536,192]{1,0:T(8,128)(2,1)} copy(bf16[1536,192]{0,1:T(8,128)(2,1)} %param.8) | data formatting | bytes 1179648 | tf_op args[2]
  11.2 4.0 %first_forward.1 = (bf16[4,384,256]{2,1,0:T(8,128)(2,1)}, bf16[192,256]{1,0:T(8,128)(2,1)}, f32[192,256]{1,0:T(8,128)}, f32[2,384,256]{2,1,0:T(8,128)}, bf16[2,384,256]{2,1,0:T(8,128)(2,1)}) custom-call(bf16[384,256]{1,0:T(8,128)(2,1)} %x_ref.1, bf16[384,256]{1,0:T(8,128)(2,1)} %copy-done.20, bf16[384,256]{1,0:T(8,128)(2,1)} %copy-done.4, ...), custom_call_target="tpu_custom_call" | custom-call | tf_op jit(solution)/shard_map/first_forward/pallas_call | solution.py:142
  15.7 1.6 %collective-permute-done.3.got_ref = bf16[2,384,256]{2,1,0:T(8,128)(2,1)S(1)} collective-permute-done((bf16[2,384,256]{2,1,0:T(8,128)(2,1)}, bf16[2,384,256]{2,1,0:T(8,128)(2,1)S(1)}, u32[]{:S(2)}, u32[]{:S(2)}) %collective-permute-start.3) | collective-permute-done | bytes 393248 | tf_op jit(solution)/shard_map/ppermute | solution.py:118
  17.2 0.7 copy-done.9
  18.0 2.1 %mix_sum.1.chip_ref = bf16[2,384,256]{2,1,0:T(8,128)(2,1)} custom-call(f32[2,384,256]{2,1,0:T(8,128)} %get-tuple-element.41.keep_ref, bf16[2,384,256]{2,1,0:T(8,128)(2,1)} %copy-done.9), custom_call_target="tpu_custom_call" | custom-call | tf_op jit(solution)/shard_map/mix_sum/pallas_call | solution.py:142
  20.1 1.5 %collective-permute-start.4 = (bf16[2,384,256]{2,1,0:T(8,128)(2,1)}, bf16[2,384,256]{2,1,0:T(8,128)(2,1)S(1)}, u32[]{:S(2)}, u32[]{:S(2)}) collective-permute-start(bf16[2,384,256]{2,1,0:T(8,128)(2,1)} %mix_sum.1.chip_ref), channel_id=1, source_target_pairs={{0,2},{1,3},{2,0},{3,1},{4,6},{5,7},{6,4},{7,5},{8,10},{9,11},{10,... | collective-permute-start | bytes 1179656 | tf_op jit(solution)/shard_map/ppermute | solution.py:118
  21.6 1.6 %split_grad.1 = (bf16[2,48,256]{2,1,0:T(8,128)(2,1)}, bf16[2,48,256]{2,1,0:T(8,128)(2,1)}, bf16[2,48,256]{2,1,0:T(8,128)(2,1)}, bf16[2,48,256]{2,1,0:T(8,128)(2,1)}) custom-call(bf16[2,48,1024]{2,1,0:T(8,128)(2,1)} %g_ref.1), custom_call_target="tpu_custom_call" | custom-call | tf_op jit(solution)/shard_map/split_grad/pallas_call | solution.py:142
  23.6 2.6 %collective-permute-start.7 = (bf16[2,48,256]{2,1,0:T(8,128)(2,1)}, bf16[2,48,256]{2,1,0:T(8,128)(2,1)S(1)}, u32[]{:S(2)}, u32[]{:S(2)}) collective-permute-start(bf16[2,48,256]{2,1,0:T(8,128)(2,1)} %get-tuple-element.45), channel_id=1, source_target_pairs={{0,8},{4,12},{8,0},{12,4},{1,9},{5,13},{9,1},{13,5},{2,10},{6,14},... | collective-permute-start | bytes 147464 | tf_op jit(solution)/shard_map/ppermute | solution.py:118
  26.7 0.8 collective-permute-done.6.refs_1_
  27.5 2.7 %collective-permute-done.7.refs_2_ = bf16[2,48,256]{2,1,0:T(8,128)(2,1)S(1)} collective-permute-done((bf16[2,48,256]{2,1,0:T(8,128)(2,1)}, bf16[2,48,256]{2,1,0:T(8,128)(2,1)S(1)}, u32[]{:S(2)}, u32[]{:S(2)}) %collective-permute-start.7) | collective-permute-done | bytes 49184 | tf_op jit(solution)/shard_map/ppermute | solution.py:118
  31.3 1.6 %join_grad.1 = bf16[2,4,48,256]{3,2,1,0:T(8,128)(2,1)} custom-call(bf16[2,48,256]{2,1,0:T(8,128)(2,1)} %get-tuple-element.43.refs_0_, bf16[2,48,256]{2,1,0:T(8,128)(2,1)} %copy-done.23, bf16[2,48,256]{2,1,0:T(8,128)(2,1)} %copy-done.24, bf16[2,48,256]{2,1,0:T(8,128)(2,1)} %copy-done.25), custom_call_target="tpu_custom_call" | custom-call | tf_op jit(solution)/shard_map/join_grad/pallas_call | solution.py:142
  33.4 0.7 copy-done.8
  34.1 2.2 %middle.1.a_ref.mid_ref = bf16[2,384,256]{2,1,0:T(8,128)(2,1)} custom-call(bf16[384,256]{1,0:T(8,128)(2,1)} %x_ref.1, bf16[384,256]{1,0:T(8,128)(2,1)} %copy-done.4, bf16[2,384,256]{2,1,0:T(8,128)(2,1)} %mix_sum.1.chip_ref, bf16[2,384,256]{2,1,0:T(8,128)(2,1)} %copy-done.8), custom_call_target="tpu_custom_call" | custom-call | tf_op jit(solution)/shard_map/middle/pallas_call | solution.py:142
  36.9 2.5 %collective-permute-done.10.g2 = bf16[384,256]{1,0:T(8,128)(2,1)S(1)} collective-permute-done((bf16[384,256]{1,0:T(8,128)(2,1)}, bf16[384,256]{1,0:T(8,128)(2,1)S(1)}, u32[]{:S(2)}, u32[]{:S(2)}) %collective-permute-start.10) | collective-permute-done | bytes 196640 | tf_op jit(solution)/shard_map/ppermute | solution.py:118
  39.3 1.2 copy.13.p_ref
  41.4 0.7 copy-done.12
  42.2 4.8 %second_block.1 = (bf16[4,384,256]{2,1,0:T(8,128)(2,1)}, bf16[192,256]{1,0:T(8,128)(2,1)}, bf16[192,256]{1,0:T(8,128)(2,1)}, f32[2,384,256]{2,1,0:T(8,128)}, bf1...) custom-call(bf16[2,384,256]{2,1,0:T(8,128)(2,1)} %middle.1.a_ref.mid_ref, ...), custom_call_target="tpu_custom_call" | custom-call | tf_op jit(solution)/shard_map/second_block/pallas_call | solution.py:142
  47.3 1.6 %collective-permute-done.14.got_ref = bf16[2,384,256]{2,1,0:T(8,128)(2,1)S(1)} collective-permute-done((bf16[2,384,256]{2,1,0:T(8,128)(2,1)}, bf16[2,384,256]{2,1,0:T(8,128)(2,1)S(1)}, u32[]{:S(2)}, u32[]{:S(2)}) %collective-permute-start.14) | collective-permute-done | bytes 393248 | tf_op jit(solution)/shard_map/ppermute | solution.py:118
  48.9 0.8 copy-done.10
  49.7 2.1 %squash_sum.1.chip_ref = bf16[2,384,256]{2,1,0:T(8,128)(2,1)} custom-call(f32[2,384,256]{2,1,0:T(8,128)} %get-tuple-element.51.keep_ref, bf16[2,384,256]{2,1,0:T(8,128)(2,1)} %copy-done.10), custom_call_target="tpu_custom_call" | custom-call | tf_op jit(solution)/shard_map/squash_sum/pallas_call | solution.py:142
  52.3 11.0 %collective-permute-done.15.other_ref = bf16[2,384,256]{2,1,0:T(8,128)(2,1)S(1)} collective-permute-done((bf16[2,384,256]{2,1,0:T(8,128)(2,1)}, bf16[2,384,256]{2,1,0:T(8,128)(2,1)S(1)}, u32[]{:S(2)}, u32[]{:S(2)}) %collective-permute-start.15) | collective-permute-done | bytes 393248 | tf_op jit(solution)/shard_map/ppermute | solution.py:118
  63.3 0.7 copy-done.11
  64.1 2.8 %middle_grad.1.a_ref.g_ref.g0.g2 = bf16[2,384,256]{2,1,0:T(8,128)(2,1)} custom-call(bf16[384,256]{1,0:T(8,128)(2,1)} %bitcast.4, bf16[384,256]{1,0:T(8,128)(2,1)} %copy-done.1, bf16[2,384,256]{2,1,0:T(8,128)(2,1)} %middle.1.a_ref.mid_ref, bf16[2,384,256]{2,1,0:T(8,128)(2,1)} %squash_sum.1.chip_ref, bf16[2,384,256]{2,1,0:T(8,128)(2,1)} %copy-done.11), custom_call_target="tpu_custom_call" | custom-call | tf_op jit(solution)/shard_map/middle_grad/pallas_call | solution.py:142
  67.4 3.0 %second_weights.1 = (f32[384,384]{1,0:T(8,128)}, bf16[384,384]{1,0:T(8,128)(2,1)}, bf16[384,384]{1,0:T(8,128)(2,1)}, bf16[384,384]{1,0:T(8,128)(2,1)}) custom-call(bf16[4,384,256]{2,1,0:T(8,128)(2,1)} %get-tuple-element.67.z_ref, bf16[192,256]{1,0:T(8,128)(2,1)} %get-tuple-element.68.gu_ref, bf16[192,256]{1,0:T(8,128)(2,1)} %get-tuple-element.69.v_ref, ...), custom_call_target="tpu_custom_call" | custom-call | tf_op jit(solution)/shard_map/second_weights/pallas_call | solution.py:142
  70.4 2.6 %collective-permute-start.22 = (bf16[384,384]{1,0:T(8,128)(2,1)}, bf16[384,384]{1,0:T(8,128)(2,1)S(1)}, u32[]{:S(2)}, u32[]{:S(2)}) collective-permute-start(bf16[384,384]{1,0:T(8,128)(2,1)} %get-tuple-element.71), channel_id=1, source_target_pairs={{0,4},{4,0},{8,12},{12,8},{1,5},{5,1},{9,13},{13,9},{2,6},{6,2},{1... | collective-permute-start | bytes 884744 | tf_op jit(solution)/shard_map/ppermute | solution.py:118
  73.0 0.7 copy-done
  73.8 3.8 %first_backward.1 = (bf16[192,256]{1,0:T(8,128)(2,1)}, f32[2,384,256]{2,1,0:T(8,128)}, bf16[2,384,256]{2,1,0:T(8,128)(2,1)}) custom-call(bf16[2,384,256]{2,1,0:T(8,128)(2,1)} %middle_grad.1.a_ref.g_ref.g0.g2, bf16[2,384,256]{2,1,0:T(8,128)(2,1)} %copy-done, bf16[3,192,1536]{2,1,0:T(8,128)(2,1)} %k_ref.5, bf16[1536,192]{1,0:T(8,128)(2,1)} %copy.12.p_ref, ...), custom_call_target="tpu_custom_call" | custom-call | tf_op jit(solution)/shard_map/first_backward/pallas_call | solution.py:142
  78.2 0.9 collective-permute-start.24
  79.1 3.0 %first_weights.1 = (f32[384,384]{1,0:T(8,128)}, bf16[384,384]{1,0:T(8,128)(2,1)}, bf16[384,384]{1,0:T(8,128)(2,1)}, bf16[384,384]{1,0:T(8,128)(2,1)}) custom-call(bf16[4,384,256]{2,1,0:T(8,128)(2,1)} %get-tuple-element.58.z_ref, bf16[192,256]{1,0:T(8,128)(2,1)} %get-tuple-element.59.gu_ref, bf16[192,256]{1,0:T(8,128)(2,1)} %get-tuple-element.60.v_ref, ...), custom_call_target="tpu_custom_call" | custom-call | tf_op jit(solution)/shard_map/first_weights/pallas_call | solution.py:142
  82.1 3.0 %collective-permute-start.19 = (bf16[384,384]{1,0:T(8,128)(2,1)}, bf16[384,384]{1,0:T(8,128)(2,1)S(1)}, u32[]{:S(2)}, u32[]{:S(2)}) collective-permute-start(bf16[384,384]{1,0:T(8,128)(2,1)} %get-tuple-element.62), channel_id=1, source_target_pairs={{0,4},{4,0},{8,12},{12,8},{1,5},{5,1},{9,13},{13,9},{2,6},{6,2},{1... | collective-permute-start | bytes 884744 | tf_op jit(solution)/shard_map/ppermute | solution.py:118
  85.1 13.1 %collective-permute-done.23.r2 = bf16[384,384]{1,0:T(8,128)(2,1)S(1)} collective-permute-done((bf16[384,384]{1,0:T(8,128)(2,1)S(1)}, bf16[384,384]{1,0:T(8,128)(2,1)S(1)}, u32[]{:S(2)}, u32[]{:S(2)}) %collective-permute-start.23) | collective-permute-done | bytes 294944 | tf_op jit(solution)/shard_map/ppermute | solution.py:118
  98.2 3.4 %collective-permute-start.20 = (bf16[384,384]{1,0:T(8,128)(2,1)}, bf16[384,384]{1,0:T(8,128)(2,1)S(1)}, u32[]{:S(2)}, u32[]{:S(2)}) collective-permute-start(bf16[384,384]{1,0:T(8,128)(2,1)} %get-tuple-element.63), channel_id=1, source_target_pairs={{0,8},{4,12},{8,0},{12,4},{1,9},{5,13},{9,1},{13,5},{2,10},{6,14},... | collective-permute-start | bytes 884744 | tf_op jit(solution)/shard_map/ppermute | solution.py:118
  101.6 1.0 collective-permute-start.21
  102.6 2.1 %out_sum.1 = (f32[384,256]{1,0:T(8,128)}, bf16[384,256]{1,0:T(8,128)(2,1)}) custom-call(f32[2,384,256]{2,1,0:T(8,128)} %get-tuple-element.47.keep_ref, bf16[2,384,256]{2,1,0:T(8,128)(2,1)} %copy-done.6), custom_call_target="tpu_custom_call" | custom-call | tf_op jit(solution)/shard_map/out_sum/pallas_call | solution.py:142
  105.4 2.1 %entry_sum.1 = (f32[384,256]{1,0:T(8,128)}, bf16[384,256]{1,0:T(8,128)(2,1)}) custom-call(f32[2,384,256]{2,1,0:T(8,128)} %get-tuple-element.54.keep_ref, bf16[2,384,256]{2,1,0:T(8,128)(2,1)} %copy-done.7), custom_call_target="tpu_custom_call" | custom-call | tf_op jit(solution)/shard_map/entry_sum/pallas_call | solution.py:142
  107.5 11.1 %collective-permute-done.24.r3 = bf16[384,384]{1,0:T(8,128)(2,1)S(1)} collective-permute-done((bf16[384,384]{1,0:T(8,128)(2,1)S(1)}, bf16[384,384]{1,0:T(8,128)(2,1)S(1)}, u32[]{:S(2)}, u32[]{:S(2)}) %collective-permute-start.24) | collective-permute-done | bytes 294944 | tf_op jit(solution)/shard_map/ppermute | solution.py:118
  119.3 2.6 %second_weights_total.1 = (f32[3,192,384]{2,1,0:T(8,128)}, f32[384,192]{1,0:T(8,128)}) custom-call(f32[384,384]{1,0:T(8,128)} %get-tuple-element.70.own_ref, bf16[384,384]{1,0:T(8,128)(2,1)} %copy-done.13, bf16[384,384]{1,0:T(8,128)(2,1)} %copy-done.16, bf16[384,384]{1,0:T(8,128)(2,1)} %copy-done.17), custom_call_target="tpu_custom_call" | custom-call | tf_op jit(solution)/shard_map/second_weights_total/pallas_call | solution.py:142
  121.9 1.9 %copy.16 = f32[384,192]{0,1:T(8,128)} copy(f32[384,192]{1,0:T(8,128)} %get-tuple-element.81) | data formatting | bytes 589824
  123.8 0.7 copy-done.19
  124.4 1.9 %out.1 = bf16[384,256]{1,0:T(8,128)(2,1)} custom-call(bf16[2,384,256]{2,1,0:T(8,128)(2,1)} %middle.1.a_ref.mid_ref, f32[384,256]{1,0:T(8,128)} %get-tuple-element.49.own_ref, bf16[384,256]{1,0:T(8,128)(2,1)} %copy-done.19), custom_call_target="tpu_custom_call" | custom-call | tf_op jit(solution)/shard_map/out/pallas_call | solution.py:142
  126.4 4.4 %collective-permute-done.21.r3 = bf16[384,384]{1,0:T(8,128)(2,1)S(1)} collective-permute-done((bf16[384,384]{1,0:T(8,128)(2,1)}, bf16[384,384]{1,0:T(8,128)(2,1)S(1)}, u32[]{:S(2)}, u32[]{:S(2)}) %collective-permute-start.21) | collective-permute-done | bytes 294944 | tf_op jit(solution)/shard_map/ppermute | solution.py:118
  130.8 0.7 copy-done.18
  131.5 2.6 %first_weights_total.1 = (f32[3,192,384]{2,1,0:T(8,128)}, f32[384,192]{1,0:T(8,128)}) custom-call(f32[384,384]{1,0:T(8,128)} %get-tuple-element.61.own_ref, bf16[384,384]{1,0:T(8,128)(2,1)} %copy-done.14, bf16[384,384]{1,0:T(8,128)(2,1)} %copy-done.15, bf16[384,384]{1,0:T(8,128)(2,1)} %copy-done.18), custom_call_target="tpu_custom_call" | custom-call | tf_op jit(solution)/shard_map/first_weights_total/pallas_call | solution.py:142
  134.1 1.9 %copy.15 = f32[384,192]{0,1:T(8,128)} copy(f32[384,192]{1,0:T(8,128)} %get-tuple-element.79) | data formatting | bytes 589824
  135.9 0.7 copy-done.22
  136.6 2.2 %entry.1 = bf16[384,256]{1,0:T(8,128)(2,1)} custom-call(bf16[2,384,256]{2,1,0:T(8,128)(2,1)} %middle_grad.1.a_ref.g_ref.g0.g2, bf16[384,256]{1,0:T(8,128)(2,1)} %x_ref.1, f32[384,256]{1,0:T(8,128)} %get-tuple-element.56.own_ref, bf16[384,256]{1,0:T(8,128)(2,1)} %copy-done.22), custom_call_target="tpu_custom_call" | custom-call | tf_op jit(solution)/shard_map/entry/pallas_call | solution.py:142
  (81 shorter events, 9.3 us)
Async XLA Ops:
  0.6 6.9 %collective-permute-start = (bf16[384,256]{1,0:T(8,128)(2,1)}, bf16[384,256]{1,0:T(8,128)(2,1)S(1)}, u32[]{:S(2)}, u32[]{:S(2)}) collective-permute-start(bf16[384,256]{1,0:T(8,128)(2,1)} %x_ref.1), channel_id=1, source_target_pairs={{0,2},{1,3},{2,0},{3,1},{4,6},{5,7},{6,4},{7,5},{8,10},{9,11},{10,... | collective-permute-start | bytes 589832 | tf_op jit(solution)/shard_map/ppermute | solution.py:118
  2.2 7.7 %collective-permute-start.1 = (bf16[384,256]{1,0:T(8,128)(2,1)}, bf16[384,256]{1,0:T(8,128)(2,1)S(1)}, u32[]{:S(2)}, u32[]{:S(2)}) collective-permute-start(bf16[384,256]{1,0:T(8,128)(2,1)} %x_ref.1), channel_id=1, source_target_pairs={{0,1},{1,0},{2,3},{3,2},{4,5},{5,4},{6,7},{7,6},{8,9},{9,8},{10,11... | collective-permute-start | bytes 589832 | tf_op jit(solution)/shard_map/ppermute | solution.py:118
  7.5 2.3 %copy-start.4 = (bf16[384,256]{1,0:T(8,128)(2,1)}, bf16[384,256]{1,0:T(8,128)(2,1)S(1)}, u32[]{:S(2)}) copy-start(bf16[384,256]{1,0:T(8,128)(2,1)S(1)} %collective-permute-done.x2) | copy-start | bytes 589828
  7.6 2.3 %collective-permute-start.2 = (bf16[384,256]{1,0:T(8,128)(2,1)S(1)}, bf16[384,256]{1,0:T(8,128)(2,1)S(1)}, u32[]{:S(2)}, u32[]{:S(2)}) collective-permute-start(bf16[384,256]{1,0:T(8,128)(2,1)S(1)} %collective-permute-done.x2), channel_id=1, source_target_pairs={{0,1},{1,0},{2,3},{3,2},{4,5},{5,4},{6,7},{7,6},{8,9},{9,8},{10,11... | collective-permute-start | bytes 589832 | tf_op jit(solution)/shard_map/ppermute | solution.py:118
  9.8 0.7 copy-start.20
  15.2 2.0 %collective-permute-start.3 = (bf16[2,384,256]{2,1,0:T(8,128)(2,1)}, bf16[2,384,256]{2,1,0:T(8,128)(2,1)S(1)}, u32[]{:S(2)}, u32[]{:S(2)}) collective-permute-start(bf16[2,384,256]{2,1,0:T(8,128)(2,1)} %get-tuple-element.42), channel_id=1, source_target_pairs={{0,1},{1,0},{2,3},{3,2},{4,5},{5,4},{6,7},{7,6},{8,9},{9,8},{10,11... | collective-permute-start | bytes 1179656 | tf_op jit(solution)/shard_map/ppermute | solution.py:118
  17.2 0.7 copy-start.9
  18.0 21.4 %copy-start.5 = (bf16[1536,192]{0,1:T(8,128)(2,1)S(1)}, bf16[1536,192]{0,1:T(8,128)(2,1)}, u32[]{:S(2)}) copy-start(bf16[1536,192]{0,1:T(8,128)(2,1)} %param.10) | copy-start | bytes 1769476
  20.1 13.3 %collective-permute-start.4 = (bf16[2,384,256]{2,1,0:T(8,128)(2,1)}, bf16[2,384,256]{2,1,0:T(8,128)(2,1)S(1)}, u32[]{:S(2)}, u32[]{:S(2)}) collective-permute-start(bf16[2,384,256]{2,1,0:T(8,128)(2,1)} %mix_sum.1.chip_ref), channel_id=1, source_target_pairs={{0,2},{1,3},{2,0},{3,1},{4,6},{5,7},{6,4},{7,5},{8,10},{9,11},{10,... | collective-permute-start | bytes 1179656 | tf_op jit(solution)/shard_map/ppermute | solution.py:118
  23.2 4.3 %collective-permute-start.6 = (bf16[2,48,256]{2,1,0:T(8,128)(2,1)}, bf16[2,48,256]{2,1,0:T(8,128)(2,1)S(1)}, u32[]{:S(2)}, u32[]{:S(2)}) collective-permute-start(bf16[2,48,256]{2,1,0:T(8,128)(2,1)} %get-tuple-element.44), channel_id=1, source_target_pairs={{0,4},{4,0},{8,12},{12,8},{1,5},{5,1},{9,13},{13,9},{2,6},{6,2},{1... | collective-permute-start | bytes 147464 | tf_op jit(solution)/shard_map/ppermute | solution.py:118
  23.6 6.5 %collective-permute-start.7 = (bf16[2,48,256]{2,1,0:T(8,128)(2,1)}, bf16[2,48,256]{2,1,0:T(8,128)(2,1)S(1)}, u32[]{:S(2)}, u32[]{:S(2)}) collective-permute-start(bf16[2,48,256]{2,1,0:T(8,128)(2,1)} %get-tuple-element.45), channel_id=1, source_target_pairs={{0,8},{4,12},{8,0},{12,4},{1,9},{5,13},{9,1},{13,5},{2,10},{6,14},... | collective-permute-start | bytes 147464 | tf_op jit(solution)/shard_map/ppermute | solution.py:118
  26.2 4.4 %collective-permute-start.8 = (bf16[2,48,256]{2,1,0:T(8,128)(2,1)}, bf16[2,48,256]{2,1,0:T(8,128)(2,1)S(1)}, u32[]{:S(2)}, u32[]{:S(2)}) collective-permute-start(bf16[2,48,256]{2,1,0:T(8,128)(2,1)} %get-tuple-element.46), channel_id=1, source_target_pairs={{0,12},{4,8},{8,4},{12,0},{1,13},{5,9},{9,5},{13,1},{2,14},{6,10},... | collective-permute-start | bytes 147464 | tf_op jit(solution)/shard_map/ppermute | solution.py:118
  27.5 3.2 %copy-start.23 = (bf16[2,48,256]{2,1,0:T(8,128)(2,1)}, bf16[2,48,256]{2,1,0:T(8,128)(2,1)S(1)}, u32[]{:S(2)}) copy-start(bf16[2,48,256]{2,1,0:T(8,128)(2,1)S(1)} %collective-permute-done.6.refs_1_) | copy-start | bytes 147460
  32.9 6.5 %collective-permute-start.10 = (bf16[384,256]{1,0:T(8,128)(2,1)}, bf16[384,256]{1,0:T(8,128)(2,1)S(1)}, u32[]{:S(2)}, u32[]{:S(2)}) collective-permute-start(bf16[384,256]{1,0:T(8,128)(2,1)} %bitcast.1), channel_id=1, source_target_pairs={{0,2},{1,3},{2,0},{3,1},{4,6},{5,7},{6,4},{7,5},{8,10},{9,11},{10,... | collective-permute-start | bytes 589832 | tf_op jit(solution)/shard_map/ppermute | solution.py:118
  33.4 0.7 copy-start.8
  36.3 4.4 %collective-permute-start.5 = (bf16[2,384,256]{2,1,0:T(8,128)(2,1)}, bf16[2,384,256]{2,1,0:T(8,128)(2,1)S(1)}, u32[]{:S(2)}, u32[]{:S(2)}) collective-permute-start(bf16[2,384,256]{2,1,0:T(8,128)(2,1)} %middle.1.a_ref.mid_ref), channel_id=1, source_target_pairs={{0,1},{1,0},{2,3},{3,2},{4,5},{5,4},{6,7},{7,6},{8,9},{9,8},{10,11... | collective-permute-start | bytes 1179656 | tf_op jit(solution)/shard_map/ppermute | solution.py:118
  36.4 4.2 %collective-permute-start.9 = (bf16[384,256]{1,0:T(8,128)(2,1)}, bf16[384,256]{1,0:T(8,128)(2,1)S(1)}, u32[]{:S(2)}, u32[]{:S(2)}) collective-permute-start(bf16[384,256]{1,0:T(8,128)(2,1)} %bitcast.2), channel_id=1, source_target_pairs={{0,1},{1,0},{2,3},{3,2},{4,5},{5,4},{6,7},{7,6},{8,9},{9,8},{10,11... | collective-permute-start | bytes 589832 | tf_op jit(solution)/shard_map/ppermute | solution.py:118
  39.3 1.5 %copy-start.1 = (bf16[384,256]{1,0:T(8,128)(2,1)}, bf16[384,256]{1,0:T(8,128)(2,1)S(1)}, u32[]{:S(2)}) copy-start(bf16[384,256]{1,0:T(8,128)(2,1)S(1)} %collective-permute-done.10.g2) | copy-start | bytes 589828
  39.3 1.4 %collective-permute-start.11 = (bf16[384,256]{1,0:T(8,128)(2,1)S(1)}, bf16[384,256]{1,0:T(8,128)(2,1)S(1)}, u32[]{:S(2)}, u32[]{:S(2)}) collective-permute-start(bf16[384,256]{1,0:T(8,128)(2,1)S(1)} %collective-permute-done.10.g2), channel_id=1, source_target_pairs={{0,1},{1,0},{2,3},{3,2},{4,5},{5,4},{6,7},{7,6},{8,9},{9,8},{10,11... | collective-permute-start | bytes 589832 | tf_op jit(solution)/shard_map/ppermute | solution.py:118
  41.4 0.7 copy-start.12
  47.0 1.9 %collective-permute-start.14 = (bf16[2,384,256]{2,1,0:T(8,128)(2,1)}, bf16[2,384,256]{2,1,0:T(8,128)(2,1)S(1)}, u32[]{:S(2)}, u32[]{:S(2)}) collective-permute-start(bf16[2,384,256]{2,1,0:T(8,128)(2,1)} %get-tuple-element.52), channel_id=1, source_target_pairs={{0,1},{1,0},{2,3},{3,2},{4,5},{5,4},{6,7},{7,6},{8,9},{9,8},{10,11... | collective-permute-start | bytes 1179656 | tf_op jit(solution)/shard_map/ppermute | solution.py:118
  48.9 0.8 copy-start.10
  49.7 17.2 %copy-start.26 = (bf16[2,384,256]{2,1,0:T(8,128)(2,1)S(1)}, bf16[2,384,256]{2,1,0:T(8,128)(2,1)}, u32[]{:S(2)}) copy-start(bf16[2,384,256]{2,1,0:T(8,128)(2,1)} %get-tuple-element.48) | copy-start | bytes 1179652
  51.8 11.5 %collective-permute-start.15 = (bf16[2,384,256]{2,1,0:T(8,128)(2,1)}, bf16[2,384,256]{2,1,0:T(8,128)(2,1)S(1)}, u32[]{:S(2)}, u32[]{:S(2)}) collective-permute-start(bf16[2,384,256]{2,1,0:T(8,128)(2,1)} %squash_sum.1.chip_ref), channel_id=1, source_target_pairs={{0,2},{1,3},{2,0},{3,1},{4,6},{5,7},{6,4},{7,5},{8,10},{9,11},{10,... | collective-permute-start | bytes 1179656 | tf_op jit(solution)/shard_map/ppermute | solution.py:118
  63.3 0.7 copy-start.11
  66.9 6.2 %collective-permute-start.16 = (bf16[2,384,256]{2,1,0:T(8,128)(2,1)}, bf16[2,384,256]{2,1,0:T(8,128)(2,1)S(1)}, u32[]{:S(2)}, u32[]{:S(2)}) collective-permute-start(bf16[2,384,256]{2,1,0:T(8,128)(2,1)} %middle_grad.1.a_ref.g_ref.g0.g2), channel_id=1, source_target_pairs={{0,1},{1,0},{2,3},{3,2},{4,5},{5,4},{6,7},{7,6},{8,9},{9,8},{10,11... | collective-permute-start | bytes 1179656 | tf_op jit(solution)/shard_map/ppermute | solution.py:118
  66.9 34.7 %collective-permute-start.12 = (bf16[2,384,256]{2,1,0:T(8,128)(2,1)S(1)}, bf16[2,384,256]{2,1,0:T(8,128)(2,1)S(1)}, u32[]{:S(2)}, u32[]{:S(2)}) collective-permute-start(bf16[2,384,256]{2,1,0:T(8,128)(2,1)S(1)} %copy-done.26), channel_id=1, source_target_pairs={{0,1},{1,0},{2,3},{3,2},{4,5},{5,4},{6,7},{7,6},{8,9},{9,8},{10,11... | collective-permute-start | bytes 1179656 | tf_op jit(solution)/shard_map/ppermute | solution.py:118
  70.4 11.7 %collective-permute-start.22 = (bf16[384,384]{1,0:T(8,128)(2,1)}, bf16[384,384]{1,0:T(8,128)(2,1)S(1)}, u32[]{:S(2)}, u32[]{:S(2)}) collective-permute-start(bf16[384,384]{1,0:T(8,128)(2,1)} %get-tuple-element.71), channel_id=1, source_target_pairs={{0,4},{4,0},{8,12},{12,8},{1,5},{5,1},{9,13},{13,9},{2,6},{6,2},{1... | collective-permute-start | bytes 884744 | tf_op jit(solution)/shard_map/ppermute | solution.py:118
  73.0 0.7 copy-start
  73.8 3.8 %copy-start.28 = (bf16[384,384]{1,0:T(8,128)(2,1)S(1)}, bf16[384,384]{1,0:T(8,128)(2,1)}, u32[]{:S(2)}) copy-start(bf16[384,384]{1,0:T(8,128)(2,1)} %get-tuple-element.72) | copy-start | bytes 884740
  73.8 4.4 %copy-start.27 = (bf16[384,384]{1,0:T(8,128)(2,1)S(1)}, bf16[384,384]{1,0:T(8,128)(2,1)}, u32[]{:S(2)}) copy-start(bf16[384,384]{1,0:T(8,128)(2,1)} %get-tuple-element.73) | copy-start | bytes 884740
  77.6 27.1 %collective-permute-start.17 = (bf16[2,384,256]{2,1,0:T(8,128)(2,1)}, bf16[2,384,256]{2,1,0:T(8,128)(2,1)S(1)}, u32[]{:S(2)}, u32[]{:S(2)}) collective-permute-start(bf16[2,384,256]{2,1,0:T(8,128)(2,1)} %get-tuple-element.55), channel_id=1, source_target_pairs={{0,1},{1,0},{2,3},{3,2},{4,5},{5,4},{6,7},{7,6},{8,9},{9,8},{10,11... | collective-permute-start | bytes 1179656 | tf_op jit(solution)/shard_map/ppermute | solution.py:118
  77.6 20.6 %collective-permute-start.23 = (bf16[384,384]{1,0:T(8,128)(2,1)S(1)}, bf16[384,384]{1,0:T(8,128)(2,1)S(1)}, u32[]{:S(2)}, u32[]{:S(2)}) collective-permute-start(bf16[384,384]{1,0:T(8,128)(2,1)S(1)} %copy-done.28), channel_id=1, source_target_pairs={{0,8},{4,12},{8,0},{12,4},{1,9},{5,13},{9,1},{13,5},{2,10},{6,14},... | collective-permute-start | bytes 884744 | tf_op jit(solution)/shard_map/ppermute | solution.py:118
  78.2 40.4 %collective-permute-start.24 = (bf16[384,384]{1,0:T(8,128)(2,1)S(1)}, bf16[384,384]{1,0:T(8,128)(2,1)S(1)}, u32[]{:S(2)}, u32[]{:S(2)}) collective-permute-start(bf16[384,384]{1,0:T(8,128)(2,1)S(1)} %copy-done.27), channel_id=1, source_target_pairs={{0,12},{4,8},{8,4},{12,0},{1,13},{5,9},{9,5},{13,1},{2,14},{6,10},... | collective-permute-start | bytes 884744 | tf_op jit(solution)/shard_map/ppermute | solution.py:118
  82.1 37.0 %copy-start.13 = (bf16[384,384]{1,0:T(8,128)(2,1)}, bf16[384,384]{1,0:T(8,128)(2,1)S(1)}, u32[]{:S(2)}) copy-start(bf16[384,384]{1,0:T(8,128)(2,1)S(1)} %collective-permute-done.22.r1) | copy-start | bytes 884740
  82.1 44.2 %collective-permute-start.19 = (bf16[384,384]{1,0:T(8,128)(2,1)}, bf16[384,384]{1,0:T(8,128)(2,1)S(1)}, u32[]{:S(2)}, u32[]{:S(2)}) collective-permute-start(bf16[384,384]{1,0:T(8,128)(2,1)} %get-tuple-element.62), channel_id=1, source_target_pairs={{0,4},{4,0},{8,12},{12,8},{1,5},{5,1},{9,13},{13,9},{2,6},{6,2},{1... | collective-permute-start | bytes 884744 | tf_op jit(solution)/shard_map/ppermute | solution.py:118
  98.2 20.9 %copy-start.16 = (bf16[384,384]{1,0:T(8,128)(2,1)}, bf16[384,384]{1,0:T(8,128)(2,1)S(1)}, u32[]{:S(2)}) copy-start(bf16[384,384]{1,0:T(8,128)(2,1)S(1)} %collective-permute-done.23.r2) | copy-start | bytes 884740
  98.2 28.1 %collective-permute-start.20 = (bf16[384,384]{1,0:T(8,128)(2,1)}, bf16[384,384]{1,0:T(8,128)(2,1)S(1)}, u32[]{:S(2)}, u32[]{:S(2)}) collective-permute-start(bf16[384,384]{1,0:T(8,128)(2,1)} %get-tuple-element.63), channel_id=1, source_target_pairs={{0,8},{4,12},{8,0},{12,4},{1,9},{5,13},{9,1},{13,5},{2,10},{6,14},... | collective-permute-start | bytes 884744 | tf_op jit(solution)/shard_map/ppermute | solution.py:118
  101.6 1.0 copy-start.6
  101.6 29.2 %collective-permute-start.21 = (bf16[384,384]{1,0:T(8,128)(2,1)}, bf16[384,384]{1,0:T(8,128)(2,1)S(1)}, u32[]{:S(2)}, u32[]{:S(2)}) collective-permute-start(bf16[384,384]{1,0:T(8,128)(2,1)} %get-tuple-element.64), channel_id=1, source_target_pairs={{0,12},{4,8},{8,4},{12,0},{1,13},{5,9},{9,5},{13,1},{2,14},{6,10},... | collective-permute-start | bytes 884744 | tf_op jit(solution)/shard_map/ppermute | solution.py:118
  104.6 0.7 copy-start.7
  104.6 19.1 %collective-permute-start.13 = (bf16[384,256]{1,0:T(8,128)(2,1)}, bf16[384,256]{1,0:T(8,128)(2,1)S(1)}, u32[]{:S(2)}, u32[]{:S(2)}) collective-permute-start(bf16[384,256]{1,0:T(8,128)(2,1)} %get-tuple-element.50), channel_id=1, source_target_pairs={{0,2},{1,3},{2,0},{3,1},{4,6},{5,7},{6,4},{7,5},{8,10},{9,11},{10,... | collective-permute-start | bytes 589832 | tf_op jit(solution)/shard_map/ppermute | solution.py:118
  118.6 0.7 copy-start.17
  118.6 17.4 %collective-permute-start.18 = (bf16[384,256]{1,0:T(8,128)(2,1)}, bf16[384,256]{1,0:T(8,128)(2,1)S(1)}, u32[]{:S(2)}, u32[]{:S(2)}) collective-permute-start(bf16[384,256]{1,0:T(8,128)(2,1)} %get-tuple-element.57), channel_id=1, source_target_pairs={{0,2},{1,3},{2,0},{3,1},{4,6},{5,7},{6,4},{7,5},{8,10},{9,11},{10,... | collective-permute-start | bytes 589832 | tf_op jit(solution)/shard_map/ppermute | solution.py:118
  126.4 4.4 %copy-start.14 = (bf16[384,384]{1,0:T(8,128)(2,1)}, bf16[384,384]{1,0:T(8,128)(2,1)S(1)}, u32[]{:S(2)}) copy-start(bf16[384,384]{1,0:T(8,128)(2,1)S(1)} %collective-permute-done.19.r1) | copy-start | bytes 884740
  126.4 4.4 %copy-start.15 = (bf16[384,384]{1,0:T(8,128)(2,1)}, bf16[384,384]{1,0:T(8,128)(2,1)S(1)}, u32[]{:S(2)}) copy-start(bf16[384,384]{1,0:T(8,128)(2,1)S(1)} %collective-permute-done.20.r2) | copy-start | bytes 884740
  130.8 0.7 copy-start.18
  135.9 0.7 copy-start.22
  (6 other events, 3.9 us)

commit v2 on v1

--- a/solution.py
+++ b/solution.py
@@ -1,3 +1,5 @@
+import functools
+
 import jax
 import jax.numpy as jnp
 from jax import lax
@@ -138,30 +140,28 @@
     return gelu_and_slope(s)[1]
 
 
-def call(body, outs, args, name, specs=None, scratch=()):
+VMEM = pl.BlockSpec(memory_space=pltpu.VMEM)
+
+
+def call(body, outs, args, name, scratch=(), final=False):
+    struct = jax.ShapeDtypeStruct if final else pltpu.VMEM
     return pl.pallas_call(
         body,
-        out_shape=[jax.ShapeDtypeStruct(s, d) for s, d in outs],
-        in_specs=specs or [whole(a.shape) for a in args],
-        out_specs=[whole(s) for s, _ in outs],
-        grid=(1,),
+        out_shape=[struct(s, d) for s, d in outs],
+        in_specs=[VMEM] * len(args),
+        out_specs=[VMEM] * len(outs),
         scratch_shapes=scratch,
+        compiler_params=pltpu.CompilerParams(vmem_limit_bytes=16 << 20),
         name=name,
-    )(*args)
-
-
-def whole(shape):
-    return pl.BlockSpec(shape, lambda _: (0,) * len(shape))
+    )(*[pltpu.with_memory_space_constraint(a, pltpu.VMEM) for a in args])
 
 
 def fast_shards(x, taps_a, point_a, taps_b, point_b, grad_heads):
     rows, bins = x.shape
     hid, chans = taps_a.shape[1], taps_a.shape[2]
     heads, val, _ = grad_heads.shape
-    tap = pl.BlockSpec((None, hid, chans), lambda _: (1, 0, 0))
-    tile = whole((rows, bins))
-    pair = whole((2, rows, bins))
-    point = whole(point_a.shape)
+    tap_a, tap_b = taps_a[1], taps_b[1]
+    cols_a, cols_b = point_a.T, point_b.T
 
     def block(m, j):
         return pl.ds(pl.multiple_of((m ^ j) * rows, rows), rows)
@@ -202,9 +202,9 @@
         v_ref[...] = v
         s_ref[...] = slope
         for i, j in enumerate((1, 3)):
-            send_ref[i] = dot(p_ref[block(m, j), :], v).astype(BF16)
+            send_ref[i] = dot(p_ref[:, block(m, j)], v, ((0,), (0,))).astype(BF16)
         for i, j in enumerate((0, 2)):
-            keep_ref[i] = dot(p_ref[block(m, j), :], v)
+            keep_ref[i] = dot(p_ref[:, block(m, j)], v, ((0,), (0,)))
 
     z_a, v_a, slope_a, keep, send = call(
         first_body,
@@ -215,9 +215,8 @@
             ((2, rows, bins), F32),
             ((2, rows, bins), BF16),
         ],
-        (x, x_near, x_far, x_cross, taps_a, point_a),
+        (x, x_near, x_far, x_cross, tap_a, cols_a),
         "first_forward",
-        [tile, tile, tile, tile, tap, point],
     )
     got = swap(send, "mp", 1)
 
@@ -256,7 +255,7 @@
         v_ref[...] = v
         gv = jnp.zeros((hid, bins), F32)
         for j, ref in enumerate((g0, g1, g2, g3)):
-            gv = gv + dot(p_ref[block(m, j), :], ref[...], ((0,), (0,)))
+            gv = gv + dot(p_ref[:, block(m, j)], ref[...])
         gu = (gv * slope).astype(BF16)
         gu_ref[...] = gu
         for i, j in enumerate((1, 3)):
@@ -264,9 +263,9 @@
         for i, j in enumerate((0, 2)):
             keep_ref[i] = dot(k_ref[:, block(m, j)], gu, ((0,), (0,)))
         for i, j in enumerate((1, 3)):
-            ysend_ref[i] = dot(p_ref[block(m, j), :], v).astype(BF16)
+            ysend_ref[i] = dot(p_ref[:, block(m, j)], v, ((0,), (0,))).astype(BF16)
         for i, j in enumerate((0, 2)):
-            ykeep_ref[i] = dot(p_ref[block(m, j), :], v)
+            ykeep_ref[i] = dot(p_ref[:, block(m, j)], v, ((0,), (0,)))
 
     z_b, v_b, gu_b, keep, send, ykeep, ysend = call(
         second_body,
@@ -279,9 +278,8 @@
             ((2, rows, bins), F32),
             ((2, rows, bins), BF16),
         ],
-        (mid, mid_near, g_own, g_near, g_far, g_cross, taps_b, point_b),
+        (mid, mid_near, g_own, g_near, g_far, g_cross, tap_b, cols_b),
         "second_block",
-        [pair, pair, tile, tile, tile, tile, tap, point],
     )
     got = swap(send, "mp", 1)
     chip = near_sum(keep, got, "squash_sum")
@@ -317,14 +315,14 @@
         mixed = own_ref[...] + got_ref[...].astype(F32)
         out_ref[...] = (mid_ref[0].astype(F32) + mixed).astype(BF16)
 
-    (second_out,) = call(out_body, [((rows, bins), BF16)], (mid, y_own, y_got), "out")
+    (second_out,) = call(out_body, [((rows, bins), BF16)], (mid, y_own, y_got), "out", final=True)
 
     def first_back_body(a_ref, b_ref, k_ref, p_ref, s_ref, gu_ref, keep_ref, send_ref):
         m = lax.axis_index("mp")
         gv = jnp.zeros((hid, bins), F32)
         for j in range(4):
             part = (a_ref, b_ref)[j & 1][j >> 1]
-            gv = gv + dot(p_ref[block(m, j), :], part, ((0,), (0,)))
+            gv = gv + dot(p_ref[:, block(m, j)], part)
         gu = (gv * s_ref[...]).astype(BF16)
         gu_ref[...] = gu
         for i, j in enumerate((1, 3)):
@@ -335,9 +333,8 @@
     gu_a, keep, send = call(
         first_back_body,
         [((hid, bins), BF16), ((2, rows, bins), F32), ((2, rows, bins), BF16)],
-        (g_mid, g_mid_near, taps_a, point_a, slope_a),
+        (g_mid, g_mid_near, tap_a, cols_a, slope_a),
         "first_backward",
-        [pair, pair, tap, point, whole((hid, bins))],
     )
     got = swap(send, "mp", 1)
     e_own, e_send = last_sum(keep, got, "entry_sum")
@@ -349,14 +346,13 @@
             g_ref[0].astype(F32) + grad * slope_of(x_ref[...].astype(F32))
         ).astype(BF16)
 
-    (entry,) = call(entry_body, [((rows, bins), BF16)], (g_mid, x, e_own, e_got), "entry")
-
-    def weight_body(z_ref, gu_ref, v_ref, g0, g1, g2, g3, own_ref, *rest):
-        outs, g_ref = rest[:3], rest[3]
+    (entry,) = call(entry_body, [((rows, bins), BF16)], (g_mid, x, e_own, e_got), "entry", final=True)
+
+    def weight_body(fill, z_ref, gu_ref, v_ref, *rest):
+        grads, (own_ref, *outs, g_ref) = rest[:-5], rest[-5:]
         m = lax.axis_index("mp")
         c = lax.axis_index("ctx")
-        for j, ref in enumerate((g0, g1, g2, g3)):
-            g_ref[j] = ref[...]
+        fill(g_ref, grads)
         for k in (1, 2, 3, 0):
             j = m ^ c ^ k
             taps = dot(gu_ref[...], z_ref[j], ((1,), (1,)))
@@ -365,13 +361,20 @@
             out[:hid, :] = taps.astype(out.dtype)
             out[hid:, :] = proj.astype(out.dtype)
 
-    def weights(z, gu, v, grads, specs, name):
+    def fill_tiles(g_ref, grads):
+        for j, ref in enumerate(grads):
+            g_ref[j] = ref[...]
+
+    def fill_pairs(g_ref, grads):
+        for j in range(4):
+            g_ref[j] = grads[j & 1][j >> 1]
+
+    def weights(z, gu, v, grads, fill, name):
         own, *sends = call(
-            weight_body,
+            functools.partial(weight_body, fill),
             [((2 * hid, rows), F32)] + [((2 * hid, rows), BF16)] * 3,
             (z, gu, v, *grads),
             name,
-            [whole(z.shape), whole(gu.shape), whole(v.shape), *specs],
             [pltpu.VMEM((4, rows, bins), BF16)],
         )
         gots = [swap(part, "ctx", k + 1) for k, part in enumerate(sends)]
@@ -385,26 +388,22 @@
             taps_ref[0] = jnp.zeros((hid, rows), F32)
             taps_ref[1] = total(pl.ds(0, hid))
             taps_ref[2] = jnp.zeros((hid, rows), F32)
-            proj_ref[...] = total(pl.ds(hid, hid)).T
-
-        return call(
+            proj_ref[...] = total(pl.ds(hid, hid))
+
+        taps, proj = call(
             total_body,
-            [((3, hid, rows), F32), ((rows, hid), F32)],
+            [((3, hid, rows), F32), ((hid, rows), F32)],
             (own, *gots),
             name + "_total",
+            final=True,
         )
+        return taps, proj.T
 
     taps_b_grad, point_b_grad = weights(
-        z_b, gu_b, v_b, (g_own, g_near, g_far, g_cross), [tile] * 4, "second_weights"
-    )
-    upper = [pl.BlockSpec((None, rows, bins), lambda _, i=i: (i, 0, 0)) for i in (0, 1)]
+        z_b, gu_b, v_b, (g_own, g_near, g_far, g_cross), fill_tiles, "second_weights"
+    )
     taps_a_grad, point_a_grad = weights(
-        z_a,
-        gu_a,
-        v_a,
-        (g_mid, g_mid_near, g_mid, g_mid_near),
-        [upper[0], upper[0], upper[1], upper[1]],
-        "first_weights",
+        z_a, gu_a, v_a, (g_mid, g_mid_near), fill_pairs, "first_weights"
     )
     return second_out, entry, taps_a_grad, point_a_grad, taps_b_grad, point_b_grad
 

time: 140 us -> 108 us (0.77)
  the two profiles are of different devices: /device:TPU:8 before, /device:TPU:12 now
where the time goes in v2:
time: 108 us
  waiting for transfers between devices  69 us (64%)
  starting transfers between devices  23.6 us (22%)
  Pallas kernels  10.2 us (9%)
  local copies, waits for them, and re-layouts  4.22 us (4%)
    ppermute x25, waiting for transfers between devices, swap(): return lax.ppermute(value, axis, [(i, i ^ bits) for i in range(size)])  69 us
    ppermute x25, starting transfers between devices, swap(): return lax.ppermute(value, axis, [(i, i ^ bits) for i in range(size)])  23.6 us
    pallas_call x17, Pallas kernels, call(): pl.pallas_call(body, out_shape=[struct(s, d) for s, d in outs], in_specs=...  10.2 us
    squeeze x2, local copies, waits for them, and re-layouts, fast_shards(): tap_a, tap_b = (taps_a[1], taps_b[1])  2.21 us
  transfers between devices with their start and end apart: 25, of which 15 were waited for; matrix products, arithmetic and copies ran while one was open for 2% of the time, Pallas kernels for 5%

profile of v2, /device:TPU:12, one launch (start us, length us, event | category | flops | bytes accessed | tf_op | source)
XLA Modules:
  0.0 107.8 jit_solution(7459755406504720558)
XLA Ops:
  0.6 1.6 %collective-permute-start = (bf16[384,256]{1,0:T(8,128)(2,1)}, bf16[384,256]{1,0:T(8,128)(2,1)S(1)}, u32[]{:S(2)}, u32[]{:S(2)}) collective-permute-start(bf16[384,256]{1,0:T(8,128)(2,1)} %x_ref.1), channel_id=1, source_target_pairs={{0,2},{1,3},{2,0},{3,1},{4,6},{5,7},{6,4},{7,5},{8,10},{9,11},{10,... | collective-permute-start | bytes 589832 | tf_op jit(solution)/shard_map/ppermute | solution.py:120
  2.2 5.4 %collective-permute-done.x2 = bf16[384,256]{1,0:T(8,128)(2,1)S(1)} collective-permute-done((bf16[384,256]{1,0:T(8,128)(2,1)}, bf16[384,256]{1,0:T(8,128)(2,1)S(1)}, u32[]{:S(2)}, u32[]{:S(2)}) %collective-permute-start) | collective-permute-done | bytes 196640 | tf_op jit(solution)/shard_map/ppermute | solution.py:120
  7.6 1.1 %slice_bitcast_fusion.1.k_ref = bf16[192,1536]{1,0:T(8,128)(2,1)S(1)} fusion(bf16[3,192,1536]{2,1,0:T(8,128)(2,1)} %param.7), kind=kLoop, calls=%fused_computation.1 | loop fusion | bytes 1179648 | tf_op jit(solution)/shard_map/squeeze | solution.py:163
  8.7 0.3 collective-permute-done.2.x3
  9.0 1.1 copy-done
  10.1 0.9 copy-done.2
  11.0 1.4 %first_forward.1 = (bf16[4,384,256]{2,1,0:T(8,128)(2,1)S(1)}, bf16[192,256]{1,0:T(8,128)(2,1)S(1)}, f32[192,256]{1,0:T(8,128)S(1)}, f32[2,384,256]{2,1,0:T(8,128)S(1)}, bf16[2,384,256]{2,1,0:T(8,128)(2,1)S(1)}) custom-call(bf16[384,256]{1,0:T(8,128)(2,1)S(1)} %copy-done.2, bf16[384,256]{1,0:T(8,128)(2,1)S(1)} %collective-permute-done.1.x1, ...), custom_call_target="tpu_custom_call" | custom-call | tf_op jit(solution)/shard_map/first_forward/pallas_call | solution.py:148
  12.4 0.3 collective-permute-start.3
  12.6 1.5 %collective-permute-done.3.got_ref = bf16[2,384,256]{2,1,0:T(8,128)(2,1)S(1)} collective-permute-done((bf16[2,384,256]{2,1,0:T(8,128)(2,1)S(1)}, bf16[2,384,256]{2,1,0:T(8,128)(2,1)S(1)}, u32[]{:S(2)}, u32[]{:S(2)}) %collective-permute-start.3) | collective-permute-done | bytes 393248 | tf_op jit(solution)/shard_map/ppermute | solution.py:120
  14.2 1.6 %collective-permute-start.4 = (bf16[2,384,256]{2,1,0:T(8,128)(2,1)S(1)}, bf16[2,384,256]{2,1,0:T(8,128)(2,1)S(1)}, u32[]{:S(2)}, u32[]{:S(2)}) collective-permute-start(bf16[2,384,256]{2,1,0:T(8,128)(2,1)S(1)} %mix_sum.1.chip_ref), channel_id=1, source_target_pairs={{0,2},{1,3},{2,0},{3,1},{4,6},{5,7},{6,4},{7,5},{8,10},{9,11},{10,... | collective-permute-start | bytes 1179656 | tf_op jit(solution)/shard_map/ppermute | solution.py:120
  15.8 0.5 collective-permute-start.6
  16.3 2.6 %collective-permute-start.7 = (bf16[2,48,256]{2,1,0:T(8,128)(2,1)S(1)}, bf16[2,48,256]{2,1,0:T(8,128)(2,1)S(1)}, u32[]{:S(2)}, u32[]{:S(2)}) collective-permute-start(bf16[2,48,256]{2,1,0:T(8,128)(2,1)S(1)} %get-tuple-element.45), channel_id=1, source_target_pairs={{0,8},{4,12},{8,0},{12,4},{1,9},{5,13},{9,1},{13,5},{2,10},{6,14},... | collective-permute-start | bytes 147464 | tf_op jit(solution)/shard_map/ppermute | solution.py:120
  18.9 0.4 collective-permute-start.8
  19.4 0.6 collective-permute-done.6.refs_1_
  20.0 2.4 %collective-permute-done.7.refs_2_ = bf16[2,48,256]{2,1,0:T(8,128)(2,1)S(1)} collective-permute-done((bf16[2,48,256]{2,1,0:T(8,128)(2,1)S(1)}, bf16[2,48,256]{2,1,0:T(8,128)(2,1)S(1)}, u32[]{:S(2)}, u32[]{:S(2)}) %collective-permute-start.7) | collective-permute-done | bytes 49184 | tf_op jit(solution)/shard_map/ppermute | solution.py:120
  22.4 1.1 %collective-permute-done.8.refs_3_ = bf16[2,48,256]{2,1,0:T(8,128)(2,1)S(1)} collective-permute-done((bf16[2,48,256]{2,1,0:T(8,128)(2,1)S(1)}, bf16[2,48,256]{2,1,0:T(8,128)(2,1)S(1)}, u32[]{:S(2)}, u32[]{:S(2)}) %collective-permute-start.8) | collective-permute-done | bytes 49184 | tf_op jit(solution)/shard_map/ppermute | solution.py:120
  23.6 0.6 collective-permute-start.10
  24.2 5.5 %collective-permute-done.10.g2.rest_2_ = bf16[384,256]{1,0:T(8,128)(2,1)S(1)} collective-permute-done((bf16[384,256]{1,0:T(8,128)(2,1)S(1)}, bf16[384,256]{1,0:T(8,128)(2,1)S(1)}, u32[]{:S(2)}, u32[]{:S(2)}) %collective-permute-start.10) | collective-permute-done | bytes 196640 | tf_op jit(solution)/shard_map/ppermute | solution.py:120
  29.9 0.6 collective-permute-start.5
  30.4 1.1 %slice_bitcast_fusion.k_ref = bf16[192,1536]{1,0:T(8,128)(2,1)S(1)} fusion(bf16[3,192,1536]{2,1,0:T(8,128)(2,1)} %param.9), kind=kLoop, calls=%fused_computation | loop fusion | bytes 1179648 | tf_op jit(solution)/shard_map/squeeze | solution.py:163
  31.6 0.2 collective-permute-done.5.b_ref
  31.8 1.4 %second_block.1 = (bf16[4,384,256]{2,1,0:T(8,128)(2,1)S(1)}, bf16[192,256]{1,0:T(8,128)(2,1)S(1)}, bf16[192,256]{1,0:T(8,128)(2,1)S(1)}, f32[2,384,256]{2,1,0:T(...) custom-call(bf16[2,384,256]{2,1,0:T(8,128)(2,1)S(1)} %middle.1.a_ref.mid_, ...), custom_call_target="tpu_custom_call" | custom-call | tf_op jit(solution)/shard_map/second_block/pallas_call | solution.py:148
  33.2 0.4 collective-permute-start.14
  33.7 1.3 %collective-permute-done.14.got_ref = bf16[2,384,256]{2,1,0:T(8,128)(2,1)S(1)} collective-permute-done((bf16[2,384,256]{2,1,0:T(8,128)(2,1)S(1)}, bf16[2,384,256]{2,1,0:T(8,128)(2,1)S(1)}, u32[]{:S(2)}, u32[]{:S(2)}) %collective-permute-start.14) | collective-permute-done | bytes 393248 | tf_op jit(solution)/shard_map/ppermute | solution.py:120
  35.1 1.6 %collective-permute-start.15 = (bf16[2,384,256]{2,1,0:T(8,128)(2,1)S(1)}, bf16[2,384,256]{2,1,0:T(8,128)(2,1)S(1)}, u32[]{:S(2)}, u32[]{:S(2)}) collective-permute-start(bf16[2,384,256]{2,1,0:T(8,128)(2,1)S(1)} %squash_sum.1.chip_ref), channel_id=1, source_target_pairs={{0,2},{1,3},{2,0},{3,1},{4,6},{5,7},{6,4},{7,5},{8,10},{9,11},{10,... | collective-permute-start | bytes 1179656 | tf_op jit(solution)/shard_map/ppermute | solution.py:120
  36.7 9.9 %collective-permute-done.15.other_ref = bf16[2,384,256]{2,1,0:T(8,128)(2,1)S(1)} collective-permute-done((bf16[2,384,256]{2,1,0:T(8,128)(2,1)S(1)}, bf16[2,384,256]{2,1,0:T(8,128)(2,1)S(1)}, u32[]{:S(2)}, u32[]{:S(2)}) %collective-permute-start.15) | collective-permute-done | bytes 393248 | tf_op jit(solution)/shard_map/ppermute | solution.py:120
  46.5 0.6 middle_grad.1.a_ref.g_ref.rest_0_
  47.3 0.5 collective-permute-start.12
  47.8 0.7 second_weights.1
  48.4 2.5 %collective-permute-start.22 = (bf16[384,384]{1,0:T(8,128)(2,1)S(1)}, bf16[384,384]{1,0:T(8,128)(2,1)S(1)}, u32[]{:S(2)}, u32[]{:S(2)}) collective-permute-start(bf16[384,384]{1,0:T(8,128)(2,1)S(1)} %get-tuple-element.71), channel_id=1, source_target_pairs={{0,4},{4,0},{8,12},{12,8},{1,5},{5,1},{9,13},{13,9},{2,6},{6,2},{1... | collective-permute-start | bytes 884744 | tf_op jit(solution)/shard_map/ppermute | solution.py:120
  50.9 1.1 %first_backward.1 = (bf16[192,256]{1,0:T(8,128)(2,1)S(1)}, f32[2,384,256]{2,1,0:T(8,128)S(1)}, bf16[2,384,256]{2,1,0:T(8,128)(2,1)S(1)}) custom-call(bf16[2,384,256]{2,1,0:T(8,128)(2,1)S(1)} %middle_grad.1.a_ref.g_ref.rest_0_, bf16[2,384,256]{2,1,0:T(8,128)(2,1)S(1)} %collective-permute-done.16.b_ref.rest_1_, ...), custom_call_target="tpu_custom_call" | custom-call | tf_op jit(solution)/shard_map/first_backward/pallas_call | solution.py:148
  52.1 0.7 collective-permute-start.23
  52.9 1.3 %collective-permute-start.24 = (bf16[384,384]{1,0:T(8,128)(2,1)S(1)}, bf16[384,384]{1,0:T(8,128)(2,1)S(1)}, u32[]{:S(2)}, u32[]{:S(2)}) collective-permute-start(bf16[384,384]{1,0:T(8,128)(2,1)S(1)} %get-tuple-element.73), channel_id=1, source_target_pairs={{0,12},{4,8},{8,4},{12,0},{1,13},{5,9},{9,5},{13,1},{2,14},{6,10},... | collective-permute-start | bytes 884744 | tf_op jit(solution)/shard_map/ppermute | solution.py:120
  54.2 0.7 first_weights.1
  54.9 6.1 %collective-permute-done.22.r1 = bf16[384,384]{1,0:T(8,128)(2,1)S(1)} collective-permute-done((bf16[384,384]{1,0:T(8,128)(2,1)S(1)}, bf16[384,384]{1,0:T(8,128)(2,1)S(1)}, u32[]{:S(2)}, u32[]{:S(2)}) %collective-permute-start.22) | collective-permute-done | bytes 294944 | tf_op jit(solution)/shard_map/ppermute | solution.py:120
  60.9 2.5 %collective-permute-start.19 = (bf16[384,384]{1,0:T(8,128)(2,1)S(1)}, bf16[384,384]{1,0:T(8,128)(2,1)S(1)}, u32[]{:S(2)}, u32[]{:S(2)}) collective-permute-start(bf16[384,384]{1,0:T(8,128)(2,1)S(1)} %get-tuple-element.62), channel_id=1, source_target_pairs={{0,4},{4,0},{8,12},{12,8},{1,5},{5,1},{9,13},{13,9},{2,6},{6,2},{1... | collective-permute-start | bytes 884744 | tf_op jit(solution)/shard_map/ppermute | solution.py:120
  63.4 9.5 %collective-permute-done.23.r2 = bf16[384,384]{1,0:T(8,128)(2,1)S(1)} collective-permute-done((bf16[384,384]{1,0:T(8,128)(2,1)S(1)}, bf16[384,384]{1,0:T(8,128)(2,1)S(1)}, u32[]{:S(2)}, u32[]{:S(2)}) %collective-permute-start.23) | collective-permute-done | bytes 294944 | tf_op jit(solution)/shard_map/ppermute | solution.py:120
  72.9 3.4 %collective-permute-start.20 = (bf16[384,384]{1,0:T(8,128)(2,1)S(1)}, bf16[384,384]{1,0:T(8,128)(2,1)S(1)}, u32[]{:S(2)}, u32[]{:S(2)}) collective-permute-start(bf16[384,384]{1,0:T(8,128)(2,1)S(1)} %get-tuple-element.63), channel_id=1, source_target_pairs={{0,8},{4,12},{8,0},{12,4},{1,9},{5,13},{9,1},{13,5},{2,10},{6,14},... | collective-permute-start | bytes 884744 | tf_op jit(solution)/shard_map/ppermute | solution.py:120
  76.3 1.3 %collective-permute-start.21 = (bf16[384,384]{1,0:T(8,128)(2,1)S(1)}, bf16[384,384]{1,0:T(8,128)(2,1)S(1)}, u32[]{:S(2)}, u32[]{:S(2)}) collective-permute-start(bf16[384,384]{1,0:T(8,128)(2,1)S(1)} %get-tuple-element.64), channel_id=1, source_target_pairs={{0,12},{4,8},{8,4},{12,0},{1,13},{5,9},{9,5},{13,1},{2,14},{6,10},... | collective-permute-start | bytes 884744 | tf_op jit(solution)/shard_map/ppermute | solution.py:120
  77.7 0.6 collective-permute-start.13
  78.4 15.3 %collective-permute-done.24.r3 = bf16[384,384]{1,0:T(8,128)(2,1)S(1)} collective-permute-done((bf16[384,384]{1,0:T(8,128)(2,1)S(1)}, bf16[384,384]{1,0:T(8,128)(2,1)S(1)}, u32[]{:S(2)}, u32[]{:S(2)}) %collective-permute-start.24) | collective-permute-done | bytes 294944 | tf_op jit(solution)/shard_map/ppermute | solution.py:120
  93.7 0.5 collective-permute-start.18
  94.2 1.1 %second_weights_total.1 = (f32[3,192,384]{2,1,0:T(8,128)}, f32[192,384]{1,0:T(8,128)}) custom-call(f32[384,384]{1,0:T(8,128)S(1)} %get-tuple-element.70.own_ref, bf16[384,384]{1,0:T(8,128)(2,1)S(1)} %collective-permute-done.22.r1, bf16[384,384]{1,0:T(8,128)(2,1)S(1)} %collective-permute-done.23.r2, bf16[384,384]{1,0:T(8,128)(2,1)S(1)} %collective-permute-done.24.r3), custom_call_target="tpu_custom_call" | custom-call | tf_op jit(solution)/shard_map/second_weights_total/pallas_call | solution.py:148
  95.3 0.7 out.1
  96.0 2.2 %collective-permute-done.20.r2 = bf16[384,384]{1,0:T(8,128)(2,1)S(1)} collective-permute-done((bf16[384,384]{1,0:T(8,128)(2,1)S(1)}, bf16[384,384]{1,0:T(8,128)(2,1)S(1)}, u32[]{:S(2)}, u32[]{:S(2)}) %collective-permute-start.20) | collective-permute-done | bytes 294944 | tf_op jit(solution)/shard_map/ppermute | solution.py:120
  98.2 7.5 %collective-permute-done.21.r3 = bf16[384,384]{1,0:T(8,128)(2,1)S(1)} collective-permute-done((bf16[384,384]{1,0:T(8,128)(2,1)S(1)}, bf16[384,384]{1,0:T(8,128)(2,1)S(1)}, u32[]{:S(2)}, u32[]{:S(2)}) %collective-permute-start.21) | collective-permute-done | bytes 294944 | tf_op jit(solution)/shard_map/ppermute | solution.py:120
  105.7 1.1 %first_weights_total.1 = (f32[3,192,384]{2,1,0:T(8,128)}, f32[192,384]{1,0:T(8,128)}) custom-call(f32[384,384]{1,0:T(8,128)S(1)} %get-tuple-element.61.own_ref, bf16[384,384]{1,0:T(8,128)(2,1)S(1)} %collective-permute-done.19.r1, bf16[384,384]{1,0:T(8,128)(2,1)S(1)} %collective-permute-done.20.r2, bf16[384,384]{1,0:T(8,128)(2,1)S(1)} %collective-permute-done.21.r3), custom_call_target="tpu_custom_call" | custom-call | tf_op jit(solution)/shard_map/first_weights_total/pallas_call | solution.py:148
  106.8 1.0 entry.1
  (33 shorter events, 0.7 us)
Async XLA Ops:
  0.6 6.9 %collective-permute-start = (bf16[384,256]{1,0:T(8,128)(2,1)}, bf16[384,256]{1,0:T(8,128)(2,1)S(1)}, u32[]{:S(2)}, u32[]{:S(2)}) collective-permute-start(bf16[384,256]{1,0:T(8,128)(2,1)} %x_ref.1), channel_id=1, source_target_pairs={{0,2},{1,3},{2,0},{3,1},{4,6},{5,7},{6,4},{7,5},{8,10},{9,11},{10,... | collective-permute-start | bytes 589832 | tf_op jit(solution)/shard_map/ppermute | solution.py:120
  2.2 6.5 %collective-permute-start.1 = (bf16[384,256]{1,0:T(8,128)(2,1)}, bf16[384,256]{1,0:T(8,128)(2,1)S(1)}, u32[]{:S(2)}, u32[]{:S(2)}) collective-permute-start(bf16[384,256]{1,0:T(8,128)(2,1)} %x_ref.1), channel_id=1, source_target_pairs={{0,1},{1,0},{2,3},{3,2},{4,5},{5,4},{6,7},{7,6},{8,9},{9,8},{10,11... | collective-permute-start | bytes 589832 | tf_op jit(solution)/shard_map/ppermute | solution.py:120
  7.5 1.4 %collective-permute-start.2 = (bf16[384,256]{1,0:T(8,128)(2,1)S(1)}, bf16[384,256]{1,0:T(8,128)(2,1)S(1)}, u32[]{:S(2)}, u32[]{:S(2)}) collective-permute-start(bf16[384,256]{1,0:T(8,128)(2,1)S(1)} %collective-permute-done.x2), channel_id=1, source_target_pairs={{0,1},{1,0},{2,3},{3,2},{4,5},{5,4},{6,7},{7,6},{8,9},{9,8},{10,11... | collective-permute-start | bytes 589832 | tf_op jit(solution)/shard_map/ppermute | solution.py:120
  9.0 1.1 copy-start
  10.1 0.9 copy-start.2
  11.0 4.8 %copy-start.5 = (bf16[2,48,1024]{2,1,0:T(8,128)(2,1)S(1)}, bf16[2,48,1024]{2,1,0:T(8,128)(2,1)}, u32[]{:S(2)}) copy-start(bf16[2,48,1024]{2,1,0:T(8,128)(2,1)} %g_ref.1) | copy-start | bytes 589828
  11.0 18.7 %copy-start.3 = (bf16[384,256]{1,0:T(8,128)(2,1)S(1)}, bf16[384,256]{1,0:T(8,128)(2,1)}, u32[]{:S(2)}) copy-start(bf16[384,256]{1,0:T(8,128)(2,1)} %x_ref.1) | copy-start | bytes 589828
  12.4 1.8 %collective-permute-start.3 = (bf16[2,384,256]{2,1,0:T(8,128)(2,1)S(1)}, bf16[2,384,256]{2,1,0:T(8,128)(2,1)S(1)}, u32[]{:S(2)}, u32[]{:S(2)}) collective-permute-start(bf16[2,384,256]{2,1,0:T(8,128)(2,1)S(1)} %get-tuple-element.42), channel_id=1, source_target_pairs={{0,1},{1,0},{2,3},{3,2},{4,5},{5,4},{6,7},{7,6},{8,9},{9,8},{10,11... | collective-permute-start | bytes 1179656 | tf_op jit(solution)/shard_map/ppermute | solution.py:120
  14.2 17.6 %copy-start.4 = (bf16[1536,192]{0,1:T(8,128)(2,1)S(1)}, bf16[1536,192]{0,1:T(8,128)(2,1)}, u32[]{:S(2)}) copy-start(bf16[1536,192]{0,1:T(8,128)(2,1)} %param.10) | copy-start | bytes 1769476
  14.2 15.5 %collective-permute-start.4 = (bf16[2,384,256]{2,1,0:T(8,128)(2,1)S(1)}, bf16[2,384,256]{2,1,0:T(8,128)(2,1)S(1)}, u32[]{:S(2)}, u32[]{:S(2)}) collective-permute-start(bf16[2,384,256]{2,1,0:T(8,128)(2,1)S(1)} %mix_sum.1.chip_ref), channel_id=1, source_target_pairs={{0,2},{1,3},{2,0},{3,1},{4,6},{5,7},{6,4},{7,5},{8,10},{9,11},{10,... | collective-permute-start | bytes 1179656 | tf_op jit(solution)/shard_map/ppermute | solution.py:120
  15.8 4.2 %collective-permute-start.6 = (bf16[2,48,256]{2,1,0:T(8,128)(2,1)S(1)}, bf16[2,48,256]{2,1,0:T(8,128)(2,1)S(1)}, u32[]{:S(2)}, u32[]{:S(2)}) collective-permute-start(bf16[2,48,256]{2,1,0:T(8,128)(2,1)S(1)} %get-tuple-element.44), channel_id=1, source_target_pairs={{0,4},{4,0},{8,12},{12,8},{1,5},{5,1},{9,13},{13,9},{2,6},{6,2},{1... | collective-permute-start | bytes 147464 | tf_op jit(solution)/shard_map/ppermute | solution.py:120
  16.3 6.1 %collective-permute-start.7 = (bf16[2,48,256]{2,1,0:T(8,128)(2,1)S(1)}, bf16[2,48,256]{2,1,0:T(8,128)(2,1)S(1)}, u32[]{:S(2)}, u32[]{:S(2)}) collective-permute-start(bf16[2,48,256]{2,1,0:T(8,128)(2,1)S(1)} %get-tuple-element.45), channel_id=1, source_target_pairs={{0,8},{4,12},{8,0},{12,4},{1,9},{5,13},{9,1},{13,5},{2,10},{6,14},... | collective-permute-start | bytes 147464 | tf_op jit(solution)/shard_map/ppermute | solution.py:120
  18.9 4.6 %collective-permute-start.8 = (bf16[2,48,256]{2,1,0:T(8,128)(2,1)S(1)}, bf16[2,48,256]{2,1,0:T(8,128)(2,1)S(1)}, u32[]{:S(2)}, u32[]{:S(2)}) collective-permute-start(bf16[2,48,256]{2,1,0:T(8,128)(2,1)S(1)} %get-tuple-element.46), channel_id=1, source_target_pairs={{0,12},{4,8},{8,4},{12,0},{1,13},{5,9},{9,5},{13,1},{2,14},{6,10},... | collective-permute-start | bytes 147464 | tf_op jit(solution)/shard_map/ppermute | solution.py:120
  23.6 6.2 %collective-permute-start.10 = (bf16[384,256]{1,0:T(8,128)(2,1)S(1)}, bf16[384,256]{1,0:T(8,128)(2,1)S(1)}, u32[]{:S(2)}, u32[]{:S(2)}) collective-permute-start(bf16[384,256]{1,0:T(8,128)(2,1)S(1)} %bitcast.9), channel_id=1, source_target_pairs={{0,2},{1,3},{2,0},{3,1},{4,6},{5,7},{6,4},{7,5},{8,10},{9,11},{10,... | collective-permute-start | bytes 589832 | tf_op jit(solution)/shard_map/ppermute | solution.py:120
  24.2 7.4 %collective-permute-start.9 = (bf16[384,256]{1,0:T(8,128)(2,1)S(1)}, bf16[384,256]{1,0:T(8,128)(2,1)S(1)}, u32[]{:S(2)}, u32[]{:S(2)}) collective-permute-start(bf16[384,256]{1,0:T(8,128)(2,1)S(1)} %bitcast.10), channel_id=1, source_target_pairs={{0,1},{1,0},{2,3},{3,2},{4,5},{5,4},{6,7},{7,6},{8,9},{9,8},{10,11... | collective-permute-start | bytes 589832 | tf_op jit(solution)/shard_map/ppermute | solution.py:120
  29.7 1.8 %collective-permute-start.11 = (bf16[384,256]{1,0:T(8,128)(2,1)S(1)}, bf16[384,256]{1,0:T(8,128)(2,1)S(1)}, u32[]{:S(2)}, u32[]{:S(2)}) collective-permute-start(bf16[384,256]{1,0:T(8,128)(2,1)S(1)} %collective-permute-done.10.g2.rest_2_), channel_id=1, source_target_pairs={{0,1},{1,0},{2,3},{3,2},{4,5},{5,4},{6,7},{7,6},{8,9},{9,8},{10,11... | collective-permute-start | bytes 589832 | tf_op jit(solution)/shard_map/ppermute | solution.py:120
  29.9 1.9 %collective-permute-start.5 = (bf16[2,384,256]{2,1,0:T(8,128)(2,1)S(1)}, bf16[2,384,256]{2,1,0:T(8,128)(2,1)S(1)}, u32[]{:S(2)}, u32[]{:S(2)}) collective-permute-start(bf16[2,384,256]{2,1,0:T(8,128)(2,1)S(1)} %middle.1.a_ref.mid_ref), channel_id=1, source_target_pairs={{0,1},{1,0},{2,3},{3,2},{4,5},{5,4},{6,7},{7,6},{8,9},{9,8},{10,11... | collective-permute-start | bytes 1179656 | tf_op jit(solution)/shard_map/ppermute | solution.py:120
  33.2 1.8 %collective-permute-start.14 = (bf16[2,384,256]{2,1,0:T(8,128)(2,1)S(1)}, bf16[2,384,256]{2,1,0:T(8,128)(2,1)S(1)}, u32[]{:S(2)}, u32[]{:S(2)}) collective-permute-start(bf16[2,384,256]{2,1,0:T(8,128)(2,1)S(1)} %get-tuple-element.52), channel_id=1, source_target_pairs={{0,1},{1,0},{2,3},{3,2},{4,5},{5,4},{6,7},{7,6},{8,9},{9,8},{10,11... | collective-permute-start | bytes 1179656 | tf_op jit(solution)/shard_map/ppermute | solution.py:120
  35.1 15.9 %copy-start.1 = (bf16[1536,192]{0,1:T(8,128)(2,1)S(1)}, bf16[1536,192]{0,1:T(8,128)(2,1)}, u32[]{:S(2)}) copy-start(bf16[1536,192]{0,1:T(8,128)(2,1)} %param.8) | copy-start | bytes 1769476
  35.1 11.5 %collective-permute-start.15 = (bf16[2,384,256]{2,1,0:T(8,128)(2,1)S(1)}, bf16[2,384,256]{2,1,0:T(8,128)(2,1)S(1)}, u32[]{:S(2)}, u32[]{:S(2)}) collective-permute-start(bf16[2,384,256]{2,1,0:T(8,128)(2,1)S(1)} %squash_sum.1.chip_ref), channel_id=1, source_target_pairs={{0,2},{1,3},{2,0},{3,1},{4,6},{5,7},{6,4},{7,5},{8,10},{9,11},{10,... | collective-permute-start | bytes 1179656 | tf_op jit(solution)/shard_map/ppermute | solution.py:120
  47.2 3.8 %collective-permute-start.16 = (bf16[2,384,256]{2,1,0:T(8,128)(2,1)S(1)}, bf16[2,384,256]{2,1,0:T(8,128)(2,1)S(1)}, u32[]{:S(2)}, u32[]{:S(2)}) collective-permute-start(bf16[2,384,256]{2,1,0:T(8,128)(2,1)S(1)} %middle_grad.1.a_ref.g_ref.rest_0_), channel_id=1, source_target_pairs={{0,1},{1,0},{2,3},{3,2},{4,5},{5,4},{6,7},{7,6},{8,9},{9,8},{10,11... | collective-permute-start | bytes 1179656 | tf_op jit(solution)/shard_map/ppermute | solution.py:120
  47.3 29.1 %collective-permute-start.12 = (bf16[2,384,256]{2,1,0:T(8,128)(2,1)S(1)}, bf16[2,384,256]{2,1,0:T(8,128)(2,1)S(1)}, u32[]{:S(2)}, u32[]{:S(2)}) collective-permute-start(bf16[2,384,256]{2,1,0:T(8,128)(2,1)S(1)} %get-tuple-element.48), channel_id=1, source_target_pairs={{0,1},{1,0},{2,3},{3,2},{4,5},{5,4},{6,7},{7,6},{8,9},{9,8},{10,11... | collective-permute-start | bytes 1179656 | tf_op jit(solution)/shard_map/ppermute | solution.py:120
  48.4 12.5 %collective-permute-start.22 = (bf16[384,384]{1,0:T(8,128)(2,1)S(1)}, bf16[384,384]{1,0:T(8,128)(2,1)S(1)}, u32[]{:S(2)}, u32[]{:S(2)}) collective-permute-start(bf16[384,384]{1,0:T(8,128)(2,1)S(1)} %get-tuple-element.71), channel_id=1, source_target_pairs={{0,4},{4,0},{8,12},{12,8},{1,5},{5,1},{9,13},{13,9},{2,6},{6,2},{1... | collective-permute-start | bytes 884744 | tf_op jit(solution)/shard_map/ppermute | solution.py:120
  52.0 25.7 %collective-permute-start.17 = (bf16[2,384,256]{2,1,0:T(8,128)(2,1)S(1)}, bf16[2,384,256]{2,1,0:T(8,128)(2,1)S(1)}, u32[]{:S(2)}, u32[]{:S(2)}) collective-permute-start(bf16[2,384,256]{2,1,0:T(8,128)(2,1)S(1)} %get-tuple-element.55), channel_id=1, source_target_pairs={{0,1},{1,0},{2,3},{3,2},{4,5},{5,4},{6,7},{7,6},{8,9},{9,8},{10,11... | collective-permute-start | bytes 1179656 | tf_op jit(solution)/shard_map/ppermute | solution.py:120
  52.1 20.8 %collective-permute-start.23 = (bf16[384,384]{1,0:T(8,128)(2,1)S(1)}, bf16[384,384]{1,0:T(8,128)(2,1)S(1)}, u32[]{:S(2)}, u32[]{:S(2)}) collective-permute-start(bf16[384,384]{1,0:T(8,128)(2,1)S(1)} %get-tuple-element.72), channel_id=1, source_target_pairs={{0,8},{4,12},{8,0},{12,4},{1,9},{5,13},{9,1},{13,5},{2,10},{6,14},... | collective-permute-start | bytes 884744 | tf_op jit(solution)/shard_map/ppermute | solution.py:120
  52.9 40.8 %collective-permute-start.24 = (bf16[384,384]{1,0:T(8,128)(2,1)S(1)}, bf16[384,384]{1,0:T(8,128)(2,1)S(1)}, u32[]{:S(2)}, u32[]{:S(2)}) collective-permute-start(bf16[384,384]{1,0:T(8,128)(2,1)S(1)} %get-tuple-element.73), channel_id=1, source_target_pairs={{0,12},{4,8},{8,4},{12,0},{1,13},{5,9},{9,5},{13,1},{2,14},{6,10},... | collective-permute-start | bytes 884744 | tf_op jit(solution)/shard_map/ppermute | solution.py:120
  60.9 35.1 %collective-permute-start.19 = (bf16[384,384]{1,0:T(8,128)(2,1)S(1)}, bf16[384,384]{1,0:T(8,128)(2,1)S(1)}, u32[]{:S(2)}, u32[]{:S(2)}) collective-permute-start(bf16[384,384]{1,0:T(8,128)(2,1)S(1)} %get-tuple-element.62), channel_id=1, source_target_pairs={{0,4},{4,0},{8,12},{12,8},{1,5},{5,1},{9,13},{13,9},{2,6},{6,2},{1... | collective-permute-start | bytes 884744 | tf_op jit(solution)/shard_map/ppermute | solution.py:120
  72.9 25.3 %collective-permute-start.20 = (bf16[384,384]{1,0:T(8,128)(2,1)S(1)}, bf16[384,384]{1,0:T(8,128)(2,1)S(1)}, u32[]{:S(2)}, u32[]{:S(2)}) collective-permute-start(bf16[384,384]{1,0:T(8,128)(2,1)S(1)} %get-tuple-element.63), channel_id=1, source_target_pairs={{0,8},{4,12},{8,0},{12,4},{1,9},{5,13},{9,1},{13,5},{2,10},{6,14},... | collective-permute-start | bytes 884744 | tf_op jit(solution)/shard_map/ppermute | solution.py:120
  76.3 29.4 %collective-permute-start.21 = (bf16[384,384]{1,0:T(8,128)(2,1)S(1)}, bf16[384,384]{1,0:T(8,128)(2,1)S(1)}, u32[]{:S(2)}, u32[]{:S(2)}) collective-permute-start(bf16[384,384]{1,0:T(8,128)(2,1)S(1)} %get-tuple-element.64), channel_id=1, source_target_pairs={{0,12},{4,8},{8,4},{12,0},{1,13},{5,9},{9,5},{13,1},{2,14},{6,10},... | collective-permute-start | bytes 884744 | tf_op jit(solution)/shard_map/ppermute | solution.py:120
  77.7 17.6 %collective-permute-start.13 = (bf16[384,256]{1,0:T(8,128)(2,1)S(1)}, bf16[384,256]{1,0:T(8,128)(2,1)S(1)}, u32[]{:S(2)}, u32[]{:S(2)}) collective-permute-start(bf16[384,256]{1,0:T(8,128)(2,1)S(1)} %get-tuple-element.50), channel_id=1, source_target_pairs={{0,2},{1,3},{2,0},{3,1},{4,6},{5,7},{6,4},{7,5},{8,10},{9,11},{10,... | collective-permute-start | bytes 589832 | tf_op jit(solution)/shard_map/ppermute | solution.py:120
  93.7 13.2 %collective-permute-start.18 = (bf16[384,256]{1,0:T(8,128)(2,1)S(1)}, bf16[384,256]{1,0:T(8,128)(2,1)S(1)}, u32[]{:S(2)}, u32[]{:S(2)}) collective-permute-start(bf16[384,256]{1,0:T(8,128)(2,1)S(1)} %get-tuple-element.57), channel_id=1, source_target_pairs={{0,2},{1,3},{2,0},{3,1},{4,6},{5,7},{6,4},{7,5},{8,10},{9,11},{10,... | collective-permute-start | bytes 589832 | tf_op jit(solution)/shard_map/ppermute | solution.py:120

commit v3 on v2

--- a/solution.py
+++ b/solution.py
@@ -160,19 +160,49 @@
     rows, bins = x.shape
     hid, chans = taps_a.shape[1], taps_a.shape[2]
     heads, val, _ = grad_heads.shape
-    tap_a, tap_b = taps_a[1], taps_b[1]
-    cols_a, cols_b = point_a.T, point_b.T
-
     def block(m, j):
         return pl.ds(pl.multiple_of((m ^ j) * rows, rows), rows)
 
-    def split_body(g_ref, *outs):
+    x_far = swap(x, "mp", 2)
+    x_near = swap(x, "mp", 1)
+
+    def load_body(x_ref, ta, tb, ca, cb, g_ref, *rest):
+        outs, sems = rest[:-1], rest[-1]
         c = lax.axis_index("ctx")
+        sources = [x_ref, ta.at[1], tb.at[1], ca, cb]
         for k in range(4):
-            outs[k][...] = g_ref[:, :, pl.ds(pl.multiple_of((c ^ k) * bins, bins), bins)]
-
-    pieces = call(split_body, [((heads, val, bins), BF16)] * 4, (grad_heads,), "split_grad")
+            at = pl.multiple_of((c ^ k) * bins, bins)
+            sources.append(g_ref.at[:, :, pl.ds(at, bins)])
+        copies = [
+            pltpu.make_async_copy(source, out, sems.at[i])
+            for i, (source, out) in enumerate(zip(sources, outs))
+        ]
+        for copy in copies:
+            copy.start()
+        for copy in copies:
+            copy.wait()
+
+    weight = ((hid, chans), BF16)
+    piece = ((heads, val, bins), BF16)
+    x_own, tap_a, tap_b, cols_a, cols_b, *pieces = pl.pallas_call(
+        load_body,
+        out_shape=[pltpu.VMEM((rows, bins), BF16)]
+        + [pltpu.VMEM(*weight)] * 4
+        + [pltpu.VMEM(*piece)] * 4,
+        in_specs=[pl.BlockSpec(memory_space=pltpu.HBM)] * 6,
+        out_specs=[VMEM] * 9,
+        scratch_shapes=[pltpu.SemaphoreType.DMA((9,))],
+        compiler_params=pltpu.CompilerParams(vmem_limit_bytes=16 << 20),
+        name="load",
+    )(
+        *[
+            pltpu.with_memory_space_constraint(source, pltpu.HBM)
+            for source in (x, taps_a, taps_b, point_a.T, point_b.T, grad_heads)
+        ]
+    )
     pieces = [pieces[0]] + [swap(pieces[k], "ctx", k) for k in (1, 2, 3)]
+    x_far, x_own = lax.optimization_barrier((x_far, x_own))
+    x_cross = swap(x_far, "mp", 1)
 
     def join_body(*refs):
         c = lax.axis_index("ctx")
@@ -186,11 +216,7 @@
     g_near = swap(g_own, "mp", 1)
     g_cross = swap(g_far, "mp", 1)
 
-    x_far = swap(x, "mp", 2)
-    x_near = swap(x, "mp", 1)
-    x_cross = swap(x_far, "mp", 1)
-
-    def first_body(x0, x1, x2, x3, k_ref, p_ref, z_ref, v_ref, s_ref, keep_ref, send_ref):
+    def first_body(x0, x1, x2, x3, k_ref, p_ref, _, z_ref, v_ref, s_ref, keep_ref, send_ref):
         m = lax.axis_index("mp")
         u = jnp.zeros((hid, bins), F32)
         for j, ref in enumerate((x0, x1, x2, x3)):
@@ -215,16 +241,16 @@
             ((2, rows, bins), F32),
             ((2, rows, bins), BF16),
         ],
-        (x, x_near, x_far, x_cross, tap_a, cols_a),
+        (x_own, x_near, x_far, x_cross, tap_a, cols_a, g_own),
         "first_forward",
     )
     got = swap(send, "mp", 1)
 
-    def near_body(keep_ref, got_ref, out_ref):
-        out_ref[...] = (keep_ref[...] + got_ref[...].astype(F32)).astype(BF16)
-
-    def near_sum(keep, got, name):
-        return call(near_body, [((2, rows, bins), BF16)], (keep, got), name)[0]
+    def near_body(keep_ref, got_ref, *rest):
+        rest[-1][...] = (keep_ref[...] + got_ref[...].astype(F32)).astype(BF16)
+
+    def near_sum(keep, got, name, after=()):
+        return call(near_body, [((2, rows, bins), BF16)], (keep, got, *after), name)[0]
 
     chip = near_sum(keep, got, "mix_sum")
     other = swap(chip, "mp", 2)
@@ -235,7 +261,7 @@
             out_ref[i] = (ref[...].astype(F32) + mixed).astype(BF16)
 
     (mid,) = call(
-        middle_body, [((2, rows, bins), BF16)], (x, x_far, chip, other), "middle"
+        middle_body, [((2, rows, bins), BF16)], (x_own, x_far, chip, other), "middle"
     )
     mid_near = swap(mid, "mp", 1)
 
@@ -281,9 +307,88 @@
         (mid, mid_near, g_own, g_near, g_far, g_cross, tap_b, cols_b),
         "second_block",
     )
+    def weight_body(fill, z_ref, gu_ref, v_ref, *rest):
+        grads, (keep_k, keep_p, send_k, send_p, g_ref) = rest[:-5], rest[-5:]
+        j = lax.axis_index("mp") ^ lax.axis_index("ctx")
+        fill(g_ref, grads)
+
+        def taps(k):
+            return dot(gu_ref[...], z_ref[j ^ k], ((1,), (1,)))
+
+        def proj(k):
+            return dot(v_ref[...], g_ref[j ^ k], ((1,), (1,)))
+
+        for i, k in enumerate((1, 3)):
+            send_k[i] = taps(k).astype(BF16)
+        for i, k in enumerate((2, 3)):
+            send_p[i] = proj(k).astype(BF16)
+        for i, k in enumerate((0, 2)):
+            keep_k[i] = taps(k)
+        for i, k in enumerate((0, 1)):
+            keep_p[i] = proj(k)
+
+    def fill_tiles(g_ref, grads):
+        for j, ref in enumerate(grads):
+            g_ref[j] = ref[...]
+
+    def fill_pairs(g_ref, grads):
+        for j in range(4):
+            g_ref[j] = grads[j & 1][j >> 1]
+
+    two = (2, hid, rows)
+
+    def weights(z, gu, v, grads, fill, name):
+        return call(
+            functools.partial(weight_body, fill),
+            [(two, F32), (two, F32), (two, BF16), (two, BF16)],
+            (z, gu, v, *grads),
+            name,
+            [pltpu.VMEM((4, rows, bins), BF16)],
+        )
+
+    def half_body(keep_k, keep_p, got_k, got_p, own_k, own_p, send_k, send_p):
+        own_k[...] = keep_k[0] + got_k[0].astype(F32)
+        own_p[...] = keep_p[0] + got_p[0].astype(F32)
+        send_k[...] = (keep_k[1] + got_k[1].astype(F32)).astype(BF16)
+        send_p[...] = (keep_p[1] + got_p[1].astype(F32)).astype(BF16)
+
+    def first_swap(send_k, send_p):
+        return swap(send_k, "ctx", 1), swap(send_p, "ctx", 2)
+
+    def half_sum(keep_k, keep_p, got_k, got_p, name):
+        one = (hid, rows)
+        return call(
+            half_body,
+            [(one, F32), (one, F32), (one, BF16), (one, BF16)],
+            (keep_k, keep_p, got_k, got_p),
+            name,
+        )
+
+    def total_body(own_k, own_p, got_k, got_p, taps_ref, proj_ref):
+        taps_ref[0] = jnp.zeros((hid, rows), F32)
+        taps_ref[1] = own_k[...] + got_k[...].astype(F32)
+        taps_ref[2] = jnp.zeros((hid, rows), F32)
+        proj_ref[...] = own_p[...] + got_p[...].astype(F32)
+
+    def total(own_k, own_p, got_k, got_p, name):
+        taps, proj = call(
+            total_body,
+            [((3, hid, rows), F32), ((hid, rows), F32)],
+            (own_k, own_p, got_k, got_p),
+            name,
+            final=True,
+        )
+        return taps, proj.T
+
+    parts_b = weights(
+        z_b, gu_b, v_b, (g_own, g_near, g_far, g_cross), fill_tiles, "second_weights"
+    )
     got = swap(send, "mp", 1)
-    chip = near_sum(keep, got, "squash_sum")
+    chip = near_sum(keep, got, "squash_sum", parts_b[:1])
     other = swap(chip, "mp", 2)
+    other, *got_b = lax.optimization_barrier((other, *first_swap(*parts_b[2:])))
+    parts_b = half_sum(*parts_b[:2], *got_b, "second_half")
+    parts_b = (*parts_b[:2], swap(parts_b[2], "ctx", 2), swap(parts_b[3], "ctx", 1))
 
     def back_body(g0, g2, mid_ref, chip_ref, other_ref, out_ref):
         for i, ref in enumerate((g0, g2)):
@@ -317,7 +422,7 @@
 
     (second_out,) = call(out_body, [((rows, bins), BF16)], (mid, y_own, y_got), "out", final=True)
 
-    def first_back_body(a_ref, b_ref, k_ref, p_ref, s_ref, gu_ref, keep_ref, send_ref):
+    def first_back_body(a_ref, b_ref, k_ref, p_ref, s_ref, _a, _b, gu_ref, keep_ref, send_ref):
         m = lax.axis_index("mp")
         gv = jnp.zeros((hid, bins), F32)
         for j in range(4):
@@ -333,9 +438,10 @@
     gu_a, keep, send = call(
         first_back_body,
         [((hid, bins), BF16), ((2, rows, bins), F32), ((2, rows, bins), BF16)],
-        (g_mid, g_mid_near, tap_a, cols_a, slope_a),
+        (g_mid, g_mid_near, tap_a, cols_a, slope_a, *parts_b[2:]),
         "first_backward",
     )
+    parts_a = weights(z_a, gu_a, v_a, (g_mid, g_mid_near), fill_pairs, "first_weights")
     got = swap(send, "mp", 1)
     e_own, e_send = last_sum(keep, got, "entry_sum")
     e_got = swap(e_send, "mp", 2)
@@ -346,65 +452,12 @@
             g_ref[0].astype(F32) + grad * slope_of(x_ref[...].astype(F32))
         ).astype(BF16)
 
-    (entry,) = call(entry_body, [((rows, bins), BF16)], (g_mid, x, e_own, e_got), "entry", final=True)
-
-    def weight_body(fill, z_ref, gu_ref, v_ref, *rest):
-        grads, (own_ref, *outs, g_ref) = rest[:-5], rest[-5:]
-        m = lax.axis_index("mp")
-        c = lax.axis_index("ctx")
-        fill(g_ref, grads)
-        for k in (1, 2, 3, 0):
-            j = m ^ c ^ k
-            taps = dot(gu_ref[...], z_ref[j], ((1,), (1,)))
-            proj = dot(v_ref[...], g_ref[j], ((1,), (1,)))
-            out = own_ref if k == 0 else outs[k - 1]
-            out[:hid, :] = taps.astype(out.dtype)
-            out[hid:, :] = proj.astype(out.dtype)
-
-    def fill_tiles(g_ref, grads):
-        for j, ref in enumerate(grads):
-            g_ref[j] = ref[...]
-
-    def fill_pairs(g_ref, grads):
-        for j in range(4):
-            g_ref[j] = grads[j & 1][j >> 1]
-
-    def weights(z, gu, v, grads, fill, name):
-        own, *sends = call(
-            functools.partial(weight_body, fill),
-            [((2 * hid, rows), F32)] + [((2 * hid, rows), BF16)] * 3,
-            (z, gu, v, *grads),
-            name,
-            [pltpu.VMEM((4, rows, bins), BF16)],
-        )
-        gots = [swap(part, "ctx", k + 1) for k, part in enumerate(sends)]
-
-        def total_body(own_ref, r1, r2, r3, taps_ref, proj_ref):
-            def total(part):
-                return own_ref[part, :] + (
-                    r1[part, :].astype(F32) + r2[part, :].astype(F32) + r3[part, :].astype(F32)
-                )
-
-            taps_ref[0] = jnp.zeros((hid, rows), F32)
-            taps_ref[1] = total(pl.ds(0, hid))
-            taps_ref[2] = jnp.zeros((hid, rows), F32)
-            proj_ref[...] = total(pl.ds(hid, hid))
-
-        taps, proj = call(
-            total_body,
-            [((3, hid, rows), F32), ((hid, rows), F32)],
-            (own, *gots),
-            name + "_total",
-            final=True,
-        )
-        return taps, proj.T
-
-    taps_b_grad, point_b_grad = weights(
-        z_b, gu_b, v_b, (g_own, g_near, g_far, g_cross), fill_tiles, "second_weights"
-    )
-    taps_a_grad, point_a_grad = weights(
-        z_a, gu_a, v_a, (g_mid, g_mid_near), fill_pairs, "first_weights"
-    )
+    (entry,) = call(entry_body, [((rows, bins), BF16)], (g_mid, x_own, e_own, e_got), "entry", final=True)
+
+    taps_b_grad, point_b_grad = total(*parts_b, "second_total")
+    parts_a = half_sum(*parts_a[:2], *first_swap(*parts_a[2:]), "first_half")
+    parts_a = (*parts_a[:2], swap(parts_a[2], "ctx", 2), swap(parts_a[3], "ctx", 1))
+    taps_a_grad, point_a_grad = total(*parts_a, "first_total")
     return second_out, entry, taps_a_grad, point_a_grad, taps_b_grad, point_b_grad
 
 

time: 108 us -> 101 us (0.935)
  the two profiles are of different devices: /device:TPU:12 before, /device:TPU:0 now
where the time goes in v3:
time: 101 us
  waiting for transfers between devices  64.4 us (64%)
  starting transfers between devices  23.5 us (23%)
  Pallas kernels  12.1 us (12%)
    ppermute x27, waiting for transfers between devices, swap(): return lax.ppermute(value, axis, [(i, i ^ bits) for i in range(size)])  64.4 us
    ppermute x27, starting transfers between devices, swap(): return lax.ppermute(value, axis, [(i, i ^ bits) for i in range(size)])  23.5 us
    pallas_call x18, Pallas kernels, call(): pl.pallas_call(body, out_shape=[struct(s, d) for s, d in outs], in_specs=...  10.4 us
  transfers between devices with their start and end apart: 27, of which 16 were waited for; matrix products, arithmetic and copies ran while one was open for 0% of the time, Pallas kernels for 8%

profile of v3, /device:TPU:0, one launch (start us, length us, event | category | flops | bytes accessed | tf_op | source)
XLA Modules:
  0.0 100.8 jit_solution(11771737164692743629)
XLA Ops:
  0.6 3.0 %collective-permute-start = (bf16[384,256]{1,0:T(8,128)(2,1)}, bf16[384,256]{1,0:T(8,128)(2,1)S(1)}, u32[]{:S(2)}, u32[]{:S(2)}) collective-permute-start(bf16[384,256]{1,0:T(8,128)(2,1)} %x_ref.1), channel_id=1, source_target_pairs={{0,2},{1,3},{2,0},{3,1},{4,6},{5,7},{6,4},{7,5},{8,10},{9,11},{10,... | collective-permute-start | bytes 589832 | tf_op jit(solution)/shard_map/ppermute | solution.py:120
  3.6 1.8 %load.1 = (bf16[384,256]{1,0:T(8,128)(2,1)S(1)}, bf16[192,1536]{1,0:T(8,128)(2,1)S(1)}, bf16[192,1536]{1,0:T(8,128)(2,1)S(1)}, bf16[192,1536]{1,0:T(8,128)(2,1)S...) custom-call(bf16[384,256]{1,0:T(8,128)(2,1)} %x_ref.1, ...), custom_call_target="tpu_custom_call" | custom-call | tf_op jit(solution)/shard_map/load/pallas_call | solution.py:187
  5.4 3.3 %collective-permute-done.x2 = bf16[384,256]{1,0:T(8,128)(2,1)S(1)} collective-permute-done((bf16[384,256]{1,0:T(8,128)(2,1)}, bf16[384,256]{1,0:T(8,128)(2,1)S(1)}, u32[]{:S(2)}, u32[]{:S(2)}) %collective-permute-start) | collective-permute-done | bytes 196640 | tf_op jit(solution)/shard_map/ppermute | solution.py:120
  8.8 1.8 %collective-permute-start.3 = (bf16[2,48,256]{2,1,0:T(8,128)(2,1)S(1)}, bf16[2,48,256]{2,1,0:T(8,128)(2,1)S(1)}, u32[]{:S(2)}, u32[]{:S(2)}) collective-permute-start(bf16[2,48,256]{2,1,0:T(8,128)(2,1)S(1)} %get-tuple-element.65), channel_id=1, source_target_pairs={{0,4},{4,0},{8,12},{12,8},{1,5},{5,1},{9,13},{13,9},{2,6},{6,2},{1... | collective-permute-start | bytes 147464 | tf_op jit(solution)/shard_map/ppermute | solution.py:120
  10.6 2.6 %collective-permute-start.4 = (bf16[2,48,256]{2,1,0:T(8,128)(2,1)S(1)}, bf16[2,48,256]{2,1,0:T(8,128)(2,1)S(1)}, u32[]{:S(2)}, u32[]{:S(2)}) collective-permute-start(bf16[2,48,256]{2,1,0:T(8,128)(2,1)S(1)} %get-tuple-element.66), channel_id=1, source_target_pairs={{0,8},{4,12},{8,0},{12,4},{1,9},{5,13},{9,1},{13,5},{2,10},{6,14},... | collective-permute-start | bytes 147464 | tf_op jit(solution)/shard_map/ppermute | solution.py:120
  13.2 3.6 %collective-permute-done.4.refs_2_ = bf16[2,48,256]{2,1,0:T(8,128)(2,1)S(1)} collective-permute-done((bf16[2,48,256]{2,1,0:T(8,128)(2,1)S(1)}, bf16[2,48,256]{2,1,0:T(8,128)(2,1)S(1)}, u32[]{:S(2)}, u32[]{:S(2)}) %collective-permute-start.4) | collective-permute-done | bytes 49184 | tf_op jit(solution)/shard_map/ppermute | solution.py:120
  16.7 2.3 %collective-permute-done.5.refs_3_ = bf16[2,48,256]{2,1,0:T(8,128)(2,1)S(1)} collective-permute-done((bf16[2,48,256]{2,1,0:T(8,128)(2,1)S(1)}, bf16[2,48,256]{2,1,0:T(8,128)(2,1)S(1)}, u32[]{:S(2)}, u32[]{:S(2)}) %collective-permute-start.5) | collective-permute-done | bytes 49184 | tf_op jit(solution)/shard_map/ppermute | solution.py:120
  19.1 1.4 %first_forward.1 = (bf16[4,384,256]{2,1,0:T(8,128)(2,1)S(1)}, bf16[192,256]{1,0:T(8,128)(2,1)S(1)}, f32[192,256]{1,0:T(8,128)S(1)}, f32[2,384,256]{2,1,0:T(8,128)S(1)}, bf16[2,384,256]{2,1,0:T(8,128)(2,1)S(1)}) custom-call(bf16[384,256]{1,0:T(8,128)(2,1)S(1)} %get-tuple-element.60.x0.x_ref, bf16[384,256]{1,0:T(8,128)(2,1)S(1)} %collective-permute-done.1.x1, ...), custom_call_target="tpu_custom_call" | custom-call | tf_op jit(solution)/shard_map/first_forward/pallas_call | solution.py:148
  20.6 1.7 %collective-permute-done.6.got_ref = bf16[2,384,256]{2,1,0:T(8,128)(2,1)S(1)} collective-permute-done((bf16[2,384,256]{2,1,0:T(8,128)(2,1)S(1)}, bf16[2,384,256]{2,1,0:T(8,128)(2,1)S(1)}, u32[]{:S(2)}, u32[]{:S(2)}) %collective-permute-start.6) | collective-permute-done | bytes 393248 | tf_op jit(solution)/shard_map/ppermute | solution.py:120
  22.3 1.6 %collective-permute-start.7 = (bf16[2,384,256]{2,1,0:T(8,128)(2,1)S(1)}, bf16[2,384,256]{2,1,0:T(8,128)(2,1)S(1)}, u32[]{:S(2)}, u32[]{:S(2)}) collective-permute-start(bf16[2,384,256]{2,1,0:T(8,128)(2,1)S(1)} %mix_sum.1.chip_ref), channel_id=1, source_target_pairs={{0,2},{1,3},{2,0},{3,1},{4,6},{5,7},{6,4},{7,5},{8,10},{9,11},{10,... | collective-permute-start | bytes 1179656 | tf_op jit(solution)/shard_map/ppermute | solution.py:120
  23.9 0.5 collective-permute-start.10
  24.4 9.9 %collective-permute-done.7.other_ref = bf16[2,384,256]{2,1,0:T(8,128)(2,1)S(1)} collective-permute-done((bf16[2,384,256]{2,1,0:T(8,128)(2,1)S(1)}, bf16[2,384,256]{2,1,0:T(8,128)(2,1)S(1)}, u32[]{:S(2)}, u32[]{:S(2)}) %collective-permute-start.7) | collective-permute-done | bytes 393248 | tf_op jit(solution)/shard_map/ppermute | solution.py:120
  34.4 0.1 middle.1.a_ref.mid_ref
  34.5 0.1 collective-permute-start.8
  34.6 0.5 collective-permute-start.9
  35.1 2.7 %collective-permute-done.10.g2.rest_2_ = bf16[384,256]{1,0:T(8,128)(2,1)S(1)} collective-permute-done((bf16[384,256]{1,0:T(8,128)(2,1)S(1)}, bf16[384,256]{1,0:T(8,128)(2,1)S(1)}, u32[]{:S(2)}, u32[]{:S(2)}) %collective-permute-start.10) | collective-permute-done | bytes 196640 | tf_op jit(solution)/shard_map/ppermute | solution.py:120
  37.8 1.4 %collective-permute-done.11.g3.rest_3_ = bf16[384,256]{1,0:T(8,128)(2,1)S(1)} collective-permute-done((bf16[384,256]{1,0:T(8,128)(2,1)S(1)}, bf16[384,256]{1,0:T(8,128)(2,1)S(1)}, u32[]{:S(2)}, u32[]{:S(2)}) %collective-permute-start.11) | collective-permute-done | bytes 196640 | tf_op jit(solution)/shard_map/ppermute | solution.py:120
  39.2 1.4 %second_block.1 = (bf16[4,384,256]{2,1,0:T(8,128)(2,1)S(1)}, bf16[192,256]{1,0:T(8,128)(2,1)S(1)}, bf16[192,256]{1,0:T(8,128)(2,1)S(1)}, f32[2,384,256]{2,1,0:T(...) custom-call(bf16[2,384,256]{2,1,0:T(8,128)(2,1)S(1)} %middle.1.a_ref.mid_, ...), custom_call_target="tpu_custom_call" | custom-call | tf_op jit(solution)/shard_map/second_block/pallas_call | solution.py:148
  40.6 0.2 collective-permute-start.14
  40.8 0.7 second_weights.1
  41.5 0.9 collective-permute-done.14.got_ref
  42.5 1.6 %collective-permute-start.15 = (bf16[2,384,256]{2,1,0:T(8,128)(2,1)S(1)}, bf16[2,384,256]{2,1,0:T(8,128)(2,1)S(1)}, u32[]{:S(2)}, u32[]{:S(2)}) collective-permute-start(bf16[2,384,256]{2,1,0:T(8,128)(2,1)S(1)} %squash_sum.1.chip_ref), channel_id=1, source_target_pairs={{0,2},{1,3},{2,0},{3,1},{4,6},{5,7},{6,4},{7,5},{8,10},{9,11},{10,... | collective-permute-start | bytes 1179656 | tf_op jit(solution)/shard_map/ppermute | solution.py:120
  44.0 2.0 %collective-permute-start.17 = (bf16[2,192,384]{2,1,0:T(8,128)(2,1)S(1)}, bf16[2,192,384]{2,1,0:T(8,128)(2,1)S(1)}, u32[]{:S(2)}, u32[]{:S(2)}) collective-permute-start(bf16[2,192,384]{2,1,0:T(8,128)(2,1)S(1)} %get-tuple-element.83), channel_id=1, source_target_pairs={{0,8},{4,12},{8,0},{12,4},{1,9},{5,13},{9,1},{13,5},{2,10},{6,14},... | collective-permute-start | bytes 884744 | tf_op jit(solution)/shard_map/ppermute | solution.py:120
  46.0 12.7 %collective-permute-done.16.got_k = bf16[2,192,384]{2,1,0:T(8,128)(2,1)S(1)} collective-permute-done((bf16[2,192,384]{2,1,0:T(8,128)(2,1)S(1)}, bf16[2,192,384]{2,1,0:T(8,128)(2,1)S(1)}, u32[]{:S(2)}, u32[]{:S(2)}) %collective-permute-start.16) | collective-permute-done | bytes 294944 | tf_op jit(solution)/shard_map/ppermute | solution.py:120
  58.8 1.3 %collective-permute-done.17.got_p = bf16[2,192,384]{2,1,0:T(8,128)(2,1)S(1)} collective-permute-done((bf16[2,192,384]{2,1,0:T(8,128)(2,1)S(1)}, bf16[2,192,384]{2,1,0:T(8,128)(2,1)S(1)}, u32[]{:S(2)}, u32[]{:S(2)}) %collective-permute-start.17) | collective-permute-done | bytes 294944 | tf_op jit(solution)/shard_map/ppermute | solution.py:120
  60.1 0.6 middle_grad.1.a_ref.g_ref.rest_0_
  60.8 0.1 second_half.1
  60.9 0.4 collective-permute-start.19
  61.3 2.4 %collective-permute-start.20 = (bf16[192,384]{1,0:T(8,128)(2,1)S(1)}, bf16[192,384]{1,0:T(8,128)(2,1)S(1)}, u32[]{:S(2)}, u32[]{:S(2)}) collective-permute-start(bf16[192,384]{1,0:T(8,128)(2,1)S(1)} %get-tuple-element.90), channel_id=1, source_target_pairs={{0,4},{4,0},{8,12},{12,8},{1,5},{5,1},{9,13},{13,9},{2,6},{6,2},{1... | collective-permute-start | bytes 442376 | tf_op jit(solution)/shard_map/ppermute | solution.py:120
  63.8 7.2 %collective-permute-done.19._a.got_k = bf16[192,384]{1,0:T(8,128)(2,1)S(1)} collective-permute-done((bf16[192,384]{1,0:T(8,128)(2,1)S(1)}, bf16[192,384]{1,0:T(8,128)(2,1)S(1)}, u32[]{:S(2)}, u32[]{:S(2)}) %collective-permute-start.19) | collective-permute-done | bytes 147488 | tf_op jit(solution)/shard_map/ppermute | solution.py:120
  71.0 0.1 collective-permute-done.20._b.got_p
  71.1 1.1 %first_backward.1 = (bf16[192,256]{1,0:T(8,128)(2,1)S(1)}, f32[2,384,256]{2,1,0:T(8,128)S(1)}, bf16[2,384,256]{2,1,0:T(8,128)(2,1)S(1)}) custom-call(bf16[2,384,256]{2,1,0:T(8,128)(2,1)S(1)} %middle_grad.1.a_ref.g_ref.rest_0_, bf16[2,384,256]{2,1,0:T(8,128)(2,1)S(1)} %collective-permute-done.18.b_ref.rest_1_, bf16[192,1536]{1,0:T(8,128)(2,1)S(1)} %get-tuple-element.62.k_ref, ...), custom_call_target="tpu_custom_call" | custom-call | tf_op jit(solution)/shard_map/first_backward/pallas_call | solution.py:148
  72.2 0.1 collective-permute-start.21
  72.3 0.7 first_weights.1
  73.1 2.2 %collective-permute-start.24 = (bf16[2,192,384]{2,1,0:T(8,128)(2,1)S(1)}, bf16[2,192,384]{2,1,0:T(8,128)(2,1)S(1)}, u32[]{:S(2)}, u32[]{:S(2)}) collective-permute-start(bf16[2,192,384]{2,1,0:T(8,128)(2,1)S(1)} %get-tuple-element.101), channel_id=1, source_target_pairs={{0,8},{4,12},{8,0},{12,4},{1,9},{5,13},{9,1},{13,5},{2,10},{6,14},... | collective-permute-start | bytes 884744 | tf_op jit(solution)/shard_map/ppermute | solution.py:120
  75.3 0.6 collective-permute-start.13
  76.0 1.6 %collective-permute-start.22 = (bf16[384,256]{1,0:T(8,128)(2,1)S(1)}, bf16[384,256]{1,0:T(8,128)(2,1)S(1)}, u32[]{:S(2)}, u32[]{:S(2)}) collective-permute-start(bf16[384,256]{1,0:T(8,128)(2,1)S(1)} %get-tuple-element.94), channel_id=1, source_target_pairs={{0,2},{1,3},{2,0},{3,1},{4,6},{5,7},{6,4},{7,5},{8,10},{9,11},{10,... | collective-permute-start | bytes 589832 | tf_op jit(solution)/shard_map/ppermute | solution.py:120
  77.5 10.2 %collective-permute-done.23.got_k = bf16[2,192,384]{2,1,0:T(8,128)(2,1)S(1)} collective-permute-done((bf16[2,192,384]{2,1,0:T(8,128)(2,1)S(1)}, bf16[2,192,384]{2,1,0:T(8,128)(2,1)S(1)}, u32[]{:S(2)}, u32[]{:S(2)}) %collective-permute-start.23) | collective-permute-done | bytes 294944 | tf_op jit(solution)/shard_map/ppermute | solution.py:120
  87.7 2.1 %collective-permute-done.24.got_p = bf16[2,192,384]{2,1,0:T(8,128)(2,1)S(1)} collective-permute-done((bf16[2,192,384]{2,1,0:T(8,128)(2,1)S(1)}, bf16[2,192,384]{2,1,0:T(8,128)(2,1)S(1)}, u32[]{:S(2)}, u32[]{:S(2)}) %collective-permute-start.24) | collective-permute-done | bytes 294944 | tf_op jit(solution)/shard_map/ppermute | solution.py:120
  89.8 0.1 first_half.1
  89.9 0.3 collective-permute-start.25
  90.2 1.9 %collective-permute-start.26 = (bf16[192,384]{1,0:T(8,128)(2,1)S(1)}, bf16[192,384]{1,0:T(8,128)(2,1)S(1)}, u32[]{:S(2)}, u32[]{:S(2)}) collective-permute-start(bf16[192,384]{1,0:T(8,128)(2,1)S(1)} %get-tuple-element.105), channel_id=1, source_target_pairs={{0,4},{4,0},{8,12},{12,8},{1,5},{5,1},{9,13},{13,9},{2,6},{6,2},{1... | collective-permute-start | bytes 442376 | tf_op jit(solution)/shard_map/ppermute | solution.py:120
  92.2 0.7 out.1
  92.9 1.1 %second_total.1 = (f32[3,192,384]{2,1,0:T(8,128)}, f32[192,384]{1,0:T(8,128)}) custom-call(f32[192,384]{1,0:T(8,128)S(1)} %get-tuple-element.108.own_k, f32[192,384]{1,0:T(8,128)S(1)} %get-tuple-element.109.own_p, bf16[192,384]{1,0:T(8,128)(2,1)S(1)} %collective-permute-done.19._a.got_k, bf16[192,384]{1,0:T(8,128)(2,1)S(1)} %collective-permute-done.20._b.got_p), custom_call_target="tpu_custom_call" | custom-call | tf_op jit(solution)/shard_map/second_total/pallas_call | solution.py:148
  94.0 4.6 %collective-permute-done.25.got_k = bf16[192,384]{1,0:T(8,128)(2,1)S(1)} collective-permute-done((bf16[192,384]{1,0:T(8,128)(2,1)S(1)}, bf16[192,384]{1,0:T(8,128)(2,1)S(1)}, u32[]{:S(2)}, u32[]{:S(2)}) %collective-permute-start.25) | collective-permute-done | bytes 147488 | tf_op jit(solution)/shard_map/ppermute | solution.py:120
  98.6 0.2 collective-permute-done.26.got_p
  98.7 1.1 %first_total.1 = (f32[3,192,384]{2,1,0:T(8,128)}, f32[192,384]{1,0:T(8,128)}) custom-call(f32[192,384]{1,0:T(8,128)S(1)} %get-tuple-element.102.own_k, f32[192,384]{1,0:T(8,128)S(1)} %get-tuple-element.103.own_p, bf16[192,384]{1,0:T(8,128)(2,1)S(1)} %collective-permute-done.25.got_k, bf16[192,384]{1,0:T(8,128)(2,1)S(1)} %collective-permute-done.26.got_p), custom_call_target="tpu_custom_call" | custom-call | tf_op jit(solution)/shard_map/first_total/pallas_call | solution.py:148
  99.8 1.0 entry.1
  (25 shorter events, 0.5 us)
Async XLA Ops:
  0.6 8.1 %collective-permute-start = (bf16[384,256]{1,0:T(8,128)(2,1)}, bf16[384,256]{1,0:T(8,128)(2,1)S(1)}, u32[]{:S(2)}, u32[]{:S(2)}) collective-permute-start(bf16[384,256]{1,0:T(8,128)(2,1)} %x_ref.1), channel_id=1, source_target_pairs={{0,2},{1,3},{2,0},{3,1},{4,6},{5,7},{6,4},{7,5},{8,10},{9,11},{10,... | collective-permute-start | bytes 589832 | tf_op jit(solution)/shard_map/ppermute | solution.py:120
  3.6 15.4 %collective-permute-start.1 = (bf16[384,256]{1,0:T(8,128)(2,1)}, bf16[384,256]{1,0:T(8,128)(2,1)S(1)}, u32[]{:S(2)}, u32[]{:S(2)}) collective-permute-start(bf16[384,256]{1,0:T(8,128)(2,1)} %x_ref.1), channel_id=1, source_target_pairs={{0,1},{1,0},{2,3},{3,2},{4,5},{5,4},{6,7},{7,6},{8,9},{9,8},{10,11... | collective-permute-start | bytes 589832 | tf_op jit(solution)/shard_map/ppermute | solution.py:120
  8.7 10.3 %collective-permute-start.2 = (bf16[384,256]{1,0:T(8,128)(2,1)S(1)}, bf16[384,256]{1,0:T(8,128)(2,1)S(1)}, u32[]{:S(2)}, u32[]{:S(2)}) collective-permute-start(bf16[384,256]{1,0:T(8,128)(2,1)S(1)} %collective-permute-done.x2), channel_id=1, source_target_pairs={{0,1},{1,0},{2,3},{3,2},{4,5},{5,4},{6,7},{7,6},{8,9},{9,8},{10,11... | collective-permute-start | bytes 589832 | tf_op jit(solution)/shard_map/ppermute | solution.py:120
  8.8 4.4 %collective-permute-start.3 = (bf16[2,48,256]{2,1,0:T(8,128)(2,1)S(1)}, bf16[2,48,256]{2,1,0:T(8,128)(2,1)S(1)}, u32[]{:S(2)}, u32[]{:S(2)}) collective-permute-start(bf16[2,48,256]{2,1,0:T(8,128)(2,1)S(1)} %get-tuple-element.65), channel_id=1, source_target_pairs={{0,4},{4,0},{8,12},{12,8},{1,5},{5,1},{9,13},{13,9},{2,6},{6,2},{1... | collective-permute-start | bytes 147464 | tf_op jit(solution)/shard_map/ppermute | solution.py:120
  10.6 6.2 %collective-permute-start.4 = (bf16[2,48,256]{2,1,0:T(8,128)(2,1)S(1)}, bf16[2,48,256]{2,1,0:T(8,128)(2,1)S(1)}, u32[]{:S(2)}, u32[]{:S(2)}) collective-permute-start(bf16[2,48,256]{2,1,0:T(8,128)(2,1)S(1)} %get-tuple-element.66), channel_id=1, source_target_pairs={{0,8},{4,12},{8,0},{12,4},{1,9},{5,13},{9,1},{13,5},{2,10},{6,14},... | collective-permute-start | bytes 147464 | tf_op jit(solution)/shard_map/ppermute | solution.py:120
  13.2 5.9 %collective-permute-start.5 = (bf16[2,48,256]{2,1,0:T(8,128)(2,1)S(1)}, bf16[2,48,256]{2,1,0:T(8,128)(2,1)S(1)}, u32[]{:S(2)}, u32[]{:S(2)}) collective-permute-start(bf16[2,48,256]{2,1,0:T(8,128)(2,1)S(1)} %get-tuple-element.67), channel_id=1, source_target_pairs={{0,12},{4,8},{8,4},{12,0},{1,13},{5,9},{9,5},{13,1},{2,14},{6,10},... | collective-permute-start | bytes 147464 | tf_op jit(solution)/shard_map/ppermute | solution.py:120
  20.5 1.8 %collective-permute-start.6 = (bf16[2,384,256]{2,1,0:T(8,128)(2,1)S(1)}, bf16[2,384,256]{2,1,0:T(8,128)(2,1)S(1)}, u32[]{:S(2)}, u32[]{:S(2)}) collective-permute-start(bf16[2,384,256]{2,1,0:T(8,128)(2,1)S(1)} %get-tuple-element.69), channel_id=1, source_target_pairs={{0,1},{1,0},{2,3},{3,2},{4,5},{5,4},{6,7},{7,6},{8,9},{9,8},{10,11... | collective-permute-start | bytes 1179656 | tf_op jit(solution)/shard_map/ppermute | solution.py:120
  22.3 12.0 %collective-permute-start.7 = (bf16[2,384,256]{2,1,0:T(8,128)(2,1)S(1)}, bf16[2,384,256]{2,1,0:T(8,128)(2,1)S(1)}, u32[]{:S(2)}, u32[]{:S(2)}) collective-permute-start(bf16[2,384,256]{2,1,0:T(8,128)(2,1)S(1)} %mix_sum.1.chip_ref), channel_id=1, source_target_pairs={{0,2},{1,3},{2,0},{3,1},{4,6},{5,7},{6,4},{7,5},{8,10},{9,11},{10,... | collective-permute-start | bytes 1179656 | tf_op jit(solution)/shard_map/ppermute | solution.py:120
  23.9 13.8 %collective-permute-start.10 = (bf16[384,256]{1,0:T(8,128)(2,1)S(1)}, bf16[384,256]{1,0:T(8,128)(2,1)S(1)}, u32[]{:S(2)}, u32[]{:S(2)}) collective-permute-start(bf16[384,256]{1,0:T(8,128)(2,1)S(1)} %bitcast.6), channel_id=1, source_target_pairs={{0,2},{1,3},{2,0},{3,1},{4,6},{5,7},{6,4},{7,5},{8,10},{9,11},{10,... | collective-permute-start | bytes 589832 | tf_op jit(solution)/shard_map/ppermute | solution.py:120
  34.5 4.7 %collective-permute-start.8 = (bf16[2,384,256]{2,1,0:T(8,128)(2,1)S(1)}, bf16[2,384,256]{2,1,0:T(8,128)(2,1)S(1)}, u32[]{:S(2)}, u32[]{:S(2)}) collective-permute-start(bf16[2,384,256]{2,1,0:T(8,128)(2,1)S(1)} %middle.1.a_ref.mid_ref), channel_id=1, source_target_pairs={{0,1},{1,0},{2,3},{3,2},{4,5},{5,4},{6,7},{7,6},{8,9},{9,8},{10,11... | collective-permute-start | bytes 1179656 | tf_op jit(solution)/shard_map/ppermute | solution.py:120
  34.6 3.2 %collective-permute-start.9 = (bf16[384,256]{1,0:T(8,128)(2,1)S(1)}, bf16[384,256]{1,0:T(8,128)(2,1)S(1)}, u32[]{:S(2)}, u32[]{:S(2)}) collective-permute-start(bf16[384,256]{1,0:T(8,128)(2,1)S(1)} %bitcast.7), channel_id=1, source_target_pairs={{0,1},{1,0},{2,3},{3,2},{4,5},{5,4},{6,7},{7,6},{8,9},{9,8},{10,11... | collective-permute-start | bytes 589832 | tf_op jit(solution)/shard_map/ppermute | solution.py:120
  37.8 1.4 %collective-permute-start.11 = (bf16[384,256]{1,0:T(8,128)(2,1)S(1)}, bf16[384,256]{1,0:T(8,128)(2,1)S(1)}, u32[]{:S(2)}, u32[]{:S(2)}) collective-permute-start(bf16[384,256]{1,0:T(8,128)(2,1)S(1)} %collective-permute-done.10.g2.rest_2_), channel_id=1, source_target_pairs={{0,1},{1,0},{2,3},{3,2},{4,5},{5,4},{6,7},{7,6},{8,9},{9,8},{10,11... | collective-permute-start | bytes 589832 | tf_op jit(solution)/shard_map/ppermute | solution.py:120
  40.6 1.8 %collective-permute-start.14 = (bf16[2,384,256]{2,1,0:T(8,128)(2,1)S(1)}, bf16[2,384,256]{2,1,0:T(8,128)(2,1)S(1)}, u32[]{:S(2)}, u32[]{:S(2)}) collective-permute-start(bf16[2,384,256]{2,1,0:T(8,128)(2,1)S(1)} %get-tuple-element.77), channel_id=1, source_target_pairs={{0,1},{1,0},{2,3},{3,2},{4,5},{5,4},{6,7},{7,6},{8,9},{9,8},{10,11... | collective-permute-start | bytes 1179656 | tf_op jit(solution)/shard_map/ppermute | solution.py:120
  42.5 17.6 %collective-permute-start.15 = (bf16[2,384,256]{2,1,0:T(8,128)(2,1)S(1)}, bf16[2,384,256]{2,1,0:T(8,128)(2,1)S(1)}, u32[]{:S(2)}, u32[]{:S(2)}) collective-permute-start(bf16[2,384,256]{2,1,0:T(8,128)(2,1)S(1)} %squash_sum.1.chip_ref), channel_id=1, source_target_pairs={{0,2},{1,3},{2,0},{3,1},{4,6},{5,7},{6,4},{7,5},{8,10},{9,11},{10,... | collective-permute-start | bytes 1179656 | tf_op jit(solution)/shard_map/ppermute | solution.py:120
  44.0 14.7 %collective-permute-start.16 = (bf16[2,192,384]{2,1,0:T(8,128)(2,1)S(1)}, bf16[2,192,384]{2,1,0:T(8,128)(2,1)S(1)}, u32[]{:S(2)}, u32[]{:S(2)}) collective-permute-start(bf16[2,192,384]{2,1,0:T(8,128)(2,1)S(1)} %get-tuple-element.82), channel_id=1, source_target_pairs={{0,4},{4,0},{8,12},{12,8},{1,5},{5,1},{9,13},{13,9},{2,6},{6,2},{1... | collective-permute-start | bytes 884744 | tf_op jit(solution)/shard_map/ppermute | solution.py:120
  44.0 16.0 %collective-permute-start.17 = (bf16[2,192,384]{2,1,0:T(8,128)(2,1)S(1)}, bf16[2,192,384]{2,1,0:T(8,128)(2,1)S(1)}, u32[]{:S(2)}, u32[]{:S(2)}) collective-permute-start(bf16[2,192,384]{2,1,0:T(8,128)(2,1)S(1)} %get-tuple-element.83), channel_id=1, source_target_pairs={{0,8},{4,12},{8,0},{12,4},{1,9},{5,13},{9,1},{13,5},{2,10},{6,14},... | collective-permute-start | bytes 884744 | tf_op jit(solution)/shard_map/ppermute | solution.py:120
  60.7 10.4 %collective-permute-start.18 = (bf16[2,384,256]{2,1,0:T(8,128)(2,1)S(1)}, bf16[2,384,256]{2,1,0:T(8,128)(2,1)S(1)}, u32[]{:S(2)}, u32[]{:S(2)}) collective-permute-start(bf16[2,384,256]{2,1,0:T(8,128)(2,1)S(1)} %middle_grad.1.a_ref.g_ref.rest_0_), channel_id=1, source_target_pairs={{0,1},{1,0},{2,3},{3,2},{4,5},{5,4},{6,7},{7,6},{8,9},{9,8},{10,11... | collective-permute-start | bytes 1179656 | tf_op jit(solution)/shard_map/ppermute | solution.py:120
  60.9 10.1 %collective-permute-start.19 = (bf16[192,384]{1,0:T(8,128)(2,1)S(1)}, bf16[192,384]{1,0:T(8,128)(2,1)S(1)}, u32[]{:S(2)}, u32[]{:S(2)}) collective-permute-start(bf16[192,384]{1,0:T(8,128)(2,1)S(1)} %get-tuple-element.89), channel_id=1, source_target_pairs={{0,8},{4,12},{8,0},{12,4},{1,9},{5,13},{9,1},{13,5},{2,10},{6,14},... | collective-permute-start | bytes 442376 | tf_op jit(solution)/shard_map/ppermute | solution.py:120
  61.3 9.8 %collective-permute-start.20 = (bf16[192,384]{1,0:T(8,128)(2,1)S(1)}, bf16[192,384]{1,0:T(8,128)(2,1)S(1)}, u32[]{:S(2)}, u32[]{:S(2)}) collective-permute-start(bf16[192,384]{1,0:T(8,128)(2,1)S(1)} %get-tuple-element.90), channel_id=1, source_target_pairs={{0,4},{4,0},{8,12},{12,8},{1,5},{5,1},{9,13},{13,9},{2,6},{6,2},{1... | collective-permute-start | bytes 442376 | tf_op jit(solution)/shard_map/ppermute | solution.py:120
  63.8 11.5 %collective-permute-start.12 = (bf16[2,384,256]{2,1,0:T(8,128)(2,1)S(1)}, bf16[2,384,256]{2,1,0:T(8,128)(2,1)S(1)}, u32[]{:S(2)}, u32[]{:S(2)}) collective-permute-start(bf16[2,384,256]{2,1,0:T(8,128)(2,1)S(1)} %get-tuple-element.73), channel_id=1, source_target_pairs={{0,1},{1,0},{2,3},{3,2},{4,5},{5,4},{6,7},{7,6},{8,9},{9,8},{10,11... | collective-permute-start | bytes 1179656 | tf_op jit(solution)/shard_map/ppermute | solution.py:120
  72.2 3.7 %collective-permute-start.21 = (bf16[2,384,256]{2,1,0:T(8,128)(2,1)S(1)}, bf16[2,384,256]{2,1,0:T(8,128)(2,1)S(1)}, u32[]{:S(2)}, u32[]{:S(2)}) collective-permute-start(bf16[2,384,256]{2,1,0:T(8,128)(2,1)S(1)} %get-tuple-element.92), channel_id=1, source_target_pairs={{0,1},{1,0},{2,3},{3,2},{4,5},{5,4},{6,7},{7,6},{8,9},{9,8},{10,11... | collective-permute-start | bytes 1179656 | tf_op jit(solution)/shard_map/ppermute | solution.py:120
  73.0 14.7 %collective-permute-start.23 = (bf16[2,192,384]{2,1,0:T(8,128)(2,1)S(1)}, bf16[2,192,384]{2,1,0:T(8,128)(2,1)S(1)}, u32[]{:S(2)}, u32[]{:S(2)}) collective-permute-start(bf16[2,192,384]{2,1,0:T(8,128)(2,1)S(1)} %get-tuple-element.100), channel_id=1, source_target_pairs={{0,4},{4,0},{8,12},{12,8},{1,5},{5,1},{9,13},{13,9},{2,6},{6,2},{1... | collective-permute-start | bytes 884744 | tf_op jit(solution)/shard_map/ppermute | solution.py:120
  73.1 16.7 %collective-permute-start.24 = (bf16[2,192,384]{2,1,0:T(8,128)(2,1)S(1)}, bf16[2,192,384]{2,1,0:T(8,128)(2,1)S(1)}, u32[]{:S(2)}, u32[]{:S(2)}) collective-permute-start(bf16[2,192,384]{2,1,0:T(8,128)(2,1)S(1)} %get-tuple-element.101), channel_id=1, source_target_pairs={{0,8},{4,12},{8,0},{12,4},{1,9},{5,13},{9,1},{13,5},{2,10},{6,14},... | collective-permute-start | bytes 884744 | tf_op jit(solution)/shard_map/ppermute | solution.py:120
  75.3 16.9 %collective-permute-start.13 = (bf16[384,256]{1,0:T(8,128)(2,1)S(1)}, bf16[384,256]{1,0:T(8,128)(2,1)S(1)}, u32[]{:S(2)}, u32[]{:S(2)}) collective-permute-start(bf16[384,256]{1,0:T(8,128)(2,1)S(1)} %get-tuple-element.75), channel_id=1, source_target_pairs={{0,2},{1,3},{2,0},{3,1},{4,6},{5,7},{6,4},{7,5},{8,10},{9,11},{10,... | collective-permute-start | bytes 589832 | tf_op jit(solution)/shard_map/ppermute | solution.py:120
  76.0 23.8 %collective-permute-start.22 = (bf16[384,256]{1,0:T(8,128)(2,1)S(1)}, bf16[384,256]{1,0:T(8,128)(2,1)S(1)}, u32[]{:S(2)}, u32[]{:S(2)}) collective-permute-start(bf16[384,256]{1,0:T(8,128)(2,1)S(1)} %get-tuple-element.94), channel_id=1, source_target_pairs={{0,2},{1,3},{2,0},{3,1},{4,6},{5,7},{6,4},{7,5},{8,10},{9,11},{10,... | collective-permute-start | bytes 589832 | tf_op jit(solution)/shard_map/ppermute | solution.py:120
  89.9 8.6 %collective-permute-start.25 = (bf16[192,384]{1,0:T(8,128)(2,1)S(1)}, bf16[192,384]{1,0:T(8,128)(2,1)S(1)}, u32[]{:S(2)}, u32[]{:S(2)}) collective-permute-start(bf16[192,384]{1,0:T(8,128)(2,1)S(1)} %get-tuple-element.104), channel_id=1, source_target_pairs={{0,8},{4,12},{8,0},{12,4},{1,9},{5,13},{9,1},{13,5},{2,10},{6,14},... | collective-permute-start | bytes 442376 | tf_op jit(solution)/shard_map/ppermute | solution.py:120
  90.2 8.5 %collective-permute-start.26 = (bf16[192,384]{1,0:T(8,128)(2,1)S(1)}, bf16[192,384]{1,0:T(8,128)(2,1)S(1)}, u32[]{:S(2)}, u32[]{:S(2)}) collective-permute-start(bf16[192,384]{1,0:T(8,128)(2,1)S(1)} %get-tuple-element.105), channel_id=1, source_target_pairs={{0,4},{4,0},{8,12},{12,8},{1,5},{5,1},{9,13},{13,9},{2,6},{6,2},{1... | collective-permute-start | bytes 442376 | tf_op jit(solution)/shard_map/ppermute | solution.py:120

commit v4 on v3

--- a/solution.py
+++ b/solution.py
@@ -1,5 +1,3 @@
-import functools
-
 import jax
 import jax.numpy as jnp
 from jax import lax
@@ -166,13 +164,11 @@
     x_far = swap(x, "mp", 2)
     x_near = swap(x, "mp", 1)
 
+    raw_far = swap(grad_heads, "mp", 2)
+
     def load_body(x_ref, ta, tb, ca, cb, g_ref, *rest):
         outs, sems = rest[:-1], rest[-1]
-        c = lax.axis_index("ctx")
-        sources = [x_ref, ta.at[1], tb.at[1], ca, cb]
-        for k in range(4):
-            at = pl.multiple_of((c ^ k) * bins, bins)
-            sources.append(g_ref.at[:, :, pl.ds(at, bins)])
+        sources = [x_ref, ta.at[1], tb.at[1], ca, cb, g_ref]
         copies = [
             pltpu.make_async_copy(source, out, sems.at[i])
             for i, (source, out) in enumerate(zip(sources, outs))
@@ -182,16 +178,14 @@
         for copy in copies:
             copy.wait()
 
-    weight = ((hid, chans), BF16)
-    piece = ((heads, val, bins), BF16)
-    x_own, tap_a, tap_b, cols_a, cols_b, *pieces = pl.pallas_call(
+    x_own, tap_a, tap_b, cols_a, cols_b, raw_own = pl.pallas_call(
         load_body,
         out_shape=[pltpu.VMEM((rows, bins), BF16)]
-        + [pltpu.VMEM(*weight)] * 4
-        + [pltpu.VMEM(*piece)] * 4,
+        + [pltpu.VMEM((hid, chans), BF16)] * 4
+        + [pltpu.VMEM(grad_heads.shape, BF16)],
         in_specs=[pl.BlockSpec(memory_space=pltpu.HBM)] * 6,
-        out_specs=[VMEM] * 9,
-        scratch_shapes=[pltpu.SemaphoreType.DMA((9,))],
+        out_specs=[VMEM] * 6,
+        scratch_shapes=[pltpu.SemaphoreType.DMA((6,))],
         compiler_params=pltpu.CompilerParams(vmem_limit_bytes=16 << 20),
         name="load",
     )(
@@ -200,21 +194,29 @@
             for source in (x, taps_a, taps_b, point_a.T, point_b.T, grad_heads)
         ]
     )
-    pieces = [pieces[0]] + [swap(pieces[k], "ctx", k) for k in (1, 2, 3)]
     x_far, x_own = lax.optimization_barrier((x_far, x_own))
     x_cross = swap(x_far, "mp", 1)
+
+    def split_body(own_ref, far_ref, *outs):
+        c = lax.axis_index("ctx")
+        for k in range(4):
+            at = pl.ds(pl.multiple_of((c ^ k) * bins, bins), bins)
+            for i, ref in enumerate((own_ref, far_ref)):
+                outs[k][i] = ref[:, :, at]
+
+    piece = ((2, heads, val, bins), BF16)
+    pieces = call(split_body, [piece] * 4, (raw_own, raw_far), "split_grad")
+    pieces = [pieces[0]] + [swap(pieces[k], "ctx", k) for k in (1, 2, 3)]
 
     def join_body(*refs):
         c = lax.axis_index("ctx")
         out = refs[4]
         for k in range(4):
-            out[:, c ^ k] = refs[k][...]
-
-    (g_own,) = call(join_body, [((heads, 4, val, bins), BF16)], pieces, "join_grad")
-    g_own = g_own.reshape(rows, bins)
-    g_far = swap(g_own, "mp", 2)
-    g_near = swap(g_own, "mp", 1)
-    g_cross = swap(g_far, "mp", 1)
+            out[:, :, c ^ k] = refs[k][...]
+
+    (g_pair,) = call(join_body, [((2, heads, 4, val, bins), BF16)], pieces, "join_grad")
+    g_pair = g_pair.reshape(2, rows, bins)
+    g_near = swap(g_pair, "mp", 1)
 
     def first_body(x0, x1, x2, x3, k_ref, p_ref, _, z_ref, v_ref, s_ref, keep_ref, send_ref):
         m = lax.axis_index("mp")
@@ -241,7 +243,7 @@
             ((2, rows, bins), F32),
             ((2, rows, bins), BF16),
         ],
-        (x_own, x_near, x_far, x_cross, tap_a, cols_a, g_own),
+        (x_own, x_near, x_far, x_cross, tap_a, cols_a, raw_far),
         "first_forward",
     )
     got = swap(send, "mp", 1)
@@ -266,7 +268,7 @@
     mid_near = swap(mid, "mp", 1)
 
     def second_body(
-        a_ref, b_ref, g0, g1, g2, g3, k_ref, p_ref,
+        a_ref, b_ref, ga_ref, gb_ref, k_ref, p_ref,
         z_ref, v_ref, gu_ref, keep_ref, send_ref, ykeep_ref, ysend_ref,
     ):
         m = lax.axis_index("mp")
@@ -280,8 +282,8 @@
         v = v.astype(BF16)
         v_ref[...] = v
         gv = jnp.zeros((hid, bins), F32)
-        for j, ref in enumerate((g0, g1, g2, g3)):
-            gv = gv + dot(p_ref[:, block(m, j)], ref[...])
+        for j in range(4):
+            gv = gv + dot(p_ref[:, block(m, j)], (ga_ref, gb_ref)[j & 1][j >> 1])
         gu = (gv * slope).astype(BF16)
         gu_ref[...] = gu
         for i, j in enumerate((1, 3)):
@@ -304,13 +306,14 @@
             ((2, rows, bins), F32),
             ((2, rows, bins), BF16),
         ],
-        (mid, mid_near, g_own, g_near, g_far, g_cross, tap_b, cols_b),
+        (mid, mid_near, g_pair, g_near, tap_b, cols_b),
         "second_block",
     )
-    def weight_body(fill, z_ref, gu_ref, v_ref, *rest):
+    def weight_body(z_ref, gu_ref, v_ref, *rest):
         grads, (keep_k, keep_p, send_k, send_p, g_ref) = rest[:-5], rest[-5:]
         j = lax.axis_index("mp") ^ lax.axis_index("ctx")
-        fill(g_ref, grads)
+        for i in range(4):
+            g_ref[i] = grads[i & 1][i >> 1]
 
         def taps(k):
             return dot(gu_ref[...], z_ref[j ^ k], ((1,), (1,)))
@@ -327,21 +330,13 @@
         for i, k in enumerate((0, 1)):
             keep_p[i] = proj(k)
 
-    def fill_tiles(g_ref, grads):
-        for j, ref in enumerate(grads):
-            g_ref[j] = ref[...]
-
-    def fill_pairs(g_ref, grads):
-        for j in range(4):
-            g_ref[j] = grads[j & 1][j >> 1]
-
     two = (2, hid, rows)
 
-    def weights(z, gu, v, grads, fill, name):
+    def weights(z, gu, v, grads, name, after=()):
         return call(
-            functools.partial(weight_body, fill),
+            weight_body,
             [(two, F32), (two, F32), (two, BF16), (two, BF16)],
-            (z, gu, v, *grads),
+            (z, gu, v, *grads, *after),
             name,
             [pltpu.VMEM((4, rows, bins), BF16)],
         )
@@ -380,38 +375,37 @@
         )
         return taps, proj.T
 
-    parts_b = weights(
-        z_b, gu_b, v_b, (g_own, g_near, g_far, g_cross), fill_tiles, "second_weights"
-    )
+    parts_b = weights(z_b, gu_b, v_b, (g_pair, g_near), "second_weights")
     got = swap(send, "mp", 1)
     chip = near_sum(keep, got, "squash_sum", parts_b[:1])
     other = swap(chip, "mp", 2)
     other, *got_b = lax.optimization_barrier((other, *first_swap(*parts_b[2:])))
     parts_b = half_sum(*parts_b[:2], *got_b, "second_half")
+    own_b = parts_b[0]
     parts_b = (*parts_b[:2], swap(parts_b[2], "ctx", 2), swap(parts_b[3], "ctx", 1))
 
-    def back_body(g0, g2, mid_ref, chip_ref, other_ref, out_ref):
-        for i, ref in enumerate((g0, g2)):
+    def back_body(g_ref, mid_ref, chip_ref, other_ref, out_ref):
+        for i in (0, 1):
             grad = chip_ref[i].astype(F32) + other_ref[1 - i].astype(F32)
             out_ref[i] = (
-                ref[...].astype(F32) + grad * slope_of(mid_ref[i].astype(F32))
+                g_ref[i].astype(F32) + grad * slope_of(mid_ref[i].astype(F32))
             ).astype(BF16)
 
     (g_mid,) = call(
-        back_body, [((2, rows, bins), BF16)], (g_own, g_far, mid, chip, other), "middle_grad"
+        back_body, [((2, rows, bins), BF16)], (g_pair, mid, chip, other), "middle_grad"
     )
     g_mid_near = swap(g_mid, "mp", 1)
 
     ygot = swap(ysend, "mp", 1)
 
-    def last_sum_body(keep_ref, got_ref, own_ref, send_ref):
+    def last_sum_body(keep_ref, got_ref, *rest):
+        own_ref, send_ref = rest[-2:]
         own_ref[...] = keep_ref[0] + got_ref[0].astype(F32)
         send_ref[...] = (keep_ref[1] + got_ref[1].astype(F32)).astype(BF16)
 
-    def last_sum(keep, got, name):
-        return call(
-            last_sum_body, [((rows, bins), F32), ((rows, bins), BF16)], (keep, got), name
-        )
+    def last_sum(keep, got, name, after=()):
+        outs = [((rows, bins), F32), ((rows, bins), BF16)]
+        return call(last_sum_body, outs, (keep, got, *after), name)
 
     y_own, y_send = last_sum(ykeep, ygot, "out_sum")
     y_got = swap(y_send, "mp", 2)
@@ -422,7 +416,7 @@
 
     (second_out,) = call(out_body, [((rows, bins), BF16)], (mid, y_own, y_got), "out", final=True)
 
-    def first_back_body(a_ref, b_ref, k_ref, p_ref, s_ref, _a, _b, gu_ref, keep_ref, send_ref):
+    def first_back_body(a_ref, b_ref, k_ref, p_ref, s_ref, _, gu_ref, keep_ref, send_ref):
         m = lax.axis_index("mp")
         gv = jnp.zeros((hid, bins), F32)
         for j in range(4):
@@ -438,10 +432,10 @@
     gu_a, keep, send = call(
         first_back_body,
         [((hid, bins), BF16), ((2, rows, bins), F32), ((2, rows, bins), BF16)],
-        (g_mid, g_mid_near, tap_a, cols_a, slope_a, *parts_b[2:]),
+        (g_mid, g_mid_near, tap_a, cols_a, slope_a, own_b),
         "first_backward",
     )
-    parts_a = weights(z_a, gu_a, v_a, (g_mid, g_mid_near), fill_pairs, "first_weights")
+    parts_a = weights(z_a, gu_a, v_a, (g_mid, g_mid_near), "first_weights", parts_b[2:])
     got = swap(send, "mp", 1)
     e_own, e_send = last_sum(keep, got, "entry_sum")
     e_got = swap(e_send, "mp", 2)

time: 101 us -> 92.6 us (0.917)
  waiting for transfers between devices: 64.4 us -> 55.4 us
    ppermute x27 -> x26, waiting for transfers between devices: 64.4 us -> 55.4 us  [swap(): return lax.ppermute(value, axis, [(i, i ^ bits) for i in range(size)])]
    ppermute x27 -> x26, starting transfers between devices: 23.5 us -> 24.1 us  [swap(): return lax.ppermute(value, axis, [(i, i ^ bits) for i in range(size)])]
    pallas_call x18 -> x19, Pallas kernels: 10.4 us -> 10.4 us  [call(): pl.pallas_call(body, out_shape=[struct(s, d) for s, d in outs], in_specs=...]
  transfers between devices with their start and end apart: 27 -> 26, of which waited for: 16 -> 16; matrix products, arithmetic and copies ran while one was open for 0% -> 0% of each run, Pallas kernels for 8% -> 8%
where the time goes in v4:
time: 92.6 us; the launch traced here: 92.5 us
  waiting for transfers between devices  55.4 us (60%)
  starting transfers between devices  24.1 us (26%)
  Pallas kernels  12.2 us (13%)
    ppermute x26, waiting for transfers between devices, swap(): return lax.ppermute(value, axis, [(i, i ^ bits) for i in range(size)])  55.4 us
    ppermute x26, starting transfers between devices, swap(): return lax.ppermute(value, axis, [(i, i ^ bits) for i in range(size)])  24.1 us
    pallas_call x19, Pallas kernels, call(): pl.pallas_call(body, out_shape=[struct(s, d) for s, d in outs], in_specs=...  10.4 us
  transfers between devices with their start and end apart: 26, of which 16 were waited for; matrix products, arithmetic and copies ran while one was open for 0% of the time, Pallas kernels for 8%

profile of v4, /device:TPU:0, one launch (start us, length us, event | category | flops | bytes accessed | tf_op | source)
XLA Modules:
  0.0 92.5 jit_solution(17137301371418776683)
XLA Ops:
  0.6 3.0 %collective-permute-start = (bf16[384,256]{1,0:T(8,128)(2,1)}, bf16[384,256]{1,0:T(8,128)(2,1)S(1)}, u32[]{:S(2)}, u32[]{:S(2)}) collective-permute-start(bf16[384,256]{1,0:T(8,128)(2,1)} %x_ref.1), channel_id=1, source_target_pairs={{0,2},{1,3},{2,0},{3,1},{4,6},{5,7},{6,4},{7,5},{8,10},{9,11},{10,... | collective-permute-start | bytes 589832 | tf_op jit(solution)/shard_map/ppermute | solution.py:118
  3.6 0.2 collective-permute-start.3
  3.8 1.8 %load.1 = (bf16[384,256]{1,0:T(8,128)(2,1)S(1)}, bf16[192,1536]{1,0:T(8,128)(2,1)S(1)}, bf16[192,1536]{1,0:T(8,128)(2,1)S(1)}, bf16[192,1536]{1,0:T(8,128)(2,1)S...) custom-call(bf16[384,256]{1,0:T(8,128)(2,1)} %x_ref.1, bf16[3,192,1536]{2,1,0:T(8,128)(2,1)} %ta.1, ...), custom_call_target="tpu_custom_call" | custom-call | tf_op jit(solution)/shard_map/load/pallas_call | solution.py:181
  5.6 4.0 %collective-permute-done.x2 = bf16[384,256]{1,0:T(8,128)(2,1)S(1)} collective-permute-done((bf16[384,256]{1,0:T(8,128)(2,1)}, bf16[384,256]{1,0:T(8,128)(2,1)S(1)}, u32[]{:S(2)}, u32[]{:S(2)}) %collective-permute-start) | collective-permute-done | bytes 196640 | tf_op jit(solution)/shard_map/ppermute | solution.py:118
  9.6 3.4 %collective-permute-done.3._.far_ref = bf16[2,48,1024]{2,1,0:T(8,128)(2,1)S(1)} collective-permute-done((bf16[2,48,1024]{2,1,0:T(8,128)(2,1)}, bf16[2,48,1024]{2,1,0:T(8,128)(2,1)S(1)}, u32[]{:S(2)}, u32[]{:S(2)}) %collective-permute-start.3) | collective-permute-done | bytes 196640 | tf_op jit(solution)/shard_map/ppermute | solution.py:118
  13.0 1.4 %first_forward.1 = (bf16[4,384,256]{2,1,0:T(8,128)(2,1)S(1)}, bf16[192,256]{1,0:T(8,128)(2,1)S(1)}, f32[192,256]{1,0:T(8,128)S(1)}, f32[2,384,256]{2,1,0:T(8,128)S(1)}, bf16[2,384,256]{2,1,0:T(8,128)(2,1)S(1)}) custom-call(bf16[384,256]{1,0:T(8,128)(2,1)S(1)} %get-tuple-element.61.x0.x_ref, bf16[384,256]{1,0:T(8,128)(2,1)S(1)} %collective-permute-done.1.x1, ...), custom_call_target="tpu_custom_call" | custom-call | tf_op jit(solution)/shard_map/first_forward/pallas_call | solution.py:146
  14.4 1.7 %collective-permute-done.4.got_ref = bf16[2,384,256]{2,1,0:T(8,128)(2,1)S(1)} collective-permute-done((bf16[2,384,256]{2,1,0:T(8,128)(2,1)S(1)}, bf16[2,384,256]{2,1,0:T(8,128)(2,1)S(1)}, u32[]{:S(2)}, u32[]{:S(2)}) %collective-permute-start.4) | collective-permute-done | bytes 393248 | tf_op jit(solution)/shard_map/ppermute | solution.py:118
  16.2 1.8 %collective-permute-start.5 = (bf16[2,384,256]{2,1,0:T(8,128)(2,1)S(1)}, bf16[2,384,256]{2,1,0:T(8,128)(2,1)S(1)}, u32[]{:S(2)}, u32[]{:S(2)}) collective-permute-start(bf16[2,384,256]{2,1,0:T(8,128)(2,1)S(1)} %mix_sum.1.chip_ref), channel_id=1, source_target_pairs={{0,2},{1,3},{2,0},{3,1},{4,6},{5,7},{6,4},{7,5},{8,10},{9,11},{10,... | collective-permute-start | bytes 1179656 | tf_op jit(solution)/shard_map/ppermute | solution.py:118
  18.1 1.6 %collective-permute-start.7 = (bf16[2,2,48,256]{3,2,1,0:T(8,128)(2,1)S(1)}, bf16[2,2,48,256]{3,2,1,0:T(8,128)(2,1)S(1)}, u32[]{:S(2)}, u32[]{:S(2)}) collective-permute-start(bf16[2,2,48,256]{3,2,1,0:T(8,128)(2,1)S(1)} %get-tuple-element.69), channel_id=1, source_target_pairs={{0,4},{4,0},{8,12},{12,8},{1,5},{5,1},{9,13},{13,9},{2,6},{6,2},{1... | collective-permute-start | bytes 294920 | tf_op jit(solution)/shard_map/ppermute | solution.py:118
  19.7 2.6 %collective-permute-start.8 = (bf16[2,2,48,256]{3,2,1,0:T(8,128)(2,1)S(1)}, bf16[2,2,48,256]{3,2,1,0:T(8,128)(2,1)S(1)}, u32[]{:S(2)}, u32[]{:S(2)}) collective-permute-start(bf16[2,2,48,256]{3,2,1,0:T(8,128)(2,1)S(1)} %get-tuple-element.70), channel_id=1, source_target_pairs={{0,8},{4,12},{8,0},{12,4},{1,9},{5,13},{9,1},{13,5},{2,10},{6,14},... | collective-permute-start | bytes 294920 | tf_op jit(solution)/shard_map/ppermute | solution.py:118
  22.3 0.2 collective-permute-start.9
  22.5 0.2 collective-permute-done.7.refs_1_
  22.7 7.4 %collective-permute-done.8.refs_2_ = bf16[2,2,48,256]{3,2,1,0:T(8,128)(2,1)S(1)} collective-permute-done((bf16[2,2,48,256]{3,2,1,0:T(8,128)(2,1)S(1)}, bf16[2,2,48,256]{3,2,1,0:T(8,128)(2,1)S(1)}, u32[]{:S(2)}, u32[]{:S(2)}) %collective-permute-start.8) | collective-permute-done | bytes 98336 | tf_op jit(solution)/shard_map/ppermute | solution.py:118
  30.3 0.1 middle.1.a_ref.mid_ref
  30.4 0.5 collective-permute-start.6
  31.0 1.0 %collective-permute-done.10.gb_ref.rest_1_ = bf16[2,384,256]{2,1,0:T(8,128)(2,1)S(1)} collective-permute-done((bf16[2,384,256]{2,1,0:T(8,128)(2,1)S(1)}, bf16[2,384,256]{2,1,0:T(8,128)(2,1)S(1)}, u32[]{:S(2)}, u32[]{:S(2)}) %collective-permute-start.10) | collective-permute-done | bytes 393248 | tf_op jit(solution)/shard_map/ppermute | solution.py:118
  32.0 0.6 collective-permute-done.6.b_ref
  32.5 1.4 %second_block.1 = (bf16[4,384,256]{2,1,0:T(8,128)(2,1)S(1)}, bf16[192,256]{1,0:T(8,128)(2,1)S(1)}, bf16[192,256]{1,0:T(8,128)(2,1)S(1)}, f32[2,384,256]{2,1,0:T(...) custom-call(bf16[2,384,256]{2,1,0:T(8,128)(2,1)S(1)} %middle.1.a_ref.mid_, ...), custom_call_target="tpu_custom_call" | custom-call | tf_op jit(solution)/shard_map/second_block/pallas_call | solution.py:146
  33.9 0.2 collective-permute-start.13
  34.2 0.7 second_weights.1
  34.9 0.9 collective-permute-done.13.got_ref
  35.8 0.6 collective-permute-start.14
  36.4 1.6 %collective-permute-start.15 = (bf16[2,192,384]{2,1,0:T(8,128)(2,1)S(1)}, bf16[2,192,384]{2,1,0:T(8,128)(2,1)S(1)}, u32[]{:S(2)}, u32[]{:S(2)}) collective-permute-start(bf16[2,192,384]{2,1,0:T(8,128)(2,1)S(1)} %get-tuple-element.84), channel_id=1, source_target_pairs={{0,4},{4,0},{8,12},{12,8},{1,5},{5,1},{9,13},{13,9},{2,6},{6,2},{1... | collective-permute-start | bytes 884744 | tf_op jit(solution)/shard_map/ppermute | solution.py:118
  38.0 1.4 %collective-permute-start.16 = (bf16[2,192,384]{2,1,0:T(8,128)(2,1)S(1)}, bf16[2,192,384]{2,1,0:T(8,128)(2,1)S(1)}, u32[]{:S(2)}, u32[]{:S(2)}) collective-permute-start(bf16[2,192,384]{2,1,0:T(8,128)(2,1)S(1)} %get-tuple-element.85), channel_id=1, source_target_pairs={{0,8},{4,12},{8,0},{12,4},{1,9},{5,13},{9,1},{13,5},{2,10},{6,14},... | collective-permute-start | bytes 884744 | tf_op jit(solution)/shard_map/ppermute | solution.py:118
  39.4 12.0 %collective-permute-done.15.got_k = bf16[2,192,384]{2,1,0:T(8,128)(2,1)S(1)} collective-permute-done((bf16[2,192,384]{2,1,0:T(8,128)(2,1)S(1)}, bf16[2,192,384]{2,1,0:T(8,128)(2,1)S(1)}, u32[]{:S(2)}, u32[]{:S(2)}) %collective-permute-start.15) | collective-permute-done | bytes 294944 | tf_op jit(solution)/shard_map/ppermute | solution.py:118
  51.4 2.4 %collective-permute-done.16.got_p = bf16[2,192,384]{2,1,0:T(8,128)(2,1)S(1)} collective-permute-done((bf16[2,192,384]{2,1,0:T(8,128)(2,1)S(1)}, bf16[2,192,384]{2,1,0:T(8,128)(2,1)S(1)}, u32[]{:S(2)}, u32[]{:S(2)}) %collective-permute-start.16) | collective-permute-done | bytes 294944 | tf_op jit(solution)/shard_map/ppermute | solution.py:118
  53.8 0.6 middle_grad.1.a_ref.g_ref.rest_0_
  54.5 0.1 second_half.1
  54.6 0.4 collective-permute-start.20
  55.0 2.7 %collective-permute-start.21 = (bf16[192,384]{1,0:T(8,128)(2,1)S(1)}, bf16[192,384]{1,0:T(8,128)(2,1)S(1)}, u32[]{:S(2)}, u32[]{:S(2)}) collective-permute-start(bf16[192,384]{1,0:T(8,128)(2,1)S(1)} %get-tuple-element.100), channel_id=1, source_target_pairs={{0,4},{4,0},{8,12},{12,8},{1,5},{5,1},{9,13},{13,9},{2,6},{6,2},{1... | collective-permute-start | bytes 442376 | tf_op jit(solution)/shard_map/ppermute | solution.py:118
  57.7 1.1 %first_backward.1 = (bf16[192,256]{1,0:T(8,128)(2,1)S(1)}, f32[2,384,256]{2,1,0:T(8,128)S(1)}, bf16[2,384,256]{2,1,0:T(8,128)(2,1)S(1)}) custom-call(bf16[2,384,256]{2,1,0:T(8,128)(2,1)S(1)} %middle_grad.1.a_ref.g_ref.rest_0_, bf16[2,384,256]{2,1,0:T(8,128)(2,1)S(1)} %collective-permute-done.17.b_ref.rest_1_, bf16[192,1536]{1,0:T(8,128)(2,1)S(1)} %get-tuple-element.63.k_ref, ...), custom_call_target="tpu_custom_call" | custom-call | tf_op jit(solution)/shard_map/first_backward/pallas_call | solution.py:146
  58.8 0.6 collective-permute-start.18
  59.4 5.6 %collective-permute-done.20.rest_2_.got_k = bf16[192,384]{1,0:T(8,128)(2,1)S(1)} collective-permute-done((bf16[192,384]{1,0:T(8,128)(2,1)S(1)}, bf16[192,384]{1,0:T(8,128)(2,1)S(1)}, u32[]{:S(2)}, u32[]{:S(2)}) %collective-permute-start.20) | collective-permute-done | bytes 147488 | tf_op jit(solution)/shard_map/ppermute | solution.py:118
  65.0 0.1 collective-permute-done.21.rest_3_.got_p
  65.1 0.7 first_weights.1
  65.9 2.1 %collective-permute-start.23 = (bf16[2,192,384]{2,1,0:T(8,128)(2,1)S(1)}, bf16[2,192,384]{2,1,0:T(8,128)(2,1)S(1)}, u32[]{:S(2)}, u32[]{:S(2)}) collective-permute-start(bf16[2,192,384]{2,1,0:T(8,128)(2,1)S(1)} %get-tuple-element.104), channel_id=1, source_target_pairs={{0,8},{4,12},{8,0},{12,4},{1,9},{5,13},{9,1},{13,5},{2,10},{6,14},... | collective-permute-start | bytes 884744 | tf_op jit(solution)/shard_map/ppermute | solution.py:118
  68.0 1.5 %collective-permute-start.12 = (bf16[384,256]{1,0:T(8,128)(2,1)S(1)}, bf16[384,256]{1,0:T(8,128)(2,1)S(1)}, u32[]{:S(2)}, u32[]{:S(2)}) collective-permute-start(bf16[384,256]{1,0:T(8,128)(2,1)S(1)} %get-tuple-element.77), channel_id=1, source_target_pairs={{0,2},{1,3},{2,0},{3,1},{4,6},{5,7},{6,4},{7,5},{8,10},{9,11},{10,... | collective-permute-start | bytes 589832 | tf_op jit(solution)/shard_map/ppermute | solution.py:118
  69.7 0.6 collective-permute-start.19
  70.3 9.4 %collective-permute-done.22.got_k = bf16[2,192,384]{2,1,0:T(8,128)(2,1)S(1)} collective-permute-done((bf16[2,192,384]{2,1,0:T(8,128)(2,1)S(1)}, bf16[2,192,384]{2,1,0:T(8,128)(2,1)S(1)}, u32[]{:S(2)}, u32[]{:S(2)}) %collective-permute-start.22) | collective-permute-done | bytes 294944 | tf_op jit(solution)/shard_map/ppermute | solution.py:118
  79.7 2.3 %collective-permute-done.23.got_p = bf16[2,192,384]{2,1,0:T(8,128)(2,1)S(1)} collective-permute-done((bf16[2,192,384]{2,1,0:T(8,128)(2,1)S(1)}, bf16[2,192,384]{2,1,0:T(8,128)(2,1)S(1)}, u32[]{:S(2)}, u32[]{:S(2)}) %collective-permute-start.23) | collective-permute-done | bytes 294944 | tf_op jit(solution)/shard_map/ppermute | solution.py:118
  82.1 0.3 collective-permute-start.24
  82.5 1.7 %collective-permute-start.25 = (bf16[192,384]{1,0:T(8,128)(2,1)S(1)}, bf16[192,384]{1,0:T(8,128)(2,1)S(1)}, u32[]{:S(2)}, u32[]{:S(2)}) collective-permute-start(bf16[192,384]{1,0:T(8,128)(2,1)S(1)} %get-tuple-element.108), channel_id=1, source_target_pairs={{0,4},{4,0},{8,12},{12,8},{1,5},{5,1},{9,13},{13,9},{2,6},{6,2},{1... | collective-permute-start | bytes 442376 | tf_op jit(solution)/shard_map/ppermute | solution.py:118
  84.1 0.7 out.1
  84.9 1.1 %second_total.1 = (f32[3,192,384]{2,1,0:T(8,128)}, f32[192,384]{1,0:T(8,128)}) custom-call(f32[192,384]{1,0:T(8,128)S(1)} %get-tuple-element.91._.own_k, f32[192,384]{1,0:T(8,128)S(1)} %get-tuple-element.111.own_p, bf16[192,384]{1,0:T(8,128)(2,1)S(1)} %collective-permute-done.20.rest_2_.got_k, bf16[192,384]{1,0:T(8,128)(2,1)S(1)} %collective-permute-done.21.rest_3_.got_p), custom_call_target="tpu_custom_call" | custom-call | tf_op jit(solution)/shard_map/second_total/pallas_call | solution.py:146
  86.0 3.7 %collective-permute-done.24.got_k = bf16[192,384]{1,0:T(8,128)(2,1)S(1)} collective-permute-done((bf16[192,384]{1,0:T(8,128)(2,1)S(1)}, bf16[192,384]{1,0:T(8,128)(2,1)S(1)}, u32[]{:S(2)}, u32[]{:S(2)}) %collective-permute-start.24) | collective-permute-done | bytes 147488 | tf_op jit(solution)/shard_map/ppermute | solution.py:118
  89.6 0.8 collective-permute-done.25.got_p
  90.4 1.1 %first_total.1 = (f32[3,192,384]{2,1,0:T(8,128)}, f32[192,384]{1,0:T(8,128)}) custom-call(f32[192,384]{1,0:T(8,128)S(1)} %get-tuple-element.105.own_k, f32[192,384]{1,0:T(8,128)S(1)} %get-tuple-element.106.own_p, bf16[192,384]{1,0:T(8,128)(2,1)S(1)} %collective-permute-done.24.got_k, bf16[192,384]{1,0:T(8,128)(2,1)S(1)} %collective-permute-done.25.got_p), custom_call_target="tpu_custom_call" | custom-call | tf_op jit(solution)/shard_map/first_total/pallas_call | solution.py:146
  91.5 1.0 %entry.1 = bf16[384,256]{1,0:T(8,128)(2,1)} custom-call(bf16[2,384,256]{2,1,0:T(8,128)(2,1)S(1)} %middle_grad.1.a_ref.g_ref.rest_0_, bf16[384,256]{1,0:T(8,128)(2,1)S(1)} %get-tuple-element.61.x0.x_ref, f32[384,256]{1,0:T(8,128)S(1)} %get-tuple-element.94.own_ref, bf16[384,256]{1,0:T(8,128)(2,1)S(1)} %collective-permute-done.19.got_ref), custom_call_target="tpu_custom_call" | custom-call | tf_op jit(solution)/shard_map/entry/pallas_call | solution.py:146
  (24 shorter events, 0.8 us)
Async XLA Ops:
  0.6 8.9 %collective-permute-start = (bf16[384,256]{1,0:T(8,128)(2,1)}, bf16[384,256]{1,0:T(8,128)(2,1)S(1)}, u32[]{:S(2)}, u32[]{:S(2)}) collective-permute-start(bf16[384,256]{1,0:T(8,128)(2,1)} %x_ref.1), channel_id=1, source_target_pairs={{0,2},{1,3},{2,0},{3,1},{4,6},{5,7},{6,4},{7,5},{8,10},{9,11},{10,... | collective-permute-start | bytes 589832 | tf_op jit(solution)/shard_map/ppermute | solution.py:118
  3.6 9.3 %collective-permute-start.1 = (bf16[384,256]{1,0:T(8,128)(2,1)}, bf16[384,256]{1,0:T(8,128)(2,1)S(1)}, u32[]{:S(2)}, u32[]{:S(2)}) collective-permute-start(bf16[384,256]{1,0:T(8,128)(2,1)} %x_ref.1), channel_id=1, source_target_pairs={{0,1},{1,0},{2,3},{3,2},{4,5},{5,4},{6,7},{7,6},{8,9},{9,8},{10,11... | collective-permute-start | bytes 589832 | tf_op jit(solution)/shard_map/ppermute | solution.py:118
  3.6 9.3 %collective-permute-start.3 = (bf16[2,48,1024]{2,1,0:T(8,128)(2,1)}, bf16[2,48,1024]{2,1,0:T(8,128)(2,1)S(1)}, u32[]{:S(2)}, u32[]{:S(2)}) collective-permute-start(bf16[2,48,1024]{2,1,0:T(8,128)(2,1)} %g_ref.1), channel_id=1, source_target_pairs={{0,2},{1,3},{2,0},{3,1},{4,6},{5,7},{6,4},{7,5},{8,10},{9,11},{10,... | collective-permute-start | bytes 589832 | tf_op jit(solution)/shard_map/ppermute | solution.py:118
  9.6 3.4 %collective-permute-start.2 = (bf16[384,256]{1,0:T(8,128)(2,1)S(1)}, bf16[384,256]{1,0:T(8,128)(2,1)S(1)}, u32[]{:S(2)}, u32[]{:S(2)}) collective-permute-start(bf16[384,256]{1,0:T(8,128)(2,1)S(1)} %collective-permute-done.x2), channel_id=1, source_target_pairs={{0,1},{1,0},{2,3},{3,2},{4,5},{5,4},{6,7},{7,6},{8,9},{9,8},{10,11... | collective-permute-start | bytes 589832 | tf_op jit(solution)/shard_map/ppermute | solution.py:118
  14.3 1.8 %collective-permute-start.4 = (bf16[2,384,256]{2,1,0:T(8,128)(2,1)S(1)}, bf16[2,384,256]{2,1,0:T(8,128)(2,1)S(1)}, u32[]{:S(2)}, u32[]{:S(2)}) collective-permute-start(bf16[2,384,256]{2,1,0:T(8,128)(2,1)S(1)} %get-tuple-element.66), channel_id=1, source_target_pairs={{0,1},{1,0},{2,3},{3,2},{4,5},{5,4},{6,7},{7,6},{8,9},{9,8},{10,11... | collective-permute-start | bytes 1179656 | tf_op jit(solution)/shard_map/ppermute | solution.py:118
  16.2 14.1 %collective-permute-start.5 = (bf16[2,384,256]{2,1,0:T(8,128)(2,1)S(1)}, bf16[2,384,256]{2,1,0:T(8,128)(2,1)S(1)}, u32[]{:S(2)}, u32[]{:S(2)}) collective-permute-start(bf16[2,384,256]{2,1,0:T(8,128)(2,1)S(1)} %mix_sum.1.chip_ref), channel_id=1, source_target_pairs={{0,2},{1,3},{2,0},{3,1},{4,6},{5,7},{6,4},{7,5},{8,10},{9,11},{10,... | collective-permute-start | bytes 1179656 | tf_op jit(solution)/shard_map/ppermute | solution.py:118
  18.1 4.7 %collective-permute-start.7 = (bf16[2,2,48,256]{3,2,1,0:T(8,128)(2,1)S(1)}, bf16[2,2,48,256]{3,2,1,0:T(8,128)(2,1)S(1)}, u32[]{:S(2)}, u32[]{:S(2)}) collective-permute-start(bf16[2,2,48,256]{3,2,1,0:T(8,128)(2,1)S(1)} %get-tuple-element.69), channel_id=1, source_target_pairs={{0,4},{4,0},{8,12},{12,8},{1,5},{5,1},{9,13},{13,9},{2,6},{6,2},{1... | collective-permute-start | bytes 294920 | tf_op jit(solution)/shard_map/ppermute | solution.py:118
  19.7 10.4 %collective-permute-start.8 = (bf16[2,2,48,256]{3,2,1,0:T(8,128)(2,1)S(1)}, bf16[2,2,48,256]{3,2,1,0:T(8,128)(2,1)S(1)}, u32[]{:S(2)}, u32[]{:S(2)}) collective-permute-start(bf16[2,2,48,256]{3,2,1,0:T(8,128)(2,1)S(1)} %get-tuple-element.70), channel_id=1, source_target_pairs={{0,8},{4,12},{8,0},{12,4},{1,9},{5,13},{9,1},{13,5},{2,10},{6,14},... | collective-permute-start | bytes 294920 | tf_op jit(solution)/shard_map/ppermute | solution.py:118
  22.3 7.9 %collective-permute-start.9 = (bf16[2,2,48,256]{3,2,1,0:T(8,128)(2,1)S(1)}, bf16[2,2,48,256]{3,2,1,0:T(8,128)(2,1)S(1)}, u32[]{:S(2)}, u32[]{:S(2)}) collective-permute-start(bf16[2,2,48,256]{3,2,1,0:T(8,128)(2,1)S(1)} %get-tuple-element.71), channel_id=1, source_target_pairs={{0,12},{4,8},{8,4},{12,0},{1,13},{5,9},{9,5},{13,1},{2,14},{6,10},... | collective-permute-start | bytes 294920 | tf_op jit(solution)/shard_map/ppermute | solution.py:118
  30.2 1.8 %collective-permute-start.10 = (bf16[2,384,256]{2,1,0:T(8,128)(2,1)S(1)}, bf16[2,384,256]{2,1,0:T(8,128)(2,1)S(1)}, u32[]{:S(2)}, u32[]{:S(2)}) collective-permute-start(bf16[2,384,256]{2,1,0:T(8,128)(2,1)S(1)} %bitcast.5), channel_id=1, source_target_pairs={{0,1},{1,0},{2,3},{3,2},{4,5},{5,4},{6,7},{7,6},{8,9},{9,8},{10,11... | collective-permute-start | bytes 1179656 | tf_op jit(solution)/shard_map/ppermute | solution.py:118
  30.4 2.1 %collective-permute-start.6 = (bf16[2,384,256]{2,1,0:T(8,128)(2,1)S(1)}, bf16[2,384,256]{2,1,0:T(8,128)(2,1)S(1)}, u32[]{:S(2)}, u32[]{:S(2)}) collective-permute-start(bf16[2,384,256]{2,1,0:T(8,128)(2,1)S(1)} %middle.1.a_ref.mid_ref), channel_id=1, source_target_pairs={{0,1},{1,0},{2,3},{3,2},{4,5},{5,4},{6,7},{7,6},{8,9},{9,8},{10,11... | collective-permute-start | bytes 1179656 | tf_op jit(solution)/shard_map/ppermute | solution.py:118
  33.9 1.8 %collective-permute-start.13 = (bf16[2,384,256]{2,1,0:T(8,128)(2,1)S(1)}, bf16[2,384,256]{2,1,0:T(8,128)(2,1)S(1)}, u32[]{:S(2)}, u32[]{:S(2)}) collective-permute-start(bf16[2,384,256]{2,1,0:T(8,128)(2,1)S(1)} %get-tuple-element.79), channel_id=1, source_target_pairs={{0,1},{1,0},{2,3},{3,2},{4,5},{5,4},{6,7},{7,6},{8,9},{9,8},{10,11... | collective-permute-start | bytes 1179656 | tf_op jit(solution)/shard_map/ppermute | solution.py:118
  35.8 18.0 %collective-permute-start.14 = (bf16[2,384,256]{2,1,0:T(8,128)(2,1)S(1)}, bf16[2,384,256]{2,1,0:T(8,128)(2,1)S(1)}, u32[]{:S(2)}, u32[]{:S(2)}) collective-permute-start(bf16[2,384,256]{2,1,0:T(8,128)(2,1)S(1)} %squash_sum.1.chip_ref), channel_id=1, source_target_pairs={{0,2},{1,3},{2,0},{3,1},{4,6},{5,7},{6,4},{7,5},{8,10},{9,11},{10,... | collective-permute-start | bytes 1179656 | tf_op jit(solution)/shard_map/ppermute | solution.py:118
  36.4 15.0 %collective-permute-start.15 = (bf16[2,192,384]{2,1,0:T(8,128)(2,1)S(1)}, bf16[2,192,384]{2,1,0:T(8,128)(2,1)S(1)}, u32[]{:S(2)}, u32[]{:S(2)}) collective-permute-start(bf16[2,192,384]{2,1,0:T(8,128)(2,1)S(1)} %get-tuple-element.84), channel_id=1, source_target_pairs={{0,4},{4,0},{8,12},{12,8},{1,5},{5,1},{9,13},{13,9},{2,6},{6,2},{1... | collective-permute-start | bytes 884744 | tf_op jit(solution)/shard_map/ppermute | solution.py:118
  38.0 15.8 %collective-permute-start.16 = (bf16[2,192,384]{2,1,0:T(8,128)(2,1)S(1)}, bf16[2,192,384]{2,1,0:T(8,128)(2,1)S(1)}, u32[]{:S(2)}, u32[]{:S(2)}) collective-permute-start(bf16[2,192,384]{2,1,0:T(8,128)(2,1)S(1)} %get-tuple-element.85), channel_id=1, source_target_pairs={{0,8},{4,12},{8,0},{12,4},{1,9},{5,13},{9,1},{13,5},{2,10},{6,14},... | collective-permute-start | bytes 884744 | tf_op jit(solution)/shard_map/ppermute | solution.py:118
  54.4 3.3 %collective-permute-start.17 = (bf16[2,384,256]{2,1,0:T(8,128)(2,1)S(1)}, bf16[2,384,256]{2,1,0:T(8,128)(2,1)S(1)}, u32[]{:S(2)}, u32[]{:S(2)}) collective-permute-start(bf16[2,384,256]{2,1,0:T(8,128)(2,1)S(1)} %middle_grad.1.a_ref.g_ref.rest_0_), channel_id=1, source_target_pairs={{0,1},{1,0},{2,3},{3,2},{4,5},{5,4},{6,7},{7,6},{8,9},{9,8},{10,11... | collective-permute-start | bytes 1179656 | tf_op jit(solution)/shard_map/ppermute | solution.py:118
  54.6 10.4 %collective-permute-start.20 = (bf16[192,384]{1,0:T(8,128)(2,1)S(1)}, bf16[192,384]{1,0:T(8,128)(2,1)S(1)}, u32[]{:S(2)}, u32[]{:S(2)}) collective-permute-start(bf16[192,384]{1,0:T(8,128)(2,1)S(1)} %get-tuple-element.99), channel_id=1, source_target_pairs={{0,8},{4,12},{8,0},{12,4},{1,9},{5,13},{9,1},{13,5},{2,10},{6,14},... | collective-permute-start | bytes 442376 | tf_op jit(solution)/shard_map/ppermute | solution.py:118
  55.0 10.1 %collective-permute-start.21 = (bf16[192,384]{1,0:T(8,128)(2,1)S(1)}, bf16[192,384]{1,0:T(8,128)(2,1)S(1)}, u32[]{:S(2)}, u32[]{:S(2)}) collective-permute-start(bf16[192,384]{1,0:T(8,128)(2,1)S(1)} %get-tuple-element.100), channel_id=1, source_target_pairs={{0,4},{4,0},{8,12},{12,8},{1,5},{5,1},{9,13},{13,9},{2,6},{6,2},{1... | collective-permute-start | bytes 442376 | tf_op jit(solution)/shard_map/ppermute | solution.py:118
  57.7 10.2 %collective-permute-start.11 = (bf16[2,384,256]{2,1,0:T(8,128)(2,1)S(1)}, bf16[2,384,256]{2,1,0:T(8,128)(2,1)S(1)}, u32[]{:S(2)}, u32[]{:S(2)}) collective-permute-start(bf16[2,384,256]{2,1,0:T(8,128)(2,1)S(1)} %get-tuple-element.75), channel_id=1, source_target_pairs={{0,1},{1,0},{2,3},{3,2},{4,5},{5,4},{6,7},{7,6},{8,9},{9,8},{10,11... | collective-permute-start | bytes 1179656 | tf_op jit(solution)/shard_map/ppermute | solution.py:118
  58.8 10.8 %collective-permute-start.18 = (bf16[2,384,256]{2,1,0:T(8,128)(2,1)S(1)}, bf16[2,384,256]{2,1,0:T(8,128)(2,1)S(1)}, u32[]{:S(2)}, u32[]{:S(2)}) collective-permute-start(bf16[2,384,256]{2,1,0:T(8,128)(2,1)S(1)} %get-tuple-element.93), channel_id=1, source_target_pairs={{0,1},{1,0},{2,3},{3,2},{4,5},{5,4},{6,7},{7,6},{8,9},{9,8},{10,11... | collective-permute-start | bytes 1179656 | tf_op jit(solution)/shard_map/ppermute | solution.py:118
  65.8 13.9 %collective-permute-start.22 = (bf16[2,192,384]{2,1,0:T(8,128)(2,1)S(1)}, bf16[2,192,384]{2,1,0:T(8,128)(2,1)S(1)}, u32[]{:S(2)}, u32[]{:S(2)}) collective-permute-start(bf16[2,192,384]{2,1,0:T(8,128)(2,1)S(1)} %get-tuple-element.103), channel_id=1, source_target_pairs={{0,4},{4,0},{8,12},{12,8},{1,5},{5,1},{9,13},{13,9},{2,6},{6,2},{1... | collective-permute-start | bytes 884744 | tf_op jit(solution)/shard_map/ppermute | solution.py:118
  65.9 16.2 %collective-permute-start.23 = (bf16[2,192,384]{2,1,0:T(8,128)(2,1)S(1)}, bf16[2,192,384]{2,1,0:T(8,128)(2,1)S(1)}, u32[]{:S(2)}, u32[]{:S(2)}) collective-permute-start(bf16[2,192,384]{2,1,0:T(8,128)(2,1)S(1)} %get-tuple-element.104), channel_id=1, source_target_pairs={{0,8},{4,12},{8,0},{12,4},{1,9},{5,13},{9,1},{13,5},{2,10},{6,14},... | collective-permute-start | bytes 884744 | tf_op jit(solution)/shard_map/ppermute | solution.py:118
  68.0 16.1 %collective-permute-start.12 = (bf16[384,256]{1,0:T(8,128)(2,1)S(1)}, bf16[384,256]{1,0:T(8,128)(2,1)S(1)}, u32[]{:S(2)}, u32[]{:S(2)}) collective-permute-start(bf16[384,256]{1,0:T(8,128)(2,1)S(1)} %get-tuple-element.77), channel_id=1, source_target_pairs={{0,2},{1,3},{2,0},{3,1},{4,6},{5,7},{6,4},{7,5},{8,10},{9,11},{10,... | collective-permute-start | bytes 589832 | tf_op jit(solution)/shard_map/ppermute | solution.py:118
  69.7 21.8 %collective-permute-start.19 = (bf16[384,256]{1,0:T(8,128)(2,1)S(1)}, bf16[384,256]{1,0:T(8,128)(2,1)S(1)}, u32[]{:S(2)}, u32[]{:S(2)}) collective-permute-start(bf16[384,256]{1,0:T(8,128)(2,1)S(1)} %get-tuple-element.95), channel_id=1, source_target_pairs={{0,2},{1,3},{2,0},{3,1},{4,6},{5,7},{6,4},{7,5},{8,10},{9,11},{10,... | collective-permute-start | bytes 589832 | tf_op jit(solution)/shard_map/ppermute | solution.py:118
  82.1 7.5 %collective-permute-start.24 = (bf16[192,384]{1,0:T(8,128)(2,1)S(1)}, bf16[192,384]{1,0:T(8,128)(2,1)S(1)}, u32[]{:S(2)}, u32[]{:S(2)}) collective-permute-start(bf16[192,384]{1,0:T(8,128)(2,1)S(1)} %get-tuple-element.107), channel_id=1, source_target_pairs={{0,8},{4,12},{8,0},{12,4},{1,9},{5,13},{9,1},{13,5},{2,10},{6,14},... | collective-permute-start | bytes 442376 | tf_op jit(solution)/shard_map/ppermute | solution.py:118
  82.5 7.9 %collective-permute-start.25 = (bf16[192,384]{1,0:T(8,128)(2,1)S(1)}, bf16[192,384]{1,0:T(8,128)(2,1)S(1)}, u32[]{:S(2)}, u32[]{:S(2)}) collective-permute-start(bf16[192,384]{1,0:T(8,128)(2,1)S(1)} %get-tuple-element.108), channel_id=1, source_target_pairs={{0,4},{4,0},{8,12},{12,8},{1,5},{5,1},{9,13},{13,9},{2,6},{6,2},{1... | collective-permute-start | bytes 442376 | tf_op jit(solution)/shard_map/ppermute | solution.py:118

commit v5 on v4

--- a/solution.py
+++ b/solution.py
@@ -1,3 +1,5 @@
+import functools
+
 import jax
 import jax.numpy as jnp
 from jax import lax
@@ -309,11 +311,8 @@
         (mid, mid_near, g_pair, g_near, tap_b, cols_b),
         "second_block",
     )
-    def weight_body(z_ref, gu_ref, v_ref, *rest):
-        grads, (keep_k, keep_p, send_k, send_p, g_ref) = rest[:-5], rest[-5:]
+    def weight_pieces(z_ref, gu_ref, v_ref, g_ref, keep_k, keep_p, send_k, send_p):
         j = lax.axis_index("mp") ^ lax.axis_index("ctx")
-        for i in range(4):
-            g_ref[i] = grads[i & 1][i >> 1]
 
         def taps(k):
             return dot(gu_ref[...], z_ref[j ^ k], ((1,), (1,)))
@@ -330,44 +329,42 @@
         for i, k in enumerate((0, 1)):
             keep_p[i] = proj(k)
 
-    two = (2, hid, rows)
-
-    def weights(z, gu, v, grads, name, after=()):
-        return call(
-            weight_body,
-            [(two, F32), (two, F32), (two, BF16), (two, BF16)],
-            (z, gu, v, *grads, *after),
-            name,
-            [pltpu.VMEM((4, rows, bins), BF16)],
-        )
+    one, two, three = ((n, hid, rows) for n in (1, 2, 3))
+
+    def second_weight_body(z_ref, gu_ref, v_ref, ga_ref, gb_ref, *rest):
+        g_ref = rest[4]
+        for i in range(4):
+            g_ref[i] = (ga_ref, gb_ref)[i & 1][i >> 1]
+        weight_pieces(z_ref, gu_ref, v_ref, g_ref, *rest[:4])
+
+    def half_sum(keep, got, own):
+        own[0] = keep[0] + got[0].astype(F32)
+        return (keep[1] + got[1].astype(F32)).astype(BF16)
+
+    def first_weight_body(z_ref, gu_ref, v_ref, g0, g1, g2, g3, *rest):
+        keep_k, keep_p, got_k, got_p = rest[:4]
+        own_k, own_p = rest[8:10]
+        g_ref = rest[10]
+        for i, ref in enumerate((g0, g1, g2, g3)):
+            g_ref[i] = ref[...]
+        send_k, send_p = rest[6:8]
+        send_p[2] = half_sum(keep_k, got_k, own_k)
+        send_k[2] = half_sum(keep_p, got_p, own_p)
+        weight_pieces(z_ref, gu_ref, v_ref, g_ref, *rest[4:8])
 
     def half_body(keep_k, keep_p, got_k, got_p, own_k, own_p, send_k, send_p):
-        own_k[...] = keep_k[0] + got_k[0].astype(F32)
-        own_p[...] = keep_p[0] + got_p[0].astype(F32)
-        send_k[...] = (keep_k[1] + got_k[1].astype(F32)).astype(BF16)
-        send_p[...] = (keep_p[1] + got_p[1].astype(F32)).astype(BF16)
-
-    def first_swap(send_k, send_p):
-        return swap(send_k, "ctx", 1), swap(send_p, "ctx", 2)
-
-    def half_sum(keep_k, keep_p, got_k, got_p, name):
-        one = (hid, rows)
-        return call(
-            half_body,
-            [(one, F32), (one, F32), (one, BF16), (one, BF16)],
-            (keep_k, keep_p, got_k, got_p),
-            name,
-        )
-
-    def total_body(own_k, own_p, got_k, got_p, taps_ref, proj_ref):
+        send_k[...] = half_sum(keep_k, got_k, own_k)
+        send_p[...] = half_sum(keep_p, got_p, own_p)
+
+    def total_body(place_k, place_p, own_k, own_p, got_k, got_p, taps_ref, proj_ref):
         taps_ref[0] = jnp.zeros((hid, rows), F32)
-        taps_ref[1] = own_k[...] + got_k[...].astype(F32)
+        taps_ref[1] = own_k[0] + got_k[place_k].astype(F32)
         taps_ref[2] = jnp.zeros((hid, rows), F32)
-        proj_ref[...] = own_p[...] + got_p[...].astype(F32)
-
-    def total(own_k, own_p, got_k, got_p, name):
+        proj_ref[...] = own_p[0] + got_p[place_p].astype(F32)
+
+    def total(place, own_k, own_p, got_k, got_p, name):
         taps, proj = call(
-            total_body,
+            functools.partial(total_body, place, place),
             [((3, hid, rows), F32), ((hid, rows), F32)],
             (own_k, own_p, got_k, got_p),
             name,
@@ -375,26 +372,30 @@
         )
         return taps, proj.T
 
-    parts_b = weights(z_b, gu_b, v_b, (g_pair, g_near), "second_weights")
+    pack = [pltpu.VMEM((4, rows, bins), BF16)]
+    *keep_b, send_k, send_p = call(
+        second_weight_body,
+        [(two, F32), (two, F32), (two, BF16), (two, BF16)],
+        (z_b, gu_b, v_b, g_pair, g_near),
+        "second_weights",
+        pack,
+    )
     got = swap(send, "mp", 1)
-    chip = near_sum(keep, got, "squash_sum", parts_b[:1])
+    chip = near_sum(keep, got, "squash_sum", keep_b[:1])
     other = swap(chip, "mp", 2)
-    other, *got_b = lax.optimization_barrier((other, *first_swap(*parts_b[2:])))
-    parts_b = half_sum(*parts_b[:2], *got_b, "second_half")
-    own_b = parts_b[0]
-    parts_b = (*parts_b[:2], swap(parts_b[2], "ctx", 2), swap(parts_b[3], "ctx", 1))
-
-    def back_body(g_ref, mid_ref, chip_ref, other_ref, out_ref):
+    got_b = swap(send_k, "ctx", 1), swap(send_p, "ctx", 2)
+
+    def back_body(g_ref, mid_ref, chip_ref, other_ref, *outs):
         for i in (0, 1):
             grad = chip_ref[i].astype(F32) + other_ref[1 - i].astype(F32)
-            out_ref[i] = (
+            outs[i][...] = (
                 g_ref[i].astype(F32) + grad * slope_of(mid_ref[i].astype(F32))
             ).astype(BF16)
 
-    (g_mid,) = call(
-        back_body, [((2, rows, bins), BF16)], (g_pair, mid, chip, other), "middle_grad"
-    )
-    g_mid_near = swap(g_mid, "mp", 1)
+    g_mid = call(
+        back_body, [((rows, bins), BF16)] * 2, (g_pair, mid, chip, other), "middle_grad"
+    )
+    g_mid = [g_mid[0], swap(g_mid[0], "mp", 1), g_mid[1], swap(g_mid[1], "mp", 1)]
 
     ygot = swap(ysend, "mp", 1)
 
@@ -416,12 +417,12 @@
 
     (second_out,) = call(out_body, [((rows, bins), BF16)], (mid, y_own, y_got), "out", final=True)
 
-    def first_back_body(a_ref, b_ref, k_ref, p_ref, s_ref, _, gu_ref, keep_ref, send_ref):
+    def first_back_body(*refs):
+        grads, (k_ref, p_ref, s_ref, gu_ref, keep_ref, send_ref) = refs[:4], refs[4:]
         m = lax.axis_index("mp")
         gv = jnp.zeros((hid, bins), F32)
         for j in range(4):
-            part = (a_ref, b_ref)[j & 1][j >> 1]
-            gv = gv + dot(p_ref[:, block(m, j)], part)
+            gv = gv + dot(p_ref[:, block(m, j)], grads[j][...])
         gu = (gv * s_ref[...]).astype(BF16)
         gu_ref[...] = gu
         for i, j in enumerate((1, 3)):
@@ -432,10 +433,17 @@
     gu_a, keep, send = call(
         first_back_body,
         [((hid, bins), BF16), ((2, rows, bins), F32), ((2, rows, bins), BF16)],
-        (g_mid, g_mid_near, tap_a, cols_a, slope_a, own_b),
+        (*g_mid, tap_a, cols_a, slope_a),
         "first_backward",
     )
-    parts_a = weights(z_a, gu_a, v_a, (g_mid, g_mid_near), "first_weights", parts_b[2:])
+    *keep_a, send_k, send_p, own_bk, own_bp = call(
+        first_weight_body,
+        [(two, F32), (two, F32), (three, BF16), (three, BF16), (one, F32), (one, F32)],
+        (z_a, gu_a, v_a, *g_mid, *keep_b, *got_b),
+        "first_weights",
+        pack,
+    )
+    got_k, got_p = swap(send_k, "ctx", 1), swap(send_p, "ctx", 2)
     got = swap(send, "mp", 1)
     e_own, e_send = last_sum(keep, got, "entry_sum")
     e_got = swap(e_send, "mp", 2)
@@ -443,15 +451,20 @@
     def entry_body(g_ref, x_ref, own_ref, got_ref, out_ref):
         grad = own_ref[...] + got_ref[...].astype(F32)
         out_ref[...] = (
-            g_ref[0].astype(F32) + grad * slope_of(x_ref[...].astype(F32))
+            g_ref[...].astype(F32) + grad * slope_of(x_ref[...].astype(F32))
         ).astype(BF16)
 
-    (entry,) = call(entry_body, [((rows, bins), BF16)], (g_mid, x_own, e_own, e_got), "entry", final=True)
-
-    taps_b_grad, point_b_grad = total(*parts_b, "second_total")
-    parts_a = half_sum(*parts_a[:2], *first_swap(*parts_a[2:]), "first_half")
-    parts_a = (*parts_a[:2], swap(parts_a[2], "ctx", 2), swap(parts_a[3], "ctx", 1))
-    taps_a_grad, point_a_grad = total(*parts_a, "first_total")
+    (entry,) = call(entry_body, [((rows, bins), BF16)], (g_mid[0], x_own, e_own, e_got), "entry", final=True)
+
+    own_ak, own_ap, send_k, send_p = call(
+        half_body,
+        [(one, F32), (one, F32), (one[1:], BF16), (one[1:], BF16)],
+        (*keep_a, got_k, got_p),
+        "first_half",
+    )
+    last_k, last_p = swap(send_k, "ctx", 2), swap(send_p, "ctx", 1)
+    taps_b_grad, point_b_grad = total(2, own_bk, own_bp, got_p, got_k, "second_total")
+    taps_a_grad, point_a_grad = total(Ellipsis, own_ak, own_ap, last_k, last_p, "first_total")
     return second_out, entry, taps_a_grad, point_a_grad, taps_b_grad, point_b_grad
 
 

time: 92.6 us -> 85.6 us (0.924)
  waiting for transfers between devices: 55.4 us -> 49.6 us
  starting transfers between devices: 24.1 us -> 22.9 us
    ppermute x26 -> x25, waiting for transfers between devices: 55.4 us -> 49.6 us  [swap(): return lax.ppermute(value, axis, [(i, i ^ bits) for i in range(size)])]
    ppermute x26 -> x25, starting transfers between devices: 24.1 us -> 22.9 us  [swap(): return lax.ppermute(value, axis, [(i, i ^ bits) for i in range(size)])]
    pallas_call x19 -> x18, Pallas kernels: 10.4 us -> 10.4 us  [call(): pl.pallas_call(body, out_shape=[struct(s, d) for s, d in outs], in_specs=...]
  transfers between devices with their start and end apart: 26 -> 25, of which waited for: 16 -> 17; matrix products, arithmetic and copies ran while one was open for 0% -> 0% of each run, Pallas kernels for 8% -> 10%
where the time goes in v5:
time: 85.6 us; the launch traced here: 85.4 us
  waiting for transfers between devices  49.6 us (58%)
  starting transfers between devices  22.9 us (27%)
  Pallas kernels  12.2 us (14%)
    ppermute x25, waiting for transfers between devices, swap(): return lax.ppermute(value, axis, [(i, i ^ bits) for i in range(size)])  49.6 us
    ppermute x25, starting transfers between devices, swap(): return lax.ppermute(value, axis, [(i, i ^ bits) for i in range(size)])  22.9 us
    pallas_call x18, Pallas kernels, call(): pl.pallas_call(body, out_shape=[struct(s, d) for s, d in outs], in_specs=...  10.4 us
    pallas_call x1, Pallas kernels, fast_shards(): pl.pallas_call(load_body, out_shape=[pltpu.VMEM((rows, bins), BF16)] + [p...  1.79 us
  transfers between devices with their start and end apart: 25, of which 17 were waited for; matrix products, arithmetic and copies ran while one was open for 0% of the time, Pallas kernels for 10%

profile of v5, /device:TPU:0, one launch (start us, length us, event | category | flops | bytes accessed | tf_op | source)
XLA Modules:
  0.0 85.4 jit_solution(17180181837003311013)
XLA Ops:
  0.6 3.0 %collective-permute-start = (bf16[384,256]{1,0:T(8,128)(2,1)}, bf16[384,256]{1,0:T(8,128)(2,1)S(1)}, u32[]{:S(2)}, u32[]{:S(2)}) collective-permute-start(bf16[384,256]{1,0:T(8,128)(2,1)} %x_ref.1), channel_id=1, source_target_pairs={{0,2},{1,3},{2,0},{3,1},{4,6},{5,7},{6,4},{7,5},{8,10},{9,11},{10,... | collective-permute-start | bytes 589832 | tf_op jit(solution)/shard_map/ppermute | solution.py:120
  3.6 0.2 collective-permute-start.3
  3.8 1.8 %load.1 = (bf16[384,256]{1,0:T(8,128)(2,1)S(1)}, bf16[192,1536]{1,0:T(8,128)(2,1)S(1)}, bf16[192,1536]{1,0:T(8,128)(2,1)S(1)}, bf16[192,1536]{1,0:T(8,128)(2,1)S...) custom-call(bf16[384,256]{1,0:T(8,128)(2,1)} %x_ref.1, bf16[3,192,1536]{2,1,0:T(8,128)(2,1)} %ta.1, ...), custom_call_target="tpu_custom_call" | custom-call | tf_op jit(solution)/shard_map/load/pallas_call | solution.py:183
  5.6 4.0 %collective-permute-done.x2 = bf16[384,256]{1,0:T(8,128)(2,1)S(1)} collective-permute-done((bf16[384,256]{1,0:T(8,128)(2,1)}, bf16[384,256]{1,0:T(8,128)(2,1)S(1)}, u32[]{:S(2)}, u32[]{:S(2)}) %collective-permute-start) | collective-permute-done | bytes 196640 | tf_op jit(solution)/shard_map/ppermute | solution.py:120
  9.6 3.4 %collective-permute-done.3._.far_ref = bf16[2,48,1024]{2,1,0:T(8,128)(2,1)S(1)} collective-permute-done((bf16[2,48,1024]{2,1,0:T(8,128)(2,1)}, bf16[2,48,1024]{2,1,0:T(8,128)(2,1)S(1)}, u32[]{:S(2)}, u32[]{:S(2)}) %collective-permute-start.3) | collective-permute-done | bytes 196640 | tf_op jit(solution)/shard_map/ppermute | solution.py:120
  13.0 1.4 %first_forward.1 = (bf16[4,384,256]{2,1,0:T(8,128)(2,1)S(1)}, bf16[192,256]{1,0:T(8,128)(2,1)S(1)}, f32[192,256]{1,0:T(8,128)S(1)}, f32[2,384,256]{2,1,0:T(8,128)S(1)}, bf16[2,384,256]{2,1,0:T(8,128)(2,1)S(1)}) custom-call(bf16[384,256]{1,0:T(8,128)(2,1)S(1)} %get-tuple-element.58.x0.x_ref, bf16[384,256]{1,0:T(8,128)(2,1)S(1)} %collective-permute-done.1.x1, ...), custom_call_target="tpu_custom_call" | custom-call | tf_op jit(solution)/shard_map/first_forward/pallas_call | solution.py:148
  14.4 1.7 %collective-permute-done.4.got_ref = bf16[2,384,256]{2,1,0:T(8,128)(2,1)S(1)} collective-permute-done((bf16[2,384,256]{2,1,0:T(8,128)(2,1)S(1)}, bf16[2,384,256]{2,1,0:T(8,128)(2,1)S(1)}, u32[]{:S(2)}, u32[]{:S(2)}) %collective-permute-start.4) | collective-permute-done | bytes 393248 | tf_op jit(solution)/shard_map/ppermute | solution.py:120
  16.2 1.8 %collective-permute-start.5 = (bf16[2,384,256]{2,1,0:T(8,128)(2,1)S(1)}, bf16[2,384,256]{2,1,0:T(8,128)(2,1)S(1)}, u32[]{:S(2)}, u32[]{:S(2)}) collective-permute-start(bf16[2,384,256]{2,1,0:T(8,128)(2,1)S(1)} %mix_sum.1.chip_ref), channel_id=1, source_target_pairs={{0,2},{1,3},{2,0},{3,1},{4,6},{5,7},{6,4},{7,5},{8,10},{9,11},{10,... | collective-permute-start | bytes 1179656 | tf_op jit(solution)/shard_map/ppermute | solution.py:120
  18.1 1.6 %collective-permute-start.7 = (bf16[2,2,48,256]{3,2,1,0:T(8,128)(2,1)S(1)}, bf16[2,2,48,256]{3,2,1,0:T(8,128)(2,1)S(1)}, u32[]{:S(2)}, u32[]{:S(2)}) collective-permute-start(bf16[2,2,48,256]{3,2,1,0:T(8,128)(2,1)S(1)} %get-tuple-element.66), channel_id=1, source_target_pairs={{0,4},{4,0},{8,12},{12,8},{1,5},{5,1},{9,13},{13,9},{2,6},{6,2},{1... | collective-permute-start | bytes 294920 | tf_op jit(solution)/shard_map/ppermute | solution.py:120
  19.7 2.6 %collective-permute-start.8 = (bf16[2,2,48,256]{3,2,1,0:T(8,128)(2,1)S(1)}, bf16[2,2,48,256]{3,2,1,0:T(8,128)(2,1)S(1)}, u32[]{:S(2)}, u32[]{:S(2)}) collective-permute-start(bf16[2,2,48,256]{3,2,1,0:T(8,128)(2,1)S(1)} %get-tuple-element.67), channel_id=1, source_target_pairs={{0,8},{4,12},{8,0},{12,4},{1,9},{5,13},{9,1},{13,5},{2,10},{6,14},... | collective-permute-start | bytes 294920 | tf_op jit(solution)/shard_map/ppermute | solution.py:120
  22.3 0.2 collective-permute-start.9
  22.5 0.2 collective-permute-done.7.refs_1_
  22.7 7.4 %collective-permute-done.8.refs_2_ = bf16[2,2,48,256]{3,2,1,0:T(8,128)(2,1)S(1)} collective-permute-done((bf16[2,2,48,256]{3,2,1,0:T(8,128)(2,1)S(1)}, bf16[2,2,48,256]{3,2,1,0:T(8,128)(2,1)S(1)}, u32[]{:S(2)}, u32[]{:S(2)}) %collective-permute-start.8) | collective-permute-done | bytes 98336 | tf_op jit(solution)/shard_map/ppermute | solution.py:120
  30.3 0.1 middle.1.a_ref.mid_ref
  30.4 0.5 collective-permute-start.6
  31.0 1.0 %collective-permute-done.10.gb_ref = bf16[2,384,256]{2,1,0:T(8,128)(2,1)S(1)} collective-permute-done((bf16[2,384,256]{2,1,0:T(8,128)(2,1)S(1)}, bf16[2,384,256]{2,1,0:T(8,128)(2,1)S(1)}, u32[]{:S(2)}, u32[]{:S(2)}) %collective-permute-start.10) | collective-permute-done | bytes 393248 | tf_op jit(solution)/shard_map/ppermute | solution.py:120
  32.0 0.6 collective-permute-done.6.b_ref
  32.5 1.4 %second_block.1 = (bf16[4,384,256]{2,1,0:T(8,128)(2,1)S(1)}, bf16[192,256]{1,0:T(8,128)(2,1)S(1)}, bf16[192,256]{1,0:T(8,128)(2,1)S(1)}, f32[2,384,256]{2,1,0:T(...) custom-call(bf16[2,384,256]{2,1,0:T(8,128)(2,1)S(1)} %middle.1.a_ref.mid_, ...), custom_call_target="tpu_custom_call" | custom-call | tf_op jit(solution)/shard_map/second_block/pallas_call | solution.py:148
  33.9 0.2 collective-permute-start.13
  34.2 0.7 second_weights.1
  34.9 0.9 %collective-permute-done.13.got_ref = bf16[2,384,256]{2,1,0:T(8,128)(2,1)S(1)} collective-permute-done((bf16[2,384,256]{2,1,0:T(8,128)(2,1)S(1)}, bf16[2,384,256]{2,1,0:T(8,128)(2,1)S(1)}, u32[]{:S(2)}, u32[]{:S(2)}) %collective-permute-start.13) | collective-permute-done | bytes 393248 | tf_op jit(solution)/shard_map/ppermute | solution.py:120
  35.8 0.6 collective-permute-start.14
  36.4 1.6 %collective-permute-start.19 = (bf16[2,192,384]{2,1,0:T(8,128)(2,1)S(1)}, bf16[2,192,384]{2,1,0:T(8,128)(2,1)S(1)}, u32[]{:S(2)}, u32[]{:S(2)}) collective-permute-start(bf16[2,192,384]{2,1,0:T(8,128)(2,1)S(1)} %get-tuple-element.92), channel_id=1, source_target_pairs={{0,4},{4,0},{8,12},{12,8},{1,5},{5,1},{9,13},{13,9},{2,6},{6,2},{1... | collective-permute-start | bytes 884744 | tf_op jit(solution)/shard_map/ppermute | solution.py:120
  38.0 1.4 %collective-permute-start.20 = (bf16[2,192,384]{2,1,0:T(8,128)(2,1)S(1)}, bf16[2,192,384]{2,1,0:T(8,128)(2,1)S(1)}, u32[]{:S(2)}, u32[]{:S(2)}) collective-permute-start(bf16[2,192,384]{2,1,0:T(8,128)(2,1)S(1)} %get-tuple-element.93), channel_id=1, source_target_pairs={{0,8},{4,12},{8,0},{12,4},{1,9},{5,13},{9,1},{13,5},{2,10},{6,14},... | collective-permute-start | bytes 884744 | tf_op jit(solution)/shard_map/ppermute | solution.py:120
  39.4 7.6 %collective-permute-done.14.other_ref = bf16[2,384,256]{2,1,0:T(8,128)(2,1)S(1)} collective-permute-done((bf16[2,384,256]{2,1,0:T(8,128)(2,1)S(1)}, bf16[2,384,256]{2,1,0:T(8,128)(2,1)S(1)}, u32[]{:S(2)}, u32[]{:S(2)}) %collective-permute-start.14) | collective-permute-done | bytes 393248 | tf_op jit(solution)/shard_map/ppermute | solution.py:120
  47.1 0.6 middle_grad.1
  47.8 0.5 collective-permute-start.15
  48.3 0.9 collective-permute-done.16.refs_3_.g3
  49.2 0.3 collective-permute-done.15.refs_1_.g1
  49.5 1.1 %first_backward.1 = (bf16[192,256]{1,0:T(8,128)(2,1)S(1)}, f32[2,384,256]{2,1,0:T(8,128)S(1)}, bf16[2,384,256]{2,1,0:T(8,128)(2,1)S(1)}) custom-call(bf16[384,256]{1,0:T(8,128)(2,1)S(1)} %get-tuple-element.81.refs_0_.g_ref.g0, bf16[384,256]{1,0:T(8,128)(2,1)S(1)} %collective-permute-done.15.refs_1_.g1, bf16[384,256]{1,0:T(8,128)(2,1)S(1)} %get-tuple-element.82.refs_2_.g2, ...), custom_call_target="tpu_custom_call" | custom-call | tf_op jit(solution)/shard_map/first_backward/pallas_call | solution.py:148
  50.6 0.3 collective-permute-start.17
  50.9 0.6 collective-permute-done.19.rest_2_
  51.4 2.4 %collective-permute-done.20.rest_3_ = bf16[2,192,384]{2,1,0:T(8,128)(2,1)S(1)} collective-permute-done((bf16[2,192,384]{2,1,0:T(8,128)(2,1)S(1)}, bf16[2,192,384]{2,1,0:T(8,128)(2,1)S(1)}, u32[]{:S(2)}, u32[]{:S(2)}) %collective-permute-start.20) | collective-permute-done | bytes 294944 | tf_op jit(solution)/shard_map/ppermute | solution.py:120
  53.8 0.8 first_weights.1
  54.6 0.5 collective-permute-start.21
  55.1 2.6 %collective-permute-start.22 = (bf16[3,192,384]{2,1,0:T(8,128)(2,1)S(1)}, bf16[3,192,384]{2,1,0:T(8,128)(2,1)S(1)}, u32[]{:S(2)}, u32[]{:S(2)}) collective-permute-start(bf16[3,192,384]{2,1,0:T(8,128)(2,1)S(1)} %get-tuple-element.97), channel_id=1, source_target_pairs={{0,8},{4,12},{8,0},{12,4},{1,9},{5,13},{9,1},{13,5},{2,10},{6,14},... | collective-permute-start | bytes 1327112 | tf_op jit(solution)/shard_map/ppermute | solution.py:120
  57.8 1.5 %collective-permute-start.12 = (bf16[384,256]{1,0:T(8,128)(2,1)S(1)}, bf16[384,256]{1,0:T(8,128)(2,1)S(1)}, u32[]{:S(2)}, u32[]{:S(2)}) collective-permute-start(bf16[384,256]{1,0:T(8,128)(2,1)S(1)} %get-tuple-element.74), channel_id=1, source_target_pairs={{0,2},{1,3},{2,0},{3,1},{4,6},{5,7},{6,4},{7,5},{8,10},{9,11},{10,... | collective-permute-start | bytes 589832 | tf_op jit(solution)/shard_map/ppermute | solution.py:120
  59.4 0.6 collective-permute-start.18
  60.0 13.3 %collective-permute-done.21.got_k.got_p = bf16[3,192,384]{2,1,0:T(8,128)(2,1)S(1)} collective-permute-done((bf16[3,192,384]{2,1,0:T(8,128)(2,1)S(1)}, bf16[3,192,384]{2,1,0:T(8,128)(2,1)S(1)}, u32[]{:S(2)}, u32[]{:S(2)}) %collective-permute-start.21) | collective-permute-done | bytes 442400 | tf_op jit(solution)/shard_map/ppermute | solution.py:120
  73.3 3.5 %collective-permute-done.22.got_p.got_k = bf16[3,192,384]{2,1,0:T(8,128)(2,1)S(1)} collective-permute-done((bf16[3,192,384]{2,1,0:T(8,128)(2,1)S(1)}, bf16[3,192,384]{2,1,0:T(8,128)(2,1)S(1)}, u32[]{:S(2)}, u32[]{:S(2)}) %collective-permute-start.22) | collective-permute-done | bytes 442400 | tf_op jit(solution)/shard_map/ppermute | solution.py:120
  76.8 0.1 first_half.1
  77.0 2.6 %collective-permute-start.24 = (bf16[192,384]{1,0:T(8,128)(2,1)S(1)}, bf16[192,384]{1,0:T(8,128)(2,1)S(1)}, u32[]{:S(2)}, u32[]{:S(2)}) collective-permute-start(bf16[192,384]{1,0:T(8,128)(2,1)S(1)} %get-tuple-element.101), channel_id=1, source_target_pairs={{0,4},{4,0},{8,12},{12,8},{1,5},{5,1},{9,13},{13,9},{2,6},{6,2},{1... | collective-permute-start | bytes 442376 | tf_op jit(solution)/shard_map/ppermute | solution.py:120
  79.6 0.7 out.1
  80.4 1.1 %second_total.1 = (f32[3,192,384]{2,1,0:T(8,128)}, f32[192,384]{1,0:T(8,128)}) custom-call(f32[1,192,384]{2,1,0:T(8,128)S(1)} %get-tuple-element.104.own_k, f32[1,192,384]{2,1,0:T(8,128)S(1)} %get-tuple-element.105.own_p, bf16[3,192,384]{2,1,0:T(8,128)(2,1)S(1)} %collective-permute-done.22.got_p.got_k, ...), custom_call_target="tpu_custom_call" | custom-call | tf_op jit(solution)/shard_map/second_total/pallas_call | solution.py:148
  81.5 1.0 %entry.1 = bf16[384,256]{1,0:T(8,128)(2,1)} custom-call(bf16[384,256]{1,0:T(8,128)(2,1)S(1)} %get-tuple-element.81.refs_0_.g_ref.g0, bf16[384,256]{1,0:T(8,128)(2,1)S(1)} %get-tuple-element.58.x0.x_ref, f32[384,256]{1,0:T(8,128)S(1)} %get-tuple-element.86.own_ref, bf16[384,256]{1,0:T(8,128)(2,1)S(1)} %collective-permute-done.18.got_ref), custom_call_target="tpu_custom_call" | custom-call | tf_op jit(solution)/shard_map/entry/pallas_call | solution.py:148
  82.4 1.4 %collective-permute-done.23.got_k = bf16[192,384]{1,0:T(8,128)(2,1)S(1)} collective-permute-done((bf16[192,384]{1,0:T(8,128)(2,1)S(1)}, bf16[192,384]{1,0:T(8,128)(2,1)S(1)}, u32[]{:S(2)}, u32[]{:S(2)}) %collective-permute-start.23) | collective-permute-done | bytes 147488 | tf_op jit(solution)/shard_map/ppermute | solution.py:120
  83.9 0.5 collective-permute-done.24.got_p
  84.3 1.1 %first_total.1 = (f32[3,192,384]{2,1,0:T(8,128)}, f32[192,384]{1,0:T(8,128)}) custom-call(f32[1,192,384]{2,1,0:T(8,128)S(1)} %get-tuple-element.98.own_k, f32[1,192,384]{2,1,0:T(8,128)S(1)} %get-tuple-element.99.own_p, bf16[192,384]{1,0:T(8,128)(2,1)S(1)} %collective-permute-done.23.got_k, bf16[192,384]{1,0:T(8,128)(2,1)S(1)} %collective-permute-done.24.got_p), custom_call_target="tpu_custom_call" | custom-call | tf_op jit(solution)/shard_map/first_total/pallas_call | solution.py:148
  (21 shorter events, 0.7 us)
Async XLA Ops:
  0.6 8.9 %collective-permute-start = (bf16[384,256]{1,0:T(8,128)(2,1)}, bf16[384,256]{1,0:T(8,128)(2,1)S(1)}, u32[]{:S(2)}, u32[]{:S(2)}) collective-permute-start(bf16[384,256]{1,0:T(8,128)(2,1)} %x_ref.1), channel_id=1, source_target_pairs={{0,2},{1,3},{2,0},{3,1},{4,6},{5,7},{6,4},{7,5},{8,10},{9,11},{10,... | collective-permute-start | bytes 589832 | tf_op jit(solution)/shard_map/ppermute | solution.py:120
  3.6 9.3 %collective-permute-start.1 = (bf16[384,256]{1,0:T(8,128)(2,1)}, bf16[384,256]{1,0:T(8,128)(2,1)S(1)}, u32[]{:S(2)}, u32[]{:S(2)}) collective-permute-start(bf16[384,256]{1,0:T(8,128)(2,1)} %x_ref.1), channel_id=1, source_target_pairs={{0,1},{1,0},{2,3},{3,2},{4,5},{5,4},{6,7},{7,6},{8,9},{9,8},{10,11... | collective-permute-start | bytes 589832 | tf_op jit(solution)/shard_map/ppermute | solution.py:120
  3.6 9.3 %collective-permute-start.3 = (bf16[2,48,1024]{2,1,0:T(8,128)(2,1)}, bf16[2,48,1024]{2,1,0:T(8,128)(2,1)S(1)}, u32[]{:S(2)}, u32[]{:S(2)}) collective-permute-start(bf16[2,48,1024]{2,1,0:T(8,128)(2,1)} %g_ref.1), channel_id=1, source_target_pairs={{0,2},{1,3},{2,0},{3,1},{4,6},{5,7},{6,4},{7,5},{8,10},{9,11},{10,... | collective-permute-start | bytes 589832 | tf_op jit(solution)/shard_map/ppermute | solution.py:120
  9.6 3.4 %collective-permute-start.2 = (bf16[384,256]{1,0:T(8,128)(2,1)S(1)}, bf16[384,256]{1,0:T(8,128)(2,1)S(1)}, u32[]{:S(2)}, u32[]{:S(2)}) collective-permute-start(bf16[384,256]{1,0:T(8,128)(2,1)S(1)} %collective-permute-done.x2), channel_id=1, source_target_pairs={{0,1},{1,0},{2,3},{3,2},{4,5},{5,4},{6,7},{7,6},{8,9},{9,8},{10,11... | collective-permute-start | bytes 589832 | tf_op jit(solution)/shard_map/ppermute | solution.py:120
  14.3 1.8 %collective-permute-start.4 = (bf16[2,384,256]{2,1,0:T(8,128)(2,1)S(1)}, bf16[2,384,256]{2,1,0:T(8,128)(2,1)S(1)}, u32[]{:S(2)}, u32[]{:S(2)}) collective-permute-start(bf16[2,384,256]{2,1,0:T(8,128)(2,1)S(1)} %get-tuple-element.63), channel_id=1, source_target_pairs={{0,1},{1,0},{2,3},{3,2},{4,5},{5,4},{6,7},{7,6},{8,9},{9,8},{10,11... | collective-permute-start | bytes 1179656 | tf_op jit(solution)/shard_map/ppermute | solution.py:120
  16.2 14.1 %collective-permute-start.5 = (bf16[2,384,256]{2,1,0:T(8,128)(2,1)S(1)}, bf16[2,384,256]{2,1,0:T(8,128)(2,1)S(1)}, u32[]{:S(2)}, u32[]{:S(2)}) collective-permute-start(bf16[2,384,256]{2,1,0:T(8,128)(2,1)S(1)} %mix_sum.1.chip_ref), channel_id=1, source_target_pairs={{0,2},{1,3},{2,0},{3,1},{4,6},{5,7},{6,4},{7,5},{8,10},{9,11},{10,... | collective-permute-start | bytes 1179656 | tf_op jit(solution)/shard_map/ppermute | solution.py:120
  18.1 4.7 %collective-permute-start.7 = (bf16[2,2,48,256]{3,2,1,0:T(8,128)(2,1)S(1)}, bf16[2,2,48,256]{3,2,1,0:T(8,128)(2,1)S(1)}, u32[]{:S(2)}, u32[]{:S(2)}) collective-permute-start(bf16[2,2,48,256]{3,2,1,0:T(8,128)(2,1)S(1)} %get-tuple-element.66), channel_id=1, source_target_pairs={{0,4},{4,0},{8,12},{12,8},{1,5},{5,1},{9,13},{13,9},{2,6},{6,2},{1... | collective-permute-start | bytes 294920 | tf_op jit(solution)/shard_map/ppermute | solution.py:120
  19.7 10.4 %collective-permute-start.8 = (bf16[2,2,48,256]{3,2,1,0:T(8,128)(2,1)S(1)}, bf16[2,2,48,256]{3,2,1,0:T(8,128)(2,1)S(1)}, u32[]{:S(2)}, u32[]{:S(2)}) collective-permute-start(bf16[2,2,48,256]{3,2,1,0:T(8,128)(2,1)S(1)} %get-tuple-element.67), channel_id=1, source_target_pairs={{0,8},{4,12},{8,0},{12,4},{1,9},{5,13},{9,1},{13,5},{2,10},{6,14},... | collective-permute-start | bytes 294920 | tf_op jit(solution)/shard_map/ppermute | solution.py:120
  22.3 7.9 %collective-permute-start.9 = (bf16[2,2,48,256]{3,2,1,0:T(8,128)(2,1)S(1)}, bf16[2,2,48,256]{3,2,1,0:T(8,128)(2,1)S(1)}, u32[]{:S(2)}, u32[]{:S(2)}) collective-permute-start(bf16[2,2,48,256]{3,2,1,0:T(8,128)(2,1)S(1)} %get-tuple-element.68), channel_id=1, source_target_pairs={{0,12},{4,8},{8,4},{12,0},{1,13},{5,9},{9,5},{13,1},{2,14},{6,10},... | collective-permute-start | bytes 294920 | tf_op jit(solution)/shard_map/ppermute | solution.py:120
  30.2 1.8 %collective-permute-start.10 = (bf16[2,384,256]{2,1,0:T(8,128)(2,1)S(1)}, bf16[2,384,256]{2,1,0:T(8,128)(2,1)S(1)}, u32[]{:S(2)}, u32[]{:S(2)}) collective-permute-start(bf16[2,384,256]{2,1,0:T(8,128)(2,1)S(1)} %bitcast.5), channel_id=1, source_target_pairs={{0,1},{1,0},{2,3},{3,2},{4,5},{5,4},{6,7},{7,6},{8,9},{9,8},{10,11... | collective-permute-start | bytes 1179656 | tf_op jit(solution)/shard_map/ppermute | solution.py:120
  30.4 2.1 %collective-permute-start.6 = (bf16[2,384,256]{2,1,0:T(8,128)(2,1)S(1)}, bf16[2,384,256]{2,1,0:T(8,128)(2,1)S(1)}, u32[]{:S(2)}, u32[]{:S(2)}) collective-permute-start(bf16[2,384,256]{2,1,0:T(8,128)(2,1)S(1)} %middle.1.a_ref.mid_ref), channel_id=1, source_target_pairs={{0,1},{1,0},{2,3},{3,2},{4,5},{5,4},{6,7},{7,6},{8,9},{9,8},{10,11... | collective-permute-start | bytes 1179656 | tf_op jit(solution)/shard_map/ppermute | solution.py:120
  33.9 1.8 %collective-permute-start.13 = (bf16[2,384,256]{2,1,0:T(8,128)(2,1)S(1)}, bf16[2,384,256]{2,1,0:T(8,128)(2,1)S(1)}, u32[]{:S(2)}, u32[]{:S(2)}) collective-permute-start(bf16[2,384,256]{2,1,0:T(8,128)(2,1)S(1)} %get-tuple-element.76), channel_id=1, source_target_pairs={{0,1},{1,0},{2,3},{3,2},{4,5},{5,4},{6,7},{7,6},{8,9},{9,8},{10,11... | collective-permute-start | bytes 1179656 | tf_op jit(solution)/shard_map/ppermute | solution.py:120
  35.8 11.3 %collective-permute-start.14 = (bf16[2,384,256]{2,1,0:T(8,128)(2,1)S(1)}, bf16[2,384,256]{2,1,0:T(8,128)(2,1)S(1)}, u32[]{:S(2)}, u32[]{:S(2)}) collective-permute-start(bf16[2,384,256]{2,1,0:T(8,128)(2,1)S(1)} %squash_sum.1.chip_ref), channel_id=1, source_target_pairs={{0,2},{1,3},{2,0},{3,1},{4,6},{5,7},{6,4},{7,5},{8,10},{9,11},{10,... | collective-permute-start | bytes 1179656 | tf_op jit(solution)/shard_map/ppermute | solution.py:120
  36.4 15.0 %collective-permute-start.19 = (bf16[2,192,384]{2,1,0:T(8,128)(2,1)S(1)}, bf16[2,192,384]{2,1,0:T(8,128)(2,1)S(1)}, u32[]{:S(2)}, u32[]{:S(2)}) collective-permute-start(bf16[2,192,384]{2,1,0:T(8,128)(2,1)S(1)} %get-tuple-element.92), channel_id=1, source_target_pairs={{0,4},{4,0},{8,12},{12,8},{1,5},{5,1},{9,13},{13,9},{2,6},{6,2},{1... | collective-permute-start | bytes 884744 | tf_op jit(solution)/shard_map/ppermute | solution.py:120
  38.0 15.8 %collective-permute-start.20 = (bf16[2,192,384]{2,1,0:T(8,128)(2,1)S(1)}, bf16[2,192,384]{2,1,0:T(8,128)(2,1)S(1)}, u32[]{:S(2)}, u32[]{:S(2)}) collective-permute-start(bf16[2,192,384]{2,1,0:T(8,128)(2,1)S(1)} %get-tuple-element.93), channel_id=1, source_target_pairs={{0,8},{4,12},{8,0},{12,4},{1,9},{5,13},{9,1},{13,5},{2,10},{6,14},... | collective-permute-start | bytes 884744 | tf_op jit(solution)/shard_map/ppermute | solution.py:120
  47.7 1.5 %collective-permute-start.16 = (bf16[384,256]{1,0:T(8,128)(2,1)S(1)}, bf16[384,256]{1,0:T(8,128)(2,1)S(1)}, u32[]{:S(2)}, u32[]{:S(2)}) collective-permute-start(bf16[384,256]{1,0:T(8,128)(2,1)S(1)} %get-tuple-element.82.refs_2_.g2), channel_id=1, source_target_pairs={{0,1},{1,0},{2,3},{3,2},{4,5},{5,4},{6,7},{7,6},{8,9},{9,8},{10,11... | collective-permute-start | bytes 589832 | tf_op jit(solution)/shard_map/ppermute | solution.py:120
  47.8 1.7 %collective-permute-start.15 = (bf16[384,256]{1,0:T(8,128)(2,1)S(1)}, bf16[384,256]{1,0:T(8,128)(2,1)S(1)}, u32[]{:S(2)}, u32[]{:S(2)}) collective-permute-start(bf16[384,256]{1,0:T(8,128)(2,1)S(1)} %get-tuple-element.81.refs_0_.g_ref.g0), channel_id=1, source_target_pairs={{0,1},{1,0},{2,3},{3,2},{4,5},{5,4},{6,7},{7,6},{8,9},{9,8},{10,11... | collective-permute-start | bytes 589832 | tf_op jit(solution)/shard_map/ppermute | solution.py:120
  48.3 9.4 %collective-permute-start.11 = (bf16[2,384,256]{2,1,0:T(8,128)(2,1)S(1)}, bf16[2,384,256]{2,1,0:T(8,128)(2,1)S(1)}, u32[]{:S(2)}, u32[]{:S(2)}) collective-permute-start(bf16[2,384,256]{2,1,0:T(8,128)(2,1)S(1)} %get-tuple-element.72), channel_id=1, source_target_pairs={{0,1},{1,0},{2,3},{3,2},{4,5},{5,4},{6,7},{7,6},{8,9},{9,8},{10,11... | collective-permute-start | bytes 1179656 | tf_op jit(solution)/shard_map/ppermute | solution.py:120
  50.6 8.7 %collective-permute-start.17 = (bf16[2,384,256]{2,1,0:T(8,128)(2,1)S(1)}, bf16[2,384,256]{2,1,0:T(8,128)(2,1)S(1)}, u32[]{:S(2)}, u32[]{:S(2)}) collective-permute-start(bf16[2,384,256]{2,1,0:T(8,128)(2,1)S(1)} %get-tuple-element.85), channel_id=1, source_target_pairs={{0,1},{1,0},{2,3},{3,2},{4,5},{5,4},{6,7},{7,6},{8,9},{9,8},{10,11... | collective-permute-start | bytes 1179656 | tf_op jit(solution)/shard_map/ppermute | solution.py:120
  54.6 18.7 %collective-permute-start.21 = (bf16[3,192,384]{2,1,0:T(8,128)(2,1)S(1)}, bf16[3,192,384]{2,1,0:T(8,128)(2,1)S(1)}, u32[]{:S(2)}, u32[]{:S(2)}) collective-permute-start(bf16[3,192,384]{2,1,0:T(8,128)(2,1)S(1)} %get-tuple-element.96), channel_id=1, source_target_pairs={{0,4},{4,0},{8,12},{12,8},{1,5},{5,1},{9,13},{13,9},{2,6},{6,2},{1... | collective-permute-start | bytes 1327112 | tf_op jit(solution)/shard_map/ppermute | solution.py:120
  55.1 21.7 %collective-permute-start.22 = (bf16[3,192,384]{2,1,0:T(8,128)(2,1)S(1)}, bf16[3,192,384]{2,1,0:T(8,128)(2,1)S(1)}, u32[]{:S(2)}, u32[]{:S(2)}) collective-permute-start(bf16[3,192,384]{2,1,0:T(8,128)(2,1)S(1)} %get-tuple-element.97), channel_id=1, source_target_pairs={{0,8},{4,12},{8,0},{12,4},{1,9},{5,13},{9,1},{13,5},{2,10},{6,14},... | collective-permute-start | bytes 1327112 | tf_op jit(solution)/shard_map/ppermute | solution.py:120
  57.8 21.9 %collective-permute-start.12 = (bf16[384,256]{1,0:T(8,128)(2,1)S(1)}, bf16[384,256]{1,0:T(8,128)(2,1)S(1)}, u32[]{:S(2)}, u32[]{:S(2)}) collective-permute-start(bf16[384,256]{1,0:T(8,128)(2,1)S(1)} %get-tuple-element.74), channel_id=1, source_target_pairs={{0,2},{1,3},{2,0},{3,1},{4,6},{5,7},{6,4},{7,5},{8,10},{9,11},{10,... | collective-permute-start | bytes 589832 | tf_op jit(solution)/shard_map/ppermute | solution.py:120
  59.4 22.1 %collective-permute-start.18 = (bf16[384,256]{1,0:T(8,128)(2,1)S(1)}, bf16[384,256]{1,0:T(8,128)(2,1)S(1)}, u32[]{:S(2)}, u32[]{:S(2)}) collective-permute-start(bf16[384,256]{1,0:T(8,128)(2,1)S(1)} %get-tuple-element.87), channel_id=1, source_target_pairs={{0,2},{1,3},{2,0},{3,1},{4,6},{5,7},{6,4},{7,5},{8,10},{9,11},{10,... | collective-permute-start | bytes 589832 | tf_op jit(solution)/shard_map/ppermute | solution.py:120
  76.9 7.0 %collective-permute-start.23 = (bf16[192,384]{1,0:T(8,128)(2,1)S(1)}, bf16[192,384]{1,0:T(8,128)(2,1)S(1)}, u32[]{:S(2)}, u32[]{:S(2)}) collective-permute-start(bf16[192,384]{1,0:T(8,128)(2,1)S(1)} %get-tuple-element.100), channel_id=1, source_target_pairs={{0,8},{4,12},{8,0},{12,4},{1,9},{5,13},{9,1},{13,5},{2,10},{6,14},... | collective-permute-start | bytes 442376 | tf_op jit(solution)/shard_map/ppermute | solution.py:120
  77.0 7.3 %collective-permute-start.24 = (bf16[192,384]{1,0:T(8,128)(2,1)S(1)}, bf16[192,384]{1,0:T(8,128)(2,1)S(1)}, u32[]{:S(2)}, u32[]{:S(2)}) collective-permute-start(bf16[192,384]{1,0:T(8,128)(2,1)S(1)} %get-tuple-element.101), channel_id=1, source_target_pairs={{0,4},{4,0},{8,12},{12,8},{1,5},{5,1},{9,13},{13,9},{2,6},{6,2},{1... | collective-permute-start | bytes 442376 | tf_op jit(solution)/shard_map/ppermute | solution.py:120

commit v6 on v5

--- a/solution.py
+++ b/solution.py
@@ -250,13 +250,10 @@
     )
     got = swap(send, "mp", 1)
 
-    def near_body(keep_ref, got_ref, *rest):
-        rest[-1][...] = (keep_ref[...] + got_ref[...].astype(F32)).astype(BF16)
-
-    def near_sum(keep, got, name, after=()):
-        return call(near_body, [((2, rows, bins), BF16)], (keep, got, *after), name)[0]
-
-    chip = near_sum(keep, got, "mix_sum")
+    def mix_body(keep_ref, got_ref, out_ref):
+        out_ref[...] = (keep_ref[...] + got_ref[...].astype(F32)).astype(BF16)
+
+    (chip,) = call(mix_body, [((2, rows, bins), BF16)], (keep, got), "mix_sum")
     other = swap(chip, "mp", 2)
 
     def middle_body(x0, x2, chip_ref, other_ref, out_ref):
@@ -311,66 +308,101 @@
         (mid, mid_near, g_pair, g_near, tap_b, cols_b),
         "second_block",
     )
-    def weight_pieces(z_ref, gu_ref, v_ref, g_ref, keep_k, keep_p, send_k, send_p):
-        j = lax.axis_index("mp") ^ lax.axis_index("ctx")
-
-        def taps(k):
-            return dot(gu_ref[...], z_ref[j ^ k], ((1,), (1,)))
-
-        def proj(k):
-            return dot(v_ref[...], g_ref[j ^ k], ((1,), (1,)))
-
-        for i, k in enumerate((1, 3)):
-            send_k[i] = taps(k).astype(BF16)
-        for i, k in enumerate((2, 3)):
-            send_p[i] = proj(k).astype(BF16)
-        for i, k in enumerate((0, 2)):
-            keep_k[i] = taps(k)
-        for i, k in enumerate((0, 1)):
-            keep_p[i] = proj(k)
+    def place(k):
+        return lax.axis_index("mp") ^ lax.axis_index("ctx") ^ k
+
+    def taps_pieces(z_ref, gu_ref, keep, send):
+        for i in (0, 1):
+            send[i] = dot(gu_ref[...], z_ref[place(1 + 2 * i)], ((1,), (1,))).astype(BF16)
+        for i in (0, 1):
+            keep[i] = dot(gu_ref[...], z_ref[place(2 * i)], ((1,), (1,)))
+
+    def proj_pieces(v_ref, g_ref, keep, send):
+        for i in (0, 1):
+            send[i] = dot(v_ref[...], g_ref[place(2 + i)], ((1,), (1,))).astype(BF16)
+        for i in (0, 1):
+            keep[i] = dot(v_ref[...], g_ref[place(i)], ((1,), (1,)))
 
     one, two, three = ((n, hid, rows) for n in (1, 2, 3))
 
     def second_weight_body(z_ref, gu_ref, v_ref, ga_ref, gb_ref, *rest):
-        g_ref = rest[4]
+        keep_k, keep_p, send_k, send_p, g_ref = rest
         for i in range(4):
             g_ref[i] = (ga_ref, gb_ref)[i & 1][i >> 1]
-        weight_pieces(z_ref, gu_ref, v_ref, g_ref, *rest[:4])
+        proj_pieces(v_ref, g_ref, keep_p, send_p)
+        taps_pieces(z_ref, gu_ref, keep_k, send_k)
 
     def half_sum(keep, got, own):
         own[0] = keep[0] + got[0].astype(F32)
         return (keep[1] + got[1].astype(F32)).astype(BF16)
 
-    def first_weight_body(z_ref, gu_ref, v_ref, g0, g1, g2, g3, *rest):
-        keep_k, keep_p, got_k, got_p = rest[:4]
-        own_k, own_p = rest[8:10]
-        g_ref = rest[10]
+    def first_proj_body(v_ref, g0, g1, g2, g3, keep_b, got_b, keep, send, own, g_ref):
         for i, ref in enumerate((g0, g1, g2, g3)):
             g_ref[i] = ref[...]
-        send_k, send_p = rest[6:8]
-        send_p[2] = half_sum(keep_k, got_k, own_k)
-        send_k[2] = half_sum(keep_p, got_p, own_p)
-        weight_pieces(z_ref, gu_ref, v_ref, g_ref, *rest[4:8])
-
-    def half_body(keep_k, keep_p, got_k, got_p, own_k, own_p, send_k, send_p):
-        send_k[...] = half_sum(keep_k, got_k, own_k)
-        send_p[...] = half_sum(keep_p, got_p, own_p)
-
-    def total_body(place_k, place_p, own_k, own_p, got_k, got_p, taps_ref, proj_ref):
-        taps_ref[0] = jnp.zeros((hid, rows), F32)
-        taps_ref[1] = own_k[0] + got_k[place_k].astype(F32)
-        taps_ref[2] = jnp.zeros((hid, rows), F32)
-        proj_ref[...] = own_p[0] + got_p[place_p].astype(F32)
-
-    def total(place, own_k, own_p, got_k, got_p, name):
-        taps, proj = call(
-            functools.partial(total_body, place, place),
-            [((3, hid, rows), F32), ((hid, rows), F32)],
-            (own_k, own_p, got_k, got_p),
-            name,
-            final=True,
+        send[2] = half_sum(keep_b, got_b, own)
+        proj_pieces(v_ref, g_ref, keep, send)
+
+    def first_taps_body(z_ref, gu_ref, keep_b, got_b, _, keep, send, own):
+        send[2] = half_sum(keep_b, got_b, own)
+        taps_pieces(z_ref, gu_ref, keep, send)
+
+    def half_body(keep, got, own, send):
+        send[...] = half_sum(keep, got, own)
+
+    plane = ((3, hid, rows), F32)
+    hbm = pl.BlockSpec(memory_space=pltpu.HBM)
+
+    def zero_body(*refs):
+        outs, (zero, sems) = refs[:2], refs[2:]
+        zero[...] = jnp.zeros((hid, rows), F32)
+        copies = [
+            pltpu.make_async_copy(zero, out.at[tap], sems.at[2 * i + tap // 2])
+            for i, out in enumerate(outs)
+            for tap in (0, 2)
+        ]
+        for copy in copies:
+            copy.start()
+        for copy in copies:
+            copy.wait()
+
+    def total_body(place, _, own_k, own_p, got_k, got_p, taps_ref, proj_ref, k, p, sems):
+        k[...] = own_k[0] + got_k[place].astype(F32)
+        first = pltpu.make_async_copy(k, taps_ref.at[1], sems.at[0])
+        first.start()
+        p[...] = own_p[0] + got_p[place].astype(F32)
+        second = pltpu.make_async_copy(p, proj_ref, sems.at[1])
+        second.start()
+        first.wait()
+        second.wait()
+
+    def total(place, planes, own_k, own_p, got_k, got_p, name):
+        taps, proj = pl.pallas_call(
+            functools.partial(total_body, place),
+            out_shape=[jax.ShapeDtypeStruct(*plane), jax.ShapeDtypeStruct((hid, rows), F32)],
+            in_specs=[hbm] + [VMEM] * 4,
+            out_specs=[hbm, hbm],
+            scratch_shapes=[pltpu.VMEM((hid, rows), F32)] * 2 + [pltpu.SemaphoreType.DMA((2,))],
+            input_output_aliases={0: 0},
+            compiler_params=pltpu.CompilerParams(vmem_limit_bytes=16 << 20),
+            name=name,
+        )(
+            pltpu.with_memory_space_constraint(planes, pltpu.HBM),
+            *[
+                pltpu.with_memory_space_constraint(a, pltpu.VMEM)
+                for a in (own_k, own_p, got_k, got_p)
+            ],
         )
         return taps, proj.T
+
+    planes = pl.pallas_call(
+        zero_body,
+        out_shape=[pltpu.HBM(*plane)] * 2,
+        in_specs=[],
+        out_specs=[hbm, hbm],
+        scratch_shapes=[pltpu.VMEM((hid, rows), F32), pltpu.SemaphoreType.DMA((4,))],
+        compiler_params=pltpu.CompilerParams(vmem_limit_bytes=16 << 20),
+        name="zero_planes",
+    )()
 
     pack = [pltpu.VMEM((4, rows, bins), BF16)]
     *keep_b, send_k, send_p = call(
@@ -381,19 +413,24 @@
         pack,
     )
     got = swap(send, "mp", 1)
-    chip = near_sum(keep, got, "squash_sum", keep_b[:1])
-    other = swap(chip, "mp", 2)
+
+    def squash_body(keep_ref, got_ref, _, *outs):
+        for i in (0, 1):
+            outs[i][...] = (keep_ref[i] + got_ref[i].astype(F32)).astype(BF16)
+
+    chip = call(squash_body, [((rows, bins), BF16)] * 2, (keep, got, keep_b[0]), "squash_sum")
+    other = [swap(part, "mp", 2) for part in chip]
     got_b = swap(send_k, "ctx", 1), swap(send_p, "ctx", 2)
 
-    def back_body(g_ref, mid_ref, chip_ref, other_ref, *outs):
-        for i in (0, 1):
-            grad = chip_ref[i].astype(F32) + other_ref[1 - i].astype(F32)
+    def back_body(g_ref, mid_ref, chip0, chip1, other0, other1, *outs):
+        for i, (chip_ref, other_ref) in enumerate(((chip0, other1), (chip1, other0))):
+            grad = chip_ref[...].astype(F32) + other_ref[...].astype(F32)
             outs[i][...] = (
                 g_ref[i].astype(F32) + grad * slope_of(mid_ref[i].astype(F32))
             ).astype(BF16)
 
     g_mid = call(
-        back_body, [((rows, bins), BF16)] * 2, (g_pair, mid, chip, other), "middle_grad"
+        back_body, [((rows, bins), BF16)] * 2, (g_pair, mid, *chip, *other), "middle_grad"
     )
     g_mid = [g_mid[0], swap(g_mid[0], "mp", 1), g_mid[1], swap(g_mid[1], "mp", 1)]
 
@@ -436,14 +473,21 @@
         (*g_mid, tap_a, cols_a, slope_a),
         "first_backward",
     )
-    *keep_a, send_k, send_p, own_bk, own_bp = call(
-        first_weight_body,
-        [(two, F32), (two, F32), (three, BF16), (three, BF16), (one, F32), (one, F32)],
-        (z_a, gu_a, v_a, *g_mid, *keep_b, *got_b),
-        "first_weights",
+    keep_ap, send_p, own_bk = call(
+        first_proj_body,
+        [(two, F32), (three, BF16), (one, F32)],
+        (v_a, *g_mid, keep_b[0], got_b[0]),
+        "first_proj",
         pack,
     )
-    got_k, got_p = swap(send_k, "ctx", 1), swap(send_p, "ctx", 2)
+    got_p = swap(send_p, "ctx", 2)
+    keep_ak, send_k, own_bp = call(
+        first_taps_body,
+        [(two, F32), (three, BF16), (one, F32)],
+        (z_a, gu_a, keep_b[1], got_b[1], own_bk),
+        "first_taps",
+    )
+    got_k = swap(send_k, "ctx", 1)
     got = swap(send, "mp", 1)
     e_own, e_send = last_sum(keep, got, "entry_sum")
     e_got = swap(e_send, "mp", 2)
@@ -456,15 +500,13 @@
 
     (entry,) = call(entry_body, [((rows, bins), BF16)], (g_mid[0], x_own, e_own, e_got), "entry", final=True)
 
-    own_ak, own_ap, send_k, send_p = call(
-        half_body,
-        [(one, F32), (one, F32), (one[1:], BF16), (one[1:], BF16)],
-        (*keep_a, got_k, got_p),
-        "first_half",
-    )
-    last_k, last_p = swap(send_k, "ctx", 2), swap(send_p, "ctx", 1)
-    taps_b_grad, point_b_grad = total(2, own_bk, own_bp, got_p, got_k, "second_total")
-    taps_a_grad, point_a_grad = total(Ellipsis, own_ak, own_ap, last_k, last_p, "first_total")
+    half = [(one, F32), (one[1:], BF16)]
+    own_ak, send_k = call(half_body, half, (keep_ak, got_k), "taps_half")
+    last_k = swap(send_k, "ctx", 2)
+    own_ap, send_p = call(half_body, half, (keep_ap, got_p), "proj_half")
+    last_p = swap(send_p, "ctx", 1)
+    taps_b_grad, point_b_grad = total(2, planes[0], own_bk, own_bp, got_p, got_k, "second_total")
+    taps_a_grad, point_a_grad = total(Ellipsis, planes[1], own_ak, own_ap, last_k, last_p, "first_total")
     return second_out, entry, taps_a_grad, point_a_grad, taps_b_grad, point_b_grad
 
 

time: 85.6 us -> 89.5 us (1.046)
  waiting for transfers between devices: 49.6 us -> 53.5 us
  starting transfers between devices: 22.9 us -> 21.9 us
  Pallas kernels: 12.2 us -> 13.1 us
    ppermute x25 -> x26, waiting for transfers between devices: 49.6 us -> 53.5 us  [swap(): return lax.ppermute(value, axis, [(i, i ^ bits) for i in range(size)])]
    pallas_call x0 -> x3, Pallas kernels: none -> 2.77 us  [the longest x2 1.71 us: total(): pl.pallas_call(functools.partial(total_body, place), out_shape=[jax.Shape...]
    pallas_call x18, Pallas kernels: 10.4 us -> 8.5 us  [call(): pl.pallas_call(body, out_shape=[struct(s, d) for s, d in outs], in_specs=...]
    ppermute x25 -> x26, starting transfers between devices: 22.9 us -> 21.9 us  [swap(): return lax.ppermute(value, axis, [(i, i ^ bits) for i in range(size)])]
  transfers between devices with their start and end apart: 25 -> 26, of which waited for: 17 -> 17; matrix products, arithmetic and copies ran while one was open for 0% -> 0% of each run, Pallas kernels for 10% -> 10%
where the time goes in v6:
time: 89.5 us; the launch traced here: 89.3 us
  waiting for transfers between devices  53.5 us (60%)
  starting transfers between devices  21.9 us (24%)
  Pallas kernels  13.1 us (15%)
    ppermute x26, waiting for transfers between devices, swap(): return lax.ppermute(value, axis, [(i, i ^ bits) for i in range(size)])  53.5 us
    ppermute x26, starting transfers between devices, swap(): return lax.ppermute(value, axis, [(i, i ^ bits) for i in range(size)])  21.9 us
    pallas_call x18, Pallas kernels, call(): pl.pallas_call(body, out_shape=[struct(s, d) for s, d in outs], in_specs=...  8.5 us
    pallas_call x1, Pallas kernels, fast_shards(): pl.pallas_call(load_body, out_shape=[pltpu.VMEM((rows, bins), BF16)] + [p...  1.79 us
  transfers between devices with their start and end apart: 26, of which 17 were waited for; matrix products, arithmetic and copies ran while one was open for 0% of the time, Pallas kernels for 10%

profile of v6, /device:TPU:0, one launch (start us, length us, event | category | flops | bytes accessed | tf_op | source)
XLA Modules:
  0.0 89.3 jit_solution(14810485695617529457)
XLA Ops:
  0.6 3.0 %collective-permute-start = (bf16[384,256]{1,0:T(8,128)(2,1)}, bf16[384,256]{1,0:T(8,128)(2,1)S(1)}, u32[]{:S(2)}, u32[]{:S(2)}) collective-permute-start(bf16[384,256]{1,0:T(8,128)(2,1)} %x_ref.1), channel_id=1, source_target_pairs={{0,2},{1,3},{2,0},{3,1},{4,6},{5,7},{6,4},{7,5},{8,10},{9,11},{10,... | collective-permute-start | bytes 589832 | tf_op jit(solution)/shard_map/ppermute | solution.py:120
  3.6 0.2 collective-permute-start.3
  3.8 1.8 %load.1 = (bf16[384,256]{1,0:T(8,128)(2,1)S(1)}, bf16[192,1536]{1,0:T(8,128)(2,1)S(1)}, bf16[192,1536]{1,0:T(8,128)(2,1)S(1)}, bf16[192,1536]{1,0:T(8,128)(2,1)S...) custom-call(bf16[384,256]{1,0:T(8,128)(2,1)} %x_ref.1, bf16[3,192,1536]{2,1,0:T(8,128)(2,1)} %ta.1, ...), custom_call_target="tpu_custom_call" | custom-call | tf_op jit(solution)/shard_map/load/pallas_call | solution.py:183
  5.6 4.0 %collective-permute-done.x2 = bf16[384,256]{1,0:T(8,128)(2,1)S(1)} collective-permute-done((bf16[384,256]{1,0:T(8,128)(2,1)}, bf16[384,256]{1,0:T(8,128)(2,1)S(1)}, u32[]{:S(2)}, u32[]{:S(2)}) %collective-permute-start) | collective-permute-done | bytes 196640 | tf_op jit(solution)/shard_map/ppermute | solution.py:120
  9.6 3.4 %collective-permute-done.3._.far_ref = bf16[2,48,1024]{2,1,0:T(8,128)(2,1)S(1)} collective-permute-done((bf16[2,48,1024]{2,1,0:T(8,128)(2,1)}, bf16[2,48,1024]{2,1,0:T(8,128)(2,1)S(1)}, u32[]{:S(2)}, u32[]{:S(2)}) %collective-permute-start.3) | collective-permute-done | bytes 196640 | tf_op jit(solution)/shard_map/ppermute | solution.py:120
  13.0 1.4 %first_forward.1 = (bf16[4,384,256]{2,1,0:T(8,128)(2,1)S(1)}, bf16[192,256]{1,0:T(8,128)(2,1)S(1)}, f32[192,256]{1,0:T(8,128)S(1)}, f32[2,384,256]{2,1,0:T(8,128)S(1)}, bf16[2,384,256]{2,1,0:T(8,128)(2,1)S(1)}) custom-call(bf16[384,256]{1,0:T(8,128)(2,1)S(1)} %get-tuple-element.62.x0.x_ref, bf16[384,256]{1,0:T(8,128)(2,1)S(1)} %collective-permute-done.1.x1, ...), custom_call_target="tpu_custom_call" | custom-call | tf_op jit(solution)/shard_map/first_forward/pallas_call | solution.py:148
  14.4 1.7 %collective-permute-done.4.got_ref = bf16[2,384,256]{2,1,0:T(8,128)(2,1)S(1)} collective-permute-done((bf16[2,384,256]{2,1,0:T(8,128)(2,1)S(1)}, bf16[2,384,256]{2,1,0:T(8,128)(2,1)S(1)}, u32[]{:S(2)}, u32[]{:S(2)}) %collective-permute-start.4) | collective-permute-done | bytes 393248 | tf_op jit(solution)/shard_map/ppermute | solution.py:120
  16.2 1.8 %collective-permute-start.5 = (bf16[2,384,256]{2,1,0:T(8,128)(2,1)S(1)}, bf16[2,384,256]{2,1,0:T(8,128)(2,1)S(1)}, u32[]{:S(2)}, u32[]{:S(2)}) collective-permute-start(bf16[2,384,256]{2,1,0:T(8,128)(2,1)S(1)} %mix_sum.1.chip_ref), channel_id=1, source_target_pairs={{0,2},{1,3},{2,0},{3,1},{4,6},{5,7},{6,4},{7,5},{8,10},{9,11},{10,... | collective-permute-start | bytes 1179656 | tf_op jit(solution)/shard_map/ppermute | solution.py:120
  18.1 1.6 %collective-permute-start.7 = (bf16[2,2,48,256]{3,2,1,0:T(8,128)(2,1)S(1)}, bf16[2,2,48,256]{3,2,1,0:T(8,128)(2,1)S(1)}, u32[]{:S(2)}, u32[]{:S(2)}) collective-permute-start(bf16[2,2,48,256]{3,2,1,0:T(8,128)(2,1)S(1)} %get-tuple-element.70), channel_id=1, source_target_pairs={{0,4},{4,0},{8,12},{12,8},{1,5},{5,1},{9,13},{13,9},{2,6},{6,2},{1... | collective-permute-start | bytes 294920 | tf_op jit(solution)/shard_map/ppermute | solution.py:120
  19.7 2.6 %collective-permute-start.8 = (bf16[2,2,48,256]{3,2,1,0:T(8,128)(2,1)S(1)}, bf16[2,2,48,256]{3,2,1,0:T(8,128)(2,1)S(1)}, u32[]{:S(2)}, u32[]{:S(2)}) collective-permute-start(bf16[2,2,48,256]{3,2,1,0:T(8,128)(2,1)S(1)} %get-tuple-element.71), channel_id=1, source_target_pairs={{0,8},{4,12},{8,0},{12,4},{1,9},{5,13},{9,1},{13,5},{2,10},{6,14},... | collective-permute-start | bytes 294920 | tf_op jit(solution)/shard_map/ppermute | solution.py:120
  22.3 0.2 collective-permute-start.9
  22.5 0.2 collective-permute-done.7.refs_1_
  22.7 7.4 %collective-permute-done.8.refs_2_ = bf16[2,2,48,256]{3,2,1,0:T(8,128)(2,1)S(1)} collective-permute-done((bf16[2,2,48,256]{3,2,1,0:T(8,128)(2,1)S(1)}, bf16[2,2,48,256]{3,2,1,0:T(8,128)(2,1)S(1)}, u32[]{:S(2)}, u32[]{:S(2)}) %collective-permute-start.8) | collective-permute-done | bytes 98336 | tf_op jit(solution)/shard_map/ppermute | solution.py:120
  30.4 0.5 collective-permute-start.6
  31.0 1.0 %collective-permute-done.10.gb_ref = bf16[2,384,256]{2,1,0:T(8,128)(2,1)S(1)} collective-permute-done((bf16[2,384,256]{2,1,0:T(8,128)(2,1)S(1)}, bf16[2,384,256]{2,1,0:T(8,128)(2,1)S(1)}, u32[]{:S(2)}, u32[]{:S(2)}) %collective-permute-start.10) | collective-permute-done | bytes 393248 | tf_op jit(solution)/shard_map/ppermute | solution.py:120
  32.0 0.6 collective-permute-done.6.b_ref
  32.5 1.4 %second_block.1 = (bf16[4,384,256]{2,1,0:T(8,128)(2,1)S(1)}, bf16[192,256]{1,0:T(8,128)(2,1)S(1)}, bf16[192,256]{1,0:T(8,128)(2,1)S(1)}, f32[2,384,256]{2,1,0:T(...) custom-call(bf16[2,384,256]{2,1,0:T(8,128)(2,1)S(1)} %middle.1.a_ref.mid_, ...), custom_call_target="tpu_custom_call" | custom-call | tf_op jit(solution)/shard_map/second_block/pallas_call | solution.py:148
  33.9 0.2 collective-permute-start.13
  34.2 0.7 second_weights.1
  34.9 0.8 collective-permute-done.13.got_ref
  35.8 0.6 collective-permute-start.14
  36.4 1.5 %collective-permute-start.15 = (bf16[384,256]{1,0:T(8,128)(2,1)S(1)}, bf16[384,256]{1,0:T(8,128)(2,1)S(1)}, u32[]{:S(2)}, u32[]{:S(2)}) collective-permute-start(bf16[384,256]{1,0:T(8,128)(2,1)S(1)} %get-tuple-element.86.chip1), channel_id=1, source_target_pairs={{0,2},{1,3},{2,0},{3,1},{4,6},{5,7},{6,4},{7,5},{8,10},{9,11},{10,... | collective-permute-start | bytes 589832 | tf_op jit(solution)/shard_map/ppermute | solution.py:120
  37.9 1.6 %collective-permute-start.21 = (bf16[2,192,384]{2,1,0:T(8,128)(2,1)S(1)}, bf16[2,192,384]{2,1,0:T(8,128)(2,1)S(1)}, u32[]{:S(2)}, u32[]{:S(2)}) collective-permute-start(bf16[2,192,384]{2,1,0:T(8,128)(2,1)S(1)} %get-tuple-element.100), channel_id=1, source_target_pairs={{0,4},{4,0},{8,12},{12,8},{1,5},{5,1},{9,13},{13,9},{2,6},{6,2},{1... | collective-permute-start | bytes 884744 | tf_op jit(solution)/shard_map/ppermute | solution.py:120
  39.5 1.4 %collective-permute-start.20 = (bf16[2,192,384]{2,1,0:T(8,128)(2,1)S(1)}, bf16[2,192,384]{2,1,0:T(8,128)(2,1)S(1)}, u32[]{:S(2)}, u32[]{:S(2)}) collective-permute-start(bf16[2,192,384]{2,1,0:T(8,128)(2,1)S(1)} %get-tuple-element.98), channel_id=1, source_target_pairs={{0,8},{4,12},{8,0},{12,4},{1,9},{5,13},{9,1},{13,5},{2,10},{6,14},... | collective-permute-start | bytes 884744 | tf_op jit(solution)/shard_map/ppermute | solution.py:120
  40.9 2.7 %collective-permute-done.14.other0 = bf16[384,256]{1,0:T(8,128)(2,1)S(1)} collective-permute-done((bf16[384,256]{1,0:T(8,128)(2,1)S(1)}, bf16[384,256]{1,0:T(8,128)(2,1)S(1)}, u32[]{:S(2)}, u32[]{:S(2)}) %collective-permute-start.14) | collective-permute-done | bytes 196640 | tf_op jit(solution)/shard_map/ppermute | solution.py:120
  43.6 3.4 %collective-permute-done.15.other1 = bf16[384,256]{1,0:T(8,128)(2,1)S(1)} collective-permute-done((bf16[384,256]{1,0:T(8,128)(2,1)S(1)}, bf16[384,256]{1,0:T(8,128)(2,1)S(1)}, u32[]{:S(2)}, u32[]{:S(2)}) %collective-permute-start.15) | collective-permute-done | bytes 196640 | tf_op jit(solution)/shard_map/ppermute | solution.py:120
  47.1 0.6 middle_grad.1
  47.8 0.5 collective-permute-start.17
  48.3 0.9 collective-permute-done.16.refs_1_.g1
  49.2 0.3 collective-permute-done.17.refs_3_.g3
  49.5 1.1 %first_backward.1 = (bf16[192,256]{1,0:T(8,128)(2,1)S(1)}, f32[2,384,256]{2,1,0:T(8,128)S(1)}, bf16[2,384,256]{2,1,0:T(8,128)(2,1)S(1)}) custom-call(bf16[384,256]{1,0:T(8,128)(2,1)S(1)} %get-tuple-element.87.refs_0_.g_ref.g0, bf16[384,256]{1,0:T(8,128)(2,1)S(1)} %collective-permute-done.16.refs_1_.g1, bf16[384,256]{1,0:T(8,128)(2,1)S(1)} %get-tuple-element.88.refs_2_.g2, ...), custom_call_target="tpu_custom_call" | custom-call | tf_op jit(solution)/shard_map/first_backward/pallas_call | solution.py:148
  50.6 2.0 %collective-permute-done.21.got_b = bf16[2,192,384]{2,1,0:T(8,128)(2,1)S(1)} collective-permute-done((bf16[2,192,384]{2,1,0:T(8,128)(2,1)S(1)}, bf16[2,192,384]{2,1,0:T(8,128)(2,1)S(1)}, u32[]{:S(2)}, u32[]{:S(2)}) %collective-permute-start.21) | collective-permute-done | bytes 294944 | tf_op jit(solution)/shard_map/ppermute | solution.py:120
  52.6 0.5 first_proj.1
  53.1 1.9 %collective-permute-done.20.got_b = bf16[2,192,384]{2,1,0:T(8,128)(2,1)S(1)} collective-permute-done((bf16[2,192,384]{2,1,0:T(8,128)(2,1)S(1)}, bf16[2,192,384]{2,1,0:T(8,128)(2,1)S(1)}, u32[]{:S(2)}, u32[]{:S(2)}) %collective-permute-start.20) | collective-permute-done | bytes 294944 | tf_op jit(solution)/shard_map/ppermute | solution.py:120
  55.0 0.5 first_taps.1
  55.5 0.5 collective-permute-start.22
  56.0 2.7 %collective-permute-start.23 = (bf16[3,192,384]{2,1,0:T(8,128)(2,1)S(1)}, bf16[3,192,384]{2,1,0:T(8,128)(2,1)S(1)}, u32[]{:S(2)}, u32[]{:S(2)}) collective-permute-start(bf16[3,192,384]{2,1,0:T(8,128)(2,1)S(1)} %get-tuple-element.106), channel_id=1, source_target_pairs={{0,8},{4,12},{8,0},{12,4},{1,9},{5,13},{9,1},{13,5},{2,10},{6,14},... | collective-permute-start | bytes 1327112 | tf_op jit(solution)/shard_map/ppermute | solution.py:120
  58.7 0.6 collective-permute-start.12
  59.4 1.5 %collective-permute-start.19 = (bf16[384,256]{1,0:T(8,128)(2,1)S(1)}, bf16[384,256]{1,0:T(8,128)(2,1)S(1)}, u32[]{:S(2)}, u32[]{:S(2)}) collective-permute-start(bf16[384,256]{1,0:T(8,128)(2,1)S(1)} %get-tuple-element.93), channel_id=1, source_target_pairs={{0,2},{1,3},{2,0},{3,1},{4,6},{5,7},{6,4},{7,5},{8,10},{9,11},{10,... | collective-permute-start | bytes 589832 | tf_op jit(solution)/shard_map/ppermute | solution.py:120
  60.9 10.1 %collective-permute-done.22.got.got_p = bf16[3,192,384]{2,1,0:T(8,128)(2,1)S(1)} collective-permute-done((bf16[3,192,384]{2,1,0:T(8,128)(2,1)S(1)}, bf16[3,192,384]{2,1,0:T(8,128)(2,1)S(1)}, u32[]{:S(2)}, u32[]{:S(2)}) %collective-permute-start.22) | collective-permute-done | bytes 442400 | tf_op jit(solution)/shard_map/ppermute | solution.py:120
  71.1 0.4 collective-permute-start.24
  71.6 11.0 %collective-permute-done.23.got.got_k = bf16[3,192,384]{2,1,0:T(8,128)(2,1)S(1)} collective-permute-done((bf16[3,192,384]{2,1,0:T(8,128)(2,1)S(1)}, bf16[3,192,384]{2,1,0:T(8,128)(2,1)S(1)}, u32[]{:S(2)}, u32[]{:S(2)}) %collective-permute-start.23) | collective-permute-done | bytes 442400 | tf_op jit(solution)/shard_map/ppermute | solution.py:120
  82.7 1.1 %zero_planes.1 = (f32[3,192,384]{2,1,0:T(8,128)}, f32[3,192,384]{2,1,0:T(8,128)}) custom-call(), custom_call_target="tpu_custom_call" | custom-call | tf_op jit(solution)/shard_map/zero_planes/pallas_call | solution.py:397
  83.8 0.7 out.1
  84.5 0.9 second_total.1
  85.4 1.0 %entry.1 = bf16[384,256]{1,0:T(8,128)(2,1)} custom-call(bf16[384,256]{1,0:T(8,128)(2,1)S(1)} %get-tuple-element.87.refs_0_.g_ref.g0, bf16[384,256]{1,0:T(8,128)(2,1)S(1)} %get-tuple-element.62.x0.x_ref, f32[384,256]{1,0:T(8,128)S(1)} %get-tuple-element.92.own_ref, bf16[384,256]{1,0:T(8,128)(2,1)S(1)} %collective-permute-done.19.got_ref), custom_call_target="tpu_custom_call" | custom-call | tf_op jit(solution)/shard_map/entry/pallas_call | solution.py:148
  86.3 2.1 %collective-permute-done.25.got_p = bf16[192,384]{1,0:T(8,128)(2,1)S(1)} collective-permute-done((bf16[192,384]{1,0:T(8,128)(2,1)S(1)}, bf16[192,384]{1,0:T(8,128)(2,1)S(1)}, u32[]{:S(2)}, u32[]{:S(2)}) %collective-permute-start.25) | collective-permute-done | bytes 147488 | tf_op jit(solution)/shard_map/ppermute | solution.py:120
  88.5 0.9 first_total.1
  (26 shorter events, 1.0 us)
Async XLA Ops:
  0.6 8.9 %collective-permute-start = (bf16[384,256]{1,0:T(8,128)(2,1)}, bf16[384,256]{1,0:T(8,128)(2,1)S(1)}, u32[]{:S(2)}, u32[]{:S(2)}) collective-permute-start(bf16[384,256]{1,0:T(8,128)(2,1)} %x_ref.1), channel_id=1, source_target_pairs={{0,2},{1,3},{2,0},{3,1},{4,6},{5,7},{6,4},{7,5},{8,10},{9,11},{10,... | collective-permute-start | bytes 589832 | tf_op jit(solution)/shard_map/ppermute | solution.py:120
  3.6 5.9 %collective-permute-start.1 = (bf16[384,256]{1,0:T(8,128)(2,1)}, bf16[384,256]{1,0:T(8,128)(2,1)S(1)}, u32[]{:S(2)}, u32[]{:S(2)}) collective-permute-start(bf16[384,256]{1,0:T(8,128)(2,1)} %x_ref.1), channel_id=1, source_target_pairs={{0,1},{1,0},{2,3},{3,2},{4,5},{5,4},{6,7},{7,6},{8,9},{9,8},{10,11... | collective-permute-start | bytes 589832 | tf_op jit(solution)/shard_map/ppermute | solution.py:120
  3.6 9.3 %collective-permute-start.3 = (bf16[2,48,1024]{2,1,0:T(8,128)(2,1)}, bf16[2,48,1024]{2,1,0:T(8,128)(2,1)S(1)}, u32[]{:S(2)}, u32[]{:S(2)}) collective-permute-start(bf16[2,48,1024]{2,1,0:T(8,128)(2,1)} %g_ref.1), channel_id=1, source_target_pairs={{0,2},{1,3},{2,0},{3,1},{4,6},{5,7},{6,4},{7,5},{8,10},{9,11},{10,... | collective-permute-start | bytes 589832 | tf_op jit(solution)/shard_map/ppermute | solution.py:120
  9.6 3.4 %collective-permute-start.2 = (bf16[384,256]{1,0:T(8,128)(2,1)S(1)}, bf16[384,256]{1,0:T(8,128)(2,1)S(1)}, u32[]{:S(2)}, u32[]{:S(2)}) collective-permute-start(bf16[384,256]{1,0:T(8,128)(2,1)S(1)} %collective-permute-done.x2), channel_id=1, source_target_pairs={{0,1},{1,0},{2,3},{3,2},{4,5},{5,4},{6,7},{7,6},{8,9},{9,8},{10,11... | collective-permute-start | bytes 589832 | tf_op jit(solution)/shard_map/ppermute | solution.py:120
  14.3 1.8 %collective-permute-start.4 = (bf16[2,384,256]{2,1,0:T(8,128)(2,1)S(1)}, bf16[2,384,256]{2,1,0:T(8,128)(2,1)S(1)}, u32[]{:S(2)}, u32[]{:S(2)}) collective-permute-start(bf16[2,384,256]{2,1,0:T(8,128)(2,1)S(1)} %get-tuple-element.67), channel_id=1, source_target_pairs={{0,1},{1,0},{2,3},{3,2},{4,5},{5,4},{6,7},{7,6},{8,9},{9,8},{10,11... | collective-permute-start | bytes 1179656 | tf_op jit(solution)/shard_map/ppermute | solution.py:120
  16.2 14.1 %collective-permute-start.5 = (bf16[2,384,256]{2,1,0:T(8,128)(2,1)S(1)}, bf16[2,384,256]{2,1,0:T(8,128)(2,1)S(1)}, u32[]{:S(2)}, u32[]{:S(2)}) collective-permute-start(bf16[2,384,256]{2,1,0:T(8,128)(2,1)S(1)} %mix_sum.1.chip_ref), channel_id=1, source_target_pairs={{0,2},{1,3},{2,0},{3,1},{4,6},{5,7},{6,4},{7,5},{8,10},{9,11},{10,... | collective-permute-start | bytes 1179656 | tf_op jit(solution)/shard_map/ppermute | solution.py:120
  18.1 4.7 %collective-permute-start.7 = (bf16[2,2,48,256]{3,2,1,0:T(8,128)(2,1)S(1)}, bf16[2,2,48,256]{3,2,1,0:T(8,128)(2,1)S(1)}, u32[]{:S(2)}, u32[]{:S(2)}) collective-permute-start(bf16[2,2,48,256]{3,2,1,0:T(8,128)(2,1)S(1)} %get-tuple-element.70), channel_id=1, source_target_pairs={{0,4},{4,0},{8,12},{12,8},{1,5},{5,1},{9,13},{13,9},{2,6},{6,2},{1... | collective-permute-start | bytes 294920 | tf_op jit(solution)/shard_map/ppermute | solution.py:120
  19.7 10.4 %collective-permute-start.8 = (bf16[2,2,48,256]{3,2,1,0:T(8,128)(2,1)S(1)}, bf16[2,2,48,256]{3,2,1,0:T(8,128)(2,1)S(1)}, u32[]{:S(2)}, u32[]{:S(2)}) collective-permute-start(bf16[2,2,48,256]{3,2,1,0:T(8,128)(2,1)S(1)} %get-tuple-element.71), channel_id=1, source_target_pairs={{0,8},{4,12},{8,0},{12,4},{1,9},{5,13},{9,1},{13,5},{2,10},{6,14},... | collective-permute-start | bytes 294920 | tf_op jit(solution)/shard_map/ppermute | solution.py:120
  22.3 7.9 %collective-permute-start.9 = (bf16[2,2,48,256]{3,2,1,0:T(8,128)(2,1)S(1)}, bf16[2,2,48,256]{3,2,1,0:T(8,128)(2,1)S(1)}, u32[]{:S(2)}, u32[]{:S(2)}) collective-permute-start(bf16[2,2,48,256]{3,2,1,0:T(8,128)(2,1)S(1)} %get-tuple-element.72), channel_id=1, source_target_pairs={{0,12},{4,8},{8,4},{12,0},{1,13},{5,9},{9,5},{13,1},{2,14},{6,10},... | collective-permute-start | bytes 294920 | tf_op jit(solution)/shard_map/ppermute | solution.py:120
  30.2 1.8 %collective-permute-start.10 = (bf16[2,384,256]{2,1,0:T(8,128)(2,1)S(1)}, bf16[2,384,256]{2,1,0:T(8,128)(2,1)S(1)}, u32[]{:S(2)}, u32[]{:S(2)}) collective-permute-start(bf16[2,384,256]{2,1,0:T(8,128)(2,1)S(1)} %bitcast.5), channel_id=1, source_target_pairs={{0,1},{1,0},{2,3},{3,2},{4,5},{5,4},{6,7},{7,6},{8,9},{9,8},{10,11... | collective-permute-start | bytes 1179656 | tf_op jit(solution)/shard_map/ppermute | solution.py:120
  30.4 2.1 %collective-permute-start.6 = (bf16[2,384,256]{2,1,0:T(8,128)(2,1)S(1)}, bf16[2,384,256]{2,1,0:T(8,128)(2,1)S(1)}, u32[]{:S(2)}, u32[]{:S(2)}) collective-permute-start(bf16[2,384,256]{2,1,0:T(8,128)(2,1)S(1)} %middle.1.a_ref.mid_ref), channel_id=1, source_target_pairs={{0,1},{1,0},{2,3},{3,2},{4,5},{5,4},{6,7},{7,6},{8,9},{9,8},{10,11... | collective-permute-start | bytes 1179656 | tf_op jit(solution)/shard_map/ppermute | solution.py:120
  33.9 1.8 %collective-permute-start.13 = (bf16[2,384,256]{2,1,0:T(8,128)(2,1)S(1)}, bf16[2,384,256]{2,1,0:T(8,128)(2,1)S(1)}, u32[]{:S(2)}, u32[]{:S(2)}) collective-permute-start(bf16[2,384,256]{2,1,0:T(8,128)(2,1)S(1)} %get-tuple-element.80), channel_id=1, source_target_pairs={{0,1},{1,0},{2,3},{3,2},{4,5},{5,4},{6,7},{7,6},{8,9},{9,8},{10,11... | collective-permute-start | bytes 1179656 | tf_op jit(solution)/shard_map/ppermute | solution.py:120
  35.8 7.8 %collective-permute-start.14 = (bf16[384,256]{1,0:T(8,128)(2,1)S(1)}, bf16[384,256]{1,0:T(8,128)(2,1)S(1)}, u32[]{:S(2)}, u32[]{:S(2)}) collective-permute-start(bf16[384,256]{1,0:T(8,128)(2,1)S(1)} %get-tuple-element.85.chip0), channel_id=1, source_target_pairs={{0,2},{1,3},{2,0},{3,1},{4,6},{5,7},{6,4},{7,5},{8,10},{9,11},{10,... | collective-permute-start | bytes 589832 | tf_op jit(solution)/shard_map/ppermute | solution.py:120
  36.4 10.6 %collective-permute-start.15 = (bf16[384,256]{1,0:T(8,128)(2,1)S(1)}, bf16[384,256]{1,0:T(8,128)(2,1)S(1)}, u32[]{:S(2)}, u32[]{:S(2)}) collective-permute-start(bf16[384,256]{1,0:T(8,128)(2,1)S(1)} %get-tuple-element.86.chip1), channel_id=1, source_target_pairs={{0,2},{1,3},{2,0},{3,1},{4,6},{5,7},{6,4},{7,5},{8,10},{9,11},{10,... | collective-permute-start | bytes 589832 | tf_op jit(solution)/shard_map/ppermute | solution.py:120
  37.9 14.7 %collective-permute-start.21 = (bf16[2,192,384]{2,1,0:T(8,128)(2,1)S(1)}, bf16[2,192,384]{2,1,0:T(8,128)(2,1)S(1)}, u32[]{:S(2)}, u32[]{:S(2)}) collective-permute-start(bf16[2,192,384]{2,1,0:T(8,128)(2,1)S(1)} %get-tuple-element.100), channel_id=1, source_target_pairs={{0,4},{4,0},{8,12},{12,8},{1,5},{5,1},{9,13},{13,9},{2,6},{6,2},{1... | collective-permute-start | bytes 884744 | tf_op jit(solution)/shard_map/ppermute | solution.py:120
  39.5 15.5 %collective-permute-start.20 = (bf16[2,192,384]{2,1,0:T(8,128)(2,1)S(1)}, bf16[2,192,384]{2,1,0:T(8,128)(2,1)S(1)}, u32[]{:S(2)}, u32[]{:S(2)}) collective-permute-start(bf16[2,192,384]{2,1,0:T(8,128)(2,1)S(1)} %get-tuple-element.98), channel_id=1, source_target_pairs={{0,8},{4,12},{8,0},{12,4},{1,9},{5,13},{9,1},{13,5},{2,10},{6,14},... | collective-permute-start | bytes 884744 | tf_op jit(solution)/shard_map/ppermute | solution.py:120
  47.7 1.5 %collective-permute-start.16 = (bf16[384,256]{1,0:T(8,128)(2,1)S(1)}, bf16[384,256]{1,0:T(8,128)(2,1)S(1)}, u32[]{:S(2)}, u32[]{:S(2)}) collective-permute-start(bf16[384,256]{1,0:T(8,128)(2,1)S(1)} %get-tuple-element.87.refs_0_.g_ref.g0), channel_id=1, source_target_pairs={{0,1},{1,0},{2,3},{3,2},{4,5},{5,4},{6,7},{7,6},{8,9},{9,8},{10,11... | collective-permute-start | bytes 589832 | tf_op jit(solution)/shard_map/ppermute | solution.py:120
  47.8 1.7 %collective-permute-start.17 = (bf16[384,256]{1,0:T(8,128)(2,1)S(1)}, bf16[384,256]{1,0:T(8,128)(2,1)S(1)}, u32[]{:S(2)}, u32[]{:S(2)}) collective-permute-start(bf16[384,256]{1,0:T(8,128)(2,1)S(1)} %get-tuple-element.88.refs_2_.g2), channel_id=1, source_target_pairs={{0,1},{1,0},{2,3},{3,2},{4,5},{5,4},{6,7},{7,6},{8,9},{9,8},{10,11... | collective-permute-start | bytes 589832 | tf_op jit(solution)/shard_map/ppermute | solution.py:120
  48.3 10.4 %collective-permute-start.11 = (bf16[2,384,256]{2,1,0:T(8,128)(2,1)S(1)}, bf16[2,384,256]{2,1,0:T(8,128)(2,1)S(1)}, u32[]{:S(2)}, u32[]{:S(2)}) collective-permute-start(bf16[2,384,256]{2,1,0:T(8,128)(2,1)S(1)} %get-tuple-element.76), channel_id=1, source_target_pairs={{0,1},{1,0},{2,3},{3,2},{4,5},{5,4},{6,7},{7,6},{8,9},{9,8},{10,11... | collective-permute-start | bytes 1179656 | tf_op jit(solution)/shard_map/ppermute | solution.py:120
  55.5 15.6 %collective-permute-start.22 = (bf16[3,192,384]{2,1,0:T(8,128)(2,1)S(1)}, bf16[3,192,384]{2,1,0:T(8,128)(2,1)S(1)}, u32[]{:S(2)}, u32[]{:S(2)}) collective-permute-start(bf16[3,192,384]{2,1,0:T(8,128)(2,1)S(1)} %get-tuple-element.103), channel_id=1, source_target_pairs={{0,4},{4,0},{8,12},{12,8},{1,5},{5,1},{9,13},{13,9},{2,6},{6,2},{1... | collective-permute-start | bytes 1327112 | tf_op jit(solution)/shard_map/ppermute | solution.py:120
  56.0 3.4 %collective-permute-start.18 = (bf16[2,384,256]{2,1,0:T(8,128)(2,1)S(1)}, bf16[2,384,256]{2,1,0:T(8,128)(2,1)S(1)}, u32[]{:S(2)}, u32[]{:S(2)}) collective-permute-start(bf16[2,384,256]{2,1,0:T(8,128)(2,1)S(1)} %get-tuple-element.91), channel_id=1, source_target_pairs={{0,1},{1,0},{2,3},{3,2},{4,5},{5,4},{6,7},{7,6},{8,9},{9,8},{10,11... | collective-permute-start | bytes 1179656 | tf_op jit(solution)/shard_map/ppermute | solution.py:120
  56.0 26.5 %collective-permute-start.23 = (bf16[3,192,384]{2,1,0:T(8,128)(2,1)S(1)}, bf16[3,192,384]{2,1,0:T(8,128)(2,1)S(1)}, u32[]{:S(2)}, u32[]{:S(2)}) collective-permute-start(bf16[3,192,384]{2,1,0:T(8,128)(2,1)S(1)} %get-tuple-element.106), channel_id=1, source_target_pairs={{0,8},{4,12},{8,0},{12,4},{1,9},{5,13},{9,1},{13,5},{2,10},{6,14},... | collective-permute-start | bytes 1327112 | tf_op jit(solution)/shard_map/ppermute | solution.py:120
  58.7 25.0 %collective-permute-start.12 = (bf16[384,256]{1,0:T(8,128)(2,1)S(1)}, bf16[384,256]{1,0:T(8,128)(2,1)S(1)}, u32[]{:S(2)}, u32[]{:S(2)}) collective-permute-start(bf16[384,256]{1,0:T(8,128)(2,1)S(1)} %get-tuple-element.78), channel_id=1, source_target_pairs={{0,2},{1,3},{2,0},{3,1},{4,6},{5,7},{6,4},{7,5},{8,10},{9,11},{10,... | collective-permute-start | bytes 589832 | tf_op jit(solution)/shard_map/ppermute | solution.py:120
  59.4 25.9 %collective-permute-start.19 = (bf16[384,256]{1,0:T(8,128)(2,1)S(1)}, bf16[384,256]{1,0:T(8,128)(2,1)S(1)}, u32[]{:S(2)}, u32[]{:S(2)}) collective-permute-start(bf16[384,256]{1,0:T(8,128)(2,1)S(1)} %get-tuple-element.93), channel_id=1, source_target_pairs={{0,2},{1,3},{2,0},{3,1},{4,6},{5,7},{6,4},{7,5},{8,10},{9,11},{10,... | collective-permute-start | bytes 589832 | tf_op jit(solution)/shard_map/ppermute | solution.py:120
  71.1 15.2 %collective-permute-start.24 = (bf16[192,384]{1,0:T(8,128)(2,1)S(1)}, bf16[192,384]{1,0:T(8,128)(2,1)S(1)}, u32[]{:S(2)}, u32[]{:S(2)}) collective-permute-start(bf16[192,384]{1,0:T(8,128)(2,1)S(1)} %get-tuple-element.108), channel_id=1, source_target_pairs={{0,8},{4,12},{8,0},{12,4},{1,9},{5,13},{9,1},{13,5},{2,10},{6,14},... | collective-permute-start | bytes 442376 | tf_op jit(solution)/shard_map/ppermute | solution.py:120
  82.6 5.9 %collective-permute-start.25 = (bf16[192,384]{1,0:T(8,128)(2,1)S(1)}, bf16[192,384]{1,0:T(8,128)(2,1)S(1)}, u32[]{:S(2)}, u32[]{:S(2)}) collective-permute-start(bf16[192,384]{1,0:T(8,128)(2,1)S(1)} %get-tuple-element.109), channel_id=1, source_target_pairs={{0,4},{4,0},{8,12},{12,8},{1,5},{5,1},{9,13},{13,9},{2,6},{6,2},{1... | collective-permute-start | bytes 442376 | tf_op jit(solution)/shard_map/ppermute | solution.py:120

commit v7 on v6

--- a/solution.py
+++ b/solution.py
@@ -342,11 +342,12 @@
         send[2] = half_sum(keep_b, got_b, own)
         proj_pieces(v_ref, g_ref, keep, send)
 
-    def first_taps_body(z_ref, gu_ref, keep_b, got_b, _, keep, send, own):
+    def first_taps_body(z_ref, gu_ref, keep_b, got_b, keep, send, own):
         send[2] = half_sum(keep_b, got_b, own)
         taps_pieces(z_ref, gu_ref, keep, send)
 
-    def half_body(keep, got, own, send):
+    def half_body(keep, got, *rest):
+        own, send = rest[-2:]
         send[...] = half_sum(keep, got, own)
 
     plane = ((3, hid, rows), F32)
@@ -414,23 +415,22 @@
     )
     got = swap(send, "mp", 1)
 
-    def squash_body(keep_ref, got_ref, _, *outs):
+    def squash_body(keep_ref, got_ref, _, out_ref):
+        mix_body(keep_ref, got_ref, out_ref)
+
+    (chip,) = call(squash_body, [((2, rows, bins), BF16)], (keep, got, keep_b[0]), "squash_sum")
+    other = swap(chip, "mp", 2)
+    got_b = swap(send_k, "ctx", 1), swap(send_p, "ctx", 2)
+
+    def back_body(g_ref, mid_ref, chip_ref, other_ref, *outs):
         for i in (0, 1):
-            outs[i][...] = (keep_ref[i] + got_ref[i].astype(F32)).astype(BF16)
-
-    chip = call(squash_body, [((rows, bins), BF16)] * 2, (keep, got, keep_b[0]), "squash_sum")
-    other = [swap(part, "mp", 2) for part in chip]
-    got_b = swap(send_k, "ctx", 1), swap(send_p, "ctx", 2)
-
-    def back_body(g_ref, mid_ref, chip0, chip1, other0, other1, *outs):
-        for i, (chip_ref, other_ref) in enumerate(((chip0, other1), (chip1, other0))):
-            grad = chip_ref[...].astype(F32) + other_ref[...].astype(F32)
+            grad = chip_ref[i].astype(F32) + other_ref[1 - i].astype(F32)
             outs[i][...] = (
                 g_ref[i].astype(F32) + grad * slope_of(mid_ref[i].astype(F32))
             ).astype(BF16)
 
     g_mid = call(
-        back_body, [((rows, bins), BF16)] * 2, (g_pair, mid, *chip, *other), "middle_grad"
+        back_body, [((rows, bins), BF16)] * 2, (g_pair, mid, chip, other), "middle_grad"
     )
     g_mid = [g_mid[0], swap(g_mid[0], "mp", 1), g_mid[1], swap(g_mid[1], "mp", 1)]
 
@@ -484,7 +484,7 @@
     keep_ak, send_k, own_bp = call(
         first_taps_body,
         [(two, F32), (three, BF16), (one, F32)],
-        (z_a, gu_a, keep_b[1], got_b[1], own_bk),
+        (z_a, gu_a, keep_b[1], got_b[1]),
         "first_taps",
     )
     got_k = swap(send_k, "ctx", 1)
@@ -501,10 +501,10 @@
     (entry,) = call(entry_body, [((rows, bins), BF16)], (g_mid[0], x_own, e_own, e_got), "entry", final=True)
 
     half = [(one, F32), (one[1:], BF16)]
-    own_ak, send_k = call(half_body, half, (keep_ak, got_k), "taps_half")
-    last_k = swap(send_k, "ctx", 2)
     own_ap, send_p = call(half_body, half, (keep_ap, got_p), "proj_half")
     last_p = swap(send_p, "ctx", 1)
+    own_ak, send_k = call(half_body, half, (keep_ak, got_k, own_ap), "taps_half")
+    last_k = swap(send_k, "ctx", 2)
     taps_b_grad, point_b_grad = total(2, planes[0], own_bk, own_bp, got_p, got_k, "second_total")
     taps_a_grad, point_a_grad = total(Ellipsis, planes[1], own_ak, own_ap, last_k, last_p, "first_total")
     return second_out, entry, taps_a_grad, point_a_grad, taps_b_grad, point_b_grad

time: 89.5 us -> 84.2 us (0.941)
  waiting for transfers between devices: 53.5 us -> 48.1 us
    ppermute x26 -> x25, waiting for transfers between devices: 53.5 us -> 48.1 us  [swap(): return lax.ppermute(value, axis, [(i, i ^ bits) for i in range(size)])]
    ppermute x26 -> x25, starting transfers between devices: 21.9 us -> 22.1 us  [swap(): return lax.ppermute(value, axis, [(i, i ^ bits) for i in range(size)])]
  transfers between devices with their start and end apart: 26 -> 25, of which waited for: 17 -> 15; matrix products, arithmetic and copies ran while one was open for 0% -> 0% of each run, Pallas kernels for 10% -> 11%
where the time goes in v7:
time: 84.2 us; the launch traced here: 84 us
  waiting for transfers between devices  48.1 us (57%)
  starting transfers between devices  22.1 us (26%)
  Pallas kernels  13.1 us (16%)
    ppermute x25, waiting for transfers between devices, swap(): return lax.ppermute(value, axis, [(i, i ^ bits) for i in range(size)])  48.1 us
    ppermute x25, starting transfers between devices, swap(): return lax.ppermute(value, axis, [(i, i ^ bits) for i in range(size)])  22.1 us
    pallas_call x18, Pallas kernels, call(): pl.pallas_call(body, out_shape=[struct(s, d) for s, d in outs], in_specs=...  8.5 us
    pallas_call x1, Pallas kernels, fast_shards(): pl.pallas_call(load_body, out_shape=[pltpu.VMEM((rows, bins), BF16)] + [p...  1.79 us
    pallas_call x2, Pallas kernels, total(): pl.pallas_call(functools.partial(total_body, place), out_shape=[jax.Shape...  1.71 us
  transfers between devices with their start and end apart: 25, of which 15 were waited for; matrix products, arithmetic and copies ran while one was open for 0% of the time, Pallas kernels for 11%

profile of v7, /device:TPU:0, one launch (start us, length us, event | category | flops | bytes accessed | tf_op | source)
XLA Modules:
  0.0 84.0 jit_solution(12265128453337595749)
XLA Ops:
  0.6 3.0 %collective-permute-start = (bf16[384,256]{1,0:T(8,128)(2,1)}, bf16[384,256]{1,0:T(8,128)(2,1)S(1)}, u32[]{:S(2)}, u32[]{:S(2)}) collective-permute-start(bf16[384,256]{1,0:T(8,128)(2,1)} %x_ref.1), channel_id=1, source_target_pairs={{0,2},{1,3},{2,0},{3,1},{4,6},{5,7},{6,4},{7,5},{8,10},{9,11},{10,... | collective-permute-start | bytes 589832 | tf_op jit(solution)/shard_map/ppermute | solution.py:120
  3.6 0.2 collective-permute-start.3
  3.8 1.8 %load.1 = (bf16[384,256]{1,0:T(8,128)(2,1)S(1)}, bf16[192,1536]{1,0:T(8,128)(2,1)S(1)}, bf16[192,1536]{1,0:T(8,128)(2,1)S(1)}, bf16[192,1536]{1,0:T(8,128)(2,1)S...) custom-call(bf16[384,256]{1,0:T(8,128)(2,1)} %x_ref.1, bf16[3,192,1536]{2,1,0:T(8,128)(2,1)} %ta.1, ...), custom_call_target="tpu_custom_call" | custom-call | tf_op jit(solution)/shard_map/load/pallas_call | solution.py:183
  5.6 4.0 %collective-permute-done.x2 = bf16[384,256]{1,0:T(8,128)(2,1)S(1)} collective-permute-done((bf16[384,256]{1,0:T(8,128)(2,1)}, bf16[384,256]{1,0:T(8,128)(2,1)S(1)}, u32[]{:S(2)}, u32[]{:S(2)}) %collective-permute-start) | collective-permute-done | bytes 196640 | tf_op jit(solution)/shard_map/ppermute | solution.py:120
  9.6 3.4 %collective-permute-done.3._.far_ref = bf16[2,48,1024]{2,1,0:T(8,128)(2,1)S(1)} collective-permute-done((bf16[2,48,1024]{2,1,0:T(8,128)(2,1)}, bf16[2,48,1024]{2,1,0:T(8,128)(2,1)S(1)}, u32[]{:S(2)}, u32[]{:S(2)}) %collective-permute-start.3) | collective-permute-done | bytes 196640 | tf_op jit(solution)/shard_map/ppermute | solution.py:120
  13.0 1.4 %first_forward.1 = (bf16[4,384,256]{2,1,0:T(8,128)(2,1)S(1)}, bf16[192,256]{1,0:T(8,128)(2,1)S(1)}, f32[192,256]{1,0:T(8,128)S(1)}, f32[2,384,256]{2,1,0:T(8,128)S(1)}, bf16[2,384,256]{2,1,0:T(8,128)(2,1)S(1)}) custom-call(bf16[384,256]{1,0:T(8,128)(2,1)S(1)} %get-tuple-element.60.x0.x_ref, bf16[384,256]{1,0:T(8,128)(2,1)S(1)} %collective-permute-done.1.x1, ...), custom_call_target="tpu_custom_call" | custom-call | tf_op jit(solution)/shard_map/first_forward/pallas_call | solution.py:148
  14.4 1.7 %collective-permute-done.4.got_ref = bf16[2,384,256]{2,1,0:T(8,128)(2,1)S(1)} collective-permute-done((bf16[2,384,256]{2,1,0:T(8,128)(2,1)S(1)}, bf16[2,384,256]{2,1,0:T(8,128)(2,1)S(1)}, u32[]{:S(2)}, u32[]{:S(2)}) %collective-permute-start.4) | collective-permute-done | bytes 393248 | tf_op jit(solution)/shard_map/ppermute | solution.py:120
  16.2 1.8 %collective-permute-start.5 = (bf16[2,384,256]{2,1,0:T(8,128)(2,1)S(1)}, bf16[2,384,256]{2,1,0:T(8,128)(2,1)S(1)}, u32[]{:S(2)}, u32[]{:S(2)}) collective-permute-start(bf16[2,384,256]{2,1,0:T(8,128)(2,1)S(1)} %mix_sum.1.chip_ref), channel_id=1, source_target_pairs={{0,2},{1,3},{2,0},{3,1},{4,6},{5,7},{6,4},{7,5},{8,10},{9,11},{10,... | collective-permute-start | bytes 1179656 | tf_op jit(solution)/shard_map/ppermute | solution.py:120
  18.1 1.6 %collective-permute-start.7 = (bf16[2,2,48,256]{3,2,1,0:T(8,128)(2,1)S(1)}, bf16[2,2,48,256]{3,2,1,0:T(8,128)(2,1)S(1)}, u32[]{:S(2)}, u32[]{:S(2)}) collective-permute-start(bf16[2,2,48,256]{3,2,1,0:T(8,128)(2,1)S(1)} %get-tuple-element.68), channel_id=1, source_target_pairs={{0,4},{4,0},{8,12},{12,8},{1,5},{5,1},{9,13},{13,9},{2,6},{6,2},{1... | collective-permute-start | bytes 294920 | tf_op jit(solution)/shard_map/ppermute | solution.py:120
  19.7 2.6 %collective-permute-start.8 = (bf16[2,2,48,256]{3,2,1,0:T(8,128)(2,1)S(1)}, bf16[2,2,48,256]{3,2,1,0:T(8,128)(2,1)S(1)}, u32[]{:S(2)}, u32[]{:S(2)}) collective-permute-start(bf16[2,2,48,256]{3,2,1,0:T(8,128)(2,1)S(1)} %get-tuple-element.69), channel_id=1, source_target_pairs={{0,8},{4,12},{8,0},{12,4},{1,9},{5,13},{9,1},{13,5},{2,10},{6,14},... | collective-permute-start | bytes 294920 | tf_op jit(solution)/shard_map/ppermute | solution.py:120
  22.3 0.2 collective-permute-start.9
  22.5 0.2 collective-permute-done.7.refs_1_
  22.7 7.4 %collective-permute-done.8.refs_2_ = bf16[2,2,48,256]{3,2,1,0:T(8,128)(2,1)S(1)} collective-permute-done((bf16[2,2,48,256]{3,2,1,0:T(8,128)(2,1)S(1)}, bf16[2,2,48,256]{3,2,1,0:T(8,128)(2,1)S(1)}, u32[]{:S(2)}, u32[]{:S(2)}) %collective-permute-start.8) | collective-permute-done | bytes 98336 | tf_op jit(solution)/shard_map/ppermute | solution.py:120
  30.3 0.1 middle.1.a_ref.mid_ref
  30.4 0.5 collective-permute-start.6
  31.0 1.0 %collective-permute-done.10.gb_ref = bf16[2,384,256]{2,1,0:T(8,128)(2,1)S(1)} collective-permute-done((bf16[2,384,256]{2,1,0:T(8,128)(2,1)S(1)}, bf16[2,384,256]{2,1,0:T(8,128)(2,1)S(1)}, u32[]{:S(2)}, u32[]{:S(2)}) %collective-permute-start.10) | collective-permute-done | bytes 393248 | tf_op jit(solution)/shard_map/ppermute | solution.py:120
  32.0 0.6 collective-permute-done.6.b_ref
  32.5 1.4 %second_block.1 = (bf16[4,384,256]{2,1,0:T(8,128)(2,1)S(1)}, bf16[192,256]{1,0:T(8,128)(2,1)S(1)}, bf16[192,256]{1,0:T(8,128)(2,1)S(1)}, f32[2,384,256]{2,1,0:T(...) custom-call(bf16[2,384,256]{2,1,0:T(8,128)(2,1)S(1)} %middle.1.a_ref.mid_, ...), custom_call_target="tpu_custom_call" | custom-call | tf_op jit(solution)/shard_map/second_block/pallas_call | solution.py:148
  33.9 0.2 collective-permute-start.13
  34.2 0.7 second_weights.1
  34.9 0.8 collective-permute-done.13.got_ref
  35.8 0.6 collective-permute-start.14
  36.4 1.6 %collective-permute-start.21 = (bf16[2,192,384]{2,1,0:T(8,128)(2,1)S(1)}, bf16[2,192,384]{2,1,0:T(8,128)(2,1)S(1)}, u32[]{:S(2)}, u32[]{:S(2)}) collective-permute-start(bf16[2,192,384]{2,1,0:T(8,128)(2,1)S(1)} %get-tuple-element.98), channel_id=1, source_target_pairs={{0,4},{4,0},{8,12},{12,8},{1,5},{5,1},{9,13},{13,9},{2,6},{6,2},{1... | collective-permute-start | bytes 884744 | tf_op jit(solution)/shard_map/ppermute | solution.py:120
  38.0 1.4 %collective-permute-start.19 = (bf16[2,192,384]{2,1,0:T(8,128)(2,1)S(1)}, bf16[2,192,384]{2,1,0:T(8,128)(2,1)S(1)}, u32[]{:S(2)}, u32[]{:S(2)}) collective-permute-start(bf16[2,192,384]{2,1,0:T(8,128)(2,1)S(1)} %get-tuple-element.94), channel_id=1, source_target_pairs={{0,8},{4,12},{8,0},{12,4},{1,9},{5,13},{9,1},{13,5},{2,10},{6,14},... | collective-permute-start | bytes 884744 | tf_op jit(solution)/shard_map/ppermute | solution.py:120
  39.4 7.6 %collective-permute-done.14.other_ref = bf16[2,384,256]{2,1,0:T(8,128)(2,1)S(1)} collective-permute-done((bf16[2,384,256]{2,1,0:T(8,128)(2,1)S(1)}, bf16[2,384,256]{2,1,0:T(8,128)(2,1)S(1)}, u32[]{:S(2)}, u32[]{:S(2)}) %collective-permute-start.14) | collective-permute-done | bytes 393248 | tf_op jit(solution)/shard_map/ppermute | solution.py:120
  47.1 0.6 middle_grad.1
  47.8 0.5 collective-permute-start.16
  48.3 0.9 %collective-permute-done.15.refs_1_.g1 = bf16[384,256]{1,0:T(8,128)(2,1)S(1)} collective-permute-done((bf16[384,256]{1,0:T(8,128)(2,1)S(1)}, bf16[384,256]{1,0:T(8,128)(2,1)S(1)}, u32[]{:S(2)}, u32[]{:S(2)}) %collective-permute-start.15) | collective-permute-done | bytes 196640 | tf_op jit(solution)/shard_map/ppermute | solution.py:120
  49.2 0.3 collective-permute-done.16.refs_3_.g3
  49.5 1.1 %first_backward.1 = (bf16[192,256]{1,0:T(8,128)(2,1)S(1)}, f32[2,384,256]{2,1,0:T(8,128)S(1)}, bf16[2,384,256]{2,1,0:T(8,128)(2,1)S(1)}) custom-call(bf16[384,256]{1,0:T(8,128)(2,1)S(1)} %get-tuple-element.83.refs_0_.g_ref.g0, bf16[384,256]{1,0:T(8,128)(2,1)S(1)} %collective-permute-done.15.refs_1_.g1, bf16[384,256]{1,0:T(8,128)(2,1)S(1)} %get-tuple-element.84.refs_2_.g2, ...), custom_call_target="tpu_custom_call" | custom-call | tf_op jit(solution)/shard_map/first_backward/pallas_call | solution.py:148
  50.6 0.3 collective-permute-start.17
  50.8 0.6 collective-permute-done.21.got_b
  51.4 0.5 first_proj.1
  51.9 2.1 %collective-permute-start.22 = (bf16[3,192,384]{2,1,0:T(8,128)(2,1)S(1)}, bf16[3,192,384]{2,1,0:T(8,128)(2,1)S(1)}, u32[]{:S(2)}, u32[]{:S(2)}) collective-permute-start(bf16[3,192,384]{2,1,0:T(8,128)(2,1)S(1)} %get-tuple-element.100), channel_id=1, source_target_pairs={{0,8},{4,12},{8,0},{12,4},{1,9},{5,13},{9,1},{13,5},{2,10},{6,14},... | collective-permute-start | bytes 1327112 | tf_op jit(solution)/shard_map/ppermute | solution.py:120
  54.1 0.5 first_taps.1
  54.5 0.5 collective-permute-start.20
  55.1 1.3 %collective-permute-start.12 = (bf16[384,256]{1,0:T(8,128)(2,1)S(1)}, bf16[384,256]{1,0:T(8,128)(2,1)S(1)}, u32[]{:S(2)}, u32[]{:S(2)}) collective-permute-start(bf16[384,256]{1,0:T(8,128)(2,1)S(1)} %get-tuple-element.76), channel_id=1, source_target_pairs={{0,2},{1,3},{2,0},{3,1},{4,6},{5,7},{6,4},{7,5},{8,10},{9,11},{10,... | collective-permute-start | bytes 589832 | tf_op jit(solution)/shard_map/ppermute | solution.py:120
  56.5 0.8 collective-permute-start.18
  57.3 17.0 %collective-permute-done.22.got.got_k = bf16[3,192,384]{2,1,0:T(8,128)(2,1)S(1)} collective-permute-done((bf16[3,192,384]{2,1,0:T(8,128)(2,1)S(1)}, bf16[3,192,384]{2,1,0:T(8,128)(2,1)S(1)}, u32[]{:S(2)}, u32[]{:S(2)}) %collective-permute-start.22) | collective-permute-done | bytes 442400 | tf_op jit(solution)/shard_map/ppermute | solution.py:120
  74.3 0.7 collective-permute-done.20.got.got_p
  75.0 0.9 %collective-permute-start.23 = (bf16[192,384]{1,0:T(8,128)(2,1)S(1)}, bf16[192,384]{1,0:T(8,128)(2,1)S(1)}, u32[]{:S(2)}, u32[]{:S(2)}) collective-permute-start(bf16[192,384]{1,0:T(8,128)(2,1)S(1)} %get-tuple-element.103), channel_id=1, source_target_pairs={{0,8},{4,12},{8,0},{12,4},{1,9},{5,13},{9,1},{13,5},{2,10},{6,14},... | collective-permute-start | bytes 442376 | tf_op jit(solution)/shard_map/ppermute | solution.py:120
  76.0 1.4 %collective-permute-start.24 = (bf16[192,384]{1,0:T(8,128)(2,1)S(1)}, bf16[192,384]{1,0:T(8,128)(2,1)S(1)}, u32[]{:S(2)}, u32[]{:S(2)}) collective-permute-start(bf16[192,384]{1,0:T(8,128)(2,1)S(1)} %get-tuple-element.104), channel_id=1, source_target_pairs={{0,4},{4,0},{8,12},{12,8},{1,5},{5,1},{9,13},{13,9},{2,6},{6,2},{1... | collective-permute-start | bytes 442376 | tf_op jit(solution)/shard_map/ppermute | solution.py:120
  77.4 1.1 %zero_planes.1 = (f32[3,192,384]{2,1,0:T(8,128)}, f32[3,192,384]{2,1,0:T(8,128)}) custom-call(), custom_call_target="tpu_custom_call" | custom-call | tf_op jit(solution)/shard_map/zero_planes/pallas_call | solution.py:398
  78.5 0.7 out.1
  79.2 0.9 %second_total.1 = (f32[3,192,384]{2,1,0:T(8,128)}, f32[192,384]{1,0:T(8,128)}) custom-call(f32[3,192,384]{2,1,0:T(8,128)} %get-tuple-element.107._, f32[1,192,384]{2,1,0:T(8,128)S(1)} %get-tuple-element.108.own_k, f32[1,192,384]{2,1,0:T(8,128)S(1)} %get-tuple-element.109.own_p, ...), custom_call_target="tpu_custom_call", output_to_operand_aliasing={{0}: (0, {})} | custom-call | tf_op jit(solution)/shard_map/second_total/pallas_call | solution.py:380
  80.1 1.0 %entry.1 = bf16[384,256]{1,0:T(8,128)(2,1)} custom-call(bf16[384,256]{1,0:T(8,128)(2,1)S(1)} %get-tuple-element.83.refs_0_.g_ref.g0, bf16[384,256]{1,0:T(8,128)(2,1)S(1)} %get-tuple-element.60.x0.x_ref, f32[384,256]{1,0:T(8,128)S(1)} %get-tuple-element.88.own_ref, bf16[384,256]{1,0:T(8,128)(2,1)S(1)} %collective-permute-done.18.got_ref), custom_call_target="tpu_custom_call" | custom-call | tf_op jit(solution)/shard_map/entry/pallas_call | solution.py:148
  81.1 2.1 %collective-permute-done.23.got_k = bf16[192,384]{1,0:T(8,128)(2,1)S(1)} collective-permute-done((bf16[192,384]{1,0:T(8,128)(2,1)S(1)}, bf16[192,384]{1,0:T(8,128)(2,1)S(1)}, u32[]{:S(2)}, u32[]{:S(2)}) %collective-permute-start.23) | collective-permute-done | bytes 147488 | tf_op jit(solution)/shard_map/ppermute | solution.py:120
  83.2 0.9 %first_total.1 = (f32[3,192,384]{2,1,0:T(8,128)}, f32[192,384]{1,0:T(8,128)}) custom-call(f32[3,192,384]{2,1,0:T(8,128)} %get-tuple-element.90._, f32[1,192,384]{2,1,0:T(8,128)S(1)} %get-tuple-element.102.own_k, f32[1,192,384]{2,1,0:T(8,128)S(1)} %get-tuple-element.101.rest_0_.own_p, ...), custom_call_target="tpu_custom_call", output_to_operand_aliasing={{0}: (0, {})} | custom-call | tf_op jit(solution)/shard_map/first_total/pallas_call | solution.py:380
  (24 shorter events, 0.8 us)
Async XLA Ops:
  0.6 8.9 %collective-permute-start = (bf16[384,256]{1,0:T(8,128)(2,1)}, bf16[384,256]{1,0:T(8,128)(2,1)S(1)}, u32[]{:S(2)}, u32[]{:S(2)}) collective-permute-start(bf16[384,256]{1,0:T(8,128)(2,1)} %x_ref.1), channel_id=1, source_target_pairs={{0,2},{1,3},{2,0},{3,1},{4,6},{5,7},{6,4},{7,5},{8,10},{9,11},{10,... | collective-permute-start | bytes 589832 | tf_op jit(solution)/shard_map/ppermute | solution.py:120
  3.6 5.9 %collective-permute-start.1 = (bf16[384,256]{1,0:T(8,128)(2,1)}, bf16[384,256]{1,0:T(8,128)(2,1)S(1)}, u32[]{:S(2)}, u32[]{:S(2)}) collective-permute-start(bf16[384,256]{1,0:T(8,128)(2,1)} %x_ref.1), channel_id=1, source_target_pairs={{0,1},{1,0},{2,3},{3,2},{4,5},{5,4},{6,7},{7,6},{8,9},{9,8},{10,11... | collective-permute-start | bytes 589832 | tf_op jit(solution)/shard_map/ppermute | solution.py:120
  3.6 9.3 %collective-permute-start.3 = (bf16[2,48,1024]{2,1,0:T(8,128)(2,1)}, bf16[2,48,1024]{2,1,0:T(8,128)(2,1)S(1)}, u32[]{:S(2)}, u32[]{:S(2)}) collective-permute-start(bf16[2,48,1024]{2,1,0:T(8,128)(2,1)} %g_ref.1), channel_id=1, source_target_pairs={{0,2},{1,3},{2,0},{3,1},{4,6},{5,7},{6,4},{7,5},{8,10},{9,11},{10,... | collective-permute-start | bytes 589832 | tf_op jit(solution)/shard_map/ppermute | solution.py:120
  9.6 3.4 %collective-permute-start.2 = (bf16[384,256]{1,0:T(8,128)(2,1)S(1)}, bf16[384,256]{1,0:T(8,128)(2,1)S(1)}, u32[]{:S(2)}, u32[]{:S(2)}) collective-permute-start(bf16[384,256]{1,0:T(8,128)(2,1)S(1)} %collective-permute-done.x2), channel_id=1, source_target_pairs={{0,1},{1,0},{2,3},{3,2},{4,5},{5,4},{6,7},{7,6},{8,9},{9,8},{10,11... | collective-permute-start | bytes 589832 | tf_op jit(solution)/shard_map/ppermute | solution.py:120
  14.3 1.8 %collective-permute-start.4 = (bf16[2,384,256]{2,1,0:T(8,128)(2,1)S(1)}, bf16[2,384,256]{2,1,0:T(8,128)(2,1)S(1)}, u32[]{:S(2)}, u32[]{:S(2)}) collective-permute-start(bf16[2,384,256]{2,1,0:T(8,128)(2,1)S(1)} %get-tuple-element.65), channel_id=1, source_target_pairs={{0,1},{1,0},{2,3},{3,2},{4,5},{5,4},{6,7},{7,6},{8,9},{9,8},{10,11... | collective-permute-start | bytes 1179656 | tf_op jit(solution)/shard_map/ppermute | solution.py:120
  16.2 14.1 %collective-permute-start.5 = (bf16[2,384,256]{2,1,0:T(8,128)(2,1)S(1)}, bf16[2,384,256]{2,1,0:T(8,128)(2,1)S(1)}, u32[]{:S(2)}, u32[]{:S(2)}) collective-permute-start(bf16[2,384,256]{2,1,0:T(8,128)(2,1)S(1)} %mix_sum.1.chip_ref), channel_id=1, source_target_pairs={{0,2},{1,3},{2,0},{3,1},{4,6},{5,7},{6,4},{7,5},{8,10},{9,11},{10,... | collective-permute-start | bytes 1179656 | tf_op jit(solution)/shard_map/ppermute | solution.py:120
  18.1 4.7 %collective-permute-start.7 = (bf16[2,2,48,256]{3,2,1,0:T(8,128)(2,1)S(1)}, bf16[2,2,48,256]{3,2,1,0:T(8,128)(2,1)S(1)}, u32[]{:S(2)}, u32[]{:S(2)}) collective-permute-start(bf16[2,2,48,256]{3,2,1,0:T(8,128)(2,1)S(1)} %get-tuple-element.68), channel_id=1, source_target_pairs={{0,4},{4,0},{8,12},{12,8},{1,5},{5,1},{9,13},{13,9},{2,6},{6,2},{1... | collective-permute-start | bytes 294920 | tf_op jit(solution)/shard_map/ppermute | solution.py:120
  19.7 10.4 %collective-permute-start.8 = (bf16[2,2,48,256]{3,2,1,0:T(8,128)(2,1)S(1)}, bf16[2,2,48,256]{3,2,1,0:T(8,128)(2,1)S(1)}, u32[]{:S(2)}, u32[]{:S(2)}) collective-permute-start(bf16[2,2,48,256]{3,2,1,0:T(8,128)(2,1)S(1)} %get-tuple-element.69), channel_id=1, source_target_pairs={{0,8},{4,12},{8,0},{12,4},{1,9},{5,13},{9,1},{13,5},{2,10},{6,14},... | collective-permute-start | bytes 294920 | tf_op jit(solution)/shard_map/ppermute | solution.py:120
  22.3 7.9 %collective-permute-start.9 = (bf16[2,2,48,256]{3,2,1,0:T(8,128)(2,1)S(1)}, bf16[2,2,48,256]{3,2,1,0:T(8,128)(2,1)S(1)}, u32[]{:S(2)}, u32[]{:S(2)}) collective-permute-start(bf16[2,2,48,256]{3,2,1,0:T(8,128)(2,1)S(1)} %get-tuple-element.70), channel_id=1, source_target_pairs={{0,12},{4,8},{8,4},{12,0},{1,13},{5,9},{9,5},{13,1},{2,14},{6,10},... | collective-permute-start | bytes 294920 | tf_op jit(solution)/shard_map/ppermute | solution.py:120
  30.2 1.8 %collective-permute-start.10 = (bf16[2,384,256]{2,1,0:T(8,128)(2,1)S(1)}, bf16[2,384,256]{2,1,0:T(8,128)(2,1)S(1)}, u32[]{:S(2)}, u32[]{:S(2)}) collective-permute-start(bf16[2,384,256]{2,1,0:T(8,128)(2,1)S(1)} %bitcast.5), channel_id=1, source_target_pairs={{0,1},{1,0},{2,3},{3,2},{4,5},{5,4},{6,7},{7,6},{8,9},{9,8},{10,11... | collective-permute-start | bytes 1179656 | tf_op jit(solution)/shard_map/ppermute | solution.py:120
  30.4 2.1 %collective-permute-start.6 = (bf16[2,384,256]{2,1,0:T(8,128)(2,1)S(1)}, bf16[2,384,256]{2,1,0:T(8,128)(2,1)S(1)}, u32[]{:S(2)}, u32[]{:S(2)}) collective-permute-start(bf16[2,384,256]{2,1,0:T(8,128)(2,1)S(1)} %middle.1.a_ref.mid_ref), channel_id=1, source_target_pairs={{0,1},{1,0},{2,3},{3,2},{4,5},{5,4},{6,7},{7,6},{8,9},{9,8},{10,11... | collective-permute-start | bytes 1179656 | tf_op jit(solution)/shard_map/ppermute | solution.py:120
  33.9 1.8 %collective-permute-start.13 = (bf16[2,384,256]{2,1,0:T(8,128)(2,1)S(1)}, bf16[2,384,256]{2,1,0:T(8,128)(2,1)S(1)}, u32[]{:S(2)}, u32[]{:S(2)}) collective-permute-start(bf16[2,384,256]{2,1,0:T(8,128)(2,1)S(1)} %get-tuple-element.78), channel_id=1, source_target_pairs={{0,1},{1,0},{2,3},{3,2},{4,5},{5,4},{6,7},{7,6},{8,9},{9,8},{10,11... | collective-permute-start | bytes 1179656 | tf_op jit(solution)/shard_map/ppermute | solution.py:120
  35.8 11.2 %collective-permute-start.14 = (bf16[2,384,256]{2,1,0:T(8,128)(2,1)S(1)}, bf16[2,384,256]{2,1,0:T(8,128)(2,1)S(1)}, u32[]{:S(2)}, u32[]{:S(2)}) collective-permute-start(bf16[2,384,256]{2,1,0:T(8,128)(2,1)S(1)} %squash_sum.1.chip_ref), channel_id=1, source_target_pairs={{0,2},{1,3},{2,0},{3,1},{4,6},{5,7},{6,4},{7,5},{8,10},{9,11},{10,... | collective-permute-start | bytes 1179656 | tf_op jit(solution)/shard_map/ppermute | solution.py:120
  36.4 15.0 %collective-permute-start.21 = (bf16[2,192,384]{2,1,0:T(8,128)(2,1)S(1)}, bf16[2,192,384]{2,1,0:T(8,128)(2,1)S(1)}, u32[]{:S(2)}, u32[]{:S(2)}) collective-permute-start(bf16[2,192,384]{2,1,0:T(8,128)(2,1)S(1)} %get-tuple-element.98), channel_id=1, source_target_pairs={{0,4},{4,0},{8,12},{12,8},{1,5},{5,1},{9,13},{13,9},{2,6},{6,2},{1... | collective-permute-start | bytes 884744 | tf_op jit(solution)/shard_map/ppermute | solution.py:120
  38.0 16.0 %collective-permute-start.19 = (bf16[2,192,384]{2,1,0:T(8,128)(2,1)S(1)}, bf16[2,192,384]{2,1,0:T(8,128)(2,1)S(1)}, u32[]{:S(2)}, u32[]{:S(2)}) collective-permute-start(bf16[2,192,384]{2,1,0:T(8,128)(2,1)S(1)} %get-tuple-element.94), channel_id=1, source_target_pairs={{0,8},{4,12},{8,0},{12,4},{1,9},{5,13},{9,1},{13,5},{2,10},{6,14},... | collective-permute-start | bytes 884744 | tf_op jit(solution)/shard_map/ppermute | solution.py:120
  47.7 1.5 %collective-permute-start.15 = (bf16[384,256]{1,0:T(8,128)(2,1)S(1)}, bf16[384,256]{1,0:T(8,128)(2,1)S(1)}, u32[]{:S(2)}, u32[]{:S(2)}) collective-permute-start(bf16[384,256]{1,0:T(8,128)(2,1)S(1)} %get-tuple-element.83.refs_0_.g_ref.g0), channel_id=1, source_target_pairs={{0,1},{1,0},{2,3},{3,2},{4,5},{5,4},{6,7},{7,6},{8,9},{9,8},{10,11... | collective-permute-start | bytes 589832 | tf_op jit(solution)/shard_map/ppermute | solution.py:120
  47.8 1.7 %collective-permute-start.16 = (bf16[384,256]{1,0:T(8,128)(2,1)S(1)}, bf16[384,256]{1,0:T(8,128)(2,1)S(1)}, u32[]{:S(2)}, u32[]{:S(2)}) collective-permute-start(bf16[384,256]{1,0:T(8,128)(2,1)S(1)} %get-tuple-element.84.refs_2_.g2), channel_id=1, source_target_pairs={{0,1},{1,0},{2,3},{3,2},{4,5},{5,4},{6,7},{7,6},{8,9},{9,8},{10,11... | collective-permute-start | bytes 589832 | tf_op jit(solution)/shard_map/ppermute | solution.py:120
  48.3 6.8 %collective-permute-start.11 = (bf16[2,384,256]{2,1,0:T(8,128)(2,1)S(1)}, bf16[2,384,256]{2,1,0:T(8,128)(2,1)S(1)}, u32[]{:S(2)}, u32[]{:S(2)}) collective-permute-start(bf16[2,384,256]{2,1,0:T(8,128)(2,1)S(1)} %get-tuple-element.74), channel_id=1, source_target_pairs={{0,1},{1,0},{2,3},{3,2},{4,5},{5,4},{6,7},{7,6},{8,9},{9,8},{10,11... | collective-permute-start | bytes 1179656 | tf_op jit(solution)/shard_map/ppermute | solution.py:120
  50.6 5.9 %collective-permute-start.17 = (bf16[2,384,256]{2,1,0:T(8,128)(2,1)S(1)}, bf16[2,384,256]{2,1,0:T(8,128)(2,1)S(1)}, u32[]{:S(2)}, u32[]{:S(2)}) collective-permute-start(bf16[2,384,256]{2,1,0:T(8,128)(2,1)S(1)} %get-tuple-element.87), channel_id=1, source_target_pairs={{0,1},{1,0},{2,3},{3,2},{4,5},{5,4},{6,7},{7,6},{8,9},{9,8},{10,11... | collective-permute-start | bytes 1179656 | tf_op jit(solution)/shard_map/ppermute | solution.py:120
  51.9 22.4 %collective-permute-start.22 = (bf16[3,192,384]{2,1,0:T(8,128)(2,1)S(1)}, bf16[3,192,384]{2,1,0:T(8,128)(2,1)S(1)}, u32[]{:S(2)}, u32[]{:S(2)}) collective-permute-start(bf16[3,192,384]{2,1,0:T(8,128)(2,1)S(1)} %get-tuple-element.100), channel_id=1, source_target_pairs={{0,8},{4,12},{8,0},{12,4},{1,9},{5,13},{9,1},{13,5},{2,10},{6,14},... | collective-permute-start | bytes 1327112 | tf_op jit(solution)/shard_map/ppermute | solution.py:120
  54.5 20.5 %collective-permute-start.20 = (bf16[3,192,384]{2,1,0:T(8,128)(2,1)S(1)}, bf16[3,192,384]{2,1,0:T(8,128)(2,1)S(1)}, u32[]{:S(2)}, u32[]{:S(2)}) collective-permute-start(bf16[3,192,384]{2,1,0:T(8,128)(2,1)S(1)} %get-tuple-element.96), channel_id=1, source_target_pairs={{0,4},{4,0},{8,12},{12,8},{1,5},{5,1},{9,13},{13,9},{2,6},{6,2},{1... | collective-permute-start | bytes 1327112 | tf_op jit(solution)/shard_map/ppermute | solution.py:120
  55.1 23.4 %collective-permute-start.12 = (bf16[384,256]{1,0:T(8,128)(2,1)S(1)}, bf16[384,256]{1,0:T(8,128)(2,1)S(1)}, u32[]{:S(2)}, u32[]{:S(2)}) collective-permute-start(bf16[384,256]{1,0:T(8,128)(2,1)S(1)} %get-tuple-element.76), channel_id=1, source_target_pairs={{0,2},{1,3},{2,0},{3,1},{4,6},{5,7},{6,4},{7,5},{8,10},{9,11},{10,... | collective-permute-start | bytes 589832 | tf_op jit(solution)/shard_map/ppermute | solution.py:120
  56.5 23.6 %collective-permute-start.18 = (bf16[384,256]{1,0:T(8,128)(2,1)S(1)}, bf16[384,256]{1,0:T(8,128)(2,1)S(1)}, u32[]{:S(2)}, u32[]{:S(2)}) collective-permute-start(bf16[384,256]{1,0:T(8,128)(2,1)S(1)} %get-tuple-element.89), channel_id=1, source_target_pairs={{0,2},{1,3},{2,0},{3,1},{4,6},{5,7},{6,4},{7,5},{8,10},{9,11},{10,... | collective-permute-start | bytes 589832 | tf_op jit(solution)/shard_map/ppermute | solution.py:120
  75.0 8.1 %collective-permute-start.23 = (bf16[192,384]{1,0:T(8,128)(2,1)S(1)}, bf16[192,384]{1,0:T(8,128)(2,1)S(1)}, u32[]{:S(2)}, u32[]{:S(2)}) collective-permute-start(bf16[192,384]{1,0:T(8,128)(2,1)S(1)} %get-tuple-element.103), channel_id=1, source_target_pairs={{0,8},{4,12},{8,0},{12,4},{1,9},{5,13},{9,1},{13,5},{2,10},{6,14},... | collective-permute-start | bytes 442376 | tf_op jit(solution)/shard_map/ppermute | solution.py:120
  76.0 7.2 %collective-permute-start.24 = (bf16[192,384]{1,0:T(8,128)(2,1)S(1)}, bf16[192,384]{1,0:T(8,128)(2,1)S(1)}, u32[]{:S(2)}, u32[]{:S(2)}) collective-permute-start(bf16[192,384]{1,0:T(8,128)(2,1)S(1)} %get-tuple-element.104), channel_id=1, source_target_pairs={{0,4},{4,0},{8,12},{12,8},{1,5},{5,1},{9,13},{13,9},{2,6},{6,2},{1... | collective-permute-start | bytes 442376 | tf_op jit(solution)/shard_map/ppermute | solution.py:120

commit v8 on v7

--- a/solution.py
+++ b/solution.py
@@ -1,5 +1,3 @@
-import functools
-
 import jax
 import jax.numpy as jnp
 from jax import lax
@@ -323,7 +321,7 @@
         for i in (0, 1):
             keep[i] = dot(v_ref[...], g_ref[place(i)], ((1,), (1,)))
 
-    one, two, three = ((n, hid, rows) for n in (1, 2, 3))
+    one, two = ((n, hid, rows) for n in (1, 2))
 
     def second_weight_body(z_ref, gu_ref, v_ref, ga_ref, gb_ref, *rest):
         keep_k, keep_p, send_k, send_p, g_ref = rest
@@ -336,14 +334,12 @@
         own[0] = keep[0] + got[0].astype(F32)
         return (keep[1] + got[1].astype(F32)).astype(BF16)
 
-    def first_proj_body(v_ref, g0, g1, g2, g3, keep_b, got_b, keep, send, own, g_ref):
+    def first_proj_body(v_ref, g0, g1, g2, g3, _, keep, send, g_ref):
         for i, ref in enumerate((g0, g1, g2, g3)):
             g_ref[i] = ref[...]
-        send[2] = half_sum(keep_b, got_b, own)
         proj_pieces(v_ref, g_ref, keep, send)
 
-    def first_taps_body(z_ref, gu_ref, keep_b, got_b, keep, send, own):
-        send[2] = half_sum(keep_b, got_b, own)
+    def first_taps_body(z_ref, gu_ref, _, keep, send):
         taps_pieces(z_ref, gu_ref, keep, send)
 
     def half_body(keep, got, *rest):
@@ -366,19 +362,19 @@
         for copy in copies:
             copy.wait()
 
-    def total_body(place, _, own_k, own_p, got_k, got_p, taps_ref, proj_ref, k, p, sems):
-        k[...] = own_k[0] + got_k[place].astype(F32)
+    def total_body(_, own_k, own_p, got_k, got_p, taps_ref, proj_ref, k, p, sems):
+        k[...] = own_k[0] + got_k[...].astype(F32)
         first = pltpu.make_async_copy(k, taps_ref.at[1], sems.at[0])
         first.start()
-        p[...] = own_p[0] + got_p[place].astype(F32)
+        p[...] = own_p[0] + got_p[...].astype(F32)
         second = pltpu.make_async_copy(p, proj_ref, sems.at[1])
         second.start()
         first.wait()
         second.wait()
 
-    def total(place, planes, own_k, own_p, got_k, got_p, name):
+    def total(planes, own_k, own_p, got_k, got_p, name):
         taps, proj = pl.pallas_call(
-            functools.partial(total_body, place),
+            total_body,
             out_shape=[jax.ShapeDtypeStruct(*plane), jax.ShapeDtypeStruct((hid, rows), F32)],
             in_specs=[hbm] + [VMEM] * 4,
             out_specs=[hbm, hbm],
@@ -454,8 +450,12 @@
 
     (second_out,) = call(out_body, [((rows, bins), BF16)], (mid, y_own, y_got), "out", final=True)
 
+    def entry_sum_body(keep_ref, got0, got1, own_ref, send_ref):
+        own_ref[...] = keep_ref[0] + got0[...].astype(F32)
+        send_ref[...] = (keep_ref[1] + got1[...].astype(F32)).astype(BF16)
+
     def first_back_body(*refs):
-        grads, (k_ref, p_ref, s_ref, gu_ref, keep_ref, send_ref) = refs[:4], refs[4:]
+        grads, (k_ref, p_ref, s_ref, gu_ref, keep_ref, *sends) = refs[:4], refs[4:]
         m = lax.axis_index("mp")
         gv = jnp.zeros((hid, bins), F32)
         for j in range(4):
@@ -463,33 +463,34 @@
         gu = (gv * s_ref[...]).astype(BF16)
         gu_ref[...] = gu
         for i, j in enumerate((1, 3)):
-            send_ref[i] = dot(k_ref[:, block(m, j)], gu, ((0,), (0,))).astype(BF16)
+            sends[i][...] = dot(k_ref[:, block(m, j)], gu, ((0,), (0,))).astype(BF16)
         for i, j in enumerate((0, 2)):
             keep_ref[i] = dot(k_ref[:, block(m, j)], gu, ((0,), (0,)))
 
-    gu_a, keep, send = call(
+    gu_a, keep, *sends = call(
         first_back_body,
-        [((hid, bins), BF16), ((2, rows, bins), F32), ((2, rows, bins), BF16)],
+        [((hid, bins), BF16), ((2, rows, bins), F32)] + [((rows, bins), BF16)] * 2,
         (*g_mid, tap_a, cols_a, slope_a),
         "first_backward",
     )
-    keep_ap, send_p, own_bk = call(
-        first_proj_body,
-        [(two, F32), (three, BF16), (one, F32)],
-        (v_a, *g_mid, keep_b[0], got_b[0]),
-        "first_proj",
-        pack,
+    keep_ap, send_p = call(
+        first_proj_body, [(two, F32), (two, BF16)], (v_a, *g_mid, got_b[1]), "first_proj", pack
     )
     got_p = swap(send_p, "ctx", 2)
-    keep_ak, send_k, own_bp = call(
-        first_taps_body,
-        [(two, F32), (three, BF16), (one, F32)],
-        (z_a, gu_a, keep_b[1], got_b[1]),
-        "first_taps",
+    keep_ak, send_k = call(
+        first_taps_body, [(two, F32), (two, BF16)], (z_a, gu_a, got_b[0]), "first_taps"
     )
     got_k = swap(send_k, "ctx", 1)
-    got = swap(send, "mp", 1)
-    e_own, e_send = last_sum(keep, got, "entry_sum")
+    half = [(one, F32), (one[1:], BF16)]
+    own_bk, send_k = call(half_body, half, (keep_b[0], got_b[0]), "second_taps_half")
+    own_bp, send_p = call(half_body, half, (keep_b[1], got_b[1]), "second_proj_half")
+    last_b = swap(send_k, "ctx", 2), swap(send_p, "ctx", 1)
+    e_own, e_send = call(
+        entry_sum_body,
+        [((rows, bins), F32), ((rows, bins), BF16)],
+        (keep, *[swap(part, "mp", 1) for part in sends]),
+        "entry_sum",
+    )
     e_got = swap(e_send, "mp", 2)
 
     def entry_body(g_ref, x_ref, own_ref, got_ref, out_ref):
@@ -500,13 +501,12 @@
 
     (entry,) = call(entry_body, [((rows, bins), BF16)], (g_mid[0], x_own, e_own, e_got), "entry", final=True)
 
-    half = [(one, F32), (one[1:], BF16)]
-    own_ap, send_p = call(half_body, half, (keep_ap, got_p), "proj_half")
+    own_ak, send_k = call(half_body, half, (keep_ak, got_k), "taps_half")
+    last_k = swap(send_k, "ctx", 2)
+    own_ap, send_p = call(half_body, half, (keep_ap, got_p, *last_b), "proj_half")
     last_p = swap(send_p, "ctx", 1)
-    own_ak, send_k = call(half_body, half, (keep_ak, got_k, own_ap), "taps_half")
-    last_k = swap(send_k, "ctx", 2)
-    taps_b_grad, point_b_grad = total(2, planes[0], own_bk, own_bp, got_p, got_k, "second_total")
-    taps_a_grad, point_a_grad = total(Ellipsis, planes[1], own_ak, own_ap, last_k, last_p, "first_total")
+    taps_b_grad, point_b_grad = total(planes[0], own_bk, own_bp, *last_b, "second_total")
+    taps_a_grad, point_a_grad = total(planes[1], own_ak, own_ap, last_k, last_p, "first_total")
     return second_out, entry, taps_a_grad, point_a_grad, taps_b_grad, point_b_grad
 
 

time: 84.2 us -> 85.3 us (1.013)
  starting transfers between devices: 22.1 us -> 25.4 us
  waiting for transfers between devices: 48.1 us -> 45.9 us
    ppermute x25 -> x28, starting transfers between devices: 22.1 us -> 25.4 us  [swap(): return lax.ppermute(value, axis, [(i, i ^ bits) for i in range(size)])]
    ppermute x25 -> x28, waiting for transfers between devices: 48.1 us -> 45.9 us  [swap(): return lax.ppermute(value, axis, [(i, i ^ bits) for i in range(size)])]
    pallas_call x18 -> x20, Pallas kernels: 8.5 us -> 8.53 us  [call(): pl.pallas_call(body, out_shape=[struct(s, d) for s, d in outs], in_specs=...]
  transfers between devices with their start and end apart: 25 -> 28, of which waited for: 15 -> 17; matrix products, arithmetic and copies ran while one was open for 0% -> 0% of each run, Pallas kernels for 11% -> 11%
where the time goes in v8:
time: 85.3 us; the launch traced here: 85.2 us
  waiting for transfers between devices  45.9 us (54%)
  starting transfers between devices  25.4 us (30%)
  Pallas kernels  13.1 us (15%)
    ppermute x28, waiting for transfers between devices, swap(): return lax.ppermute(value, axis, [(i, i ^ bits) for i in range(size)])  45.9 us
    ppermute x28, starting transfers between devices, swap(): return lax.ppermute(value, axis, [(i, i ^ bits) for i in range(size)])  25.4 us
    pallas_call x20, Pallas kernels, call(): pl.pallas_call(body, out_shape=[struct(s, d) for s, d in outs], in_specs=...  8.53 us
    pallas_call x1, Pallas kernels, fast_shards(): pl.pallas_call(load_body, out_shape=[pltpu.VMEM((rows, bins), BF16)] + [p...  1.79 us
    pallas_call x2, Pallas kernels, total(): pl.pallas_call(total_body, out_shape=[jax.ShapeDtypeStruct(*plane), jax.S...  1.71 us
  transfers between devices with their start and end apart: 28, of which 17 were waited for; matrix products, arithmetic and copies ran while one was open for 0% of the time, Pallas kernels for 11%

profile of v8, /device:TPU:0, one launch (start us, length us, event | category | flops | bytes accessed | tf_op | source)
XLA Modules:
  0.0 85.2 jit_solution(12294635047126019192)
XLA Ops:
  0.6 3.0 %collective-permute-start = (bf16[384,256]{1,0:T(8,128)(2,1)}, bf16[384,256]{1,0:T(8,128)(2,1)S(1)}, u32[]{:S(2)}, u32[]{:S(2)}) collective-permute-start(bf16[384,256]{1,0:T(8,128)(2,1)} %x_ref.1), channel_id=1, source_target_pairs={{0,2},{1,3},{2,0},{3,1},{4,6},{5,7},{6,4},{7,5},{8,10},{9,11},{10,... | collective-permute-start | bytes 589832 | tf_op jit(solution)/shard_map/ppermute | solution.py:118
  3.8 1.8 %load.1 = (bf16[384,256]{1,0:T(8,128)(2,1)S(1)}, bf16[192,1536]{1,0:T(8,128)(2,1)S(1)}, bf16[192,1536]{1,0:T(8,128)(2,1)S(1)}, bf16[192,1536]{1,0:T(8,128)(2,1)S...) custom-call(bf16[384,256]{1,0:T(8,128)(2,1)} %x_ref.1, bf16[3,192,1536]{2,1,0:T(8,128)(2,1)} %ta.1, ...), custom_call_target="tpu_custom_call" | custom-call | tf_op jit(solution)/shard_map/load/pallas_call | solution.py:181
  5.6 4.0 %collective-permute-done.x2 = bf16[384,256]{1,0:T(8,128)(2,1)S(1)} collective-permute-done((bf16[384,256]{1,0:T(8,128)(2,1)}, bf16[384,256]{1,0:T(8,128)(2,1)S(1)}, u32[]{:S(2)}, u32[]{:S(2)}) %collective-permute-start) | collective-permute-done | bytes 196640 | tf_op jit(solution)/shard_map/ppermute | solution.py:118
  9.6 3.4 %collective-permute-done.3._.far_ref = bf16[2,48,1024]{2,1,0:T(8,128)(2,1)S(1)} collective-permute-done((bf16[2,48,1024]{2,1,0:T(8,128)(2,1)}, bf16[2,48,1024]{2,1,0:T(8,128)(2,1)S(1)}, u32[]{:S(2)}, u32[]{:S(2)}) %collective-permute-start.3) | collective-permute-done | bytes 196640 | tf_op jit(solution)/shard_map/ppermute | solution.py:118
  13.0 1.4 %first_forward.1 = (bf16[4,384,256]{2,1,0:T(8,128)(2,1)S(1)}, bf16[192,256]{1,0:T(8,128)(2,1)S(1)}, f32[192,256]{1,0:T(8,128)S(1)}, f32[2,384,256]{2,1,0:T(8,128)S(1)}, bf16[2,384,256]{2,1,0:T(8,128)(2,1)S(1)}) custom-call(bf16[384,256]{1,0:T(8,128)(2,1)S(1)} %get-tuple-element.63.x0.x_ref, bf16[384,256]{1,0:T(8,128)(2,1)S(1)} %collective-permute-done.1.x1, ...), custom_call_target="tpu_custom_call" | custom-call | tf_op jit(solution)/shard_map/first_forward/pallas_call | solution.py:146
  14.4 1.7 %collective-permute-done.4.got_ref = bf16[2,384,256]{2,1,0:T(8,128)(2,1)S(1)} collective-permute-done((bf16[2,384,256]{2,1,0:T(8,128)(2,1)S(1)}, bf16[2,384,256]{2,1,0:T(8,128)(2,1)S(1)}, u32[]{:S(2)}, u32[]{:S(2)}) %collective-permute-start.4) | collective-permute-done | bytes 393248 | tf_op jit(solution)/shard_map/ppermute | solution.py:118
  16.2 1.8 %collective-permute-start.5 = (bf16[2,384,256]{2,1,0:T(8,128)(2,1)S(1)}, bf16[2,384,256]{2,1,0:T(8,128)(2,1)S(1)}, u32[]{:S(2)}, u32[]{:S(2)}) collective-permute-start(bf16[2,384,256]{2,1,0:T(8,128)(2,1)S(1)} %mix_sum.1.chip_ref), channel_id=1, source_target_pairs={{0,2},{1,3},{2,0},{3,1},{4,6},{5,7},{6,4},{7,5},{8,10},{9,11},{10,... | collective-permute-start | bytes 1179656 | tf_op jit(solution)/shard_map/ppermute | solution.py:118
  18.1 1.6 %collective-permute-start.7 = (bf16[2,2,48,256]{3,2,1,0:T(8,128)(2,1)S(1)}, bf16[2,2,48,256]{3,2,1,0:T(8,128)(2,1)S(1)}, u32[]{:S(2)}, u32[]{:S(2)}) collective-permute-start(bf16[2,2,48,256]{3,2,1,0:T(8,128)(2,1)S(1)} %get-tuple-element.71), channel_id=1, source_target_pairs={{0,4},{4,0},{8,12},{12,8},{1,5},{5,1},{9,13},{13,9},{2,6},{6,2},{1... | collective-permute-start | bytes 294920 | tf_op jit(solution)/shard_map/ppermute | solution.py:118
  19.7 2.6 %collective-permute-start.8 = (bf16[2,2,48,256]{3,2,1,0:T(8,128)(2,1)S(1)}, bf16[2,2,48,256]{3,2,1,0:T(8,128)(2,1)S(1)}, u32[]{:S(2)}, u32[]{:S(2)}) collective-permute-start(bf16[2,2,48,256]{3,2,1,0:T(8,128)(2,1)S(1)} %get-tuple-element.72), channel_id=1, source_target_pairs={{0,8},{4,12},{8,0},{12,4},{1,9},{5,13},{9,1},{13,5},{2,10},{6,14},... | collective-permute-start | bytes 294920 | tf_op jit(solution)/shard_map/ppermute | solution.py:118
  22.5 0.2 collective-permute-done.7.refs_1_
  22.7 7.4 %collective-permute-done.8.refs_2_ = bf16[2,2,48,256]{3,2,1,0:T(8,128)(2,1)S(1)} collective-permute-done((bf16[2,2,48,256]{3,2,1,0:T(8,128)(2,1)S(1)}, bf16[2,2,48,256]{3,2,1,0:T(8,128)(2,1)S(1)}, u32[]{:S(2)}, u32[]{:S(2)}) %collective-permute-start.8) | collective-permute-done | bytes 98336 | tf_op jit(solution)/shard_map/ppermute | solution.py:118
  30.4 0.5 collective-permute-start.6
  31.0 1.0 %collective-permute-done.10.gb_ref = bf16[2,384,256]{2,1,0:T(8,128)(2,1)S(1)} collective-permute-done((bf16[2,384,256]{2,1,0:T(8,128)(2,1)S(1)}, bf16[2,384,256]{2,1,0:T(8,128)(2,1)S(1)}, u32[]{:S(2)}, u32[]{:S(2)}) %collective-permute-start.10) | collective-permute-done | bytes 393248 | tf_op jit(solution)/shard_map/ppermute | solution.py:118
  32.0 0.6 collective-permute-done.6.b_ref
  32.5 1.4 %second_block.1 = (bf16[4,384,256]{2,1,0:T(8,128)(2,1)S(1)}, bf16[192,256]{1,0:T(8,128)(2,1)S(1)}, bf16[192,256]{1,0:T(8,128)(2,1)S(1)}, f32[2,384,256]{2,1,0:T(...) custom-call(bf16[2,384,256]{2,1,0:T(8,128)(2,1)S(1)} %middle.1.a_ref.mid_, ...), custom_call_target="tpu_custom_call" | custom-call | tf_op jit(solution)/shard_map/second_block/pallas_call | solution.py:146
  33.9 0.2 collective-permute-start.13
  34.2 0.7 second_weights.1
  34.9 0.8 collective-permute-done.13.got_ref
  35.8 0.6 collective-permute-start.14
  36.4 1.6 %collective-permute-start.20 = (bf16[2,192,384]{2,1,0:T(8,128)(2,1)S(1)}, bf16[2,192,384]{2,1,0:T(8,128)(2,1)S(1)}, u32[]{:S(2)}, u32[]{:S(2)}) collective-permute-start(bf16[2,192,384]{2,1,0:T(8,128)(2,1)S(1)} %get-tuple-element.97), channel_id=1, source_target_pairs={{0,4},{4,0},{8,12},{12,8},{1,5},{5,1},{9,13},{13,9},{2,6},{6,2},{1... | collective-permute-start | bytes 884744 | tf_op jit(solution)/shard_map/ppermute | solution.py:118
  38.0 1.4 %collective-permute-start.22 = (bf16[2,192,384]{2,1,0:T(8,128)(2,1)S(1)}, bf16[2,192,384]{2,1,0:T(8,128)(2,1)S(1)}, u32[]{:S(2)}, u32[]{:S(2)}) collective-permute-start(bf16[2,192,384]{2,1,0:T(8,128)(2,1)S(1)} %get-tuple-element.102), channel_id=1, source_target_pairs={{0,8},{4,12},{8,0},{12,4},{1,9},{5,13},{9,1},{13,5},{2,10},{6,14},... | collective-permute-start | bytes 884744 | tf_op jit(solution)/shard_map/ppermute | solution.py:118
  39.4 7.6 %collective-permute-done.14.other_ref = bf16[2,384,256]{2,1,0:T(8,128)(2,1)S(1)} collective-permute-done((bf16[2,384,256]{2,1,0:T(8,128)(2,1)S(1)}, bf16[2,384,256]{2,1,0:T(8,128)(2,1)S(1)}, u32[]{:S(2)}, u32[]{:S(2)}) %collective-permute-start.14) | collective-permute-done | bytes 393248 | tf_op jit(solution)/shard_map/ppermute | solution.py:118
  47.1 0.6 middle_grad.1
  47.8 0.5 collective-permute-start.16
  48.3 0.9 %collective-permute-done.15.refs_1_.g1 = bf16[384,256]{1,0:T(8,128)(2,1)S(1)} collective-permute-done((bf16[384,256]{1,0:T(8,128)(2,1)S(1)}, bf16[384,256]{1,0:T(8,128)(2,1)S(1)}, u32[]{:S(2)}, u32[]{:S(2)}) %collective-permute-start.15) | collective-permute-done | bytes 196640 | tf_op jit(solution)/shard_map/ppermute | solution.py:118
  49.2 0.3 collective-permute-done.16.refs_3_.g3
  49.5 1.1 %first_backward.1 = (bf16[192,256]{1,0:T(8,128)(2,1)S(1)}, f32[2,384,256]{2,1,0:T(8,128)S(1)}, bf16[384,256]{1,0:T(8,128)(2,1)S(1)}, bf16[384,256]{1,0:T(8,128)(2,1)S(1)}) custom-call(bf16[384,256]{1,0:T(8,128)(2,1)S(1)} %get-tuple-element.86.refs_0_.g_ref.g0, bf16[384,256]{1,0:T(8,128)(2,1)S(1)} %collective-permute-done.15.refs_1_.g1, ...), custom_call_target="tpu_custom_call" | custom-call | tf_op jit(solution)/shard_map/first_backward/pallas_call | solution.py:146
  50.6 0.3 collective-permute-start.17
  50.8 0.6 collective-permute-done.20._.got
  51.4 0.4 first_taps.1
  51.8 1.1 %collective-permute-start.21 = (bf16[2,192,384]{2,1,0:T(8,128)(2,1)S(1)}, bf16[2,192,384]{2,1,0:T(8,128)(2,1)S(1)}, u32[]{:S(2)}, u32[]{:S(2)}) collective-permute-start(bf16[2,192,384]{2,1,0:T(8,128)(2,1)S(1)} %get-tuple-element.99), channel_id=1, source_target_pairs={{0,4},{4,0},{8,12},{12,8},{1,5},{5,1},{9,13},{13,9},{2,6},{6,2},{1... | collective-permute-start | bytes 884744 | tf_op jit(solution)/shard_map/ppermute | solution.py:118
  53.0 0.8 collective-permute-done.22._.got
  53.8 0.5 first_proj.1
  54.3 0.7 collective-permute-start.23
  55.1 2.4 %collective-permute-start.24 = (bf16[192,384]{1,0:T(8,128)(2,1)S(1)}, bf16[192,384]{1,0:T(8,128)(2,1)S(1)}, u32[]{:S(2)}, u32[]{:S(2)}) collective-permute-start(bf16[192,384]{1,0:T(8,128)(2,1)S(1)} %get-tuple-element.105), channel_id=1, source_target_pairs={{0,8},{4,12},{8,0},{12,4},{1,9},{5,13},{9,1},{13,5},{2,10},{6,14},... | collective-permute-start | bytes 442376 | tf_op jit(solution)/shard_map/ppermute | solution.py:118
  57.5 0.4 collective-permute-start.25
  58.0 1.5 %collective-permute-start.12 = (bf16[384,256]{1,0:T(8,128)(2,1)S(1)}, bf16[384,256]{1,0:T(8,128)(2,1)S(1)}, u32[]{:S(2)}, u32[]{:S(2)}) collective-permute-start(bf16[384,256]{1,0:T(8,128)(2,1)S(1)} %get-tuple-element.79), channel_id=1, source_target_pairs={{0,2},{1,3},{2,0},{3,1},{4,6},{5,7},{6,4},{7,5},{8,10},{9,11},{10,... | collective-permute-start | bytes 589832 | tf_op jit(solution)/shard_map/ppermute | solution.py:118
  59.6 7.9 %collective-permute-done.21.got = bf16[2,192,384]{2,1,0:T(8,128)(2,1)S(1)} collective-permute-done((bf16[2,192,384]{2,1,0:T(8,128)(2,1)S(1)}, bf16[2,192,384]{2,1,0:T(8,128)(2,1)S(1)}, u32[]{:S(2)}, u32[]{:S(2)}) %collective-permute-start.21) | collective-permute-done | bytes 294944 | tf_op jit(solution)/shard_map/ppermute | solution.py:118
  67.5 1.2 %collective-permute-start.19 = (bf16[384,256]{1,0:T(8,128)(2,1)S(1)}, bf16[384,256]{1,0:T(8,128)(2,1)S(1)}, u32[]{:S(2)}, u32[]{:S(2)}) collective-permute-start(bf16[384,256]{1,0:T(8,128)(2,1)S(1)} %get-tuple-element.93), channel_id=1, source_target_pairs={{0,2},{1,3},{2,0},{3,1},{4,6},{5,7},{6,4},{7,5},{8,10},{9,11},{10,... | collective-permute-start | bytes 589832 | tf_op jit(solution)/shard_map/ppermute | solution.py:118
  68.7 7.3 %collective-permute-done.24.rest_0_.got_k = bf16[192,384]{1,0:T(8,128)(2,1)S(1)} collective-permute-done((bf16[192,384]{1,0:T(8,128)(2,1)S(1)}, bf16[192,384]{1,0:T(8,128)(2,1)S(1)}, u32[]{:S(2)}, u32[]{:S(2)}) %collective-permute-start.24) | collective-permute-done | bytes 147488 | tf_op jit(solution)/shard_map/ppermute | solution.py:118
  76.1 3.1 %collective-permute-start.27 = (bf16[192,384]{1,0:T(8,128)(2,1)S(1)}, bf16[192,384]{1,0:T(8,128)(2,1)S(1)}, u32[]{:S(2)}, u32[]{:S(2)}) collective-permute-start(bf16[192,384]{1,0:T(8,128)(2,1)S(1)} %get-tuple-element.110), channel_id=1, source_target_pairs={{0,4},{4,0},{8,12},{12,8},{1,5},{5,1},{9,13},{13,9},{2,6},{6,2},{1... | collective-permute-start | bytes 442376 | tf_op jit(solution)/shard_map/ppermute | solution.py:118
  79.2 1.1 %zero_planes.1 = (f32[3,192,384]{2,1,0:T(8,128)}, f32[3,192,384]{2,1,0:T(8,128)}) custom-call(), custom_call_target="tpu_custom_call" | custom-call | tf_op jit(solution)/shard_map/zero_planes/pallas_call | solution.py:394
  80.2 0.9 %second_total.1 = (f32[3,192,384]{2,1,0:T(8,128)}, f32[192,384]{1,0:T(8,128)}) custom-call(f32[3,192,384]{2,1,0:T(8,128)} %get-tuple-element.113._, f32[1,192,384]{2,1,0:T(8,128)S(1)} %get-tuple-element.114.own_k, f32[1,192,384]{2,1,0:T(8,128)S(1)} %get-tuple-element.115.own_p, ...), custom_call_target="tpu_custom_call", output_to_operand_aliasing={{0}: (0, {})} | custom-call | tf_op jit(solution)/shard_map/second_total/pallas_call | solution.py:376
  81.1 0.7 out.1
  81.8 1.0 %entry.1 = bf16[384,256]{1,0:T(8,128)(2,1)} custom-call(bf16[384,256]{1,0:T(8,128)(2,1)S(1)} %get-tuple-element.86.refs_0_.g_ref.g0, bf16[384,256]{1,0:T(8,128)(2,1)S(1)} %get-tuple-element.63.x0.x_ref, f32[384,256]{1,0:T(8,128)S(1)} %get-tuple-element.92.own_ref, bf16[384,256]{1,0:T(8,128)(2,1)S(1)} %collective-permute-done.19.got_ref), custom_call_target="tpu_custom_call" | custom-call | tf_op jit(solution)/shard_map/entry/pallas_call | solution.py:146
  82.8 1.2 %collective-permute-done.26.got_k = bf16[192,384]{1,0:T(8,128)(2,1)S(1)} collective-permute-done((bf16[192,384]{1,0:T(8,128)(2,1)S(1)}, bf16[192,384]{1,0:T(8,128)(2,1)S(1)}, u32[]{:S(2)}, u32[]{:S(2)}) %collective-permute-start.26) | collective-permute-done | bytes 147488 | tf_op jit(solution)/shard_map/ppermute | solution.py:118
  84.0 0.3 collective-permute-done.27.got_p
  84.3 0.9 %first_total.1 = (f32[3,192,384]{2,1,0:T(8,128)}, f32[192,384]{1,0:T(8,128)}) custom-call(f32[3,192,384]{2,1,0:T(8,128)} %get-tuple-element.94._, f32[1,192,384]{2,1,0:T(8,128)S(1)} %get-tuple-element.100.own_k, f32[1,192,384]{2,1,0:T(8,128)S(1)} %get-tuple-element.108.own_p, ...), custom_call_target="tpu_custom_call", output_to_operand_aliasing={{0}: (0, {})} | custom-call | tf_op jit(solution)/shard_map/first_total/pallas_call | solution.py:376
  (32 shorter events, 1.4 us)
Async XLA Ops:
  0.6 8.9 %collective-permute-start = (bf16[384,256]{1,0:T(8,128)(2,1)}, bf16[384,256]{1,0:T(8,128)(2,1)S(1)}, u32[]{:S(2)}, u32[]{:S(2)}) collective-permute-start(bf16[384,256]{1,0:T(8,128)(2,1)} %x_ref.1), channel_id=1, source_target_pairs={{0,2},{1,3},{2,0},{3,1},{4,6},{5,7},{6,4},{7,5},{8,10},{9,11},{10,... | collective-permute-start | bytes 589832 | tf_op jit(solution)/shard_map/ppermute | solution.py:118
  3.6 5.9 %collective-permute-start.1 = (bf16[384,256]{1,0:T(8,128)(2,1)}, bf16[384,256]{1,0:T(8,128)(2,1)S(1)}, u32[]{:S(2)}, u32[]{:S(2)}) collective-permute-start(bf16[384,256]{1,0:T(8,128)(2,1)} %x_ref.1), channel_id=1, source_target_pairs={{0,1},{1,0},{2,3},{3,2},{4,5},{5,4},{6,7},{7,6},{8,9},{9,8},{10,11... | collective-permute-start | bytes 589832 | tf_op jit(solution)/shard_map/ppermute | solution.py:118
  3.6 9.3 %collective-permute-start.3 = (bf16[2,48,1024]{2,1,0:T(8,128)(2,1)}, bf16[2,48,1024]{2,1,0:T(8,128)(2,1)S(1)}, u32[]{:S(2)}, u32[]{:S(2)}) collective-permute-start(bf16[2,48,1024]{2,1,0:T(8,128)(2,1)} %g_ref.1), channel_id=1, source_target_pairs={{0,2},{1,3},{2,0},{3,1},{4,6},{5,7},{6,4},{7,5},{8,10},{9,11},{10,... | collective-permute-start | bytes 589832 | tf_op jit(solution)/shard_map/ppermute | solution.py:118
  9.6 3.4 %collective-permute-start.2 = (bf16[384,256]{1,0:T(8,128)(2,1)S(1)}, bf16[384,256]{1,0:T(8,128)(2,1)S(1)}, u32[]{:S(2)}, u32[]{:S(2)}) collective-permute-start(bf16[384,256]{1,0:T(8,128)(2,1)S(1)} %collective-permute-done.x2), channel_id=1, source_target_pairs={{0,1},{1,0},{2,3},{3,2},{4,5},{5,4},{6,7},{7,6},{8,9},{9,8},{10,11... | collective-permute-start | bytes 589832 | tf_op jit(solution)/shard_map/ppermute | solution.py:118
  14.3 1.8 %collective-permute-start.4 = (bf16[2,384,256]{2,1,0:T(8,128)(2,1)S(1)}, bf16[2,384,256]{2,1,0:T(8,128)(2,1)S(1)}, u32[]{:S(2)}, u32[]{:S(2)}) collective-permute-start(bf16[2,384,256]{2,1,0:T(8,128)(2,1)S(1)} %get-tuple-element.68), channel_id=1, source_target_pairs={{0,1},{1,0},{2,3},{3,2},{4,5},{5,4},{6,7},{7,6},{8,9},{9,8},{10,11... | collective-permute-start | bytes 1179656 | tf_op jit(solution)/shard_map/ppermute | solution.py:118
  16.2 14.1 %collective-permute-start.5 = (bf16[2,384,256]{2,1,0:T(8,128)(2,1)S(1)}, bf16[2,384,256]{2,1,0:T(8,128)(2,1)S(1)}, u32[]{:S(2)}, u32[]{:S(2)}) collective-permute-start(bf16[2,384,256]{2,1,0:T(8,128)(2,1)S(1)} %mix_sum.1.chip_ref), channel_id=1, source_target_pairs={{0,2},{1,3},{2,0},{3,1},{4,6},{5,7},{6,4},{7,5},{8,10},{9,11},{10,... | collective-permute-start | bytes 1179656 | tf_op jit(solution)/shard_map/ppermute | solution.py:118
  18.1 4.7 %collective-permute-start.7 = (bf16[2,2,48,256]{3,2,1,0:T(8,128)(2,1)S(1)}, bf16[2,2,48,256]{3,2,1,0:T(8,128)(2,1)S(1)}, u32[]{:S(2)}, u32[]{:S(2)}) collective-permute-start(bf16[2,2,48,256]{3,2,1,0:T(8,128)(2,1)S(1)} %get-tuple-element.71), channel_id=1, source_target_pairs={{0,4},{4,0},{8,12},{12,8},{1,5},{5,1},{9,13},{13,9},{2,6},{6,2},{1... | collective-permute-start | bytes 294920 | tf_op jit(solution)/shard_map/ppermute | solution.py:118
  19.7 10.4 %collective-permute-start.8 = (bf16[2,2,48,256]{3,2,1,0:T(8,128)(2,1)S(1)}, bf16[2,2,48,256]{3,2,1,0:T(8,128)(2,1)S(1)}, u32[]{:S(2)}, u32[]{:S(2)}) collective-permute-start(bf16[2,2,48,256]{3,2,1,0:T(8,128)(2,1)S(1)} %get-tuple-element.72), channel_id=1, source_target_pairs={{0,8},{4,12},{8,0},{12,4},{1,9},{5,13},{9,1},{13,5},{2,10},{6,14},... | collective-permute-start | bytes 294920 | tf_op jit(solution)/shard_map/ppermute | solution.py:118
  22.3 7.9 %collective-permute-start.9 = (bf16[2,2,48,256]{3,2,1,0:T(8,128)(2,1)S(1)}, bf16[2,2,48,256]{3,2,1,0:T(8,128)(2,1)S(1)}, u32[]{:S(2)}, u32[]{:S(2)}) collective-permute-start(bf16[2,2,48,256]{3,2,1,0:T(8,128)(2,1)S(1)} %get-tuple-element.73), channel_id=1, source_target_pairs={{0,12},{4,8},{8,4},{12,0},{1,13},{5,9},{9,5},{13,1},{2,14},{6,10},... | collective-permute-start | bytes 294920 | tf_op jit(solution)/shard_map/ppermute | solution.py:118
  30.2 1.8 %collective-permute-start.10 = (bf16[2,384,256]{2,1,0:T(8,128)(2,1)S(1)}, bf16[2,384,256]{2,1,0:T(8,128)(2,1)S(1)}, u32[]{:S(2)}, u32[]{:S(2)}) collective-permute-start(bf16[2,384,256]{2,1,0:T(8,128)(2,1)S(1)} %bitcast.5), channel_id=1, source_target_pairs={{0,1},{1,0},{2,3},{3,2},{4,5},{5,4},{6,7},{7,6},{8,9},{9,8},{10,11... | collective-permute-start | bytes 1179656 | tf_op jit(solution)/shard_map/ppermute | solution.py:118
  30.4 2.1 %collective-permute-start.6 = (bf16[2,384,256]{2,1,0:T(8,128)(2,1)S(1)}, bf16[2,384,256]{2,1,0:T(8,128)(2,1)S(1)}, u32[]{:S(2)}, u32[]{:S(2)}) collective-permute-start(bf16[2,384,256]{2,1,0:T(8,128)(2,1)S(1)} %middle.1.a_ref.mid_ref), channel_id=1, source_target_pairs={{0,1},{1,0},{2,3},{3,2},{4,5},{5,4},{6,7},{7,6},{8,9},{9,8},{10,11... | collective-permute-start | bytes 1179656 | tf_op jit(solution)/shard_map/ppermute | solution.py:118
  33.9 1.8 %collective-permute-start.13 = (bf16[2,384,256]{2,1,0:T(8,128)(2,1)S(1)}, bf16[2,384,256]{2,1,0:T(8,128)(2,1)S(1)}, u32[]{:S(2)}, u32[]{:S(2)}) collective-permute-start(bf16[2,384,256]{2,1,0:T(8,128)(2,1)S(1)} %get-tuple-element.81), channel_id=1, source_target_pairs={{0,1},{1,0},{2,3},{3,2},{4,5},{5,4},{6,7},{7,6},{8,9},{9,8},{10,11... | collective-permute-start | bytes 1179656 | tf_op jit(solution)/shard_map/ppermute | solution.py:118
  35.8 11.2 %collective-permute-start.14 = (bf16[2,384,256]{2,1,0:T(8,128)(2,1)S(1)}, bf16[2,384,256]{2,1,0:T(8,128)(2,1)S(1)}, u32[]{:S(2)}, u32[]{:S(2)}) collective-permute-start(bf16[2,384,256]{2,1,0:T(8,128)(2,1)S(1)} %squash_sum.1.chip_ref), channel_id=1, source_target_pairs={{0,2},{1,3},{2,0},{3,1},{4,6},{5,7},{6,4},{7,5},{8,10},{9,11},{10,... | collective-permute-start | bytes 1179656 | tf_op jit(solution)/shard_map/ppermute | solution.py:118
  36.4 15.0 %collective-permute-start.20 = (bf16[2,192,384]{2,1,0:T(8,128)(2,1)S(1)}, bf16[2,192,384]{2,1,0:T(8,128)(2,1)S(1)}, u32[]{:S(2)}, u32[]{:S(2)}) collective-permute-start(bf16[2,192,384]{2,1,0:T(8,128)(2,1)S(1)} %get-tuple-element.97), channel_id=1, source_target_pairs={{0,4},{4,0},{8,12},{12,8},{1,5},{5,1},{9,13},{13,9},{2,6},{6,2},{1... | collective-permute-start | bytes 884744 | tf_op jit(solution)/shard_map/ppermute | solution.py:118
  38.0 15.8 %collective-permute-start.22 = (bf16[2,192,384]{2,1,0:T(8,128)(2,1)S(1)}, bf16[2,192,384]{2,1,0:T(8,128)(2,1)S(1)}, u32[]{:S(2)}, u32[]{:S(2)}) collective-permute-start(bf16[2,192,384]{2,1,0:T(8,128)(2,1)S(1)} %get-tuple-element.102), channel_id=1, source_target_pairs={{0,8},{4,12},{8,0},{12,4},{1,9},{5,13},{9,1},{13,5},{2,10},{6,14},... | collective-permute-start | bytes 884744 | tf_op jit(solution)/shard_map/ppermute | solution.py:118
  47.7 1.5 %collective-permute-start.15 = (bf16[384,256]{1,0:T(8,128)(2,1)S(1)}, bf16[384,256]{1,0:T(8,128)(2,1)S(1)}, u32[]{:S(2)}, u32[]{:S(2)}) collective-permute-start(bf16[384,256]{1,0:T(8,128)(2,1)S(1)} %get-tuple-element.86.refs_0_.g_ref.g0), channel_id=1, source_target_pairs={{0,1},{1,0},{2,3},{3,2},{4,5},{5,4},{6,7},{7,6},{8,9},{9,8},{10,11... | collective-permute-start | bytes 589832 | tf_op jit(solution)/shard_map/ppermute | solution.py:118
  47.8 1.7 %collective-permute-start.16 = (bf16[384,256]{1,0:T(8,128)(2,1)S(1)}, bf16[384,256]{1,0:T(8,128)(2,1)S(1)}, u32[]{:S(2)}, u32[]{:S(2)}) collective-permute-start(bf16[384,256]{1,0:T(8,128)(2,1)S(1)} %get-tuple-element.87.refs_2_.g2), channel_id=1, source_target_pairs={{0,1},{1,0},{2,3},{3,2},{4,5},{5,4},{6,7},{7,6},{8,9},{9,8},{10,11... | collective-permute-start | bytes 589832 | tf_op jit(solution)/shard_map/ppermute | solution.py:118
  48.3 6.8 %collective-permute-start.11 = (bf16[2,384,256]{2,1,0:T(8,128)(2,1)S(1)}, bf16[2,384,256]{2,1,0:T(8,128)(2,1)S(1)}, u32[]{:S(2)}, u32[]{:S(2)}) collective-permute-start(bf16[2,384,256]{2,1,0:T(8,128)(2,1)S(1)} %get-tuple-element.77), channel_id=1, source_target_pairs={{0,1},{1,0},{2,3},{3,2},{4,5},{5,4},{6,7},{7,6},{8,9},{9,8},{10,11... | collective-permute-start | bytes 1179656 | tf_op jit(solution)/shard_map/ppermute | solution.py:118
  50.6 6.9 %collective-permute-start.17 = (bf16[384,256]{1,0:T(8,128)(2,1)S(1)}, bf16[384,256]{1,0:T(8,128)(2,1)S(1)}, u32[]{:S(2)}, u32[]{:S(2)}) collective-permute-start(bf16[384,256]{1,0:T(8,128)(2,1)S(1)} %get-tuple-element.90), channel_id=1, source_target_pairs={{0,1},{1,0},{2,3},{3,2},{4,5},{5,4},{6,7},{7,6},{8,9},{9,8},{10,11... | collective-permute-start | bytes 589832 | tf_op jit(solution)/shard_map/ppermute | solution.py:118
  51.8 15.6 %collective-permute-start.21 = (bf16[2,192,384]{2,1,0:T(8,128)(2,1)S(1)}, bf16[2,192,384]{2,1,0:T(8,128)(2,1)S(1)}, u32[]{:S(2)}, u32[]{:S(2)}) collective-permute-start(bf16[2,192,384]{2,1,0:T(8,128)(2,1)S(1)} %get-tuple-element.99), channel_id=1, source_target_pairs={{0,4},{4,0},{8,12},{12,8},{1,5},{5,1},{9,13},{13,9},{2,6},{6,2},{1... | collective-permute-start | bytes 884744 | tf_op jit(solution)/shard_map/ppermute | solution.py:118
  54.3 21.7 %collective-permute-start.23 = (bf16[2,192,384]{2,1,0:T(8,128)(2,1)S(1)}, bf16[2,192,384]{2,1,0:T(8,128)(2,1)S(1)}, u32[]{:S(2)}, u32[]{:S(2)}) collective-permute-start(bf16[2,192,384]{2,1,0:T(8,128)(2,1)S(1)} %get-tuple-element.104), channel_id=1, source_target_pairs={{0,8},{4,12},{8,0},{12,4},{1,9},{5,13},{9,1},{13,5},{2,10},{6,14},... | collective-permute-start | bytes 884744 | tf_op jit(solution)/shard_map/ppermute | solution.py:118
  54.9 3.1 %collective-permute-start.18 = (bf16[384,256]{1,0:T(8,128)(2,1)S(1)}, bf16[384,256]{1,0:T(8,128)(2,1)S(1)}, u32[]{:S(2)}, u32[]{:S(2)}) collective-permute-start(bf16[384,256]{1,0:T(8,128)(2,1)S(1)} %get-tuple-element.91), channel_id=1, source_target_pairs={{0,1},{1,0},{2,3},{3,2},{4,5},{5,4},{6,7},{7,6},{8,9},{9,8},{10,11... | collective-permute-start | bytes 589832 | tf_op jit(solution)/shard_map/ppermute | solution.py:118
  55.1 20.9 %collective-permute-start.24 = (bf16[192,384]{1,0:T(8,128)(2,1)S(1)}, bf16[192,384]{1,0:T(8,128)(2,1)S(1)}, u32[]{:S(2)}, u32[]{:S(2)}) collective-permute-start(bf16[192,384]{1,0:T(8,128)(2,1)S(1)} %get-tuple-element.105), channel_id=1, source_target_pairs={{0,8},{4,12},{8,0},{12,4},{1,9},{5,13},{9,1},{13,5},{2,10},{6,14},... | collective-permute-start | bytes 442376 | tf_op jit(solution)/shard_map/ppermute | solution.py:118
  57.5 18.5 %collective-permute-start.25 = (bf16[192,384]{1,0:T(8,128)(2,1)S(1)}, bf16[192,384]{1,0:T(8,128)(2,1)S(1)}, u32[]{:S(2)}, u32[]{:S(2)}) collective-permute-start(bf16[192,384]{1,0:T(8,128)(2,1)S(1)} %get-tuple-element.107), channel_id=1, source_target_pairs={{0,4},{4,0},{8,12},{12,8},{1,5},{5,1},{9,13},{13,9},{2,6},{6,2},{1... | collective-permute-start | bytes 442376 | tf_op jit(solution)/shard_map/ppermute | solution.py:118
  58.0 23.1 %collective-permute-start.12 = (bf16[384,256]{1,0:T(8,128)(2,1)S(1)}, bf16[384,256]{1,0:T(8,128)(2,1)S(1)}, u32[]{:S(2)}, u32[]{:S(2)}) collective-permute-start(bf16[384,256]{1,0:T(8,128)(2,1)S(1)} %get-tuple-element.79), channel_id=1, source_target_pairs={{0,2},{1,3},{2,0},{3,1},{4,6},{5,7},{6,4},{7,5},{8,10},{9,11},{10,... | collective-permute-start | bytes 589832 | tf_op jit(solution)/shard_map/ppermute | solution.py:118
  67.5 14.4 %collective-permute-start.19 = (bf16[384,256]{1,0:T(8,128)(2,1)S(1)}, bf16[384,256]{1,0:T(8,128)(2,1)S(1)}, u32[]{:S(2)}, u32[]{:S(2)}) collective-permute-start(bf16[384,256]{1,0:T(8,128)(2,1)S(1)} %get-tuple-element.93), channel_id=1, source_target_pairs={{0,2},{1,3},{2,0},{3,1},{4,6},{5,7},{6,4},{7,5},{8,10},{9,11},{10,... | collective-permute-start | bytes 589832 | tf_op jit(solution)/shard_map/ppermute | solution.py:118
  76.0 8.0 %collective-permute-start.26 = (bf16[192,384]{1,0:T(8,128)(2,1)S(1)}, bf16[192,384]{1,0:T(8,128)(2,1)S(1)}, u32[]{:S(2)}, u32[]{:S(2)}) collective-permute-start(bf16[192,384]{1,0:T(8,128)(2,1)S(1)} %get-tuple-element.109), channel_id=1, source_target_pairs={{0,8},{4,12},{8,0},{12,4},{1,9},{5,13},{9,1},{13,5},{2,10},{6,14},... | collective-permute-start | bytes 442376 | tf_op jit(solution)/shard_map/ppermute | solution.py:118
  76.1 8.2 %collective-permute-start.27 = (bf16[192,384]{1,0:T(8,128)(2,1)S(1)}, bf16[192,384]{1,0:T(8,128)(2,1)S(1)}, u32[]{:S(2)}, u32[]{:S(2)}) collective-permute-start(bf16[192,384]{1,0:T(8,128)(2,1)S(1)} %get-tuple-element.110), channel_id=1, source_target_pairs={{0,4},{4,0},{8,12},{12,8},{1,5},{5,1},{9,13},{13,9},{2,6},{6,2},{1... | collective-permute-start | bytes 442376 | tf_op jit(solution)/shard_map/ppermute | solution.py:118

commit v9 on v7

--- a/solution.py
+++ b/solution.py
@@ -143,7 +143,7 @@
 VMEM = pl.BlockSpec(memory_space=pltpu.VMEM)
 
 
-def call(body, outs, args, name, scratch=(), final=False):
+def call(body, outs, args, name, scratch=(), final=False, alias=None):
     struct = jax.ShapeDtypeStruct if final else pltpu.VMEM
     return pl.pallas_call(
         body,
@@ -151,6 +151,7 @@
         in_specs=[VMEM] * len(args),
         out_specs=[VMEM] * len(outs),
         scratch_shapes=scratch,
+        input_output_aliases=alias or {},
         compiler_params=pltpu.CompilerParams(vmem_limit_bytes=16 << 20),
         name=name,
     )(*[pltpu.with_memory_space_constraint(a, pltpu.VMEM) for a in args])
@@ -196,7 +197,25 @@
             for source in (x, taps_a, taps_b, point_a.T, point_b.T, grad_heads)
         ]
     )
-    x_far, x_own = lax.optimization_barrier((x_far, x_own))
+
+    def conv(refs, js, m, k_ref, z_ref, u):
+        for ref, j in zip(refs, js):
+            z = gelu(ref[...].astype(F32)).astype(BF16)
+            z_ref[j] = z
+            part = dot(k_ref[:, block(m, j)], z)
+            u = part if u is None else u + part
+        return u
+
+    stack = ((4, rows, bins), BF16)
+    inner = (hid, bins)
+
+    def near_forward_body(x0, x1, k_ref, z_ref, u_ref):
+        u_ref[...] = conv((x0, x1), (0, 1), lax.axis_index("mp"), k_ref, z_ref, None)
+
+    z_a, u_a = call(
+        near_forward_body, [stack, (inner, F32)], (x_own, x_near, tap_a), "near_forward"
+    )
+    x_far, u_a = lax.optimization_barrier((x_far, u_a))
     x_cross = swap(x_far, "mp", 1)
 
     def split_body(own_ref, far_ref, *outs):
@@ -220,34 +239,37 @@
     g_pair = g_pair.reshape(2, rows, bins)
     g_near = swap(g_pair, "mp", 1)
 
-    def first_body(x0, x1, x2, x3, k_ref, p_ref, _, z_ref, v_ref, s_ref, keep_ref, send_ref):
+    def near_half(w_ref, v, m, send_ref):
+        for i, j in enumerate((1, 3)):
+            send_ref[i] = dot(w_ref[:, block(m, j)], v, ((0,), (0,))).astype(BF16)
+
+    def own_half(w_ref, v, m, keep_ref):
+        for i, j in enumerate((0, 2)):
+            keep_ref[i] = dot(w_ref[:, block(m, j)], v, ((0,), (0,)))
+
+    def keep_body(w_ref, v_ref, keep_ref):
+        own_half(w_ref, v_ref[...], lax.axis_index("mp"), keep_ref)
+
+    def kept(w, v, name):
+        return call(keep_body, [((2, rows, bins), F32)], (w, v), name)[0]
+
+    def first_body(x2, x3, k_ref, p_ref, _, u_ref, zin_ref, z_ref, v_ref, s_ref, send_ref):
         m = lax.axis_index("mp")
-        u = jnp.zeros((hid, bins), F32)
-        for j, ref in enumerate((x0, x1, x2, x3)):
-            z = gelu(ref[...].astype(F32)).astype(BF16)
-            z_ref[j] = z
-            u = u + dot(k_ref[:, block(m, j)], z)
+        u = conv((x2, x3), (2, 3), m, k_ref, z_ref, u_ref[...])
         v, slope = gelu_and_slope(u)
         v = v.astype(BF16)
         v_ref[...] = v
         s_ref[...] = slope
-        for i, j in enumerate((1, 3)):
-            send_ref[i] = dot(p_ref[:, block(m, j)], v, ((0,), (0,))).astype(BF16)
-        for i, j in enumerate((0, 2)):
-            keep_ref[i] = dot(p_ref[:, block(m, j)], v, ((0,), (0,)))
-
-    z_a, v_a, slope_a, keep, send = call(
+        near_half(p_ref, v, m, send_ref)
+
+    z_a, v_a, slope_a, send = call(
         first_body,
-        [
-            ((4, rows, bins), BF16),
-            ((hid, bins), BF16),
-            ((hid, bins), F32),
-            ((2, rows, bins), F32),
-            ((2, rows, bins), BF16),
-        ],
-        (x_own, x_near, x_far, x_cross, tap_a, cols_a, raw_far),
+        [stack, (inner, BF16), (inner, F32), ((2, rows, bins), BF16)],
+        (x_far, x_cross, tap_a, cols_a, raw_far, u_a, z_a),
         "first_forward",
-    )
+        alias={6: 0},
+    )
+    keep = kept(cols_a, v_a, "mix_keep")
     got = swap(send, "mp", 1)
 
     def mix_body(keep_ref, got_ref, out_ref):
@@ -266,48 +288,47 @@
     )
     mid_near = swap(mid, "mp", 1)
 
+    def own_block_body(a_ref, g_ref, k_ref, p_ref, z_ref, u_ref, gv_ref):
+        m = lax.axis_index("mp")
+        parts = (a_ref.at[0], a_ref.at[1])
+        u_ref[...] = conv(parts, (0, 2), m, k_ref, z_ref, None)
+        gv = dot(p_ref[:, block(m, 0)], g_ref[0])
+        gv_ref[...] = gv + dot(p_ref[:, block(m, 2)], g_ref[1])
+
+    z_b, u_b, gv_b = call(
+        own_block_body,
+        [stack, (inner, F32), (inner, F32)],
+        (mid, g_pair, tap_b, cols_b),
+        "own_block",
+    )
+
     def second_body(
-        a_ref, b_ref, ga_ref, gb_ref, k_ref, p_ref,
-        z_ref, v_ref, gu_ref, keep_ref, send_ref, ykeep_ref, ysend_ref,
+        b_ref, g_ref, k_ref, p_ref, u_ref, gv_ref, zin_ref, z_ref, v_ref, gu_ref, send_ref
     ):
         m = lax.axis_index("mp")
-        u = jnp.zeros((hid, bins), F32)
-        for j in range(4):
-            part = (a_ref, b_ref)[j & 1][j >> 1]
-            z = gelu(part.astype(F32)).astype(BF16)
-            z_ref[j] = z
-            u = u + dot(k_ref[:, block(m, j)], z)
+        u = conv((b_ref.at[0], b_ref.at[1]), (1, 3), m, k_ref, z_ref, u_ref[...])
         v, slope = gelu_and_slope(u)
-        v = v.astype(BF16)
-        v_ref[...] = v
-        gv = jnp.zeros((hid, bins), F32)
-        for j in range(4):
-            gv = gv + dot(p_ref[:, block(m, j)], (ga_ref, gb_ref)[j & 1][j >> 1])
+        v_ref[...] = v.astype(BF16)
+        gv = gv_ref[...] + dot(p_ref[:, block(m, 1)], g_ref[0])
+        gv = gv + dot(p_ref[:, block(m, 3)], g_ref[1])
         gu = (gv * slope).astype(BF16)
         gu_ref[...] = gu
-        for i, j in enumerate((1, 3)):
-            send_ref[i] = dot(k_ref[:, block(m, j)], gu, ((0,), (0,))).astype(BF16)
-        for i, j in enumerate((0, 2)):
-            keep_ref[i] = dot(k_ref[:, block(m, j)], gu, ((0,), (0,)))
-        for i, j in enumerate((1, 3)):
-            ysend_ref[i] = dot(p_ref[:, block(m, j)], v, ((0,), (0,))).astype(BF16)
-        for i, j in enumerate((0, 2)):
-            ykeep_ref[i] = dot(p_ref[:, block(m, j)], v, ((0,), (0,)))
-
-    z_b, v_b, gu_b, keep, send, ykeep, ysend = call(
+        near_half(k_ref, gu, m, send_ref)
+
+    z_b, v_b, gu_b, send = call(
         second_body,
-        [
-            ((4, rows, bins), BF16),
-            ((hid, bins), BF16),
-            ((hid, bins), BF16),
-            ((2, rows, bins), F32),
-            ((2, rows, bins), BF16),
-            ((2, rows, bins), F32),
-            ((2, rows, bins), BF16),
-        ],
-        (mid, mid_near, g_pair, g_near, tap_b, cols_b),
+        [stack, (inner, BF16), (inner, BF16), ((2, rows, bins), BF16)],
+        (mid_near, g_near, tap_b, cols_b, u_b, gv_b, z_b),
         "second_block",
-    )
+        alias={6: 0},
+    )
+    keep = kept(tap_b, gu_b, "squash_keep")
+
+    def output_body(p_ref, v_ref, keep_ref, send_ref):
+        m = lax.axis_index("mp")
+        near_half(p_ref, v_ref[...], m, send_ref)
+        own_half(p_ref, v_ref[...], m, keep_ref)
+
     def place(k):
         return lax.axis_index("mp") ^ lax.axis_index("ctx") ^ k
 
@@ -434,6 +455,12 @@
     )
     g_mid = [g_mid[0], swap(g_mid[0], "mp", 1), g_mid[1], swap(g_mid[1], "mp", 1)]
 
+    ykeep, ysend = call(
+        output_body,
+        [((2, rows, bins), F32), ((2, rows, bins), BF16)],
+        (cols_b, v_b),
+        "output_product",
+    )
     ygot = swap(ysend, "mp", 1)
 
     def last_sum_body(keep_ref, got_ref, *rest):
@@ -455,24 +482,22 @@
     (second_out,) = call(out_body, [((rows, bins), BF16)], (mid, y_own, y_got), "out", final=True)
 
     def first_back_body(*refs):
-        grads, (k_ref, p_ref, s_ref, gu_ref, keep_ref, send_ref) = refs[:4], refs[4:]
+        grads, (k_ref, p_ref, s_ref, gu_ref, send_ref) = refs[:4], refs[4:]
         m = lax.axis_index("mp")
         gv = jnp.zeros((hid, bins), F32)
         for j in range(4):
             gv = gv + dot(p_ref[:, block(m, j)], grads[j][...])
         gu = (gv * s_ref[...]).astype(BF16)
         gu_ref[...] = gu
-        for i, j in enumerate((1, 3)):
-            send_ref[i] = dot(k_ref[:, block(m, j)], gu, ((0,), (0,))).astype(BF16)
-        for i, j in enumerate((0, 2)):
-            keep_ref[i] = dot(k_ref[:, block(m, j)], gu, ((0,), (0,)))
-
-    gu_a, keep, send = call(
+        near_half(k_ref, gu, m, send_ref)
+
+    gu_a, send = call(
         first_back_body,
-        [((hid, bins), BF16), ((2, rows, bins), F32), ((2, rows, bins), BF16)],
+        [(inner, BF16), ((2, rows, bins), BF16)],
         (*g_mid, tap_a, cols_a, slope_a),
         "first_backward",
     )
+    keep = kept(tap_a, gu_a, "entry_keep")
     keep_ap, send_p, own_bk = call(
         first_proj_body,
         [(two, F32), (three, BF16), (one, F32)],

time: 84.2 us -> 83.5 us (level)
  waiting for transfers between devices: 48.1 us -> 46.6 us
  Pallas kernels: 13.1 us -> 14 us
    ppermute x25, waiting for transfers between devices: 48.1 us -> 46.6 us  [swap(): return lax.ppermute(value, axis, [(i, i ^ bits) for i in range(size)])]
    pallas_call x18 -> x24, Pallas kernels: 8.5 us -> 9.46 us  [call(): pl.pallas_call(body, out_shape=[struct(s, d) for s, d in outs], in_specs=...]
  transfers between devices with their start and end apart: 25 -> 25, of which waited for: 15 -> 15; matrix products, arithmetic and copies ran while one was open for 0% -> 0% of each run, Pallas kernels for 11% -> 14%
where the time goes in v9:
time: 83.5 us; the launch traced here: 83.4 us
  waiting for transfers between devices  46.6 us (56%)
  starting transfers between devices  21.9 us (26%)
  Pallas kernels  14 us (17%)
  between operations  0.86 us (1%)
    ppermute x25, waiting for transfers between devices, swap(): return lax.ppermute(value, axis, [(i, i ^ bits) for i in range(size)])  46.6 us
    ppermute x25, starting transfers between devices, swap(): return lax.ppermute(value, axis, [(i, i ^ bits) for i in range(size)])  21.9 us
    pallas_call x24, Pallas kernels, call(): pl.pallas_call(body, out_shape=[struct(s, d) for s, d in outs], in_specs=...  9.46 us
    pallas_call x1, Pallas kernels, fast_shards(): pl.pallas_call(load_body, out_shape=[pltpu.VMEM((rows, bins), BF16)] + [p...  1.79 us
    pallas_call x2, Pallas kernels, total(): pl.pallas_call(functools.partial(total_body, place), out_shape=[jax.Shape...  1.71 us
  transfers between devices with their start and end apart: 25, of which 15 were waited for; matrix products, arithmetic and copies ran while one was open for 0% of the time, Pallas kernels for 14%

profile of v9, /device:TPU:0, one launch (start us, length us, event | category | flops | bytes accessed | tf_op | source)
XLA Modules:
  0.0 83.4 jit_solution(2988401840785064263)
XLA Ops:
  0.6 0.5 collective-permute-start.1
  1.2 2.6 %collective-permute-start = (bf16[384,256]{1,0:T(8,128)(2,1)}, bf16[384,256]{1,0:T(8,128)(2,1)S(1)}, u32[]{:S(2)}, u32[]{:S(2)}) collective-permute-start(bf16[384,256]{1,0:T(8,128)(2,1)} %x_ref.1), channel_id=1, source_target_pairs={{0,2},{1,3},{2,0},{3,1},{4,6},{5,7},{6,4},{7,5},{8,10},{9,11},{10,... | collective-permute-start | bytes 589832 | tf_op jit(solution)/shard_map/ppermute | solution.py:120
  3.8 1.8 %load.1 = (bf16[384,256]{1,0:T(8,128)(2,1)S(1)}, bf16[192,1536]{1,0:T(8,128)(2,1)S(1)}, bf16[192,1536]{1,0:T(8,128)(2,1)S(1)}, bf16[192,1536]{1,0:T(8,128)(2,1)S...) custom-call(bf16[384,256]{1,0:T(8,128)(2,1)} %x_ref.1, bf16[3,192,1536]{2,1,0:T(8,128)(2,1)} %ta.1, ...), custom_call_target="tpu_custom_call" | custom-call | tf_op jit(solution)/shard_map/load/pallas_call | solution.py:184
  5.6 0.5 near_forward.1
  6.1 3.6 %collective-permute-done.x2 = bf16[384,256]{1,0:T(8,128)(2,1)S(1)} collective-permute-done((bf16[384,256]{1,0:T(8,128)(2,1)}, bf16[384,256]{1,0:T(8,128)(2,1)S(1)}, u32[]{:S(2)}, u32[]{:S(2)}) %collective-permute-start) | collective-permute-done | bytes 196640 | tf_op jit(solution)/shard_map/ppermute | solution.py:120
  9.7 4.0 %collective-permute-done.3._.far_ref = bf16[2,48,1024]{2,1,0:T(8,128)(2,1)S(1)} collective-permute-done((bf16[2,48,1024]{2,1,0:T(8,128)(2,1)}, bf16[2,48,1024]{2,1,0:T(8,128)(2,1)S(1)}, u32[]{:S(2)}, u32[]{:S(2)}) %collective-permute-start.3) | collective-permute-done | bytes 196640 | tf_op jit(solution)/shard_map/ppermute | solution.py:120
  13.6 0.9 %first_forward.1 = (bf16[4,384,256]{2,1,0:T(8,128)(2,1)S(1)}, bf16[192,256]{1,0:T(8,128)(2,1)S(1)}, f32[192,256]{1,0:T(8,128)S(1)}, bf16[2,384,256]{2,1,0:T(8,128)(2,1)S(1)}) custom-call(bf16[384,256]{1,0:T(8,128)(2,1)S(1)} %collective-permute-done.x2, bf16[384,256]{1,0:T(8,128)(2,1)S(1)} %collective-permute-done.2.x3, ...), custom_call_target="tpu_custom_call", output_to_operand_aliasing={{0}: (6, {})} | custom-call | tf_op jit(solution)/shard_map/first_forward/pallas_call | solution.py:148
  14.6 0.3 mix_keep.1.keep_ref
  14.9 1.4 %collective-permute-done.4.got_ref = bf16[2,384,256]{2,1,0:T(8,128)(2,1)S(1)} collective-permute-done((bf16[2,384,256]{2,1,0:T(8,128)(2,1)S(1)}, bf16[2,384,256]{2,1,0:T(8,128)(2,1)S(1)}, u32[]{:S(2)}, u32[]{:S(2)}) %collective-permute-start.4) | collective-permute-done | bytes 393248 | tf_op jit(solution)/shard_map/ppermute | solution.py:120
  16.4 1.8 %collective-permute-start.5 = (bf16[2,384,256]{2,1,0:T(8,128)(2,1)S(1)}, bf16[2,384,256]{2,1,0:T(8,128)(2,1)S(1)}, u32[]{:S(2)}, u32[]{:S(2)}) collective-permute-start(bf16[2,384,256]{2,1,0:T(8,128)(2,1)S(1)} %mix_sum.1.chip_ref), channel_id=1, source_target_pairs={{0,2},{1,3},{2,0},{3,1},{4,6},{5,7},{6,4},{7,5},{8,10},{9,11},{10,... | collective-permute-start | bytes 1179656 | tf_op jit(solution)/shard_map/ppermute | solution.py:120
  18.2 1.6 %collective-permute-start.7 = (bf16[2,2,48,256]{3,2,1,0:T(8,128)(2,1)S(1)}, bf16[2,2,48,256]{3,2,1,0:T(8,128)(2,1)S(1)}, u32[]{:S(2)}, u32[]{:S(2)}) collective-permute-start(bf16[2,2,48,256]{3,2,1,0:T(8,128)(2,1)S(1)} %get-tuple-element.73), channel_id=1, source_target_pairs={{0,4},{4,0},{8,12},{12,8},{1,5},{5,1},{9,13},{13,9},{2,6},{6,2},{1... | collective-permute-start | bytes 294920 | tf_op jit(solution)/shard_map/ppermute | solution.py:120
  19.9 2.6 %collective-permute-start.8 = (bf16[2,2,48,256]{3,2,1,0:T(8,128)(2,1)S(1)}, bf16[2,2,48,256]{3,2,1,0:T(8,128)(2,1)S(1)}, u32[]{:S(2)}, u32[]{:S(2)}) collective-permute-start(bf16[2,2,48,256]{3,2,1,0:T(8,128)(2,1)S(1)} %get-tuple-element.74), channel_id=1, source_target_pairs={{0,8},{4,12},{8,0},{12,4},{1,9},{5,13},{9,1},{13,5},{2,10},{6,14},... | collective-permute-start | bytes 294920 | tf_op jit(solution)/shard_map/ppermute | solution.py:120
  22.9 7.4 %collective-permute-done.8.refs_2_ = bf16[2,2,48,256]{3,2,1,0:T(8,128)(2,1)S(1)} collective-permute-done((bf16[2,2,48,256]{3,2,1,0:T(8,128)(2,1)S(1)}, bf16[2,2,48,256]{3,2,1,0:T(8,128)(2,1)S(1)}, u32[]{:S(2)}, u32[]{:S(2)}) %collective-permute-start.8) | collective-permute-done | bytes 98336 | tf_op jit(solution)/shard_map/ppermute | solution.py:120
  30.6 0.5 collective-permute-start.6
  31.2 0.5 own_block.1
  31.6 0.5 collective-permute-done.10.g_ref.gb_ref
  32.2 0.6 collective-permute-done.6.b_ref
  32.7 0.8 second_block.1
  33.8 0.3 squash_keep.1.keep_ref
  34.1 0.7 second_weights.1
  34.8 0.5 collective-permute-done.13.got_ref
  35.4 0.6 collective-permute-start.14
  36.0 1.6 %collective-permute-start.21 = (bf16[2,192,384]{2,1,0:T(8,128)(2,1)S(1)}, bf16[2,192,384]{2,1,0:T(8,128)(2,1)S(1)}, u32[]{:S(2)}, u32[]{:S(2)}) collective-permute-start(bf16[2,192,384]{2,1,0:T(8,128)(2,1)S(1)} %get-tuple-element.102), channel_id=1, source_target_pairs={{0,4},{4,0},{8,12},{12,8},{1,5},{5,1},{9,13},{13,9},{2,6},{6,2},{1... | collective-permute-start | bytes 884744 | tf_op jit(solution)/shard_map/ppermute | solution.py:120
  37.6 1.4 %collective-permute-start.19 = (bf16[2,192,384]{2,1,0:T(8,128)(2,1)S(1)}, bf16[2,192,384]{2,1,0:T(8,128)(2,1)S(1)}, u32[]{:S(2)}, u32[]{:S(2)}) collective-permute-start(bf16[2,192,384]{2,1,0:T(8,128)(2,1)S(1)} %get-tuple-element.99), channel_id=1, source_target_pairs={{0,8},{4,12},{8,0},{12,4},{1,9},{5,13},{9,1},{13,5},{2,10},{6,14},... | collective-permute-start | bytes 884744 | tf_op jit(solution)/shard_map/ppermute | solution.py:120
  39.1 7.6 %collective-permute-done.14.other_ref = bf16[2,384,256]{2,1,0:T(8,128)(2,1)S(1)} collective-permute-done((bf16[2,384,256]{2,1,0:T(8,128)(2,1)S(1)}, bf16[2,384,256]{2,1,0:T(8,128)(2,1)S(1)}, u32[]{:S(2)}, u32[]{:S(2)}) %collective-permute-start.14) | collective-permute-done | bytes 393248 | tf_op jit(solution)/shard_map/ppermute | solution.py:120
  46.7 0.6 middle_grad.1
  47.4 0.5 collective-permute-start.16
  47.9 0.4 output_product.1
  48.4 0.4 collective-permute-done.15.refs_1_.g1
  49.1 0.8 first_backward.1
  50.2 0.8 %collective-permute-done.21.got_b = bf16[2,192,384]{2,1,0:T(8,128)(2,1)S(1)} collective-permute-done((bf16[2,192,384]{2,1,0:T(8,128)(2,1)S(1)}, bf16[2,192,384]{2,1,0:T(8,128)(2,1)S(1)}, u32[]{:S(2)}, u32[]{:S(2)}) %collective-permute-start.21) | collective-permute-done | bytes 294944 | tf_op jit(solution)/shard_map/ppermute | solution.py:120
  51.0 0.5 first_proj.1
  51.5 1.9 %collective-permute-start.22 = (bf16[3,192,384]{2,1,0:T(8,128)(2,1)S(1)}, bf16[3,192,384]{2,1,0:T(8,128)(2,1)S(1)}, u32[]{:S(2)}, u32[]{:S(2)}) collective-permute-start(bf16[3,192,384]{2,1,0:T(8,128)(2,1)S(1)} %get-tuple-element.104), channel_id=1, source_target_pairs={{0,8},{4,12},{8,0},{12,4},{1,9},{5,13},{9,1},{13,5},{2,10},{6,14},... | collective-permute-start | bytes 1327112 | tf_op jit(solution)/shard_map/ppermute | solution.py:120
  53.4 0.5 first_taps.1
  53.9 0.5 collective-permute-start.20
  54.5 1.6 %collective-permute-start.12 = (bf16[384,256]{1,0:T(8,128)(2,1)S(1)}, bf16[384,256]{1,0:T(8,128)(2,1)S(1)}, u32[]{:S(2)}, u32[]{:S(2)}) collective-permute-start(bf16[384,256]{1,0:T(8,128)(2,1)S(1)} %get-tuple-element.84), channel_id=1, source_target_pairs={{0,2},{1,3},{2,0},{3,1},{4,6},{5,7},{6,4},{7,5},{8,10},{9,11},{10,... | collective-permute-start | bytes 589832 | tf_op jit(solution)/shard_map/ppermute | solution.py:120
  56.1 0.3 entry_keep.1.keep_ref
  56.5 0.6 collective-permute-start.18
  57.0 16.6 %collective-permute-done.22.got.got_k = bf16[3,192,384]{2,1,0:T(8,128)(2,1)S(1)} collective-permute-done((bf16[3,192,384]{2,1,0:T(8,128)(2,1)S(1)}, bf16[3,192,384]{2,1,0:T(8,128)(2,1)S(1)}, u32[]{:S(2)}, u32[]{:S(2)}) %collective-permute-start.22) | collective-permute-done | bytes 442400 | tf_op jit(solution)/shard_map/ppermute | solution.py:120
  73.7 0.7 collective-permute-done.20.got.got_p
  74.4 0.9 %collective-permute-start.23 = (bf16[192,384]{1,0:T(8,128)(2,1)S(1)}, bf16[192,384]{1,0:T(8,128)(2,1)S(1)}, u32[]{:S(2)}, u32[]{:S(2)}) collective-permute-start(bf16[192,384]{1,0:T(8,128)(2,1)S(1)} %get-tuple-element.107), channel_id=1, source_target_pairs={{0,8},{4,12},{8,0},{12,4},{1,9},{5,13},{9,1},{13,5},{2,10},{6,14},... | collective-permute-start | bytes 442376 | tf_op jit(solution)/shard_map/ppermute | solution.py:120
  75.3 1.5 %collective-permute-start.24 = (bf16[192,384]{1,0:T(8,128)(2,1)S(1)}, bf16[192,384]{1,0:T(8,128)(2,1)S(1)}, u32[]{:S(2)}, u32[]{:S(2)}) collective-permute-start(bf16[192,384]{1,0:T(8,128)(2,1)S(1)} %get-tuple-element.108), channel_id=1, source_target_pairs={{0,4},{4,0},{8,12},{12,8},{1,5},{5,1},{9,13},{13,9},{2,6},{6,2},{1... | collective-permute-start | bytes 442376 | tf_op jit(solution)/shard_map/ppermute | solution.py:120
  76.7 1.1 %zero_planes.1 = (f32[3,192,384]{2,1,0:T(8,128)}, f32[3,192,384]{2,1,0:T(8,128)}) custom-call(), custom_call_target="tpu_custom_call" | custom-call | tf_op jit(solution)/shard_map/zero_planes/pallas_call | solution.py:419
  77.8 0.7 out.1
  78.5 0.9 %second_total.1 = (f32[3,192,384]{2,1,0:T(8,128)}, f32[192,384]{1,0:T(8,128)}) custom-call(f32[3,192,384]{2,1,0:T(8,128)} %get-tuple-element.111._, f32[1,192,384]{2,1,0:T(8,128)S(1)} %get-tuple-element.112.own_k, f32[1,192,384]{2,1,0:T(8,128)S(1)} %get-tuple-element.113.own_p, ...), custom_call_target="tpu_custom_call", output_to_operand_aliasing={{0}: (0, {})} | custom-call | tf_op jit(solution)/shard_map/second_total/pallas_call | solution.py:401
  79.4 1.0 %entry.1 = bf16[384,256]{1,0:T(8,128)(2,1)} custom-call(bf16[384,256]{1,0:T(8,128)(2,1)S(1)} %get-tuple-element.89.refs_0_.g_ref.g0, bf16[384,256]{1,0:T(8,128)(2,1)S(1)} %get-tuple-element.61.x0.x_ref, f32[384,256]{1,0:T(8,128)S(1)} %get-tuple-element.94.own_ref, bf16[384,256]{1,0:T(8,128)(2,1)S(1)} %collective-permute-done.18.got_ref), custom_call_target="tpu_custom_call" | custom-call | tf_op jit(solution)/shard_map/entry/pallas_call | solution.py:148
  80.4 2.1 %collective-permute-done.23.got_k = bf16[192,384]{1,0:T(8,128)(2,1)S(1)} collective-permute-done((bf16[192,384]{1,0:T(8,128)(2,1)S(1)}, bf16[192,384]{1,0:T(8,128)(2,1)S(1)}, u32[]{:S(2)}, u32[]{:S(2)}) %collective-permute-start.23) | collective-permute-done | bytes 147488 | tf_op jit(solution)/shard_map/ppermute | solution.py:120
  82.5 0.9 %first_total.1 = (f32[3,192,384]{2,1,0:T(8,128)}, f32[192,384]{1,0:T(8,128)}) custom-call(f32[3,192,384]{2,1,0:T(8,128)} %get-tuple-element.96._, f32[1,192,384]{2,1,0:T(8,128)S(1)} %get-tuple-element.106.own_k, f32[1,192,384]{2,1,0:T(8,128)S(1)} %get-tuple-element.105.rest_0_.own_p, ...), custom_call_target="tpu_custom_call", output_to_operand_aliasing={{0}: (0, {})} | custom-call | tf_op jit(solution)/shard_map/first_total/pallas_call | solution.py:401
  (30 shorter events, 2.4 us)
Async XLA Ops:
  0.6 5.0 %collective-permute-start.1 = (bf16[384,256]{1,0:T(8,128)(2,1)}, bf16[384,256]{1,0:T(8,128)(2,1)S(1)}, u32[]{:S(2)}, u32[]{:S(2)}) collective-permute-start(bf16[384,256]{1,0:T(8,128)(2,1)} %x_ref.1), channel_id=1, source_target_pairs={{0,1},{1,0},{2,3},{3,2},{4,5},{5,4},{6,7},{7,6},{8,9},{9,8},{10,11... | collective-permute-start | bytes 589832 | tf_op jit(solution)/shard_map/ppermute | solution.py:120
  1.2 8.5 %collective-permute-start = (bf16[384,256]{1,0:T(8,128)(2,1)}, bf16[384,256]{1,0:T(8,128)(2,1)S(1)}, u32[]{:S(2)}, u32[]{:S(2)}) collective-permute-start(bf16[384,256]{1,0:T(8,128)(2,1)} %x_ref.1), channel_id=1, source_target_pairs={{0,2},{1,3},{2,0},{3,1},{4,6},{5,7},{6,4},{7,5},{8,10},{9,11},{10,... | collective-permute-start | bytes 589832 | tf_op jit(solution)/shard_map/ppermute | solution.py:120
  3.7 9.9 %collective-permute-start.3 = (bf16[2,48,1024]{2,1,0:T(8,128)(2,1)}, bf16[2,48,1024]{2,1,0:T(8,128)(2,1)S(1)}, u32[]{:S(2)}, u32[]{:S(2)}) collective-permute-start(bf16[2,48,1024]{2,1,0:T(8,128)(2,1)} %g_ref.1), channel_id=1, source_target_pairs={{0,2},{1,3},{2,0},{3,1},{4,6},{5,7},{6,4},{7,5},{8,10},{9,11},{10,... | collective-permute-start | bytes 589832 | tf_op jit(solution)/shard_map/ppermute | solution.py:120
  9.7 4.0 %collective-permute-start.2 = (bf16[384,256]{1,0:T(8,128)(2,1)S(1)}, bf16[384,256]{1,0:T(8,128)(2,1)S(1)}, u32[]{:S(2)}, u32[]{:S(2)}) collective-permute-start(bf16[384,256]{1,0:T(8,128)(2,1)S(1)} %collective-permute-done.x2), channel_id=1, source_target_pairs={{0,1},{1,0},{2,3},{3,2},{4,5},{5,4},{6,7},{7,6},{8,9},{9,8},{10,11... | collective-permute-start | bytes 589832 | tf_op jit(solution)/shard_map/ppermute | solution.py:120
  14.5 1.8 %collective-permute-start.4 = (bf16[2,384,256]{2,1,0:T(8,128)(2,1)S(1)}, bf16[2,384,256]{2,1,0:T(8,128)(2,1)S(1)}, u32[]{:S(2)}, u32[]{:S(2)}) collective-permute-start(bf16[2,384,256]{2,1,0:T(8,128)(2,1)S(1)} %get-tuple-element.69), channel_id=1, source_target_pairs={{0,1},{1,0},{2,3},{3,2},{4,5},{5,4},{6,7},{7,6},{8,9},{9,8},{10,11... | collective-permute-start | bytes 1179656 | tf_op jit(solution)/shard_map/ppermute | solution.py:120
  16.4 14.1 %collective-permute-start.5 = (bf16[2,384,256]{2,1,0:T(8,128)(2,1)S(1)}, bf16[2,384,256]{2,1,0:T(8,128)(2,1)S(1)}, u32[]{:S(2)}, u32[]{:S(2)}) collective-permute-start(bf16[2,384,256]{2,1,0:T(8,128)(2,1)S(1)} %mix_sum.1.chip_ref), channel_id=1, source_target_pairs={{0,2},{1,3},{2,0},{3,1},{4,6},{5,7},{6,4},{7,5},{8,10},{9,11},{10,... | collective-permute-start | bytes 1179656 | tf_op jit(solution)/shard_map/ppermute | solution.py:120
  18.2 4.7 %collective-permute-start.7 = (bf16[2,2,48,256]{3,2,1,0:T(8,128)(2,1)S(1)}, bf16[2,2,48,256]{3,2,1,0:T(8,128)(2,1)S(1)}, u32[]{:S(2)}, u32[]{:S(2)}) collective-permute-start(bf16[2,2,48,256]{3,2,1,0:T(8,128)(2,1)S(1)} %get-tuple-element.73), channel_id=1, source_target_pairs={{0,4},{4,0},{8,12},{12,8},{1,5},{5,1},{9,13},{13,9},{2,6},{6,2},{1... | collective-permute-start | bytes 294920 | tf_op jit(solution)/shard_map/ppermute | solution.py:120
  19.9 10.4 %collective-permute-start.8 = (bf16[2,2,48,256]{3,2,1,0:T(8,128)(2,1)S(1)}, bf16[2,2,48,256]{3,2,1,0:T(8,128)(2,1)S(1)}, u32[]{:S(2)}, u32[]{:S(2)}) collective-permute-start(bf16[2,2,48,256]{3,2,1,0:T(8,128)(2,1)S(1)} %get-tuple-element.74), channel_id=1, source_target_pairs={{0,8},{4,12},{8,0},{12,4},{1,9},{5,13},{9,1},{13,5},{2,10},{6,14},... | collective-permute-start | bytes 294920 | tf_op jit(solution)/shard_map/ppermute | solution.py:120
  22.5 7.9 %collective-permute-start.9 = (bf16[2,2,48,256]{3,2,1,0:T(8,128)(2,1)S(1)}, bf16[2,2,48,256]{3,2,1,0:T(8,128)(2,1)S(1)}, u32[]{:S(2)}, u32[]{:S(2)}) collective-permute-start(bf16[2,2,48,256]{3,2,1,0:T(8,128)(2,1)S(1)} %get-tuple-element.75), channel_id=1, source_target_pairs={{0,12},{4,8},{8,4},{12,0},{1,13},{5,9},{9,5},{13,1},{2,14},{6,10},... | collective-permute-start | bytes 294920 | tf_op jit(solution)/shard_map/ppermute | solution.py:120
  30.4 1.8 %collective-permute-start.10 = (bf16[2,384,256]{2,1,0:T(8,128)(2,1)S(1)}, bf16[2,384,256]{2,1,0:T(8,128)(2,1)S(1)}, u32[]{:S(2)}, u32[]{:S(2)}) collective-permute-start(bf16[2,384,256]{2,1,0:T(8,128)(2,1)S(1)} %bitcast.5), channel_id=1, source_target_pairs={{0,1},{1,0},{2,3},{3,2},{4,5},{5,4},{6,7},{7,6},{8,9},{9,8},{10,11... | collective-permute-start | bytes 1179656 | tf_op jit(solution)/shard_map/ppermute | solution.py:120
  30.6 2.1 %collective-permute-start.6 = (bf16[2,384,256]{2,1,0:T(8,128)(2,1)S(1)}, bf16[2,384,256]{2,1,0:T(8,128)(2,1)S(1)}, u32[]{:S(2)}, u32[]{:S(2)}) collective-permute-start(bf16[2,384,256]{2,1,0:T(8,128)(2,1)S(1)} %middle.1.a_ref.mid_ref), channel_id=1, source_target_pairs={{0,1},{1,0},{2,3},{3,2},{4,5},{5,4},{6,7},{7,6},{8,9},{9,8},{10,11... | collective-permute-start | bytes 1179656 | tf_op jit(solution)/shard_map/ppermute | solution.py:120
  33.6 1.8 %collective-permute-start.13 = (bf16[2,384,256]{2,1,0:T(8,128)(2,1)S(1)}, bf16[2,384,256]{2,1,0:T(8,128)(2,1)S(1)}, u32[]{:S(2)}, u32[]{:S(2)}) collective-permute-start(bf16[2,384,256]{2,1,0:T(8,128)(2,1)S(1)} %get-tuple-element.86), channel_id=1, source_target_pairs={{0,1},{1,0},{2,3},{3,2},{4,5},{5,4},{6,7},{7,6},{8,9},{9,8},{10,11... | collective-permute-start | bytes 1179656 | tf_op jit(solution)/shard_map/ppermute | solution.py:120
  35.4 11.3 %collective-permute-start.14 = (bf16[2,384,256]{2,1,0:T(8,128)(2,1)S(1)}, bf16[2,384,256]{2,1,0:T(8,128)(2,1)S(1)}, u32[]{:S(2)}, u32[]{:S(2)}) collective-permute-start(bf16[2,384,256]{2,1,0:T(8,128)(2,1)S(1)} %squash_sum.1.chip_ref), channel_id=1, source_target_pairs={{0,2},{1,3},{2,0},{3,1},{4,6},{5,7},{6,4},{7,5},{8,10},{9,11},{10,... | collective-permute-start | bytes 1179656 | tf_op jit(solution)/shard_map/ppermute | solution.py:120
  36.0 15.0 %collective-permute-start.21 = (bf16[2,192,384]{2,1,0:T(8,128)(2,1)S(1)}, bf16[2,192,384]{2,1,0:T(8,128)(2,1)S(1)}, u32[]{:S(2)}, u32[]{:S(2)}) collective-permute-start(bf16[2,192,384]{2,1,0:T(8,128)(2,1)S(1)} %get-tuple-element.102), channel_id=1, source_target_pairs={{0,4},{4,0},{8,12},{12,8},{1,5},{5,1},{9,13},{13,9},{2,6},{6,2},{1... | collective-permute-start | bytes 884744 | tf_op jit(solution)/shard_map/ppermute | solution.py:120
  37.6 15.8 %collective-permute-start.19 = (bf16[2,192,384]{2,1,0:T(8,128)(2,1)S(1)}, bf16[2,192,384]{2,1,0:T(8,128)(2,1)S(1)}, u32[]{:S(2)}, u32[]{:S(2)}) collective-permute-start(bf16[2,192,384]{2,1,0:T(8,128)(2,1)S(1)} %get-tuple-element.99), channel_id=1, source_target_pairs={{0,8},{4,12},{8,0},{12,4},{1,9},{5,13},{9,1},{13,5},{2,10},{6,14},... | collective-permute-start | bytes 884744 | tf_op jit(solution)/shard_map/ppermute | solution.py:120
  47.3 1.5 %collective-permute-start.15 = (bf16[384,256]{1,0:T(8,128)(2,1)S(1)}, bf16[384,256]{1,0:T(8,128)(2,1)S(1)}, u32[]{:S(2)}, u32[]{:S(2)}) collective-permute-start(bf16[384,256]{1,0:T(8,128)(2,1)S(1)} %get-tuple-element.89.refs_0_.g_ref.g0), channel_id=1, source_target_pairs={{0,1},{1,0},{2,3},{3,2},{4,5},{5,4},{6,7},{7,6},{8,9},{9,8},{10,11... | collective-permute-start | bytes 589832 | tf_op jit(solution)/shard_map/ppermute | solution.py:120
  47.4 1.7 %collective-permute-start.16 = (bf16[384,256]{1,0:T(8,128)(2,1)S(1)}, bf16[384,256]{1,0:T(8,128)(2,1)S(1)}, u32[]{:S(2)}, u32[]{:S(2)}) collective-permute-start(bf16[384,256]{1,0:T(8,128)(2,1)S(1)} %get-tuple-element.90.refs_2_.g2), channel_id=1, source_target_pairs={{0,1},{1,0},{2,3},{3,2},{4,5},{5,4},{6,7},{7,6},{8,9},{9,8},{10,11... | collective-permute-start | bytes 589832 | tf_op jit(solution)/shard_map/ppermute | solution.py:120
  48.3 6.1 %collective-permute-start.11 = (bf16[2,384,256]{2,1,0:T(8,128)(2,1)S(1)}, bf16[2,384,256]{2,1,0:T(8,128)(2,1)S(1)}, u32[]{:S(2)}, u32[]{:S(2)}) collective-permute-start(bf16[2,384,256]{2,1,0:T(8,128)(2,1)S(1)} %get-tuple-element.82), channel_id=1, source_target_pairs={{0,1},{1,0},{2,3},{3,2},{4,5},{5,4},{6,7},{7,6},{8,9},{9,8},{10,11... | collective-permute-start | bytes 1179656 | tf_op jit(solution)/shard_map/ppermute | solution.py:120
  49.9 6.5 %collective-permute-start.17 = (bf16[2,384,256]{2,1,0:T(8,128)(2,1)S(1)}, bf16[2,384,256]{2,1,0:T(8,128)(2,1)S(1)}, u32[]{:S(2)}, u32[]{:S(2)}) collective-permute-start(bf16[2,384,256]{2,1,0:T(8,128)(2,1)S(1)} %get-tuple-element.93), channel_id=1, source_target_pairs={{0,1},{1,0},{2,3},{3,2},{4,5},{5,4},{6,7},{7,6},{8,9},{9,8},{10,11... | collective-permute-start | bytes 1179656 | tf_op jit(solution)/shard_map/ppermute | solution.py:120
  51.5 22.1 %collective-permute-start.22 = (bf16[3,192,384]{2,1,0:T(8,128)(2,1)S(1)}, bf16[3,192,384]{2,1,0:T(8,128)(2,1)S(1)}, u32[]{:S(2)}, u32[]{:S(2)}) collective-permute-start(bf16[3,192,384]{2,1,0:T(8,128)(2,1)S(1)} %get-tuple-element.104), channel_id=1, source_target_pairs={{0,8},{4,12},{8,0},{12,4},{1,9},{5,13},{9,1},{13,5},{2,10},{6,14},... | collective-permute-start | bytes 1327112 | tf_op jit(solution)/shard_map/ppermute | solution.py:120
  53.9 20.4 %collective-permute-start.20 = (bf16[3,192,384]{2,1,0:T(8,128)(2,1)S(1)}, bf16[3,192,384]{2,1,0:T(8,128)(2,1)S(1)}, u32[]{:S(2)}, u32[]{:S(2)}) collective-permute-start(bf16[3,192,384]{2,1,0:T(8,128)(2,1)S(1)} %get-tuple-element.101), channel_id=1, source_target_pairs={{0,4},{4,0},{8,12},{12,8},{1,5},{5,1},{9,13},{13,9},{2,6},{6,2},{1... | collective-permute-start | bytes 1327112 | tf_op jit(solution)/shard_map/ppermute | solution.py:120
  54.5 23.3 %collective-permute-start.12 = (bf16[384,256]{1,0:T(8,128)(2,1)S(1)}, bf16[384,256]{1,0:T(8,128)(2,1)S(1)}, u32[]{:S(2)}, u32[]{:S(2)}) collective-permute-start(bf16[384,256]{1,0:T(8,128)(2,1)S(1)} %get-tuple-element.84), channel_id=1, source_target_pairs={{0,2},{1,3},{2,0},{3,1},{4,6},{5,7},{6,4},{7,5},{8,10},{9,11},{10,... | collective-permute-start | bytes 589832 | tf_op jit(solution)/shard_map/ppermute | solution.py:120
  56.5 22.9 %collective-permute-start.18 = (bf16[384,256]{1,0:T(8,128)(2,1)S(1)}, bf16[384,256]{1,0:T(8,128)(2,1)S(1)}, u32[]{:S(2)}, u32[]{:S(2)}) collective-permute-start(bf16[384,256]{1,0:T(8,128)(2,1)S(1)} %get-tuple-element.95), channel_id=1, source_target_pairs={{0,2},{1,3},{2,0},{3,1},{4,6},{5,7},{6,4},{7,5},{8,10},{9,11},{10,... | collective-permute-start | bytes 589832 | tf_op jit(solution)/shard_map/ppermute | solution.py:120
  74.4 8.2 %collective-permute-start.23 = (bf16[192,384]{1,0:T(8,128)(2,1)S(1)}, bf16[192,384]{1,0:T(8,128)(2,1)S(1)}, u32[]{:S(2)}, u32[]{:S(2)}) collective-permute-start(bf16[192,384]{1,0:T(8,128)(2,1)S(1)} %get-tuple-element.107), channel_id=1, source_target_pairs={{0,8},{4,12},{8,0},{12,4},{1,9},{5,13},{9,1},{13,5},{2,10},{6,14},... | collective-permute-start | bytes 442376 | tf_op jit(solution)/shard_map/ppermute | solution.py:120
  75.3 7.3 %collective-permute-start.24 = (bf16[192,384]{1,0:T(8,128)(2,1)S(1)}, bf16[192,384]{1,0:T(8,128)(2,1)S(1)}, u32[]{:S(2)}, u32[]{:S(2)}) collective-permute-start(bf16[192,384]{1,0:T(8,128)(2,1)S(1)} %get-tuple-element.108), channel_id=1, source_target_pairs={{0,4},{4,0},{8,12},{12,8},{1,5},{5,1},{9,13},{13,9},{2,6},{6,2},{1... | collective-permute-start | bytes 442376 | tf_op jit(solution)/shard_map/ppermute | solution.py:120

commit v10 on v9

--- a/solution.py
+++ b/solution.py
@@ -209,11 +209,11 @@
     stack = ((4, rows, bins), BF16)
     inner = (hid, bins)
 
-    def near_forward_body(x0, x1, k_ref, z_ref, u_ref):
-        u_ref[...] = conv((x0, x1), (0, 1), lax.axis_index("mp"), k_ref, z_ref, None)
+    def near_forward_body(x0, k_ref, z_ref, u_ref):
+        u_ref[...] = conv((x0,), (0,), lax.axis_index("mp"), k_ref, z_ref, None)
 
     z_a, u_a = call(
-        near_forward_body, [stack, (inner, F32)], (x_own, x_near, tap_a), "near_forward"
+        near_forward_body, [stack, (inner, F32)], (x_own, tap_a), "near_forward"
     )
     x_far, u_a = lax.optimization_barrier((x_far, u_a))
     x_cross = swap(x_far, "mp", 1)
@@ -253,9 +253,21 @@
     def kept(w, v, name):
         return call(keep_body, [((2, rows, bins), F32)], (w, v), name)[0]
 
-    def first_body(x2, x3, k_ref, p_ref, _, u_ref, zin_ref, z_ref, v_ref, s_ref, send_ref):
+    def more_forward_body(x1, x2, k_ref, u_in, zin_ref, z_ref, u_ref):
         m = lax.axis_index("mp")
-        u = conv((x2, x3), (2, 3), m, k_ref, z_ref, u_ref[...])
+        u_ref[...] = conv((x1, x2), (1, 2), m, k_ref, z_ref, u_in[...])
+
+    z_a, u_a = call(
+        more_forward_body,
+        [stack, (inner, F32)],
+        (x_near, x_far, tap_a, u_a, z_a),
+        "more_forward",
+        alias={4: 0},
+    )
+
+    def first_body(x3, k_ref, p_ref, _, u_ref, zin_ref, z_ref, v_ref, s_ref, send_ref):
+        m = lax.axis_index("mp")
+        u = conv((x3,), (3,), m, k_ref, z_ref, u_ref[...])
         v, slope = gelu_and_slope(u)
         v = v.astype(BF16)
         v_ref[...] = v
@@ -265,9 +277,9 @@
     z_a, v_a, slope_a, send = call(
         first_body,
         [stack, (inner, BF16), (inner, F32), ((2, rows, bins), BF16)],
-        (x_far, x_cross, tap_a, cols_a, raw_far, u_a, z_a),
+        (x_cross, tap_a, cols_a, raw_far, u_a, z_a),
         "first_forward",
-        alias={6: 0},
+        alias={5: 0},
     )
     keep = kept(cols_a, v_a, "mix_keep")
     got = swap(send, "mp", 1)

time: 83.5 us -> 82.7 us (level)
  waiting for transfers between devices: 46.6 us -> 45.6 us
    ppermute x25, waiting for transfers between devices: 46.6 us -> 45.6 us  [swap(): return lax.ppermute(value, axis, [(i, i ^ bits) for i in range(size)])]
    pallas_call x24 -> x25, Pallas kernels: 9.46 us -> 9.61 us  [call(): pl.pallas_call(body, out_shape=[struct(s, d) for s, d in outs], in_specs=...]
where the time goes in v10:
time: 82.7 us; the launch traced here: 82.5 us
  waiting for transfers between devices  45.6 us (55%)
  starting transfers between devices  21.9 us (26%)
  Pallas kernels  14.2 us (17%)
  between operations  0.86 us (1%)
    ppermute x25, waiting for transfers between devices, swap(): return lax.ppermute(value, axis, [(i, i ^ bits) for i in range(size)])  45.6 us
    ppermute x25, starting transfers between devices, swap(): return lax.ppermute(value, axis, [(i, i ^ bits) for i in range(size)])  21.9 us
    pallas_call x25, Pallas kernels, call(): pl.pallas_call(body, out_shape=[struct(s, d) for s, d in outs], in_specs=...  9.61 us
    pallas_call x1, Pallas kernels, fast_shards(): pl.pallas_call(load_body, out_shape=[pltpu.VMEM((rows, bins), BF16)] + [p...  1.79 us
    pallas_call x2, Pallas kernels, total(): pl.pallas_call(functools.partial(total_body, place), out_shape=[jax.Shape...  1.71 us
  transfers between devices with their start and end apart: 25, of which 15 were waited for; matrix products, arithmetic and copies ran while one was open for 0% of the time, Pallas kernels for 14%

profile of v10, /device:TPU:0, one launch (start us, length us, event | category | flops | bytes accessed | tf_op | source)
XLA Modules:
  0.0 82.5 jit_solution(13972038023678503710)
XLA Ops:
  0.6 3.0 %collective-permute-start = (bf16[384,256]{1,0:T(8,128)(2,1)}, bf16[384,256]{1,0:T(8,128)(2,1)S(1)}, u32[]{:S(2)}, u32[]{:S(2)}) collective-permute-start(bf16[384,256]{1,0:T(8,128)(2,1)} %x_ref.1), channel_id=1, source_target_pairs={{0,2},{1,3},{2,0},{3,1},{4,6},{5,7},{6,4},{7,5},{8,10},{9,11},{10,... | collective-permute-start | bytes 589832 | tf_op jit(solution)/shard_map/ppermute | solution.py:120
  3.8 1.8 %load.1 = (bf16[384,256]{1,0:T(8,128)(2,1)S(1)}, bf16[192,1536]{1,0:T(8,128)(2,1)S(1)}, bf16[192,1536]{1,0:T(8,128)(2,1)S(1)}, bf16[192,1536]{1,0:T(8,128)(2,1)S...) custom-call(bf16[384,256]{1,0:T(8,128)(2,1)} %x_ref.1, bf16[3,192,1536]{2,1,0:T(8,128)(2,1)} %ta.1, ...), custom_call_target="tpu_custom_call" | custom-call | tf_op jit(solution)/shard_map/load/pallas_call | solution.py:184
  5.6 0.3 near_forward.1
  5.9 3.6 %collective-permute-done.x2 = bf16[384,256]{1,0:T(8,128)(2,1)S(1)} collective-permute-done((bf16[384,256]{1,0:T(8,128)(2,1)}, bf16[384,256]{1,0:T(8,128)(2,1)S(1)}, u32[]{:S(2)}, u32[]{:S(2)}) %collective-permute-start) | collective-permute-done | bytes 196640 | tf_op jit(solution)/shard_map/ppermute | solution.py:120
  9.6 0.5 more_forward.1
  10.1 2.9 %collective-permute-done.2._.far_ref = bf16[2,48,1024]{2,1,0:T(8,128)(2,1)S(1)} collective-permute-done((bf16[2,48,1024]{2,1,0:T(8,128)(2,1)}, bf16[2,48,1024]{2,1,0:T(8,128)(2,1)S(1)}, u32[]{:S(2)}, u32[]{:S(2)}) %collective-permute-start.2) | collective-permute-done | bytes 196640 | tf_op jit(solution)/shard_map/ppermute | solution.py:120
  13.0 0.7 first_forward.1
  13.7 0.3 mix_keep.1.keep_ref
  14.1 1.4 %collective-permute-done.4.got_ref = bf16[2,384,256]{2,1,0:T(8,128)(2,1)S(1)} collective-permute-done((bf16[2,384,256]{2,1,0:T(8,128)(2,1)S(1)}, bf16[2,384,256]{2,1,0:T(8,128)(2,1)S(1)}, u32[]{:S(2)}, u32[]{:S(2)}) %collective-permute-start.4) | collective-permute-done | bytes 393248 | tf_op jit(solution)/shard_map/ppermute | solution.py:120
  15.5 1.8 %collective-permute-start.5 = (bf16[2,384,256]{2,1,0:T(8,128)(2,1)S(1)}, bf16[2,384,256]{2,1,0:T(8,128)(2,1)S(1)}, u32[]{:S(2)}, u32[]{:S(2)}) collective-permute-start(bf16[2,384,256]{2,1,0:T(8,128)(2,1)S(1)} %mix_sum.1.chip_ref), channel_id=1, source_target_pairs={{0,2},{1,3},{2,0},{3,1},{4,6},{5,7},{6,4},{7,5},{8,10},{9,11},{10,... | collective-permute-start | bytes 1179656 | tf_op jit(solution)/shard_map/ppermute | solution.py:120
  17.4 1.6 %collective-permute-start.7 = (bf16[2,2,48,256]{3,2,1,0:T(8,128)(2,1)S(1)}, bf16[2,2,48,256]{3,2,1,0:T(8,128)(2,1)S(1)}, u32[]{:S(2)}, u32[]{:S(2)}) collective-permute-start(bf16[2,2,48,256]{3,2,1,0:T(8,128)(2,1)S(1)} %get-tuple-element.77), channel_id=1, source_target_pairs={{0,4},{4,0},{8,12},{12,8},{1,5},{5,1},{9,13},{13,9},{2,6},{6,2},{1... | collective-permute-start | bytes 294920 | tf_op jit(solution)/shard_map/ppermute | solution.py:120
  19.0 2.6 %collective-permute-start.8 = (bf16[2,2,48,256]{3,2,1,0:T(8,128)(2,1)S(1)}, bf16[2,2,48,256]{3,2,1,0:T(8,128)(2,1)S(1)}, u32[]{:S(2)}, u32[]{:S(2)}) collective-permute-start(bf16[2,2,48,256]{3,2,1,0:T(8,128)(2,1)S(1)} %get-tuple-element.78), channel_id=1, source_target_pairs={{0,8},{4,12},{8,0},{12,4},{1,9},{5,13},{9,1},{13,5},{2,10},{6,14},... | collective-permute-start | bytes 294920 | tf_op jit(solution)/shard_map/ppermute | solution.py:120
  22.1 7.4 %collective-permute-done.8.refs_2_ = bf16[2,2,48,256]{3,2,1,0:T(8,128)(2,1)S(1)} collective-permute-done((bf16[2,2,48,256]{3,2,1,0:T(8,128)(2,1)S(1)}, bf16[2,2,48,256]{3,2,1,0:T(8,128)(2,1)S(1)}, u32[]{:S(2)}, u32[]{:S(2)}) %collective-permute-start.8) | collective-permute-done | bytes 98336 | tf_op jit(solution)/shard_map/ppermute | solution.py:120
  29.8 0.5 collective-permute-start.6
  30.3 0.5 own_block.1
  30.8 0.5 collective-permute-done.10.g_ref.gb_ref
  31.3 0.6 collective-permute-done.6.b_ref
  31.9 0.8 second_block.1
  32.9 0.3 squash_keep.1.keep_ref
  33.3 0.7 second_weights.1
  34.0 0.5 collective-permute-done.13.got_ref
  34.6 0.6 collective-permute-start.14
  35.2 1.6 %collective-permute-start.21 = (bf16[2,192,384]{2,1,0:T(8,128)(2,1)S(1)}, bf16[2,192,384]{2,1,0:T(8,128)(2,1)S(1)}, u32[]{:S(2)}, u32[]{:S(2)}) collective-permute-start(bf16[2,192,384]{2,1,0:T(8,128)(2,1)S(1)} %get-tuple-element.106), channel_id=1, source_target_pairs={{0,4},{4,0},{8,12},{12,8},{1,5},{5,1},{9,13},{13,9},{2,6},{6,2},{1... | collective-permute-start | bytes 884744 | tf_op jit(solution)/shard_map/ppermute | solution.py:120
  36.8 1.4 %collective-permute-start.19 = (bf16[2,192,384]{2,1,0:T(8,128)(2,1)S(1)}, bf16[2,192,384]{2,1,0:T(8,128)(2,1)S(1)}, u32[]{:S(2)}, u32[]{:S(2)}) collective-permute-start(bf16[2,192,384]{2,1,0:T(8,128)(2,1)S(1)} %get-tuple-element.103), channel_id=1, source_target_pairs={{0,8},{4,12},{8,0},{12,4},{1,9},{5,13},{9,1},{13,5},{2,10},{6,14},... | collective-permute-start | bytes 884744 | tf_op jit(solution)/shard_map/ppermute | solution.py:120
  38.2 7.6 %collective-permute-done.14.other_ref = bf16[2,384,256]{2,1,0:T(8,128)(2,1)S(1)} collective-permute-done((bf16[2,384,256]{2,1,0:T(8,128)(2,1)S(1)}, bf16[2,384,256]{2,1,0:T(8,128)(2,1)S(1)}, u32[]{:S(2)}, u32[]{:S(2)}) %collective-permute-start.14) | collective-permute-done | bytes 393248 | tf_op jit(solution)/shard_map/ppermute | solution.py:120
  45.8 0.6 middle_grad.1
  46.5 0.5 collective-permute-start.16
  47.0 0.4 output_product.1
  47.6 0.4 collective-permute-done.15.refs_1_.g1
  48.2 0.8 first_backward.1
  49.3 0.8 %collective-permute-done.21.got_b = bf16[2,192,384]{2,1,0:T(8,128)(2,1)S(1)} collective-permute-done((bf16[2,192,384]{2,1,0:T(8,128)(2,1)S(1)}, bf16[2,192,384]{2,1,0:T(8,128)(2,1)S(1)}, u32[]{:S(2)}, u32[]{:S(2)}) %collective-permute-start.21) | collective-permute-done | bytes 294944 | tf_op jit(solution)/shard_map/ppermute | solution.py:120
  50.1 0.5 first_proj.1
  50.7 1.9 %collective-permute-start.22 = (bf16[3,192,384]{2,1,0:T(8,128)(2,1)S(1)}, bf16[3,192,384]{2,1,0:T(8,128)(2,1)S(1)}, u32[]{:S(2)}, u32[]{:S(2)}) collective-permute-start(bf16[3,192,384]{2,1,0:T(8,128)(2,1)S(1)} %get-tuple-element.108), channel_id=1, source_target_pairs={{0,8},{4,12},{8,0},{12,4},{1,9},{5,13},{9,1},{13,5},{2,10},{6,14},... | collective-permute-start | bytes 1327112 | tf_op jit(solution)/shard_map/ppermute | solution.py:120
  52.6 0.5 first_taps.1
  53.0 0.5 collective-permute-start.20
  53.6 1.6 %collective-permute-start.12 = (bf16[384,256]{1,0:T(8,128)(2,1)S(1)}, bf16[384,256]{1,0:T(8,128)(2,1)S(1)}, u32[]{:S(2)}, u32[]{:S(2)}) collective-permute-start(bf16[384,256]{1,0:T(8,128)(2,1)S(1)} %get-tuple-element.88), channel_id=1, source_target_pairs={{0,2},{1,3},{2,0},{3,1},{4,6},{5,7},{6,4},{7,5},{8,10},{9,11},{10,... | collective-permute-start | bytes 589832 | tf_op jit(solution)/shard_map/ppermute | solution.py:120
  55.2 0.3 entry_keep.1.keep_ref
  55.6 0.6 collective-permute-start.18
  56.2 16.5 %collective-permute-done.22.got.got_k = bf16[3,192,384]{2,1,0:T(8,128)(2,1)S(1)} collective-permute-done((bf16[3,192,384]{2,1,0:T(8,128)(2,1)S(1)}, bf16[3,192,384]{2,1,0:T(8,128)(2,1)S(1)}, u32[]{:S(2)}, u32[]{:S(2)}) %collective-permute-start.22) | collective-permute-done | bytes 442400 | tf_op jit(solution)/shard_map/ppermute | solution.py:120
  72.8 0.7 collective-permute-done.20.got.got_p
  73.5 0.9 %collective-permute-start.23 = (bf16[192,384]{1,0:T(8,128)(2,1)S(1)}, bf16[192,384]{1,0:T(8,128)(2,1)S(1)}, u32[]{:S(2)}, u32[]{:S(2)}) collective-permute-start(bf16[192,384]{1,0:T(8,128)(2,1)S(1)} %get-tuple-element.111), channel_id=1, source_target_pairs={{0,8},{4,12},{8,0},{12,4},{1,9},{5,13},{9,1},{13,5},{2,10},{6,14},... | collective-permute-start | bytes 442376 | tf_op jit(solution)/shard_map/ppermute | solution.py:120
  74.4 1.4 %collective-permute-start.24 = (bf16[192,384]{1,0:T(8,128)(2,1)S(1)}, bf16[192,384]{1,0:T(8,128)(2,1)S(1)}, u32[]{:S(2)}, u32[]{:S(2)}) collective-permute-start(bf16[192,384]{1,0:T(8,128)(2,1)S(1)} %get-tuple-element.112), channel_id=1, source_target_pairs={{0,4},{4,0},{8,12},{12,8},{1,5},{5,1},{9,13},{13,9},{2,6},{6,2},{1... | collective-permute-start | bytes 442376 | tf_op jit(solution)/shard_map/ppermute | solution.py:120
  75.9 1.1 %zero_planes.1 = (f32[3,192,384]{2,1,0:T(8,128)}, f32[3,192,384]{2,1,0:T(8,128)}) custom-call(), custom_call_target="tpu_custom_call" | custom-call | tf_op jit(solution)/shard_map/zero_planes/pallas_call | solution.py:431
  76.9 0.7 out.1
  77.7 0.9 %second_total.1 = (f32[3,192,384]{2,1,0:T(8,128)}, f32[192,384]{1,0:T(8,128)}) custom-call(f32[3,192,384]{2,1,0:T(8,128)} %get-tuple-element.115._, f32[1,192,384]{2,1,0:T(8,128)S(1)} %get-tuple-element.116.own_k, f32[1,192,384]{2,1,0:T(8,128)S(1)} %get-tuple-element.117.own_p, ...), custom_call_target="tpu_custom_call", output_to_operand_aliasing={{0}: (0, {})} | custom-call | tf_op jit(solution)/shard_map/second_total/pallas_call | solution.py:413
  78.6 1.0 %entry.1 = bf16[384,256]{1,0:T(8,128)(2,1)} custom-call(bf16[384,256]{1,0:T(8,128)(2,1)S(1)} %get-tuple-element.93.refs_0_.g_ref.g0, bf16[384,256]{1,0:T(8,128)(2,1)S(1)} %get-tuple-element.63.x0.x_ref, f32[384,256]{1,0:T(8,128)S(1)} %get-tuple-element.98.own_ref, bf16[384,256]{1,0:T(8,128)(2,1)S(1)} %collective-permute-done.18.got_ref), custom_call_target="tpu_custom_call" | custom-call | tf_op jit(solution)/shard_map/entry/pallas_call | solution.py:148
  79.5 2.2 %collective-permute-done.23.got_k = bf16[192,384]{1,0:T(8,128)(2,1)S(1)} collective-permute-done((bf16[192,384]{1,0:T(8,128)(2,1)S(1)}, bf16[192,384]{1,0:T(8,128)(2,1)S(1)}, u32[]{:S(2)}, u32[]{:S(2)}) %collective-permute-start.23) | collective-permute-done | bytes 147488 | tf_op jit(solution)/shard_map/ppermute | solution.py:120
  81.7 0.9 %first_total.1 = (f32[3,192,384]{2,1,0:T(8,128)}, f32[192,384]{1,0:T(8,128)}) custom-call(f32[3,192,384]{2,1,0:T(8,128)} %get-tuple-element.100._, f32[1,192,384]{2,1,0:T(8,128)S(1)} %get-tuple-element.110.own_k, f32[1,192,384]{2,1,0:T(8,128)S(1)} %get-tuple-element.109.rest_0_.own_p, ...), custom_call_target="tpu_custom_call", output_to_operand_aliasing={{0}: (0, {})} | custom-call | tf_op jit(solution)/shard_map/first_total/pallas_call | solution.py:413
  (31 shorter events, 2.4 us)
Async XLA Ops:
  0.6 8.9 %collective-permute-start = (bf16[384,256]{1,0:T(8,128)(2,1)}, bf16[384,256]{1,0:T(8,128)(2,1)S(1)}, u32[]{:S(2)}, u32[]{:S(2)}) collective-permute-start(bf16[384,256]{1,0:T(8,128)(2,1)} %x_ref.1), channel_id=1, source_target_pairs={{0,2},{1,3},{2,0},{3,1},{4,6},{5,7},{6,4},{7,5},{8,10},{9,11},{10,... | collective-permute-start | bytes 589832 | tf_op jit(solution)/shard_map/ppermute | solution.py:120
  3.6 5.9 %collective-permute-start.3 = (bf16[384,256]{1,0:T(8,128)(2,1)}, bf16[384,256]{1,0:T(8,128)(2,1)S(1)}, u32[]{:S(2)}, u32[]{:S(2)}) collective-permute-start(bf16[384,256]{1,0:T(8,128)(2,1)} %x_ref.1), channel_id=1, source_target_pairs={{0,1},{1,0},{2,3},{3,2},{4,5},{5,4},{6,7},{7,6},{8,9},{9,8},{10,11... | collective-permute-start | bytes 589832 | tf_op jit(solution)/shard_map/ppermute | solution.py:120
  3.6 9.3 %collective-permute-start.2 = (bf16[2,48,1024]{2,1,0:T(8,128)(2,1)}, bf16[2,48,1024]{2,1,0:T(8,128)(2,1)S(1)}, u32[]{:S(2)}, u32[]{:S(2)}) collective-permute-start(bf16[2,48,1024]{2,1,0:T(8,128)(2,1)} %g_ref.1), channel_id=1, source_target_pairs={{0,2},{1,3},{2,0},{3,1},{4,6},{5,7},{6,4},{7,5},{8,10},{9,11},{10,... | collective-permute-start | bytes 589832 | tf_op jit(solution)/shard_map/ppermute | solution.py:120
  9.6 3.4 %collective-permute-start.1 = (bf16[384,256]{1,0:T(8,128)(2,1)S(1)}, bf16[384,256]{1,0:T(8,128)(2,1)S(1)}, u32[]{:S(2)}, u32[]{:S(2)}) collective-permute-start(bf16[384,256]{1,0:T(8,128)(2,1)S(1)} %collective-permute-done.x2), channel_id=1, source_target_pairs={{0,1},{1,0},{2,3},{3,2},{4,5},{5,4},{6,7},{7,6},{8,9},{9,8},{10,11... | collective-permute-start | bytes 589832 | tf_op jit(solution)/shard_map/ppermute | solution.py:120
  13.7 1.8 %collective-permute-start.4 = (bf16[2,384,256]{2,1,0:T(8,128)(2,1)S(1)}, bf16[2,384,256]{2,1,0:T(8,128)(2,1)S(1)}, u32[]{:S(2)}, u32[]{:S(2)}) collective-permute-start(bf16[2,384,256]{2,1,0:T(8,128)(2,1)S(1)} %get-tuple-element.73), channel_id=1, source_target_pairs={{0,1},{1,0},{2,3},{3,2},{4,5},{5,4},{6,7},{7,6},{8,9},{9,8},{10,11... | collective-permute-start | bytes 1179656 | tf_op jit(solution)/shard_map/ppermute | solution.py:120
  15.5 14.1 %collective-permute-start.5 = (bf16[2,384,256]{2,1,0:T(8,128)(2,1)S(1)}, bf16[2,384,256]{2,1,0:T(8,128)(2,1)S(1)}, u32[]{:S(2)}, u32[]{:S(2)}) collective-permute-start(bf16[2,384,256]{2,1,0:T(8,128)(2,1)S(1)} %mix_sum.1.chip_ref), channel_id=1, source_target_pairs={{0,2},{1,3},{2,0},{3,1},{4,6},{5,7},{6,4},{7,5},{8,10},{9,11},{10,... | collective-permute-start | bytes 1179656 | tf_op jit(solution)/shard_map/ppermute | solution.py:120
  17.4 4.7 %collective-permute-start.7 = (bf16[2,2,48,256]{3,2,1,0:T(8,128)(2,1)S(1)}, bf16[2,2,48,256]{3,2,1,0:T(8,128)(2,1)S(1)}, u32[]{:S(2)}, u32[]{:S(2)}) collective-permute-start(bf16[2,2,48,256]{3,2,1,0:T(8,128)(2,1)S(1)} %get-tuple-element.77), channel_id=1, source_target_pairs={{0,4},{4,0},{8,12},{12,8},{1,5},{5,1},{9,13},{13,9},{2,6},{6,2},{1... | collective-permute-start | bytes 294920 | tf_op jit(solution)/shard_map/ppermute | solution.py:120
  19.0 10.4 %collective-permute-start.8 = (bf16[2,2,48,256]{3,2,1,0:T(8,128)(2,1)S(1)}, bf16[2,2,48,256]{3,2,1,0:T(8,128)(2,1)S(1)}, u32[]{:S(2)}, u32[]{:S(2)}) collective-permute-start(bf16[2,2,48,256]{3,2,1,0:T(8,128)(2,1)S(1)} %get-tuple-element.78), channel_id=1, source_target_pairs={{0,8},{4,12},{8,0},{12,4},{1,9},{5,13},{9,1},{13,5},{2,10},{6,14},... | collective-permute-start | bytes 294920 | tf_op jit(solution)/shard_map/ppermute | solution.py:120
  21.6 7.9 %collective-permute-start.9 = (bf16[2,2,48,256]{3,2,1,0:T(8,128)(2,1)S(1)}, bf16[2,2,48,256]{3,2,1,0:T(8,128)(2,1)S(1)}, u32[]{:S(2)}, u32[]{:S(2)}) collective-permute-start(bf16[2,2,48,256]{3,2,1,0:T(8,128)(2,1)S(1)} %get-tuple-element.79), channel_id=1, source_target_pairs={{0,12},{4,8},{8,4},{12,0},{1,13},{5,9},{9,5},{13,1},{2,14},{6,10},... | collective-permute-start | bytes 294920 | tf_op jit(solution)/shard_map/ppermute | solution.py:120
  29.5 1.8 %collective-permute-start.10 = (bf16[2,384,256]{2,1,0:T(8,128)(2,1)S(1)}, bf16[2,384,256]{2,1,0:T(8,128)(2,1)S(1)}, u32[]{:S(2)}, u32[]{:S(2)}) collective-permute-start(bf16[2,384,256]{2,1,0:T(8,128)(2,1)S(1)} %bitcast.5), channel_id=1, source_target_pairs={{0,1},{1,0},{2,3},{3,2},{4,5},{5,4},{6,7},{7,6},{8,9},{9,8},{10,11... | collective-permute-start | bytes 1179656 | tf_op jit(solution)/shard_map/ppermute | solution.py:120
  29.8 2.1 %collective-permute-start.6 = (bf16[2,384,256]{2,1,0:T(8,128)(2,1)S(1)}, bf16[2,384,256]{2,1,0:T(8,128)(2,1)S(1)}, u32[]{:S(2)}, u32[]{:S(2)}) collective-permute-start(bf16[2,384,256]{2,1,0:T(8,128)(2,1)S(1)} %middle.1.a_ref.mid_ref), channel_id=1, source_target_pairs={{0,1},{1,0},{2,3},{3,2},{4,5},{5,4},{6,7},{7,6},{8,9},{9,8},{10,11... | collective-permute-start | bytes 1179656 | tf_op jit(solution)/shard_map/ppermute | solution.py:120
  32.7 1.8 %collective-permute-start.13 = (bf16[2,384,256]{2,1,0:T(8,128)(2,1)S(1)}, bf16[2,384,256]{2,1,0:T(8,128)(2,1)S(1)}, u32[]{:S(2)}, u32[]{:S(2)}) collective-permute-start(bf16[2,384,256]{2,1,0:T(8,128)(2,1)S(1)} %get-tuple-element.90), channel_id=1, source_target_pairs={{0,1},{1,0},{2,3},{3,2},{4,5},{5,4},{6,7},{7,6},{8,9},{9,8},{10,11... | collective-permute-start | bytes 1179656 | tf_op jit(solution)/shard_map/ppermute | solution.py:120
  34.6 11.3 %collective-permute-start.14 = (bf16[2,384,256]{2,1,0:T(8,128)(2,1)S(1)}, bf16[2,384,256]{2,1,0:T(8,128)(2,1)S(1)}, u32[]{:S(2)}, u32[]{:S(2)}) collective-permute-start(bf16[2,384,256]{2,1,0:T(8,128)(2,1)S(1)} %squash_sum.1.chip_ref), channel_id=1, source_target_pairs={{0,2},{1,3},{2,0},{3,1},{4,6},{5,7},{6,4},{7,5},{8,10},{9,11},{10,... | collective-permute-start | bytes 1179656 | tf_op jit(solution)/shard_map/ppermute | solution.py:120
  35.2 15.0 %collective-permute-start.21 = (bf16[2,192,384]{2,1,0:T(8,128)(2,1)S(1)}, bf16[2,192,384]{2,1,0:T(8,128)(2,1)S(1)}, u32[]{:S(2)}, u32[]{:S(2)}) collective-permute-start(bf16[2,192,384]{2,1,0:T(8,128)(2,1)S(1)} %get-tuple-element.106), channel_id=1, source_target_pairs={{0,4},{4,0},{8,12},{12,8},{1,5},{5,1},{9,13},{13,9},{2,6},{6,2},{1... | collective-permute-start | bytes 884744 | tf_op jit(solution)/shard_map/ppermute | solution.py:120
  36.8 15.8 %collective-permute-start.19 = (bf16[2,192,384]{2,1,0:T(8,128)(2,1)S(1)}, bf16[2,192,384]{2,1,0:T(8,128)(2,1)S(1)}, u32[]{:S(2)}, u32[]{:S(2)}) collective-permute-start(bf16[2,192,384]{2,1,0:T(8,128)(2,1)S(1)} %get-tuple-element.103), channel_id=1, source_target_pairs={{0,8},{4,12},{8,0},{12,4},{1,9},{5,13},{9,1},{13,5},{2,10},{6,14},... | collective-permute-start | bytes 884744 | tf_op jit(solution)/shard_map/ppermute | solution.py:120
  46.4 1.5 %collective-permute-start.15 = (bf16[384,256]{1,0:T(8,128)(2,1)S(1)}, bf16[384,256]{1,0:T(8,128)(2,1)S(1)}, u32[]{:S(2)}, u32[]{:S(2)}) collective-permute-start(bf16[384,256]{1,0:T(8,128)(2,1)S(1)} %get-tuple-element.93.refs_0_.g_ref.g0), channel_id=1, source_target_pairs={{0,1},{1,0},{2,3},{3,2},{4,5},{5,4},{6,7},{7,6},{8,9},{9,8},{10,11... | collective-permute-start | bytes 589832 | tf_op jit(solution)/shard_map/ppermute | solution.py:120
  46.5 1.7 %collective-permute-start.16 = (bf16[384,256]{1,0:T(8,128)(2,1)S(1)}, bf16[384,256]{1,0:T(8,128)(2,1)S(1)}, u32[]{:S(2)}, u32[]{:S(2)}) collective-permute-start(bf16[384,256]{1,0:T(8,128)(2,1)S(1)} %get-tuple-element.94.refs_2_.g2), channel_id=1, source_target_pairs={{0,1},{1,0},{2,3},{3,2},{4,5},{5,4},{6,7},{7,6},{8,9},{9,8},{10,11... | collective-permute-start | bytes 589832 | tf_op jit(solution)/shard_map/ppermute | solution.py:120
  47.4 6.1 %collective-permute-start.11 = (bf16[2,384,256]{2,1,0:T(8,128)(2,1)S(1)}, bf16[2,384,256]{2,1,0:T(8,128)(2,1)S(1)}, u32[]{:S(2)}, u32[]{:S(2)}) collective-permute-start(bf16[2,384,256]{2,1,0:T(8,128)(2,1)S(1)} %get-tuple-element.86), channel_id=1, source_target_pairs={{0,1},{1,0},{2,3},{3,2},{4,5},{5,4},{6,7},{7,6},{8,9},{9,8},{10,11... | collective-permute-start | bytes 1179656 | tf_op jit(solution)/shard_map/ppermute | solution.py:120
  49.0 6.5 %collective-permute-start.17 = (bf16[2,384,256]{2,1,0:T(8,128)(2,1)S(1)}, bf16[2,384,256]{2,1,0:T(8,128)(2,1)S(1)}, u32[]{:S(2)}, u32[]{:S(2)}) collective-permute-start(bf16[2,384,256]{2,1,0:T(8,128)(2,1)S(1)} %get-tuple-element.97), channel_id=1, source_target_pairs={{0,1},{1,0},{2,3},{3,2},{4,5},{5,4},{6,7},{7,6},{8,9},{9,8},{10,11... | collective-permute-start | bytes 1179656 | tf_op jit(solution)/shard_map/ppermute | solution.py:120
  50.7 22.1 %collective-permute-start.22 = (bf16[3,192,384]{2,1,0:T(8,128)(2,1)S(1)}, bf16[3,192,384]{2,1,0:T(8,128)(2,1)S(1)}, u32[]{:S(2)}, u32[]{:S(2)}) collective-permute-start(bf16[3,192,384]{2,1,0:T(8,128)(2,1)S(1)} %get-tuple-element.108), channel_id=1, source_target_pairs={{0,8},{4,12},{8,0},{12,4},{1,9},{5,13},{9,1},{13,5},{2,10},{6,14},... | collective-permute-start | bytes 1327112 | tf_op jit(solution)/shard_map/ppermute | solution.py:120
  53.0 20.4 %collective-permute-start.20 = (bf16[3,192,384]{2,1,0:T(8,128)(2,1)S(1)}, bf16[3,192,384]{2,1,0:T(8,128)(2,1)S(1)}, u32[]{:S(2)}, u32[]{:S(2)}) collective-permute-start(bf16[3,192,384]{2,1,0:T(8,128)(2,1)S(1)} %get-tuple-element.105), channel_id=1, source_target_pairs={{0,4},{4,0},{8,12},{12,8},{1,5},{5,1},{9,13},{13,9},{2,6},{6,2},{1... | collective-permute-start | bytes 1327112 | tf_op jit(solution)/shard_map/ppermute | solution.py:120
  53.6 23.3 %collective-permute-start.12 = (bf16[384,256]{1,0:T(8,128)(2,1)S(1)}, bf16[384,256]{1,0:T(8,128)(2,1)S(1)}, u32[]{:S(2)}, u32[]{:S(2)}) collective-permute-start(bf16[384,256]{1,0:T(8,128)(2,1)S(1)} %get-tuple-element.88), channel_id=1, source_target_pairs={{0,2},{1,3},{2,0},{3,1},{4,6},{5,7},{6,4},{7,5},{8,10},{9,11},{10,... | collective-permute-start | bytes 589832 | tf_op jit(solution)/shard_map/ppermute | solution.py:120
  55.6 22.9 %collective-permute-start.18 = (bf16[384,256]{1,0:T(8,128)(2,1)S(1)}, bf16[384,256]{1,0:T(8,128)(2,1)S(1)}, u32[]{:S(2)}, u32[]{:S(2)}) collective-permute-start(bf16[384,256]{1,0:T(8,128)(2,1)S(1)} %get-tuple-element.99), channel_id=1, source_target_pairs={{0,2},{1,3},{2,0},{3,1},{4,6},{5,7},{6,4},{7,5},{8,10},{9,11},{10,... | collective-permute-start | bytes 589832 | tf_op jit(solution)/shard_map/ppermute | solution.py:120
  73.5 8.2 %collective-permute-start.23 = (bf16[192,384]{1,0:T(8,128)(2,1)S(1)}, bf16[192,384]{1,0:T(8,128)(2,1)S(1)}, u32[]{:S(2)}, u32[]{:S(2)}) collective-permute-start(bf16[192,384]{1,0:T(8,128)(2,1)S(1)} %get-tuple-element.111), channel_id=1, source_target_pairs={{0,8},{4,12},{8,0},{12,4},{1,9},{5,13},{9,1},{13,5},{2,10},{6,14},... | collective-permute-start | bytes 442376 | tf_op jit(solution)/shard_map/ppermute | solution.py:120
  74.4 7.3 %collective-permute-start.24 = (bf16[192,384]{1,0:T(8,128)(2,1)S(1)}, bf16[192,384]{1,0:T(8,128)(2,1)S(1)}, u32[]{:S(2)}, u32[]{:S(2)}) collective-permute-start(bf16[192,384]{1,0:T(8,128)(2,1)S(1)} %get-tuple-element.112), channel_id=1, source_target_pairs={{0,4},{4,0},{8,12},{12,8},{1,5},{5,1},{9,13},{13,9},{2,6},{6,2},{1... | collective-permute-start | bytes 442376 | tf_op jit(solution)/shard_map/ppermute | solution.py:120

commit v11 on v9

--- a/solution.py
+++ b/solution.py
@@ -165,7 +165,6 @@
         return pl.ds(pl.multiple_of((m ^ j) * rows, rows), rows)
 
     x_far = swap(x, "mp", 2)
-    x_near = swap(x, "mp", 1)
 
     raw_far = swap(grad_heads, "mp", 2)
 
@@ -209,14 +208,21 @@
     stack = ((4, rows, bins), BF16)
     inner = (hid, bins)
 
-    def near_forward_body(x0, x1, k_ref, z_ref, u_ref):
-        u_ref[...] = conv((x0, x1), (0, 1), lax.axis_index("mp"), k_ref, z_ref, None)
-
-    z_a, u_a = call(
-        near_forward_body, [stack, (inner, F32)], (x_own, x_near, tap_a), "near_forward"
-    )
+    def near_forward_body(x_ref, k_ref, z_ref, u_ref):
+        z = gelu(x_ref[...].astype(F32)).astype(BF16)
+        z_ref[...] = z
+        u_ref[...] = dot(k_ref[:, block(lax.axis_index("mp"), 0)], z)
+
+    def far_forward_body(x_ref, k_ref, u_in, z_ref, u_ref):
+        z = gelu(x_ref[...].astype(F32)).astype(BF16)
+        z_ref[...] = z
+        u_ref[...] = u_in[...] + dot(k_ref[:, block(lax.axis_index("mp"), 2)], z)
+
+    half_z = [((rows, bins), BF16), (inner, F32)]
+    z_own, u_a = call(near_forward_body, half_z, (x_own, tap_a), "near_forward")
     x_far, u_a = lax.optimization_barrier((x_far, u_a))
-    x_cross = swap(x_far, "mp", 1)
+    z_far, u_a = call(far_forward_body, half_z, (x_far, tap_a, u_a), "far_forward")
+    z_near, z_cross = swap(z_own, "mp", 1), swap(z_far, "mp", 1)
 
     def split_body(own_ref, far_ref, *outs):
         c = lax.axis_index("ctx")
@@ -253,21 +259,21 @@
     def kept(w, v, name):
         return call(keep_body, [((2, rows, bins), F32)], (w, v), name)[0]
 
-    def first_body(x2, x3, k_ref, p_ref, _, u_ref, zin_ref, z_ref, v_ref, s_ref, send_ref):
+    def first_body(z1, z3, k_ref, p_ref, _, u_ref, v_ref, s_ref, send_ref):
         m = lax.axis_index("mp")
-        u = conv((x2, x3), (2, 3), m, k_ref, z_ref, u_ref[...])
+        u = u_ref[...] + dot(k_ref[:, block(m, 1)], z1[...])
+        u = u + dot(k_ref[:, block(m, 3)], z3[...])
         v, slope = gelu_and_slope(u)
         v = v.astype(BF16)
         v_ref[...] = v
         s_ref[...] = slope
         near_half(p_ref, v, m, send_ref)
 
-    z_a, v_a, slope_a, send = call(
+    v_a, slope_a, send = call(
         first_body,
-        [stack, (inner, BF16), (inner, F32), ((2, rows, bins), BF16)],
-        (x_far, x_cross, tap_a, cols_a, raw_far, u_a, z_a),
+        [(inner, BF16), (inner, F32), ((2, rows, bins), BF16)],
+        (z_near, z_cross, tap_a, cols_a, raw_far, u_a),
         "first_forward",
-        alias={6: 0},
     )
     keep = kept(cols_a, v_a, "mix_keep")
     got = swap(send, "mp", 1)
@@ -363,7 +369,9 @@
         send[2] = half_sum(keep_b, got_b, own)
         proj_pieces(v_ref, g_ref, keep, send)
 
-    def first_taps_body(z_ref, gu_ref, keep_b, got_b, keep, send, own):
+    def first_taps_body(z0, z1, z2, z3, gu_ref, keep_b, got_b, keep, send, own, z_ref):
+        for i, ref in enumerate((z0, z1, z2, z3)):
+            z_ref[i] = ref[...]
         send[2] = half_sum(keep_b, got_b, own)
         taps_pieces(z_ref, gu_ref, keep, send)
 
@@ -509,8 +517,9 @@
     keep_ak, send_k, own_bp = call(
         first_taps_body,
         [(two, F32), (three, BF16), (one, F32)],
-        (z_a, gu_a, keep_b[1], got_b[1]),
+        (z_own, z_near, z_far, z_cross, gu_a, keep_b[1], got_b[1]),
         "first_taps",
+        pack,
     )
     got_k = swap(send_k, "ctx", 1)
     got = swap(send, "mp", 1)

time: 83.5 us -> 82.7 us (level)
  waiting for transfers between devices: 46.6 us -> 45.7 us
    ppermute x25, waiting for transfers between devices: 46.6 us -> 45.7 us  [swap(): return lax.ppermute(value, axis, [(i, i ^ bits) for i in range(size)])]
    pallas_call x24 -> x25, Pallas kernels: 9.46 us -> 9.58 us  [call(): pl.pallas_call(body, out_shape=[struct(s, d) for s, d in outs], in_specs=...]
where the time goes in v11:
time: 82.7 us; the launch traced here: 82.6 us
  waiting for transfers between devices  45.7 us (55%)
  starting transfers between devices  21.9 us (26%)
  Pallas kernels  14.1 us (17%)
  between operations  0.88 us (1%)
    ppermute x25, waiting for transfers between devices, swap(): return lax.ppermute(value, axis, [(i, i ^ bits) for i in range(size)])  45.7 us
    ppermute x25, starting transfers between devices, swap(): return lax.ppermute(value, axis, [(i, i ^ bits) for i in range(size)])  21.9 us
    pallas_call x25, Pallas kernels, call(): pl.pallas_call(body, out_shape=[struct(s, d) for s, d in outs], in_specs=...  9.58 us
    pallas_call x1, Pallas kernels, fast_shards(): pl.pallas_call(load_body, out_shape=[pltpu.VMEM((rows, bins), BF16)] + [p...  1.79 us
    pallas_call x2, Pallas kernels, total(): pl.pallas_call(functools.partial(total_body, place), out_shape=[jax.Shape...  1.71 us
  transfers between devices with their start and end apart: 25, of which 15 were waited for; matrix products, arithmetic and copies ran while one was open for 0% of the time, Pallas kernels for 14%

profile of v11, /device:TPU:0, one launch (start us, length us, event | category | flops | bytes accessed | tf_op | source)
XLA Modules:
  0.0 82.6 jit_solution(7198156335091462983)
XLA Ops:
  0.6 3.0 %collective-permute-start = (bf16[384,256]{1,0:T(8,128)(2,1)}, bf16[384,256]{1,0:T(8,128)(2,1)S(1)}, u32[]{:S(2)}, u32[]{:S(2)}) collective-permute-start(bf16[384,256]{1,0:T(8,128)(2,1)} %x_ref.1), channel_id=1, source_target_pairs={{0,2},{1,3},{2,0},{3,1},{4,6},{5,7},{6,4},{7,5},{8,10},{9,11},{10,... | collective-permute-start | bytes 589832 | tf_op jit(solution)/shard_map/ppermute | solution.py:120
  3.7 1.8 %load.1 = (bf16[384,256]{1,0:T(8,128)(2,1)S(1)}, bf16[192,1536]{1,0:T(8,128)(2,1)S(1)}, bf16[192,1536]{1,0:T(8,128)(2,1)S(1)}, bf16[192,1536]{1,0:T(8,128)(2,1)S...) custom-call(bf16[384,256]{1,0:T(8,128)(2,1)} %x_ref.1, bf16[3,192,1536]{2,1,0:T(8,128)(2,1)} %ta.1, ...), custom_call_target="tpu_custom_call" | custom-call | tf_op jit(solution)/shard_map/load/pallas_call | solution.py:183
  5.5 0.3 near_forward.1
  5.9 3.7 %collective-permute-done.x_ref.x2 = bf16[384,256]{1,0:T(8,128)(2,1)S(1)} collective-permute-done((bf16[384,256]{1,0:T(8,128)(2,1)}, bf16[384,256]{1,0:T(8,128)(2,1)S(1)}, u32[]{:S(2)}, u32[]{:S(2)}) %collective-permute-start) | collective-permute-done | bytes 196640 | tf_op jit(solution)/shard_map/ppermute | solution.py:120
  9.6 0.3 far_forward.1
  10.0 3.0 %collective-permute-done.3._.far_ref = bf16[2,48,1024]{2,1,0:T(8,128)(2,1)S(1)} collective-permute-done((bf16[2,48,1024]{2,1,0:T(8,128)(2,1)}, bf16[2,48,1024]{2,1,0:T(8,128)(2,1)S(1)}, u32[]{:S(2)}, u32[]{:S(2)}) %collective-permute-start.3) | collective-permute-done | bytes 196640 | tf_op jit(solution)/shard_map/ppermute | solution.py:120
  13.0 0.8 first_forward.1
  13.8 0.3 mix_keep.1.keep_ref
  14.1 1.4 %collective-permute-done.4.got_ref = bf16[2,384,256]{2,1,0:T(8,128)(2,1)S(1)} collective-permute-done((bf16[2,384,256]{2,1,0:T(8,128)(2,1)S(1)}, bf16[2,384,256]{2,1,0:T(8,128)(2,1)S(1)}, u32[]{:S(2)}, u32[]{:S(2)}) %collective-permute-start.4) | collective-permute-done | bytes 393248 | tf_op jit(solution)/shard_map/ppermute | solution.py:120
  15.6 1.8 %collective-permute-start.5 = (bf16[2,384,256]{2,1,0:T(8,128)(2,1)S(1)}, bf16[2,384,256]{2,1,0:T(8,128)(2,1)S(1)}, u32[]{:S(2)}, u32[]{:S(2)}) collective-permute-start(bf16[2,384,256]{2,1,0:T(8,128)(2,1)S(1)} %mix_sum.1.chip_ref), channel_id=1, source_target_pairs={{0,2},{1,3},{2,0},{3,1},{4,6},{5,7},{6,4},{7,5},{8,10},{9,11},{10,... | collective-permute-start | bytes 1179656 | tf_op jit(solution)/shard_map/ppermute | solution.py:120
  17.4 1.6 %collective-permute-start.7 = (bf16[2,2,48,256]{3,2,1,0:T(8,128)(2,1)S(1)}, bf16[2,2,48,256]{3,2,1,0:T(8,128)(2,1)S(1)}, u32[]{:S(2)}, u32[]{:S(2)}) collective-permute-start(bf16[2,2,48,256]{3,2,1,0:T(8,128)(2,1)S(1)} %get-tuple-element.76), channel_id=1, source_target_pairs={{0,4},{4,0},{8,12},{12,8},{1,5},{5,1},{9,13},{13,9},{2,6},{6,2},{1... | collective-permute-start | bytes 294920 | tf_op jit(solution)/shard_map/ppermute | solution.py:120
  19.1 2.6 %collective-permute-start.8 = (bf16[2,2,48,256]{3,2,1,0:T(8,128)(2,1)S(1)}, bf16[2,2,48,256]{3,2,1,0:T(8,128)(2,1)S(1)}, u32[]{:S(2)}, u32[]{:S(2)}) collective-permute-start(bf16[2,2,48,256]{3,2,1,0:T(8,128)(2,1)S(1)} %get-tuple-element.77), channel_id=1, source_target_pairs={{0,8},{4,12},{8,0},{12,4},{1,9},{5,13},{9,1},{13,5},{2,10},{6,14},... | collective-permute-start | bytes 294920 | tf_op jit(solution)/shard_map/ppermute | solution.py:120
  22.1 7.4 %collective-permute-done.8.refs_2_ = bf16[2,2,48,256]{3,2,1,0:T(8,128)(2,1)S(1)} collective-permute-done((bf16[2,2,48,256]{3,2,1,0:T(8,128)(2,1)S(1)}, bf16[2,2,48,256]{3,2,1,0:T(8,128)(2,1)S(1)}, u32[]{:S(2)}, u32[]{:S(2)}) %collective-permute-start.8) | collective-permute-done | bytes 98336 | tf_op jit(solution)/shard_map/ppermute | solution.py:120
  29.8 0.5 collective-permute-start.6
  30.4 0.5 own_block.1
  30.9 0.5 collective-permute-done.10.g_ref.gb_ref
  31.4 0.6 collective-permute-done.6.b_ref
  31.9 0.8 second_block.1
  33.0 0.3 squash_keep.1.keep_ref
  33.3 0.7 second_weights.1
  34.0 0.5 collective-permute-done.13.got_ref
  34.6 0.6 collective-permute-start.14
  35.2 1.6 %collective-permute-start.21 = (bf16[2,192,384]{2,1,0:T(8,128)(2,1)S(1)}, bf16[2,192,384]{2,1,0:T(8,128)(2,1)S(1)}, u32[]{:S(2)}, u32[]{:S(2)}) collective-permute-start(bf16[2,192,384]{2,1,0:T(8,128)(2,1)S(1)} %get-tuple-element.104), channel_id=1, source_target_pairs={{0,4},{4,0},{8,12},{12,8},{1,5},{5,1},{9,13},{13,9},{2,6},{6,2},{1... | collective-permute-start | bytes 884744 | tf_op jit(solution)/shard_map/ppermute | solution.py:120
  36.8 1.4 %collective-permute-start.19 = (bf16[2,192,384]{2,1,0:T(8,128)(2,1)S(1)}, bf16[2,192,384]{2,1,0:T(8,128)(2,1)S(1)}, u32[]{:S(2)}, u32[]{:S(2)}) collective-permute-start(bf16[2,192,384]{2,1,0:T(8,128)(2,1)S(1)} %get-tuple-element.101), channel_id=1, source_target_pairs={{0,8},{4,12},{8,0},{12,4},{1,9},{5,13},{9,1},{13,5},{2,10},{6,14},... | collective-permute-start | bytes 884744 | tf_op jit(solution)/shard_map/ppermute | solution.py:120
  38.3 7.6 %collective-permute-done.14.other_ref = bf16[2,384,256]{2,1,0:T(8,128)(2,1)S(1)} collective-permute-done((bf16[2,384,256]{2,1,0:T(8,128)(2,1)S(1)}, bf16[2,384,256]{2,1,0:T(8,128)(2,1)S(1)}, u32[]{:S(2)}, u32[]{:S(2)}) %collective-permute-start.14) | collective-permute-done | bytes 393248 | tf_op jit(solution)/shard_map/ppermute | solution.py:120
  45.9 0.6 middle_grad.1
  46.6 0.5 collective-permute-start.16
  47.1 0.4 output_product.1
  47.6 0.4 collective-permute-done.15.refs_1_.g1
  48.3 0.8 first_backward.1
  49.4 0.8 %collective-permute-done.21.got_b = bf16[2,192,384]{2,1,0:T(8,128)(2,1)S(1)} collective-permute-done((bf16[2,192,384]{2,1,0:T(8,128)(2,1)S(1)}, bf16[2,192,384]{2,1,0:T(8,128)(2,1)S(1)}, u32[]{:S(2)}, u32[]{:S(2)}) %collective-permute-start.21) | collective-permute-done | bytes 294944 | tf_op jit(solution)/shard_map/ppermute | solution.py:120
  50.2 0.5 first_proj.1
  50.7 1.8 %collective-permute-start.22 = (bf16[3,192,384]{2,1,0:T(8,128)(2,1)S(1)}, bf16[3,192,384]{2,1,0:T(8,128)(2,1)S(1)}, u32[]{:S(2)}, u32[]{:S(2)}) collective-permute-start(bf16[3,192,384]{2,1,0:T(8,128)(2,1)S(1)} %get-tuple-element.106), channel_id=1, source_target_pairs={{0,8},{4,12},{8,0},{12,4},{1,9},{5,13},{9,1},{13,5},{2,10},{6,14},... | collective-permute-start | bytes 1327112 | tf_op jit(solution)/shard_map/ppermute | solution.py:120
  52.6 0.5 first_taps.1
  53.1 0.5 collective-permute-start.20
  53.7 1.6 %collective-permute-start.12 = (bf16[384,256]{1,0:T(8,128)(2,1)S(1)}, bf16[384,256]{1,0:T(8,128)(2,1)S(1)}, u32[]{:S(2)}, u32[]{:S(2)}) collective-permute-start(bf16[384,256]{1,0:T(8,128)(2,1)S(1)} %get-tuple-element.87), channel_id=1, source_target_pairs={{0,2},{1,3},{2,0},{3,1},{4,6},{5,7},{6,4},{7,5},{8,10},{9,11},{10,... | collective-permute-start | bytes 589832 | tf_op jit(solution)/shard_map/ppermute | solution.py:120
  55.3 0.3 entry_keep.1.keep_ref
  55.7 0.6 collective-permute-start.18
  56.3 16.5 %collective-permute-done.22.got.got_k = bf16[3,192,384]{2,1,0:T(8,128)(2,1)S(1)} collective-permute-done((bf16[3,192,384]{2,1,0:T(8,128)(2,1)S(1)}, bf16[3,192,384]{2,1,0:T(8,128)(2,1)S(1)}, u32[]{:S(2)}, u32[]{:S(2)}) %collective-permute-start.22) | collective-permute-done | bytes 442400 | tf_op jit(solution)/shard_map/ppermute | solution.py:120
  72.9 0.7 collective-permute-done.20.got.got_p
  73.6 0.9 %collective-permute-start.23 = (bf16[192,384]{1,0:T(8,128)(2,1)S(1)}, bf16[192,384]{1,0:T(8,128)(2,1)S(1)}, u32[]{:S(2)}, u32[]{:S(2)}) collective-permute-start(bf16[192,384]{1,0:T(8,128)(2,1)S(1)} %get-tuple-element.109), channel_id=1, source_target_pairs={{0,8},{4,12},{8,0},{12,4},{1,9},{5,13},{9,1},{13,5},{2,10},{6,14},... | collective-permute-start | bytes 442376 | tf_op jit(solution)/shard_map/ppermute | solution.py:120
  74.5 1.4 %collective-permute-start.24 = (bf16[192,384]{1,0:T(8,128)(2,1)S(1)}, bf16[192,384]{1,0:T(8,128)(2,1)S(1)}, u32[]{:S(2)}, u32[]{:S(2)}) collective-permute-start(bf16[192,384]{1,0:T(8,128)(2,1)S(1)} %get-tuple-element.110), channel_id=1, source_target_pairs={{0,4},{4,0},{8,12},{12,8},{1,5},{5,1},{9,13},{13,9},{2,6},{6,2},{1... | collective-permute-start | bytes 442376 | tf_op jit(solution)/shard_map/ppermute | solution.py:120
  75.9 1.1 %zero_planes.1 = (f32[3,192,384]{2,1,0:T(8,128)}, f32[3,192,384]{2,1,0:T(8,128)}) custom-call(), custom_call_target="tpu_custom_call" | custom-call | tf_op jit(solution)/shard_map/zero_planes/pallas_call | solution.py:427
  77.0 0.7 out.1
  77.7 0.9 %second_total.1 = (f32[3,192,384]{2,1,0:T(8,128)}, f32[192,384]{1,0:T(8,128)}) custom-call(f32[3,192,384]{2,1,0:T(8,128)} %get-tuple-element.113._, f32[1,192,384]{2,1,0:T(8,128)S(1)} %get-tuple-element.114.own_k, f32[1,192,384]{2,1,0:T(8,128)S(1)} %get-tuple-element.115.own_p, ...), custom_call_target="tpu_custom_call", output_to_operand_aliasing={{0}: (0, {})} | custom-call | tf_op jit(solution)/shard_map/second_total/pallas_call | solution.py:409
  78.6 1.0 %entry.1 = bf16[384,256]{1,0:T(8,128)(2,1)} custom-call(bf16[384,256]{1,0:T(8,128)(2,1)S(1)} %get-tuple-element.92.refs_0_.g_ref.g0, bf16[384,256]{1,0:T(8,128)(2,1)S(1)} %get-tuple-element.62.x_ref.x0, f32[384,256]{1,0:T(8,128)S(1)} %get-tuple-element.97.own_ref, bf16[384,256]{1,0:T(8,128)(2,1)S(1)} %collective-permute-done.18.got_ref), custom_call_target="tpu_custom_call" | custom-call | tf_op jit(solution)/shard_map/entry/pallas_call | solution.py:148
  79.6 2.1 %collective-permute-done.23.got_k = bf16[192,384]{1,0:T(8,128)(2,1)S(1)} collective-permute-done((bf16[192,384]{1,0:T(8,128)(2,1)S(1)}, bf16[192,384]{1,0:T(8,128)(2,1)S(1)}, u32[]{:S(2)}, u32[]{:S(2)}) %collective-permute-start.23) | collective-permute-done | bytes 147488 | tf_op jit(solution)/shard_map/ppermute | solution.py:120
  81.7 0.9 %first_total.1 = (f32[3,192,384]{2,1,0:T(8,128)}, f32[192,384]{1,0:T(8,128)}) custom-call(f32[3,192,384]{2,1,0:T(8,128)} %get-tuple-element.99._, f32[1,192,384]{2,1,0:T(8,128)S(1)} %get-tuple-element.108.own_k, f32[1,192,384]{2,1,0:T(8,128)S(1)} %get-tuple-element.107.rest_0_.own_p, ...), custom_call_target="tpu_custom_call", output_to_operand_aliasing={{0}: (0, {})} | custom-call | tf_op jit(solution)/shard_map/first_total/pallas_call | solution.py:409
  (31 shorter events, 2.5 us)
Async XLA Ops:
  0.6 8.9 %collective-permute-start = (bf16[384,256]{1,0:T(8,128)(2,1)}, bf16[384,256]{1,0:T(8,128)(2,1)S(1)}, u32[]{:S(2)}, u32[]{:S(2)}) collective-permute-start(bf16[384,256]{1,0:T(8,128)(2,1)} %x_ref.1), channel_id=1, source_target_pairs={{0,2},{1,3},{2,0},{3,1},{4,6},{5,7},{6,4},{7,5},{8,10},{9,11},{10,... | collective-permute-start | bytes 589832 | tf_op jit(solution)/shard_map/ppermute | solution.py:120
  3.6 9.3 %collective-permute-start.3 = (bf16[2,48,1024]{2,1,0:T(8,128)(2,1)}, bf16[2,48,1024]{2,1,0:T(8,128)(2,1)S(1)}, u32[]{:S(2)}, u32[]{:S(2)}) collective-permute-start(bf16[2,48,1024]{2,1,0:T(8,128)(2,1)} %g_ref.1), channel_id=1, source_target_pairs={{0,2},{1,3},{2,0},{3,1},{4,6},{5,7},{6,4},{7,5},{8,10},{9,11},{10,... | collective-permute-start | bytes 589832 | tf_op jit(solution)/shard_map/ppermute | solution.py:120
  5.8 4.1 %collective-permute-start.1 = (bf16[384,256]{1,0:T(8,128)(2,1)S(1)}, bf16[384,256]{1,0:T(8,128)(2,1)S(1)}, u32[]{:S(2)}, u32[]{:S(2)}) collective-permute-start(bf16[384,256]{1,0:T(8,128)(2,1)S(1)} %get-tuple-element.67.z0), channel_id=1, source_target_pairs={{0,1},{1,0},{2,3},{3,2},{4,5},{5,4},{6,7},{7,6},{8,9},{9,8},{10,11... | collective-permute-start | bytes 589832 | tf_op jit(solution)/shard_map/ppermute | solution.py:120
  9.9 3.1 %collective-permute-start.2 = (bf16[384,256]{1,0:T(8,128)(2,1)S(1)}, bf16[384,256]{1,0:T(8,128)(2,1)S(1)}, u32[]{:S(2)}, u32[]{:S(2)}) collective-permute-start(bf16[384,256]{1,0:T(8,128)(2,1)S(1)} %get-tuple-element.69.z2), channel_id=1, source_target_pairs={{0,1},{1,0},{2,3},{3,2},{4,5},{5,4},{6,7},{7,6},{8,9},{9,8},{10,11... | collective-permute-start | bytes 589832 | tf_op jit(solution)/shard_map/ppermute | solution.py:120
  13.7 1.8 %collective-permute-start.4 = (bf16[2,384,256]{2,1,0:T(8,128)(2,1)S(1)}, bf16[2,384,256]{2,1,0:T(8,128)(2,1)S(1)}, u32[]{:S(2)}, u32[]{:S(2)}) collective-permute-start(bf16[2,384,256]{2,1,0:T(8,128)(2,1)S(1)} %get-tuple-element.72), channel_id=1, source_target_pairs={{0,1},{1,0},{2,3},{3,2},{4,5},{5,4},{6,7},{7,6},{8,9},{9,8},{10,11... | collective-permute-start | bytes 1179656 | tf_op jit(solution)/shard_map/ppermute | solution.py:120
  15.6 14.1 %collective-permute-start.5 = (bf16[2,384,256]{2,1,0:T(8,128)(2,1)S(1)}, bf16[2,384,256]{2,1,0:T(8,128)(2,1)S(1)}, u32[]{:S(2)}, u32[]{:S(2)}) collective-permute-start(bf16[2,384,256]{2,1,0:T(8,128)(2,1)S(1)} %mix_sum.1.chip_ref), channel_id=1, source_target_pairs={{0,2},{1,3},{2,0},{3,1},{4,6},{5,7},{6,4},{7,5},{8,10},{9,11},{10,... | collective-permute-start | bytes 1179656 | tf_op jit(solution)/shard_map/ppermute | solution.py:120
  17.4 4.7 %collective-permute-start.7 = (bf16[2,2,48,256]{3,2,1,0:T(8,128)(2,1)S(1)}, bf16[2,2,48,256]{3,2,1,0:T(8,128)(2,1)S(1)}, u32[]{:S(2)}, u32[]{:S(2)}) collective-permute-start(bf16[2,2,48,256]{3,2,1,0:T(8,128)(2,1)S(1)} %get-tuple-element.76), channel_id=1, source_target_pairs={{0,4},{4,0},{8,12},{12,8},{1,5},{5,1},{9,13},{13,9},{2,6},{6,2},{1... | collective-permute-start | bytes 294920 | tf_op jit(solution)/shard_map/ppermute | solution.py:120
  19.1 10.4 %collective-permute-start.8 = (bf16[2,2,48,256]{3,2,1,0:T(8,128)(2,1)S(1)}, bf16[2,2,48,256]{3,2,1,0:T(8,128)(2,1)S(1)}, u32[]{:S(2)}, u32[]{:S(2)}) collective-permute-start(bf16[2,2,48,256]{3,2,1,0:T(8,128)(2,1)S(1)} %get-tuple-element.77), channel_id=1, source_target_pairs={{0,8},{4,12},{8,0},{12,4},{1,9},{5,13},{9,1},{13,5},{2,10},{6,14},... | collective-permute-start | bytes 294920 | tf_op jit(solution)/shard_map/ppermute | solution.py:120
  21.7 7.9 %collective-permute-start.9 = (bf16[2,2,48,256]{3,2,1,0:T(8,128)(2,1)S(1)}, bf16[2,2,48,256]{3,2,1,0:T(8,128)(2,1)S(1)}, u32[]{:S(2)}, u32[]{:S(2)}) collective-permute-start(bf16[2,2,48,256]{3,2,1,0:T(8,128)(2,1)S(1)} %get-tuple-element.78), channel_id=1, source_target_pairs={{0,12},{4,8},{8,4},{12,0},{1,13},{5,9},{9,5},{13,1},{2,14},{6,10},... | collective-permute-start | bytes 294920 | tf_op jit(solution)/shard_map/ppermute | solution.py:120
  29.6 1.8 %collective-permute-start.10 = (bf16[2,384,256]{2,1,0:T(8,128)(2,1)S(1)}, bf16[2,384,256]{2,1,0:T(8,128)(2,1)S(1)}, u32[]{:S(2)}, u32[]{:S(2)}) collective-permute-start(bf16[2,384,256]{2,1,0:T(8,128)(2,1)S(1)} %bitcast.5), channel_id=1, source_target_pairs={{0,1},{1,0},{2,3},{3,2},{4,5},{5,4},{6,7},{7,6},{8,9},{9,8},{10,11... | collective-permute-start | bytes 1179656 | tf_op jit(solution)/shard_map/ppermute | solution.py:120
  29.8 2.1 %collective-permute-start.6 = (bf16[2,384,256]{2,1,0:T(8,128)(2,1)S(1)}, bf16[2,384,256]{2,1,0:T(8,128)(2,1)S(1)}, u32[]{:S(2)}, u32[]{:S(2)}) collective-permute-start(bf16[2,384,256]{2,1,0:T(8,128)(2,1)S(1)} %middle.1.a_ref.mid_ref), channel_id=1, source_target_pairs={{0,1},{1,0},{2,3},{3,2},{4,5},{5,4},{6,7},{7,6},{8,9},{9,8},{10,11... | collective-permute-start | bytes 1179656 | tf_op jit(solution)/shard_map/ppermute | solution.py:120
  32.8 1.8 %collective-permute-start.13 = (bf16[2,384,256]{2,1,0:T(8,128)(2,1)S(1)}, bf16[2,384,256]{2,1,0:T(8,128)(2,1)S(1)}, u32[]{:S(2)}, u32[]{:S(2)}) collective-permute-start(bf16[2,384,256]{2,1,0:T(8,128)(2,1)S(1)} %get-tuple-element.89), channel_id=1, source_target_pairs={{0,1},{1,0},{2,3},{3,2},{4,5},{5,4},{6,7},{7,6},{8,9},{9,8},{10,11... | collective-permute-start | bytes 1179656 | tf_op jit(solution)/shard_map/ppermute | solution.py:120
  34.6 11.3 %collective-permute-start.14 = (bf16[2,384,256]{2,1,0:T(8,128)(2,1)S(1)}, bf16[2,384,256]{2,1,0:T(8,128)(2,1)S(1)}, u32[]{:S(2)}, u32[]{:S(2)}) collective-permute-start(bf16[2,384,256]{2,1,0:T(8,128)(2,1)S(1)} %squash_sum.1.chip_ref), channel_id=1, source_target_pairs={{0,2},{1,3},{2,0},{3,1},{4,6},{5,7},{6,4},{7,5},{8,10},{9,11},{10,... | collective-permute-start | bytes 1179656 | tf_op jit(solution)/shard_map/ppermute | solution.py:120
  35.2 15.0 %collective-permute-start.21 = (bf16[2,192,384]{2,1,0:T(8,128)(2,1)S(1)}, bf16[2,192,384]{2,1,0:T(8,128)(2,1)S(1)}, u32[]{:S(2)}, u32[]{:S(2)}) collective-permute-start(bf16[2,192,384]{2,1,0:T(8,128)(2,1)S(1)} %get-tuple-element.104), channel_id=1, source_target_pairs={{0,4},{4,0},{8,12},{12,8},{1,5},{5,1},{9,13},{13,9},{2,6},{6,2},{1... | collective-permute-start | bytes 884744 | tf_op jit(solution)/shard_map/ppermute | solution.py:120
  36.8 15.8 %collective-permute-start.19 = (bf16[2,192,384]{2,1,0:T(8,128)(2,1)S(1)}, bf16[2,192,384]{2,1,0:T(8,128)(2,1)S(1)}, u32[]{:S(2)}, u32[]{:S(2)}) collective-permute-start(bf16[2,192,384]{2,1,0:T(8,128)(2,1)S(1)} %get-tuple-element.101), channel_id=1, source_target_pairs={{0,8},{4,12},{8,0},{12,4},{1,9},{5,13},{9,1},{13,5},{2,10},{6,14},... | collective-permute-start | bytes 884744 | tf_op jit(solution)/shard_map/ppermute | solution.py:120
  46.5 1.5 %collective-permute-start.15 = (bf16[384,256]{1,0:T(8,128)(2,1)S(1)}, bf16[384,256]{1,0:T(8,128)(2,1)S(1)}, u32[]{:S(2)}, u32[]{:S(2)}) collective-permute-start(bf16[384,256]{1,0:T(8,128)(2,1)S(1)} %get-tuple-element.92.refs_0_.g_ref.g0), channel_id=1, source_target_pairs={{0,1},{1,0},{2,3},{3,2},{4,5},{5,4},{6,7},{7,6},{8,9},{9,8},{10,11... | collective-permute-start | bytes 589832 | tf_op jit(solution)/shard_map/ppermute | solution.py:120
  46.6 1.7 %collective-permute-start.16 = (bf16[384,256]{1,0:T(8,128)(2,1)S(1)}, bf16[384,256]{1,0:T(8,128)(2,1)S(1)}, u32[]{:S(2)}, u32[]{:S(2)}) collective-permute-start(bf16[384,256]{1,0:T(8,128)(2,1)S(1)} %get-tuple-element.93.refs_2_.g2), channel_id=1, source_target_pairs={{0,1},{1,0},{2,3},{3,2},{4,5},{5,4},{6,7},{7,6},{8,9},{9,8},{10,11... | collective-permute-start | bytes 589832 | tf_op jit(solution)/shard_map/ppermute | solution.py:120
  47.5 6.1 %collective-permute-start.11 = (bf16[2,384,256]{2,1,0:T(8,128)(2,1)S(1)}, bf16[2,384,256]{2,1,0:T(8,128)(2,1)S(1)}, u32[]{:S(2)}, u32[]{:S(2)}) collective-permute-start(bf16[2,384,256]{2,1,0:T(8,128)(2,1)S(1)} %get-tuple-element.85), channel_id=1, source_target_pairs={{0,1},{1,0},{2,3},{3,2},{4,5},{5,4},{6,7},{7,6},{8,9},{9,8},{10,11... | collective-permute-start | bytes 1179656 | tf_op jit(solution)/shard_map/ppermute | solution.py:120
  49.1 6.5 %collective-permute-start.17 = (bf16[2,384,256]{2,1,0:T(8,128)(2,1)S(1)}, bf16[2,384,256]{2,1,0:T(8,128)(2,1)S(1)}, u32[]{:S(2)}, u32[]{:S(2)}) collective-permute-start(bf16[2,384,256]{2,1,0:T(8,128)(2,1)S(1)} %get-tuple-element.96), channel_id=1, source_target_pairs={{0,1},{1,0},{2,3},{3,2},{4,5},{5,4},{6,7},{7,6},{8,9},{9,8},{10,11... | collective-permute-start | bytes 1179656 | tf_op jit(solution)/shard_map/ppermute | solution.py:120
  50.7 22.1 %collective-permute-start.22 = (bf16[3,192,384]{2,1,0:T(8,128)(2,1)S(1)}, bf16[3,192,384]{2,1,0:T(8,128)(2,1)S(1)}, u32[]{:S(2)}, u32[]{:S(2)}) collective-permute-start(bf16[3,192,384]{2,1,0:T(8,128)(2,1)S(1)} %get-tuple-element.106), channel_id=1, source_target_pairs={{0,8},{4,12},{8,0},{12,4},{1,9},{5,13},{9,1},{13,5},{2,10},{6,14},... | collective-permute-start | bytes 1327112 | tf_op jit(solution)/shard_map/ppermute | solution.py:120
  53.1 20.4 %collective-permute-start.20 = (bf16[3,192,384]{2,1,0:T(8,128)(2,1)S(1)}, bf16[3,192,384]{2,1,0:T(8,128)(2,1)S(1)}, u32[]{:S(2)}, u32[]{:S(2)}) collective-permute-start(bf16[3,192,384]{2,1,0:T(8,128)(2,1)S(1)} %get-tuple-element.103), channel_id=1, source_target_pairs={{0,4},{4,0},{8,12},{12,8},{1,5},{5,1},{9,13},{13,9},{2,6},{6,2},{1... | collective-permute-start | bytes 1327112 | tf_op jit(solution)/shard_map/ppermute | solution.py:120
  53.7 23.3 %collective-permute-start.12 = (bf16[384,256]{1,0:T(8,128)(2,1)S(1)}, bf16[384,256]{1,0:T(8,128)(2,1)S(1)}, u32[]{:S(2)}, u32[]{:S(2)}) collective-permute-start(bf16[384,256]{1,0:T(8,128)(2,1)S(1)} %get-tuple-element.87), channel_id=1, source_target_pairs={{0,2},{1,3},{2,0},{3,1},{4,6},{5,7},{6,4},{7,5},{8,10},{9,11},{10,... | collective-permute-start | bytes 589832 | tf_op jit(solution)/shard_map/ppermute | solution.py:120
  55.7 22.9 %collective-permute-start.18 = (bf16[384,256]{1,0:T(8,128)(2,1)S(1)}, bf16[384,256]{1,0:T(8,128)(2,1)S(1)}, u32[]{:S(2)}, u32[]{:S(2)}) collective-permute-start(bf16[384,256]{1,0:T(8,128)(2,1)S(1)} %get-tuple-element.98), channel_id=1, source_target_pairs={{0,2},{1,3},{2,0},{3,1},{4,6},{5,7},{6,4},{7,5},{8,10},{9,11},{10,... | collective-permute-start | bytes 589832 | tf_op jit(solution)/shard_map/ppermute | solution.py:120
  73.6 8.1 %collective-permute-start.23 = (bf16[192,384]{1,0:T(8,128)(2,1)S(1)}, bf16[192,384]{1,0:T(8,128)(2,1)S(1)}, u32[]{:S(2)}, u32[]{:S(2)}) collective-permute-start(bf16[192,384]{1,0:T(8,128)(2,1)S(1)} %get-tuple-element.109), channel_id=1, source_target_pairs={{0,8},{4,12},{8,0},{12,4},{1,9},{5,13},{9,1},{13,5},{2,10},{6,14},... | collective-permute-start | bytes 442376 | tf_op jit(solution)/shard_map/ppermute | solution.py:120
  74.5 7.2 %collective-permute-start.24 = (bf16[192,384]{1,0:T(8,128)(2,1)S(1)}, bf16[192,384]{1,0:T(8,128)(2,1)S(1)}, u32[]{:S(2)}, u32[]{:S(2)}) collective-permute-start(bf16[192,384]{1,0:T(8,128)(2,1)S(1)} %get-tuple-element.110), channel_id=1, source_target_pairs={{0,4},{4,0},{8,12},{12,8},{1,5},{5,1},{9,13},{13,9},{2,6},{6,2},{1... | collective-permute-start | bytes 442376 | tf_op jit(solution)/shard_map/ppermute | solution.py:120

commit v12 on v11

--- a/solution.py
+++ b/solution.py
@@ -523,7 +523,7 @@
     )
     got_k = swap(send_k, "ctx", 1)
     got = swap(send, "mp", 1)
-    e_own, e_send = last_sum(keep, got, "entry_sum")
+    e_own, e_send = last_sum(keep, got, "entry_sum", (keep_ak,))
     e_got = swap(e_send, "mp", 2)
 
     def entry_body(g_ref, x_ref, own_ref, got_ref, out_ref):

time: 82.7 us -> 82.7 us (level)
  no operation moved by 1% of the time
where the time goes in v12:
time: 82.7 us; the launch traced here: 82.6 us
  waiting for transfers between devices  45.7 us (55%)
  starting transfers between devices  21.9 us (26%)
  Pallas kernels  14.1 us (17%)
  between operations  0.88 us (1%)
    ppermute x25, waiting for transfers between devices, swap(): return lax.ppermute(value, axis, [(i, i ^ bits) for i in range(size)])  45.7 us
    ppermute x25, starting transfers between devices, swap(): return lax.ppermute(value, axis, [(i, i ^ bits) for i in range(size)])  21.9 us
    pallas_call x25, Pallas kernels, call(): pl.pallas_call(body, out_shape=[struct(s, d) for s, d in outs], in_specs=...  9.58 us
    pallas_call x1, Pallas kernels, fast_shards(): pl.pallas_call(load_body, out_shape=[pltpu.VMEM((rows, bins), BF16)] + [p...  1.79 us
    pallas_call x2, Pallas kernels, total(): pl.pallas_call(functools.partial(total_body, place), out_shape=[jax.Shape...  1.71 us
  transfers between devices with their start and end apart: 25, of which 15 were waited for; matrix products, arithmetic and copies ran while one was open for 0% of the time, Pallas kernels for 14%

profile of v12, /device:TPU:0, one launch (start us, length us, event | category | flops | bytes accessed | tf_op | source)
XLA Modules:
  0.0 82.6 jit_solution(4509002011517023057)
XLA Ops:
  0.6 3.0 %collective-permute-start = (bf16[384,256]{1,0:T(8,128)(2,1)}, bf16[384,256]{1,0:T(8,128)(2,1)S(1)}, u32[]{:S(2)}, u32[]{:S(2)}) collective-permute-start(bf16[384,256]{1,0:T(8,128)(2,1)} %x_ref.1), channel_id=1, source_target_pairs={{0,2},{1,3},{2,0},{3,1},{4,6},{5,7},{6,4},{7,5},{8,10},{9,11},{10,... | collective-permute-start | bytes 589832 | tf_op jit(solution)/shard_map/ppermute | solution.py:120
  3.7 1.8 %load.1 = (bf16[384,256]{1,0:T(8,128)(2,1)S(1)}, bf16[192,1536]{1,0:T(8,128)(2,1)S(1)}, bf16[192,1536]{1,0:T(8,128)(2,1)S(1)}, bf16[192,1536]{1,0:T(8,128)(2,1)S...) custom-call(bf16[384,256]{1,0:T(8,128)(2,1)} %x_ref.1, bf16[3,192,1536]{2,1,0:T(8,128)(2,1)} %ta.1, ...), custom_call_target="tpu_custom_call" | custom-call | tf_op jit(solution)/shard_map/load/pallas_call | solution.py:183
  5.5 0.3 near_forward.1
  5.9 3.7 %collective-permute-done.x_ref.x2 = bf16[384,256]{1,0:T(8,128)(2,1)S(1)} collective-permute-done((bf16[384,256]{1,0:T(8,128)(2,1)}, bf16[384,256]{1,0:T(8,128)(2,1)S(1)}, u32[]{:S(2)}, u32[]{:S(2)}) %collective-permute-start) | collective-permute-done | bytes 196640 | tf_op jit(solution)/shard_map/ppermute | solution.py:120
  9.6 0.3 far_forward.1
  10.0 3.0 %collective-permute-done.3._.far_ref = bf16[2,48,1024]{2,1,0:T(8,128)(2,1)S(1)} collective-permute-done((bf16[2,48,1024]{2,1,0:T(8,128)(2,1)}, bf16[2,48,1024]{2,1,0:T(8,128)(2,1)S(1)}, u32[]{:S(2)}, u32[]{:S(2)}) %collective-permute-start.3) | collective-permute-done | bytes 196640 | tf_op jit(solution)/shard_map/ppermute | solution.py:120
  13.0 0.8 first_forward.1
  13.8 0.3 mix_keep.1.keep_ref
  14.1 1.4 %collective-permute-done.4.got_ref = bf16[2,384,256]{2,1,0:T(8,128)(2,1)S(1)} collective-permute-done((bf16[2,384,256]{2,1,0:T(8,128)(2,1)S(1)}, bf16[2,384,256]{2,1,0:T(8,128)(2,1)S(1)}, u32[]{:S(2)}, u32[]{:S(2)}) %collective-permute-start.4) | collective-permute-done | bytes 393248 | tf_op jit(solution)/shard_map/ppermute | solution.py:120
  15.6 1.8 %collective-permute-start.5 = (bf16[2,384,256]{2,1,0:T(8,128)(2,1)S(1)}, bf16[2,384,256]{2,1,0:T(8,128)(2,1)S(1)}, u32[]{:S(2)}, u32[]{:S(2)}) collective-permute-start(bf16[2,384,256]{2,1,0:T(8,128)(2,1)S(1)} %mix_sum.1.chip_ref), channel_id=1, source_target_pairs={{0,2},{1,3},{2,0},{3,1},{4,6},{5,7},{6,4},{7,5},{8,10},{9,11},{10,... | collective-permute-start | bytes 1179656 | tf_op jit(solution)/shard_map/ppermute | solution.py:120
  17.4 1.6 %collective-permute-start.7 = (bf16[2,2,48,256]{3,2,1,0:T(8,128)(2,1)S(1)}, bf16[2,2,48,256]{3,2,1,0:T(8,128)(2,1)S(1)}, u32[]{:S(2)}, u32[]{:S(2)}) collective-permute-start(bf16[2,2,48,256]{3,2,1,0:T(8,128)(2,1)S(1)} %get-tuple-element.76), channel_id=1, source_target_pairs={{0,4},{4,0},{8,12},{12,8},{1,5},{5,1},{9,13},{13,9},{2,6},{6,2},{1... | collective-permute-start | bytes 294920 | tf_op jit(solution)/shard_map/ppermute | solution.py:120
  19.1 2.6 %collective-permute-start.8 = (bf16[2,2,48,256]{3,2,1,0:T(8,128)(2,1)S(1)}, bf16[2,2,48,256]{3,2,1,0:T(8,128)(2,1)S(1)}, u32[]{:S(2)}, u32[]{:S(2)}) collective-permute-start(bf16[2,2,48,256]{3,2,1,0:T(8,128)(2,1)S(1)} %get-tuple-element.77), channel_id=1, source_target_pairs={{0,8},{4,12},{8,0},{12,4},{1,9},{5,13},{9,1},{13,5},{2,10},{6,14},... | collective-permute-start | bytes 294920 | tf_op jit(solution)/shard_map/ppermute | solution.py:120
  22.1 7.4 %collective-permute-done.8.refs_2_ = bf16[2,2,48,256]{3,2,1,0:T(8,128)(2,1)S(1)} collective-permute-done((bf16[2,2,48,256]{3,2,1,0:T(8,128)(2,1)S(1)}, bf16[2,2,48,256]{3,2,1,0:T(8,128)(2,1)S(1)}, u32[]{:S(2)}, u32[]{:S(2)}) %collective-permute-start.8) | collective-permute-done | bytes 98336 | tf_op jit(solution)/shard_map/ppermute | solution.py:120
  29.8 0.5 collective-permute-start.6
  30.4 0.5 own_block.1
  30.9 0.5 collective-permute-done.10.g_ref.gb_ref
  31.4 0.6 collective-permute-done.6.b_ref
  31.9 0.8 second_block.1
  33.0 0.3 squash_keep.1.keep_ref
  33.3 0.7 second_weights.1
  34.0 0.5 collective-permute-done.13.got_ref
  34.6 0.6 collective-permute-start.14
  35.2 1.6 %collective-permute-start.21 = (bf16[2,192,384]{2,1,0:T(8,128)(2,1)S(1)}, bf16[2,192,384]{2,1,0:T(8,128)(2,1)S(1)}, u32[]{:S(2)}, u32[]{:S(2)}) collective-permute-start(bf16[2,192,384]{2,1,0:T(8,128)(2,1)S(1)} %get-tuple-element.104), channel_id=1, source_target_pairs={{0,4},{4,0},{8,12},{12,8},{1,5},{5,1},{9,13},{13,9},{2,6},{6,2},{1... | collective-permute-start | bytes 884744 | tf_op jit(solution)/shard_map/ppermute | solution.py:120
  36.8 1.4 %collective-permute-start.18 = (bf16[2,192,384]{2,1,0:T(8,128)(2,1)S(1)}, bf16[2,192,384]{2,1,0:T(8,128)(2,1)S(1)}, u32[]{:S(2)}, u32[]{:S(2)}) collective-permute-start(bf16[2,192,384]{2,1,0:T(8,128)(2,1)S(1)} %get-tuple-element.98), channel_id=1, source_target_pairs={{0,8},{4,12},{8,0},{12,4},{1,9},{5,13},{9,1},{13,5},{2,10},{6,14},... | collective-permute-start | bytes 884744 | tf_op jit(solution)/shard_map/ppermute | solution.py:120
  38.3 7.6 %collective-permute-done.14.other_ref = bf16[2,384,256]{2,1,0:T(8,128)(2,1)S(1)} collective-permute-done((bf16[2,384,256]{2,1,0:T(8,128)(2,1)S(1)}, bf16[2,384,256]{2,1,0:T(8,128)(2,1)S(1)}, u32[]{:S(2)}, u32[]{:S(2)}) %collective-permute-start.14) | collective-permute-done | bytes 393248 | tf_op jit(solution)/shard_map/ppermute | solution.py:120
  45.9 0.6 middle_grad.1
  46.6 0.5 collective-permute-start.16
  47.1 0.4 output_product.1
  47.6 0.4 collective-permute-done.15.refs_1_.g1
  48.3 0.8 first_backward.1
  49.4 0.8 %collective-permute-done.21.got_b = bf16[2,192,384]{2,1,0:T(8,128)(2,1)S(1)} collective-permute-done((bf16[2,192,384]{2,1,0:T(8,128)(2,1)S(1)}, bf16[2,192,384]{2,1,0:T(8,128)(2,1)S(1)}, u32[]{:S(2)}, u32[]{:S(2)}) %collective-permute-start.21) | collective-permute-done | bytes 294944 | tf_op jit(solution)/shard_map/ppermute | solution.py:120
  50.2 0.5 first_proj.1
  50.7 1.8 %collective-permute-start.22 = (bf16[3,192,384]{2,1,0:T(8,128)(2,1)S(1)}, bf16[3,192,384]{2,1,0:T(8,128)(2,1)S(1)}, u32[]{:S(2)}, u32[]{:S(2)}) collective-permute-start(bf16[3,192,384]{2,1,0:T(8,128)(2,1)S(1)} %get-tuple-element.106), channel_id=1, source_target_pairs={{0,8},{4,12},{8,0},{12,4},{1,9},{5,13},{9,1},{13,5},{2,10},{6,14},... | collective-permute-start | bytes 1327112 | tf_op jit(solution)/shard_map/ppermute | solution.py:120
  52.6 0.5 first_taps.1
  53.1 0.5 collective-permute-start.20
  53.7 1.6 %collective-permute-start.12 = (bf16[384,256]{1,0:T(8,128)(2,1)S(1)}, bf16[384,256]{1,0:T(8,128)(2,1)S(1)}, u32[]{:S(2)}, u32[]{:S(2)}) collective-permute-start(bf16[384,256]{1,0:T(8,128)(2,1)S(1)} %get-tuple-element.87), channel_id=1, source_target_pairs={{0,2},{1,3},{2,0},{3,1},{4,6},{5,7},{6,4},{7,5},{8,10},{9,11},{10,... | collective-permute-start | bytes 589832 | tf_op jit(solution)/shard_map/ppermute | solution.py:120
  55.3 0.3 entry_keep.1.keep_ref
  55.7 0.6 collective-permute-start.19
  56.3 16.5 %collective-permute-done.22.got.got_k = bf16[3,192,384]{2,1,0:T(8,128)(2,1)S(1)} collective-permute-done((bf16[3,192,384]{2,1,0:T(8,128)(2,1)S(1)}, bf16[3,192,384]{2,1,0:T(8,128)(2,1)S(1)}, u32[]{:S(2)}, u32[]{:S(2)}) %collective-permute-start.22) | collective-permute-done | bytes 442400 | tf_op jit(solution)/shard_map/ppermute | solution.py:120
  72.9 0.7 collective-permute-done.20.got.got_p
  73.6 0.9 %collective-permute-start.23 = (bf16[192,384]{1,0:T(8,128)(2,1)S(1)}, bf16[192,384]{1,0:T(8,128)(2,1)S(1)}, u32[]{:S(2)}, u32[]{:S(2)}) collective-permute-start(bf16[192,384]{1,0:T(8,128)(2,1)S(1)} %get-tuple-element.109), channel_id=1, source_target_pairs={{0,8},{4,12},{8,0},{12,4},{1,9},{5,13},{9,1},{13,5},{2,10},{6,14},... | collective-permute-start | bytes 442376 | tf_op jit(solution)/shard_map/ppermute | solution.py:120
  74.5 1.4 %collective-permute-start.24 = (bf16[192,384]{1,0:T(8,128)(2,1)S(1)}, bf16[192,384]{1,0:T(8,128)(2,1)S(1)}, u32[]{:S(2)}, u32[]{:S(2)}) collective-permute-start(bf16[192,384]{1,0:T(8,128)(2,1)S(1)} %get-tuple-element.110), channel_id=1, source_target_pairs={{0,4},{4,0},{8,12},{12,8},{1,5},{5,1},{9,13},{13,9},{2,6},{6,2},{1... | collective-permute-start | bytes 442376 | tf_op jit(solution)/shard_map/ppermute | solution.py:120
  75.9 1.1 %zero_planes.1 = (f32[3,192,384]{2,1,0:T(8,128)}, f32[3,192,384]{2,1,0:T(8,128)}) custom-call(), custom_call_target="tpu_custom_call" | custom-call | tf_op jit(solution)/shard_map/zero_planes/pallas_call | solution.py:427
  77.0 0.7 out.1
  77.7 0.9 %second_total.1 = (f32[3,192,384]{2,1,0:T(8,128)}, f32[192,384]{1,0:T(8,128)}) custom-call(f32[3,192,384]{2,1,0:T(8,128)} %get-tuple-element.113._, f32[1,192,384]{2,1,0:T(8,128)S(1)} %get-tuple-element.114.own_k, f32[1,192,384]{2,1,0:T(8,128)S(1)} %get-tuple-element.115.own_p, ...), custom_call_target="tpu_custom_call", output_to_operand_aliasing={{0}: (0, {})} | custom-call | tf_op jit(solution)/shard_map/second_total/pallas_call | solution.py:409
  78.6 1.0 %entry.1 = bf16[384,256]{1,0:T(8,128)(2,1)} custom-call(bf16[384,256]{1,0:T(8,128)(2,1)S(1)} %get-tuple-element.92.refs_0_.g_ref.g0, bf16[384,256]{1,0:T(8,128)(2,1)S(1)} %get-tuple-element.62.x_ref.x0, f32[384,256]{1,0:T(8,128)S(1)} %get-tuple-element.100.own_ref, bf16[384,256]{1,0:T(8,128)(2,1)S(1)} %collective-permute-done.19.got_ref), custom_call_target="tpu_custom_call" | custom-call | tf_op jit(solution)/shard_map/entry/pallas_call | solution.py:148
  79.6 2.1 %collective-permute-done.23.got_k = bf16[192,384]{1,0:T(8,128)(2,1)S(1)} collective-permute-done((bf16[192,384]{1,0:T(8,128)(2,1)S(1)}, bf16[192,384]{1,0:T(8,128)(2,1)S(1)}, u32[]{:S(2)}, u32[]{:S(2)}) %collective-permute-start.23) | collective-permute-done | bytes 147488 | tf_op jit(solution)/shard_map/ppermute | solution.py:120
  81.7 0.9 %first_total.1 = (f32[3,192,384]{2,1,0:T(8,128)}, f32[192,384]{1,0:T(8,128)}) custom-call(f32[3,192,384]{2,1,0:T(8,128)} %get-tuple-element.102._, f32[1,192,384]{2,1,0:T(8,128)S(1)} %get-tuple-element.108.own_k, f32[1,192,384]{2,1,0:T(8,128)S(1)} %get-tuple-element.107.rest_0_.own_p, ...), custom_call_target="tpu_custom_call", output_to_operand_aliasing={{0}: (0, {})} | custom-call | tf_op jit(solution)/shard_map/first_total/pallas_call | solution.py:409
  (31 shorter events, 2.5 us)
Async XLA Ops:
  0.6 8.9 %collective-permute-start = (bf16[384,256]{1,0:T(8,128)(2,1)}, bf16[384,256]{1,0:T(8,128)(2,1)S(1)}, u32[]{:S(2)}, u32[]{:S(2)}) collective-permute-start(bf16[384,256]{1,0:T(8,128)(2,1)} %x_ref.1), channel_id=1, source_target_pairs={{0,2},{1,3},{2,0},{3,1},{4,6},{5,7},{6,4},{7,5},{8,10},{9,11},{10,... | collective-permute-start | bytes 589832 | tf_op jit(solution)/shard_map/ppermute | solution.py:120
  3.6 9.3 %collective-permute-start.3 = (bf16[2,48,1024]{2,1,0:T(8,128)(2,1)}, bf16[2,48,1024]{2,1,0:T(8,128)(2,1)S(1)}, u32[]{:S(2)}, u32[]{:S(2)}) collective-permute-start(bf16[2,48,1024]{2,1,0:T(8,128)(2,1)} %g_ref.1), channel_id=1, source_target_pairs={{0,2},{1,3},{2,0},{3,1},{4,6},{5,7},{6,4},{7,5},{8,10},{9,11},{10,... | collective-permute-start | bytes 589832 | tf_op jit(solution)/shard_map/ppermute | solution.py:120
  5.8 4.1 %collective-permute-start.1 = (bf16[384,256]{1,0:T(8,128)(2,1)S(1)}, bf16[384,256]{1,0:T(8,128)(2,1)S(1)}, u32[]{:S(2)}, u32[]{:S(2)}) collective-permute-start(bf16[384,256]{1,0:T(8,128)(2,1)S(1)} %get-tuple-element.67.z0), channel_id=1, source_target_pairs={{0,1},{1,0},{2,3},{3,2},{4,5},{5,4},{6,7},{7,6},{8,9},{9,8},{10,11... | collective-permute-start | bytes 589832 | tf_op jit(solution)/shard_map/ppermute | solution.py:120
  9.9 3.1 %collective-permute-start.2 = (bf16[384,256]{1,0:T(8,128)(2,1)S(1)}, bf16[384,256]{1,0:T(8,128)(2,1)S(1)}, u32[]{:S(2)}, u32[]{:S(2)}) collective-permute-start(bf16[384,256]{1,0:T(8,128)(2,1)S(1)} %get-tuple-element.69.z2), channel_id=1, source_target_pairs={{0,1},{1,0},{2,3},{3,2},{4,5},{5,4},{6,7},{7,6},{8,9},{9,8},{10,11... | collective-permute-start | bytes 589832 | tf_op jit(solution)/shard_map/ppermute | solution.py:120
  13.7 1.8 %collective-permute-start.4 = (bf16[2,384,256]{2,1,0:T(8,128)(2,1)S(1)}, bf16[2,384,256]{2,1,0:T(8,128)(2,1)S(1)}, u32[]{:S(2)}, u32[]{:S(2)}) collective-permute-start(bf16[2,384,256]{2,1,0:T(8,128)(2,1)S(1)} %get-tuple-element.72), channel_id=1, source_target_pairs={{0,1},{1,0},{2,3},{3,2},{4,5},{5,4},{6,7},{7,6},{8,9},{9,8},{10,11... | collective-permute-start | bytes 1179656 | tf_op jit(solution)/shard_map/ppermute | solution.py:120
  15.6 14.1 %collective-permute-start.5 = (bf16[2,384,256]{2,1,0:T(8,128)(2,1)S(1)}, bf16[2,384,256]{2,1,0:T(8,128)(2,1)S(1)}, u32[]{:S(2)}, u32[]{:S(2)}) collective-permute-start(bf16[2,384,256]{2,1,0:T(8,128)(2,1)S(1)} %mix_sum.1.chip_ref), channel_id=1, source_target_pairs={{0,2},{1,3},{2,0},{3,1},{4,6},{5,7},{6,4},{7,5},{8,10},{9,11},{10,... | collective-permute-start | bytes 1179656 | tf_op jit(solution)/shard_map/ppermute | solution.py:120
  17.4 4.7 %collective-permute-start.7 = (bf16[2,2,48,256]{3,2,1,0:T(8,128)(2,1)S(1)}, bf16[2,2,48,256]{3,2,1,0:T(8,128)(2,1)S(1)}, u32[]{:S(2)}, u32[]{:S(2)}) collective-permute-start(bf16[2,2,48,256]{3,2,1,0:T(8,128)(2,1)S(1)} %get-tuple-element.76), channel_id=1, source_target_pairs={{0,4},{4,0},{8,12},{12,8},{1,5},{5,1},{9,13},{13,9},{2,6},{6,2},{1... | collective-permute-start | bytes 294920 | tf_op jit(solution)/shard_map/ppermute | solution.py:120
  19.1 10.4 %collective-permute-start.8 = (bf16[2,2,48,256]{3,2,1,0:T(8,128)(2,1)S(1)}, bf16[2,2,48,256]{3,2,1,0:T(8,128)(2,1)S(1)}, u32[]{:S(2)}, u32[]{:S(2)}) collective-permute-start(bf16[2,2,48,256]{3,2,1,0:T(8,128)(2,1)S(1)} %get-tuple-element.77), channel_id=1, source_target_pairs={{0,8},{4,12},{8,0},{12,4},{1,9},{5,13},{9,1},{13,5},{2,10},{6,14},... | collective-permute-start | bytes 294920 | tf_op jit(solution)/shard_map/ppermute | solution.py:120
  21.7 7.9 %collective-permute-start.9 = (bf16[2,2,48,256]{3,2,1,0:T(8,128)(2,1)S(1)}, bf16[2,2,48,256]{3,2,1,0:T(8,128)(2,1)S(1)}, u32[]{:S(2)}, u32[]{:S(2)}) collective-permute-start(bf16[2,2,48,256]{3,2,1,0:T(8,128)(2,1)S(1)} %get-tuple-element.78), channel_id=1, source_target_pairs={{0,12},{4,8},{8,4},{12,0},{1,13},{5,9},{9,5},{13,1},{2,14},{6,10},... | collective-permute-start | bytes 294920 | tf_op jit(solution)/shard_map/ppermute | solution.py:120
  29.6 1.8 %collective-permute-start.10 = (bf16[2,384,256]{2,1,0:T(8,128)(2,1)S(1)}, bf16[2,384,256]{2,1,0:T(8,128)(2,1)S(1)}, u32[]{:S(2)}, u32[]{:S(2)}) collective-permute-start(bf16[2,384,256]{2,1,0:T(8,128)(2,1)S(1)} %bitcast.5), channel_id=1, source_target_pairs={{0,1},{1,0},{2,3},{3,2},{4,5},{5,4},{6,7},{7,6},{8,9},{9,8},{10,11... | collective-permute-start | bytes 1179656 | tf_op jit(solution)/shard_map/ppermute | solution.py:120
  29.8 2.1 %collective-permute-start.6 = (bf16[2,384,256]{2,1,0:T(8,128)(2,1)S(1)}, bf16[2,384,256]{2,1,0:T(8,128)(2,1)S(1)}, u32[]{:S(2)}, u32[]{:S(2)}) collective-permute-start(bf16[2,384,256]{2,1,0:T(8,128)(2,1)S(1)} %middle.1.a_ref.mid_ref), channel_id=1, source_target_pairs={{0,1},{1,0},{2,3},{3,2},{4,5},{5,4},{6,7},{7,6},{8,9},{9,8},{10,11... | collective-permute-start | bytes 1179656 | tf_op jit(solution)/shard_map/ppermute | solution.py:120
  32.8 1.8 %collective-permute-start.13 = (bf16[2,384,256]{2,1,0:T(8,128)(2,1)S(1)}, bf16[2,384,256]{2,1,0:T(8,128)(2,1)S(1)}, u32[]{:S(2)}, u32[]{:S(2)}) collective-permute-start(bf16[2,384,256]{2,1,0:T(8,128)(2,1)S(1)} %get-tuple-element.89), channel_id=1, source_target_pairs={{0,1},{1,0},{2,3},{3,2},{4,5},{5,4},{6,7},{7,6},{8,9},{9,8},{10,11... | collective-permute-start | bytes 1179656 | tf_op jit(solution)/shard_map/ppermute | solution.py:120
  34.6 11.3 %collective-permute-start.14 = (bf16[2,384,256]{2,1,0:T(8,128)(2,1)S(1)}, bf16[2,384,256]{2,1,0:T(8,128)(2,1)S(1)}, u32[]{:S(2)}, u32[]{:S(2)}) collective-permute-start(bf16[2,384,256]{2,1,0:T(8,128)(2,1)S(1)} %squash_sum.1.chip_ref), channel_id=1, source_target_pairs={{0,2},{1,3},{2,0},{3,1},{4,6},{5,7},{6,4},{7,5},{8,10},{9,11},{10,... | collective-permute-start | bytes 1179656 | tf_op jit(solution)/shard_map/ppermute | solution.py:120
  35.2 15.0 %collective-permute-start.21 = (bf16[2,192,384]{2,1,0:T(8,128)(2,1)S(1)}, bf16[2,192,384]{2,1,0:T(8,128)(2,1)S(1)}, u32[]{:S(2)}, u32[]{:S(2)}) collective-permute-start(bf16[2,192,384]{2,1,0:T(8,128)(2,1)S(1)} %get-tuple-element.104), channel_id=1, source_target_pairs={{0,4},{4,0},{8,12},{12,8},{1,5},{5,1},{9,13},{13,9},{2,6},{6,2},{1... | collective-permute-start | bytes 884744 | tf_op jit(solution)/shard_map/ppermute | solution.py:120
  36.8 15.8 %collective-permute-start.18 = (bf16[2,192,384]{2,1,0:T(8,128)(2,1)S(1)}, bf16[2,192,384]{2,1,0:T(8,128)(2,1)S(1)}, u32[]{:S(2)}, u32[]{:S(2)}) collective-permute-start(bf16[2,192,384]{2,1,0:T(8,128)(2,1)S(1)} %get-tuple-element.98), channel_id=1, source_target_pairs={{0,8},{4,12},{8,0},{12,4},{1,9},{5,13},{9,1},{13,5},{2,10},{6,14},... | collective-permute-start | bytes 884744 | tf_op jit(solution)/shard_map/ppermute | solution.py:120
  46.5 1.5 %collective-permute-start.15 = (bf16[384,256]{1,0:T(8,128)(2,1)S(1)}, bf16[384,256]{1,0:T(8,128)(2,1)S(1)}, u32[]{:S(2)}, u32[]{:S(2)}) collective-permute-start(bf16[384,256]{1,0:T(8,128)(2,1)S(1)} %get-tuple-element.92.refs_0_.g_ref.g0), channel_id=1, source_target_pairs={{0,1},{1,0},{2,3},{3,2},{4,5},{5,4},{6,7},{7,6},{8,9},{9,8},{10,11... | collective-permute-start | bytes 589832 | tf_op jit(solution)/shard_map/ppermute | solution.py:120
  46.6 1.7 %collective-permute-start.16 = (bf16[384,256]{1,0:T(8,128)(2,1)S(1)}, bf16[384,256]{1,0:T(8,128)(2,1)S(1)}, u32[]{:S(2)}, u32[]{:S(2)}) collective-permute-start(bf16[384,256]{1,0:T(8,128)(2,1)S(1)} %get-tuple-element.93.refs_2_.g2), channel_id=1, source_target_pairs={{0,1},{1,0},{2,3},{3,2},{4,5},{5,4},{6,7},{7,6},{8,9},{9,8},{10,11... | collective-permute-start | bytes 589832 | tf_op jit(solution)/shard_map/ppermute | solution.py:120
  47.5 6.1 %collective-permute-start.11 = (bf16[2,384,256]{2,1,0:T(8,128)(2,1)S(1)}, bf16[2,384,256]{2,1,0:T(8,128)(2,1)S(1)}, u32[]{:S(2)}, u32[]{:S(2)}) collective-permute-start(bf16[2,384,256]{2,1,0:T(8,128)(2,1)S(1)} %get-tuple-element.85), channel_id=1, source_target_pairs={{0,1},{1,0},{2,3},{3,2},{4,5},{5,4},{6,7},{7,6},{8,9},{9,8},{10,11... | collective-permute-start | bytes 1179656 | tf_op jit(solution)/shard_map/ppermute | solution.py:120
  49.1 6.5 %collective-permute-start.17 = (bf16[2,384,256]{2,1,0:T(8,128)(2,1)S(1)}, bf16[2,384,256]{2,1,0:T(8,128)(2,1)S(1)}, u32[]{:S(2)}, u32[]{:S(2)}) collective-permute-start(bf16[2,384,256]{2,1,0:T(8,128)(2,1)S(1)} %get-tuple-element.96), channel_id=1, source_target_pairs={{0,1},{1,0},{2,3},{3,2},{4,5},{5,4},{6,7},{7,6},{8,9},{9,8},{10,11... | collective-permute-start | bytes 1179656 | tf_op jit(solution)/shard_map/ppermute | solution.py:120
  50.7 22.1 %collective-permute-start.22 = (bf16[3,192,384]{2,1,0:T(8,128)(2,1)S(1)}, bf16[3,192,384]{2,1,0:T(8,128)(2,1)S(1)}, u32[]{:S(2)}, u32[]{:S(2)}) collective-permute-start(bf16[3,192,384]{2,1,0:T(8,128)(2,1)S(1)} %get-tuple-element.106), channel_id=1, source_target_pairs={{0,8},{4,12},{8,0},{12,4},{1,9},{5,13},{9,1},{13,5},{2,10},{6,14},... | collective-permute-start | bytes 1327112 | tf_op jit(solution)/shard_map/ppermute | solution.py:120
  53.1 20.4 %collective-permute-start.20 = (bf16[3,192,384]{2,1,0:T(8,128)(2,1)S(1)}, bf16[3,192,384]{2,1,0:T(8,128)(2,1)S(1)}, u32[]{:S(2)}, u32[]{:S(2)}) collective-permute-start(bf16[3,192,384]{2,1,0:T(8,128)(2,1)S(1)} %get-tuple-element.103), channel_id=1, source_target_pairs={{0,4},{4,0},{8,12},{12,8},{1,5},{5,1},{9,13},{13,9},{2,6},{6,2},{1... | collective-permute-start | bytes 1327112 | tf_op jit(solution)/shard_map/ppermute | solution.py:120
  53.7 23.3 %collective-permute-start.12 = (bf16[384,256]{1,0:T(8,128)(2,1)S(1)}, bf16[384,256]{1,0:T(8,128)(2,1)S(1)}, u32[]{:S(2)}, u32[]{:S(2)}) collective-permute-start(bf16[384,256]{1,0:T(8,128)(2,1)S(1)} %get-tuple-element.87), channel_id=1, source_target_pairs={{0,2},{1,3},{2,0},{3,1},{4,6},{5,7},{6,4},{7,5},{8,10},{9,11},{10,... | collective-permute-start | bytes 589832 | tf_op jit(solution)/shard_map/ppermute | solution.py:120
  55.7 22.9 %collective-permute-start.19 = (bf16[384,256]{1,0:T(8,128)(2,1)S(1)}, bf16[384,256]{1,0:T(8,128)(2,1)S(1)}, u32[]{:S(2)}, u32[]{:S(2)}) collective-permute-start(bf16[384,256]{1,0:T(8,128)(2,1)S(1)} %get-tuple-element.101), channel_id=1, source_target_pairs={{0,2},{1,3},{2,0},{3,1},{4,6},{5,7},{6,4},{7,5},{8,10},{9,11},{10,... | collective-permute-start | bytes 589832 | tf_op jit(solution)/shard_map/ppermute | solution.py:120
  73.6 8.1 %collective-permute-start.23 = (bf16[192,384]{1,0:T(8,128)(2,1)S(1)}, bf16[192,384]{1,0:T(8,128)(2,1)S(1)}, u32[]{:S(2)}, u32[]{:S(2)}) collective-permute-start(bf16[192,384]{1,0:T(8,128)(2,1)S(1)} %get-tuple-element.109), channel_id=1, source_target_pairs={{0,8},{4,12},{8,0},{12,4},{1,9},{5,13},{9,1},{13,5},{2,10},{6,14},... | collective-permute-start | bytes 442376 | tf_op jit(solution)/shard_map/ppermute | solution.py:120
  74.5 7.2 %collective-permute-start.24 = (bf16[192,384]{1,0:T(8,128)(2,1)S(1)}, bf16[192,384]{1,0:T(8,128)(2,1)S(1)}, u32[]{:S(2)}, u32[]{:S(2)}) collective-permute-start(bf16[192,384]{1,0:T(8,128)(2,1)S(1)} %get-tuple-element.110), channel_id=1, source_target_pairs={{0,4},{4,0},{8,12},{12,8},{1,5},{5,1},{9,13},{13,9},{2,6},{6,2},{1... | collective-permute-start | bytes 442376 | tf_op jit(solution)/shard_map/ppermute | solution.py:120
